TPU v7x, 32 devices: a whole 2x2x4 slice. The times are simulated.
32 devices in a mesh: tiles: 8 (over z, x), chan: 4 (over y, core).
Axes of the slice: x: 2, y: 2, z: 4, core: 2. Of those that a mesh axis runs over, the one named last changes fastest.
Arguments:
- features: bfloat16 [512, 64, 256], P('tiles'), may hold values from -6 to 6
- weights: bfloat16 [27, 256, 256], P(None, None, 'chan')
- gain: bfloat16 [256], P('chan'), may hold values from 0.099609375 to 1.8984375
- rulebook: int32 [6144, 4], P('tiles'), may hold values from 0 to 191, as said below
- recv_list: int32 [8, 128], P('tiles'), may hold values from 0 to 63, as said below
- coarse_send: int32 [8, 8], P('tiles'), may hold values from 0 to 7, as said below
- coarse_place: int32 [8, 8], P('tiles'), may hold values from 0 to 7, as said below
Outputs:
- skip_features: bfloat16 [512, 64, 256], P('tiles', None, 'chan')
- coarse_features: bfloat16 [64, 64, 256], P('tiles', None, 'chan')
Inputs may be any that keep to these rules, and one draw needn't show every extreme that they name: `rulebook`: Columns: input tile 0 to 63 of the device; kernel offset 0 to 26, or 27 for an empty row; direction 0 to 26, the input tile's place relative to the output tile, along each dimension 0 or equal to the kernel offset's nonzero component; target below 64 a tile of the device, else slot s = target - 64 for device d + dist(s // 16), which always exists. Empty rows have 0 in the other columns and direction 13. Each device has 192 or more live rows, some device none empty; every slot toward an existing device is named by a live row, and every tile has a row with offset 13, direction 13 and itself as input and target. `recv_list`: each tile of a device is named exactly twice in its row. `coarse_send`: strided owner map: coarse tile k of device s, global number p = s * 8 + k, goes to an owner that depends only on p % 8 (a permutation of the devices), in lane k // 8; slots of one row are distinct. `coarse_place`: the slot s + j of owner e holds the place of the coarse tile it receives; 8 marks a slot that carries nothing. Every coarse tile of the owner is written by exactly one slot.
All inputs are finite; a program needn't handle non-finite values.
Results may differ from a plain program's by a relative error of at most 0.0045.
Values may be sent and summed in bfloat16 or wider, within the bound.
No kernel may reach another device: no remote copies, remote signals or barrier semaphores. Data moves between devices by JAX's collectives and lax.ppermute only.
A program may use at most 128 MiB of HBM per device.

v0:
```python
import jax
import jax.numpy as jnp
from jax import lax
from jax.sharding import PartitionSpec as P

epsilon = 1e-05


def from_behind(block, axis, distance):
    devices = range(lax.axis_size(axis))
    route = [(i - distance, i) for i in devices if i - distance in devices]
    return lax.ppermute(block, axis, route)


def offsets(code):
    return jnp.stack([code // 9 - 1, code // 3 % 3 - 1, code % 3 - 1], axis=-1)


def shift_table(kernel, heading):
    voxel = jnp.arange(64, dtype=jnp.int32)
    corner = jnp.stack([voxel // 16, voxel // 4 % 4, voxel % 4], axis=-1)
    source = (
        corner[None, :, :]
        + offsets(jnp.minimum(kernel, 26))[:, None, :]
        - 4 * offsets(heading)[:, None, :]
    )
    inside = jnp.all((source >= 0) & (source < 4), axis=-1) & (kernel < 27)[:, None]
    source = jnp.clip(source, 0, 3)
    where_from = source[..., 0] * 16 + source[..., 1] * 4 + source[..., 2]
    return (where_from, inside)


def pool_blocks(values):
    dims_in = values.shape
    blocked = values.astype(jnp.float32).reshape(dims_in[:-2] + (2, 2, 2, 2, 2, 2, dims_in[-1]))
    return (
        jnp.mean(blocked, axis=(-6, -4, -2))
        .reshape(dims_in[:-2] + (8, dims_in[-1]))
        .astype(jnp.bfloat16)
    )


def assemble(placed):
    number = placed.shape[0]
    blocked = placed.reshape(number, 2, 2, 2, 2, 2, 2, placed.shape[-1])
    return blocked.transpose(0, 1, 4, 2, 5, 3, 6, 7).reshape(number, 64, placed.shape[-1])


def body(features, weights, gain, rulebook, recv_list, coarse_send, coarse_place):
    tile_count = features.shape[0]
    channels = features.shape[2]
    quarter = weights.shape[2]
    rule_rows = rulebook.shape[0]
    block_rows = min(128, rule_rows)
    slot_width = tile_count // 4
    chan_pos = lax.axis_index("chan")
    own_part = lax.dynamic_slice_in_dim(features, chan_pos * quarter, quarter, 2)
    grouped = rulebook.reshape(rule_rows // block_rows, block_rows, 4)
    voxel = jnp.arange(64, dtype=jnp.int32)
    tile_ids = jnp.arange(tile_count, dtype=jnp.int32)
    target_ids = jnp.arange(3 * tile_count, dtype=jnp.int32)
    flat_features = features.reshape(tile_count, 64 * channels)

    def step_rules(totals, group):
        where_from, inside = shift_table(group[:, 1], group[:, 2])
        picker = ((where_from[:, :, None] == voxel[None, None, :]) & inside[:, :, None]).astype(
            jnp.bfloat16
        )
        source_hot = (group[:, 0][:, None] == tile_ids[None, :]).astype(jnp.bfloat16)
        fetched = jnp.dot(source_hot, flat_features, preferred_element_type=jnp.float32).astype(
            jnp.bfloat16
        )
        fetched = fetched.reshape(group.shape[0], 64, channels)
        chosen = jnp.einsum(
            "bvu,buc->bvc", picker, fetched, preferred_element_type=jnp.float32
        ).astype(jnp.bfloat16)
        kernels = weights[jnp.minimum(group[:, 1], 26)]
        partial_out = jnp.einsum(
            "bvc,bcq->bvq", chosen, kernels, preferred_element_type=jnp.float32
        )
        target_hot = (target_ids[:, None] == group[:, 3][None, :]).astype(jnp.float32)
        added = jnp.dot(
            target_hot,
            partial_out.reshape(group.shape[0], 64 * quarter),
            precision=lax.Precision.HIGHEST,
            preferred_element_type=jnp.float32,
        )
        return (totals + added.reshape(3 * tile_count, 64, quarter), None)

    start = jnp.zeros((3 * tile_count, 64, quarter), jnp.float32)
    totals, unused = lax.scan(step_rules, start, grouped)
    outgoing = totals[tile_count:].astype(jnp.bfloat16).reshape(8, slot_width, 64, quarter)
    arrivals = []
    for group in range(8):
        distance = group + 1 if group < 4 else 3 - group
        arrivals.append(from_behind(outgoing[group], "tiles", distance))
    incoming = jnp.stack(arrivals, axis=0).reshape(2 * tile_count, 64 * quarter)
    receive_hot = (tile_ids[:, None] == recv_list[0][None, :]).astype(jnp.bfloat16)
    gathered_in = jnp.dot(receive_hot, incoming, preferred_element_type=jnp.float32).reshape(
        tile_count, 64, quarter
    )
    convolved = totals[:tile_count] + gathered_in
    squares = lax.psum(jnp.sum(convolved * convolved, axis=-1), "chan")
    mean_square = squares[:, :, None] / channels
    hidden = jax.nn.silu(gain.astype(jnp.float32) * convolved * lax.rsqrt(mean_square + epsilon))
    skip_features = (own_part.astype(jnp.float32) + hidden).astype(jnp.bfloat16)
    pooled = pool_blocks(skip_features)
    parents = assemble(pooled.reshape(tile_count // 8, 8, 8, quarter))
    slot_count = coarse_place.shape[1]
    parent_count = tile_count // 8
    slot_ids = jnp.arange(slot_count, dtype=jnp.int32)
    parent_ids = jnp.arange(parent_count, dtype=jnp.int32)
    send_hot = (slot_ids[:, None] == coarse_send[0][None, :]).astype(jnp.bfloat16)
    outbound = jnp.dot(
        send_hot, parents.reshape(parent_count, 64 * quarter), preferred_element_type=jnp.float32
    ).astype(jnp.bfloat16)
    outbound = outbound.reshape(slot_count, 64, quarter)
    landed = lax.all_to_all(outbound, "tiles", split_axis=0, concat_axis=0, tiled=True)
    place_hot = (parent_ids[:, None] == coarse_place[0][None, :]).astype(jnp.bfloat16)
    coarse_features = jnp.dot(
        place_hot, landed.reshape(slot_count, 64 * quarter), preferred_element_type=jnp.float32
    ).astype(jnp.bfloat16)
    coarse_features = coarse_features.reshape(parent_count, 64, quarter)
    return (skip_features, coarse_features)


def solution(mesh):
    in_specs = (
        P("tiles", None, None),
        P(None, None, "chan"),
        P("chan"),
        P("tiles", None),
        P("tiles", None),
        P("tiles", None),
        P("tiles", None),
    )
    out_specs = (P("tiles", None, "chan"), P("tiles", None, "chan"))
    return jax.shard_map(body, mesh=mesh, in_specs=in_specs, out_specs=out_specs, check_vma=False)
```

profile of v0, /device:TPU:0, one launch (start us, length us, event | category | flops | bytes accessed | tf_op | source)
XLA Modules:
  0.0 264.5 jit_solution(9480351480479693915)
XLA Ops:
  0.7 4.3 %copy.38 = bf16[8,8,64,256]{3,1,2,0:T(8,128)(2,1)} copy(bf16[8,8,64,256]{3,2,1,0:T(8,128)(2,1)} %bitcast.91) | data formatting | bytes 4194304
  4.9 160.6 %while.16 = (s32[]{:T(128)}, f32[192,64,64]{0,2,1:T(8,128)}, s32[6,128,4]{1,2,0:T(4,128)}, bf16[64,16384]{1,0:T(8,128)(2,1)}, bf16[27,256,64]{1,2,0:T(8,128)(2,1)S(1)}, /*index=5*/s32[]{:T(128)}, s32[]{:T(128)}) while((s32[]{:T(128)}, f32[192,64,64]{0,2,1:T(8,128)}, s32[6,128,4]{1,2,0:T(4,128)}, ...), condition=%wide.region_2.3_spmd.clone.clone, body=%wide.region_0.2_spmd.clone.clone.sunk | while | flops 2020381184 | bytes 46548056 | solution.py:91
  9.1 3.2 %copy.43 = bf16[16,8,64,256]{3,2,1,0:T(8,128)(2,1)} copy(bf16[16,8,64,256]{3,1,2,0:T(8,128)(2,1)S(1)} %bitcast.89) | data formatting | bytes 8388608 | tf_op jit(solution)/shard_map/while
  15.1 7.2 %fusion.70 = f32[128,64,64]{2,1,0:T(8,128)} fusion(bf16[128,256,64]{1,2,0:T(8,128)(2,1)} %gather_fusion, bf16[128,64,256]{2,1,0:T(8,128)(2,1)} %bitcast.88, s32[128,64]{1,0:T(8,128)S(1)} %copy.44, pred[128,64]{1,0:T(8,128)(4,1)S(1)} %copy.45), kind=kOutput, calls=%fused_computation.6.clone.1 | convolution fusion | flops 540016640 | bytes 10526720 | tf_op jit(solution)/shard_map/while/body/eval_jaxpr/bvc,bcq->bvq/dot_general | solution.py:78
  22.3 3.8 %copy.46 = f32[128,64,64]{0,2,1:T(8,128)S(1)} copy(f32[128,64,64]{2,1,0:T(8,128)} %fusion.70) | data formatting | bytes 4194304 | tf_op jit(solution)/shard_map/while/body/eval_jaxpr/bvc,bcq->bvq/dot_general | solution.py:78
  26.1 3.8 %select_add_fusion.2 = f32[192,64,64]{0,2,1:T(8,128)} fusion(f32[192,64,64]{0,2,1:T(8,128)} %get-tuple-element.311, f32[128,64,64]{0,2,1:T(8,128)S(1)} %copy.46, pred[]{:T(512)S(6)} %compare.18, s32[128]{0:T(128)S(1)} %get-tuple-element.302), kind=kOutput, calls=%fused_computation.5.clone.1 | convolution fusion | flops 1209556992 | bytes 8389121 | tf_op jit(solution)/shard_map/while/body/eval_jaxpr/dot_general | solution.py:82
  40.0 7.2 %fusion.70 = f32[128,64,64]{2,1,0:T(8,128)} fusion(bf16[128,256,64]{1,2,0:T(8,128)(2,1)} %gather_fusion, bf16[128,64,256]{2,1,0:T(8,128)(2,1)} %bitcast.88, s32[128,64]{1,0:T(8,128)S(1)} %copy.44, pred[128,64]{1,0:T(8,128)(4,1)S(1)} %copy.45), kind=kOutput, calls=%fused_computation.6.clone.1 | convolution fusion | flops 540016640 | bytes 10526720 | tf_op jit(solution)/shard_map/while/body/eval_jaxpr/bvc,bcq->bvq/dot_general | solution.py:78
  47.2 3.8 %copy.46 = f32[128,64,64]{0,2,1:T(8,128)S(1)} copy(f32[128,64,64]{2,1,0:T(8,128)} %fusion.70) | data formatting | bytes 4194304 | tf_op jit(solution)/shard_map/while/body/eval_jaxpr/bvc,bcq->bvq/dot_general | solution.py:78
  51.0 6.0 %select_add_fusion.2 = f32[192,64,64]{0,2,1:T(8,128)} fusion(f32[192,64,64]{0,2,1:T(8,128)} %get-tuple-element.311, f32[128,64,64]{0,2,1:T(8,128)S(1)} %copy.46, pred[]{:T(512)S(6)} %compare.18, s32[128]{0:T(128)S(1)} %get-tuple-element.302), kind=kOutput, calls=%fused_computation.5.clone.1 | convolution fusion | flops 1209556992 | bytes 8389121 | tf_op jit(solution)/shard_map/while/body/eval_jaxpr/dot_general | solution.py:82
  67.1 7.2 %fusion.70 = f32[128,64,64]{2,1,0:T(8,128)} fusion(bf16[128,256,64]{1,2,0:T(8,128)(2,1)} %gather_fusion, bf16[128,64,256]{2,1,0:T(8,128)(2,1)} %bitcast.88, s32[128,64]{1,0:T(8,128)S(1)} %copy.44, pred[128,64]{1,0:T(8,128)(4,1)S(1)} %copy.45), kind=kOutput, calls=%fused_computation.6.clone.1 | convolution fusion | flops 540016640 | bytes 10526720 | tf_op jit(solution)/shard_map/while/body/eval_jaxpr/bvc,bcq->bvq/dot_general | solution.py:78
  74.4 3.8 %copy.46 = f32[128,64,64]{0,2,1:T(8,128)S(1)} copy(f32[128,64,64]{2,1,0:T(8,128)} %fusion.70) | data formatting | bytes 4194304 | tf_op jit(solution)/shard_map/while/body/eval_jaxpr/bvc,bcq->bvq/dot_general | solution.py:78
  78.2 6.0 %select_add_fusion.2 = f32[192,64,64]{0,2,1:T(8,128)} fusion(f32[192,64,64]{0,2,1:T(8,128)} %get-tuple-element.311, f32[128,64,64]{0,2,1:T(8,128)S(1)} %copy.46, pred[]{:T(512)S(6)} %compare.18, s32[128]{0:T(128)S(1)} %get-tuple-element.302), kind=kOutput, calls=%fused_computation.5.clone.1 | convolution fusion | flops 1209556992 | bytes 8389121 | tf_op jit(solution)/shard_map/while/body/eval_jaxpr/dot_general | solution.py:82
  94.3 7.2 %fusion.70 = f32[128,64,64]{2,1,0:T(8,128)} fusion(bf16[128,256,64]{1,2,0:T(8,128)(2,1)} %gather_fusion, bf16[128,64,256]{2,1,0:T(8,128)(2,1)} %bitcast.88, s32[128,64]{1,0:T(8,128)S(1)} %copy.44, pred[128,64]{1,0:T(8,128)(4,1)S(1)} %copy.45), kind=kOutput, calls=%fused_computation.6.clone.1 | convolution fusion | flops 540016640 | bytes 10526720 | tf_op jit(solution)/shard_map/while/body/eval_jaxpr/bvc,bcq->bvq/dot_general | solution.py:78
  101.5 3.8 %copy.46 = f32[128,64,64]{0,2,1:T(8,128)S(1)} copy(f32[128,64,64]{2,1,0:T(8,128)} %fusion.70) | data formatting | bytes 4194304 | tf_op jit(solution)/shard_map/while/body/eval_jaxpr/bvc,bcq->bvq/dot_general | solution.py:78
  105.3 6.0 %select_add_fusion.2 = f32[192,64,64]{0,2,1:T(8,128)} fusion(f32[192,64,64]{0,2,1:T(8,128)} %get-tuple-element.311, f32[128,64,64]{0,2,1:T(8,128)S(1)} %copy.46, pred[]{:T(512)S(6)} %compare.18, s32[128]{0:T(128)S(1)} %get-tuple-element.302), kind=kOutput, calls=%fused_computation.5.clone.1 | convolution fusion | flops 1209556992 | bytes 8389121 | tf_op jit(solution)/shard_map/while/body/eval_jaxpr/dot_general | solution.py:82
  121.4 7.2 %fusion.70 = f32[128,64,64]{2,1,0:T(8,128)} fusion(bf16[128,256,64]{1,2,0:T(8,128)(2,1)} %gather_fusion, bf16[128,64,256]{2,1,0:T(8,128)(2,1)} %bitcast.88, s32[128,64]{1,0:T(8,128)S(1)} %copy.44, pred[128,64]{1,0:T(8,128)(4,1)S(1)} %copy.45), kind=kOutput, calls=%fused_computation.6.clone.1 | convolution fusion | flops 540016640 | bytes 10526720 | tf_op jit(solution)/shard_map/while/body/eval_jaxpr/bvc,bcq->bvq/dot_general | solution.py:78
  128.6 3.8 %copy.46 = f32[128,64,64]{0,2,1:T(8,128)S(1)} copy(f32[128,64,64]{2,1,0:T(8,128)} %fusion.70) | data formatting | bytes 4194304 | tf_op jit(solution)/shard_map/while/body/eval_jaxpr/bvc,bcq->bvq/dot_general | solution.py:78
  132.4 6.0 %select_add_fusion.2 = f32[192,64,64]{0,2,1:T(8,128)} fusion(f32[192,64,64]{0,2,1:T(8,128)} %get-tuple-element.311, f32[128,64,64]{0,2,1:T(8,128)S(1)} %copy.46, pred[]{:T(512)S(6)} %compare.18, s32[128]{0:T(128)S(1)} %get-tuple-element.302), kind=kOutput, calls=%fused_computation.5.clone.1 | convolution fusion | flops 1209556992 | bytes 8389121 | tf_op jit(solution)/shard_map/while/body/eval_jaxpr/dot_general | solution.py:82
  148.5 7.2 %fusion.70 = f32[128,64,64]{2,1,0:T(8,128)} fusion(bf16[128,256,64]{1,2,0:T(8,128)(2,1)} %gather_fusion, bf16[128,64,256]{2,1,0:T(8,128)(2,1)} %bitcast.88, s32[128,64]{1,0:T(8,128)S(1)} %copy.44, pred[128,64]{1,0:T(8,128)(4,1)S(1)} %copy.45), kind=kOutput, calls=%fused_computation.6.clone.1 | convolution fusion | flops 540016640 | bytes 10526720 | tf_op jit(solution)/shard_map/while/body/eval_jaxpr/bvc,bcq->bvq/dot_general | solution.py:78
  155.7 3.8 %copy.46 = f32[128,64,64]{0,2,1:T(8,128)S(1)} copy(f32[128,64,64]{2,1,0:T(8,128)} %fusion.70) | data formatting | bytes 4194304 | tf_op jit(solution)/shard_map/while/body/eval_jaxpr/bvc,bcq->bvq/dot_general | solution.py:78
  159.5 6.0 %select_add_fusion.2 = f32[192,64,64]{0,2,1:T(8,128)} fusion(f32[192,64,64]{0,2,1:T(8,128)} %get-tuple-element.311, f32[128,64,64]{0,2,1:T(8,128)S(1)} %copy.46, pred[]{:T(512)S(6)} %compare.18, s32[128]{0:T(128)S(1)} %get-tuple-element.302), kind=kOutput, calls=%fused_computation.5.clone.1 | convolution fusion | flops 1209556992 | bytes 8389121 | tf_op jit(solution)/shard_map/while/body/eval_jaxpr/dot_general | solution.py:82
  165.5 6.2 %copy.31 = bf16[192,64,64]{2,1,0:T(8,128)(2,1)} copy(f32[192,64,64]{0,2,1:T(8,128)} %get-tuple-element.164) | data formatting | bytes 4718592 | tf_op jit(solution)/shard_map/while | solution.py:91
  174.3 5.5 %collective-permute-start = (bf16[16,64,64]{2,1,0:T(8,128)(2,1)}, bf16[16,64,64]{2,1,0:T(8,128)(2,1)}, u32[]{:S(2)}, u32[]{:S(2)}) collective-permute-start(bf16[16,64,64]{2,1,0:T(8,128)(2,1)} %get-tuple-element.243), channel_id=1, source_target_pairs={{0,4},{4,8},{8,12},{12,16},{16,20},{20,24},{24,28},{1,5},{5,9},{9,... | collective-permute-start | bytes 393224 | tf_op jit(solution)/shard_map/ppermute | solution.py:12
  179.8 3.5 %collective-permute-start.1 = (bf16[16,64,64]{2,1,0:T(8,128)(2,1)}, bf16[16,64,64]{2,1,0:T(8,128)(2,1)}, u32[]{:S(2)}, u32[]{:S(2)}) collective-permute-start(bf16[16,64,64]{2,1,0:T(8,128)(2,1)} %get-tuple-element.242), channel_id=1, source_target_pairs={{0,8},{4,12},{8,16},{12,20},{16,24},{20,28},{1,9},{5,13},{9,17},{1... | collective-permute-start | bytes 393224 | tf_op jit(solution)/shard_map/ppermute | solution.py:12
  183.4 4.5 %collective-permute-start.2 = (bf16[16,64,64]{2,1,0:T(8,128)(2,1)}, bf16[16,64,64]{2,1,0:T(8,128)(2,1)}, u32[]{:S(2)}, u32[]{:S(2)}) collective-permute-start(bf16[16,64,64]{2,1,0:T(8,128)(2,1)} %get-tuple-element.241), channel_id=1, source_target_pairs={{0,12},{4,16},{8,20},{12,24},{16,28},{1,13},{5,17},{9,21},{13,25},... | collective-permute-start | bytes 393224 | tf_op jit(solution)/shard_map/ppermute | solution.py:12
  207.9 6.2 %collective-permute-done.6 = bf16[16,64,64]{2,1,0:T(8,128)(2,1)S(1)} collective-permute-done((bf16[16,64,64]{2,1,0:T(8,128)(2,1)S(1)}, bf16[16,64,64]{2,1,0:T(8,128)(2,1)S(1)}, u32[]{:S(2)}, u32[]{:S(2)}) %collective-permute-start.6) | collective-permute-done | bytes 131104 | tf_op jit(solution)/shard_map/ppermute | solution.py:12
  214.8 14.5 %collective-permute-done.7 = bf16[16,64,64]{2,1,0:T(8,128)(2,1)S(1)} collective-permute-done((bf16[16,64,64]{2,1,0:T(8,128)(2,1)S(1)}, bf16[16,64,64]{2,1,0:T(8,128)(2,1)S(1)}, u32[]{:S(2)}, u32[]{:S(2)}) %collective-permute-start.7) | collective-permute-done | bytes 131104 | tf_op jit(solution)/shard_map/ppermute | solution.py:12
  230.1 3.3 %reshape.246 = bf16[128,4096]{1,0:T(8,128)(2,1)S(1)} reshape(bf16[8,16,64,64]{3,2,1,0:T(8,128)(2,1)} %bitcast_dynamic-update-slice_fusion) | data formatting | bytes 2097152 | tf_op jit(solution)/shard_map/reshape | solution.py:97
  234.7 3.7 %multiply_reduce_fusion = (f32[64,64]{0,1:T(8,128)S(1)}, f32[64,64,64]{0,2,1:T(8,128)}) fusion(bf16[64,64,128]{2,1,0:T(8,128)(2,1)} %bitcast.93, s32[128]{0:T(128)S(1)} %bitcast.98, f32[192,64,64]{0,2,1:T(8,128)} %get-tuple-element.164), kind=kOutput, calls=%fused_computation.71 | convolution fusion | flops 67899392 | bytes 3162624 | tf_op jit(solution)/shard_map/dot_general | solution.py:99
  238.4 10.3 %psum.7 = f32[64,64]{0,1:T(8,128)S(1)} all-reduce(f32[64,64]{0,1:T(8,128)S(1)} %get-tuple-element.244), channel_id=1, replica_groups=mesh['tiles'=8,'chan'=4] {'chan'}, use_global_device_ids=true, to_apply=%region_4.5 | all-reduce | flops 4096 | bytes 32768 | tf_op jit(solution)/shard_map/psum | solution.py:103
  253.0 3.4 %all-to-all-start = ((bf16[8,2,2048]{2,1,0:T(2,128)(2,1)}), bf16[8,2,2048]{2,1,0:T(2,128)(2,1)S(1)}, u32[]{:S(2)}, u32[]{:S(2)}) async-start(bf16[8,2,2048]{2,1,0:T(2,128)(2,1)} %reshape.271), calls=%async_computation | async-start | bytes 131072 | tf_op jit(solution)/shard_map/all_to_all | solution.py:118
  258.7 4.5 %all-to-all-done = bf16[8,2,2048]{2,1,0:T(2,128)(2,1)S(1)} async-done(((bf16[8,2,2048]{2,1,0:T(2,128)(2,1)}), bf16[8,2,2048]{2,1,0:T(2,128)(2,1)S(1)}, u32[]{:S(2)}, u32[]{:S(2)}) %all-to-all-start) | async-done | bytes 65568 | tf_op jit(solution)/shard_map/all_to_all | solution.py:118
  (153 shorter events, 90.4 us)
Async XLA Ops:
  0.6 4.3 %copy-start = (bf16[27,256,64]{1,2,0:T(8,128)(2,1)S(1)}, bf16[27,256,64]{1,2,0:T(8,128)(2,1)}, u32[]{:S(2)}) copy-start(bf16[27,256,64]{1,2,0:T(8,128)(2,1)} %param.10) | copy-start | bytes 2654212
  171.7 19.5 %copy-start.1 = (bf16[64,64,256]{2,1,0:T(8,128)(2,1)S(1)}, bf16[64,64,256]{2,1,0:T(8,128)(2,1)}, u32[]{:S(2)}) copy-start(bf16[64,64,256]{2,1,0:T(8,128)(2,1)} %param.9) | copy-start | bytes 6291460
  174.3 20.4 %collective-permute-start = (bf16[16,64,64]{2,1,0:T(8,128)(2,1)}, bf16[16,64,64]{2,1,0:T(8,128)(2,1)}, u32[]{:S(2)}, u32[]{:S(2)}) collective-permute-start(bf16[16,64,64]{2,1,0:T(8,128)(2,1)} %get-tuple-element.243), channel_id=1, source_target_pairs={{0,4},{4,8},{8,12},{12,16},{16,20},{20,24},{24,28},{1,5},{5,9},{9,... | collective-permute-start | bytes 393224 | tf_op jit(solution)/shard_map/ppermute | solution.py:12
  179.8 17.9 %collective-permute-start.1 = (bf16[16,64,64]{2,1,0:T(8,128)(2,1)}, bf16[16,64,64]{2,1,0:T(8,128)(2,1)}, u32[]{:S(2)}, u32[]{:S(2)}) collective-permute-start(bf16[16,64,64]{2,1,0:T(8,128)(2,1)} %get-tuple-element.242), channel_id=1, source_target_pairs={{0,8},{4,12},{8,16},{12,20},{16,24},{20,28},{1,9},{5,13},{9,17},{1... | collective-permute-start | bytes 393224 | tf_op jit(solution)/shard_map/ppermute | solution.py:12
  183.4 17.3 %collective-permute-start.2 = (bf16[16,64,64]{2,1,0:T(8,128)(2,1)}, bf16[16,64,64]{2,1,0:T(8,128)(2,1)}, u32[]{:S(2)}, u32[]{:S(2)}) collective-permute-start(bf16[16,64,64]{2,1,0:T(8,128)(2,1)} %get-tuple-element.241), channel_id=1, source_target_pairs={{0,12},{4,16},{8,20},{12,24},{16,28},{1,13},{5,17},{9,21},{13,25},... | collective-permute-start | bytes 393224 | tf_op jit(solution)/shard_map/ppermute | solution.py:12
  187.8 16.0 %collective-permute-start.3 = (bf16[16,64,64]{2,1,0:T(8,128)(2,1)S(1)}, bf16[16,64,64]{2,1,0:T(8,128)(2,1)}, u32[]{:S(2)}, u32[]{:S(2)}) collective-permute-start(bf16[16,64,64]{2,1,0:T(8,128)(2,1)S(1)} %get-tuple-element.240), channel_id=1, source_target_pairs={{0,16},{4,20},{8,24},{12,28},{1,17},{5,21},{9,25},{13,29},{2,18},{... | collective-permute-start | bytes 393224 | tf_op jit(solution)/shard_map/ppermute | solution.py:12
  189.8 15.7 %collective-permute-start.4 = (bf16[16,64,64]{2,1,0:T(8,128)(2,1)S(1)}, bf16[16,64,64]{2,1,0:T(8,128)(2,1)}, u32[]{:S(2)}, u32[]{:S(2)}) collective-permute-start(bf16[16,64,64]{2,1,0:T(8,128)(2,1)S(1)} %get-tuple-element.239), channel_id=1, source_target_pairs={{4,0},{8,4},{12,8},{16,12},{20,16},{24,20},{28,24},{5,1},{9,5},{13... | collective-permute-start | bytes 393224 | tf_op jit(solution)/shard_map/ppermute | solution.py:12
  191.1 3.6 %copy-start.5 = (bf16[64]{0:T(256)(128)(2,1)S(1)}, bf16[64]{0:T(256)(128)(2,1)}, u32[]{:S(2)}) copy-start(bf16[64]{0:T(256)(128)(2,1)} %param.11) | copy-start | bytes 388
  194.7 12.4 %collective-permute-start.5 = (bf16[16,64,64]{2,1,0:T(8,128)(2,1)S(1)}, bf16[16,64,64]{2,1,0:T(8,128)(2,1)S(1)}, u32[]{:S(2)}, u32[]{:S(2)}) collective-permute-start(bf16[16,64,64]{2,1,0:T(8,128)(2,1)S(1)} %get-tuple-element.238), channel_id=1, source_target_pairs={{8,0},{12,4},{16,8},{20,12},{24,16},{28,20},{9,1},{13,5},{17,9},{2... | collective-permute-start | bytes 393224 | tf_op jit(solution)/shard_map/ppermute | solution.py:12
  197.7 16.3 %collective-permute-start.6 = (bf16[16,64,64]{2,1,0:T(8,128)(2,1)S(1)}, bf16[16,64,64]{2,1,0:T(8,128)(2,1)S(1)}, u32[]{:S(2)}, u32[]{:S(2)}) collective-permute-start(bf16[16,64,64]{2,1,0:T(8,128)(2,1)S(1)} %get-tuple-element.237), channel_id=1, source_target_pairs={{12,0},{16,4},{20,8},{24,12},{28,16},{13,1},{17,5},{21,9},{25,13},... | collective-permute-start | bytes 393224 | tf_op jit(solution)/shard_map/ppermute | solution.py:12
  200.7 28.6 %collective-permute-start.7 = (bf16[16,64,64]{2,1,0:T(8,128)(2,1)S(1)}, bf16[16,64,64]{2,1,0:T(8,128)(2,1)S(1)}, u32[]{:S(2)}, u32[]{:S(2)}) collective-permute-start(bf16[16,64,64]{2,1,0:T(8,128)(2,1)S(1)} %get-tuple-element.236), channel_id=1, source_target_pairs={{16,0},{20,4},{24,8},{28,12},{17,1},{21,5},{25,9},{29,13},{18,2},{... | collective-permute-start | bytes 393224 | tf_op jit(solution)/shard_map/ppermute | solution.py:12
  230.1 4.6 %copy-start.4 = (s32[1,128]{1,0:T(1,128)S(1)}, s32[1,128]{1,0:T(1,128)}, u32[]{:S(2)}) copy-start(s32[1,128]{1,0:T(1,128)} %param.13) | copy-start | bytes 1540
  251.1 0.8 copy-start.2
  251.3 12.2 %copy-start.3 = (s32[1,8]{1,0:T(1,128)S(1)}, s32[1,8]{1,0:T(1,128)}, u32[]{:S(2)}) copy-start(s32[1,8]{1,0:T(1,128)} %param.15) | copy-start | bytes 100
  253.0 10.2 %all-to-all-start = ((bf16[8,2,2048]{2,1,0:T(2,128)(2,1)}), bf16[8,2,2048]{2,1,0:T(2,128)(2,1)S(1)}, u32[]{:S(2)}, u32[]{:S(2)}) async-start(bf16[8,2,2048]{2,1,0:T(2,128)(2,1)} %reshape.271), calls=%async_computation | async-start | bytes 131072 | tf_op jit(solution)/shard_map/all_to_all | solution.py:118
where the time goes:
time: 266 us; the launch traced here: 265 us
  local copies, waits for them, and re-layouts  101 us (38%)
  matrix products  98.2 us (37%)
  waiting for transfers between devices  25.2 us (9%)
  starting transfers between devices  24.2 us (9%)
  blocking collectives  10.3 us (4%)
  other arithmetic  4.43 us (2%)
    dot_general x6, matrix products, step_rules(): jnp.einsum('bvc,bcq->bvq', chosen, kernels, preferred_element_type=jnp.fl...  43.3 us
    dot_general x6, matrix products, step_rules(): jnp.dot(target_hot, partial_out.reshape(group.shape[0], 64 * quarter), pr...  33.6 us
    dot_general x6, local copies, waits for them, and re-layouts, step_rules(): jnp.einsum('bvc,bcq->bvq', chosen, kernels, preferred_element_type=jnp.fl...  22.7 us
    ppermute x8, starting transfers between devices, from_behind(): return lax.ppermute(block, axis, route)  20.8 us
    ppermute x8, waiting for transfers between devices, from_behind(): return lax.ppermute(block, axis, route)  20.7 us
    unnamed x24, local copies, waits for them, and re-layouts  19.5 us
    while x6, local copies, waits for them, and re-layouts  19.3 us
    dot_general x6, matrix products, step_rules(): jnp.dot(source_hot, flat_features, preferred_element_type=jnp.float32)  17.3 us
  transfers between devices with their start and end apart: 9, of which 3 were waited for; matrix products, arithmetic and copies ran while one was open for 6% of the time, Pallas kernels for 0%

commit v1 on v0

v1 whole, which is shorter than its diff:
```python
import functools

import jax
import jax.numpy as jnp
import numpy as np
from jax import lax
from jax.experimental import pallas as pl
from jax.experimental.pallas import tpu as pltpu
from jax.sharding import PartitionSpec as P

EPS = 1e-05
REACH = 4
VOX = 64
HALF = 32
BF = jnp.bfloat16
F32 = jnp.float32
PAD = 64
UNROLL = 8


def matchings(n):
    found = []
    for d in range(REACH, 0, -1):
        for parity in (0, 1):
            pairs = [(i, i + d) for i in range(n - d) if (i // d) % 2 == parity]
            if pairs:
                rest = [i for i in range(n) if all(i not in p for p in pairs)]
                fill = list(zip(rest[::2], rest[1::2]))
                both = pairs + fill
                found.append((d, parity, both + [(b, a) for a, b in both]))
    return found


def role(e, n, d, parity):
    low = jnp.logical_and(lax.rem(lax.div(e, d), 2) == parity, e + d < n)
    high = jnp.logical_and(e >= d, lax.rem(lax.div(jnp.maximum(e - d, 0), d), 2) == parity)
    return low, high


def lane_iota(shape):
    return lax.broadcasted_iota(jnp.int32, shape, len(shape) - 1)


def dims_of(code):
    return (lax.div(code, 9) - 1, lax.rem(lax.div(code, 3), 3) - 1, lax.rem(code, 3) - 1)


def conv_kernel(n, ways, tile_count, rules_ref, f_ref, w_ref, *rest):
    sends = rest[: len(ways)]
    local_ref, y_ref, acc_ref, words_v, words_s, sem = rest[len(ways) :]
    rows = tile_count * VOX
    span = rows + 2 * PAD
    rule_rows = rules_ref.shape[1]
    e = lax.axis_index("tiles")
    tile = rules_ref[0:1, :]
    kernel = rules_ref[1:2, :]
    heading = rules_ref[2:3, :]
    code = jnp.minimum(kernel, 26)
    shift = jnp.zeros_like(code)
    need = jnp.where(kernel < 27, 0, 1 << 23) + jnp.where(lax.rem(code, 2) == 0, 1 << 21, 1 << 22)
    for dim, (step, turn) in enumerate(zip(dims_of(code), dims_of(heading))):
        move = step - 4 * turn
        shift = shift + move * (16, 4, 1)[dim]
        need = need + jnp.left_shift(jnp.full_like(move, 1), move + (3 + 7 * dim))
    words_v[0:1, :] = lax.div(code, 2) * span + PAD + tile * VOX + shift
    words_v[1:2, :] = rules_ref[3:4, :]
    words_v[2:3, :] = need
    copy = pltpu.make_async_copy(words_v, words_s, sem)
    copy.start()

    def zero(i, c):
        acc_ref[i] = jnp.zeros((VOX, 128), F32)
        return c

    lax.fori_loop(0, 3 * tile_count, zero, 0)

    chunk = 512
    depth = w_ref.shape[0]
    for q in range(0, depth, 256):
        width = min(256, depth - q)

        def product(i, c, q=q, width=width):
            at = pl.multiple_of(i * chunk, chunk)
            part = lax.dot_general(
                f_ref[pl.ds(at, chunk), :],
                w_ref[q : q + width, :],
                (((1,), (1,)), ((), ())),
                preferred_element_type=F32,
            )
            for s in range(0, width, 128):
                wide = min(128, width - s)
                base = ((q + s) // 128) * span + PAD
                y_ref[pl.ds(pl.multiple_of(base + at, 8), chunk), 0:wide] = part[:, s : s + wide]
            return c

        lax.fori_loop(0, rows // chunk, product, 0)

    voxel = lax.broadcasted_iota(jnp.int32, (VOX, 128), 0)
    lane = lane_iota((VOX, 128))
    have = jnp.where(lane < 64, 1 << 21, 1 << 22)
    for dim, place in enumerate((lax.div(voxel, 16), lax.rem(lax.div(voxel, 4), 4), lax.rem(voxel, 4))):
        have = have + jnp.left_shift(jnp.full_like(place, 15), 3 - place + 7 * dim)
    copy.wait()

    def rule(i, c):
        for u in range(UNROLL):
            r = i * UNROLL + u
            need_r = words_s[2, r]
            taken = y_ref[pl.ds(words_s[0, r], VOX), :]
            t = words_s[1, r]
            acc_ref[t] = acc_ref[t] + jnp.where((have & need_r) == need_r, taken, 0.0)
        return c

    lax.fori_loop(0, rule_rows // UNROLL, rule, 0)

    first = lane_iota((HALF, 128)) < 64

    def folded(t):
        low = acc_ref[t, 0:HALF, :]
        high = acc_ref[t, HALF:VOX, :]
        low = low + pltpu.roll(low, 64, 1)
        high = high + pltpu.roll(high, 64, 1)
        return jnp.where(first, low, high)

    slots = 2 * tile_count // 8
    for (d, parity, _), send_ref in zip(ways, sends):
        low, _high = role(e, n, d, parity)
        base = tile_count + slots * jnp.where(low, d - 1, d + 3)

        def emit(i, c, send_ref=send_ref, base=base):
            send_ref[i] = folded(base + i).astype(BF)
            return c

        lax.fori_loop(0, slots, emit, 0)

    def keep(t, c):
        local_ref[t] = folded(t)
        return c

    lax.fori_loop(0, tile_count, keep, 0)


def own_kernel(f_ref, _after, out_ref):
    c = lax.axis_index("chan")
    at = pl.multiple_of(lax.div(c, 2) * 128, 128)
    odd = lax.rem(c, 2)
    first = lane_iota((HALF, 128)) < 64

    def pack(t, s):
        block = f_ref[t, :, pl.ds(at, 128)].astype(F32)
        low, high = block[:HALF], block[HALF:]
        even_form = jnp.where(first, low, pltpu.roll(high, 64, 1))
        odd_form = jnp.where(first, pltpu.roll(low, 64, 1), high)
        out_ref[t] = jnp.where(odd == 1, odd_form, even_form)
        return s

    lax.fori_loop(0, f_ref.shape[0], pack, 0)


def combine_kernel(n, ways, local_ref, list_ref, *rest):
    blocks = rest[: len(ways)]
    conv_ref, sums_ref = rest[len(ways) :]
    e = lax.axis_index("tiles")
    tile_count = local_ref.shape[0]
    slots = blocks[0].shape[0]
    conv_ref[...] = local_ref[...]
    for (d, parity, _), block in zip(ways, blocks):
        low, high = role(e, n, d, parity)
        base = slots * jnp.where(low, d + 3, d - 1)

        @pl.when(jnp.logical_or(low, high))
        def _(block=block, base=base):
            for i in range(slots):
                t = list_ref[0, base + i]
                conv_ref[t] = conv_ref[t] + block[i].astype(F32)

    rows = tile_count * HALF
    pick = (lane_iota((2, 256)) // 64 % 2 == lax.broadcasted_iota(jnp.int32, (2, 256), 0)).astype(BF)
    step = 512
    for at in range(0, rows, step):
        value = conv_ref[at // HALF : (at + step) // HALF].reshape(step, 128)
        square = value * value
        top = square.astype(BF)
        rest_of = (square - top.astype(F32)).astype(BF)
        sums_ref[:, at : at + step] = lax.dot_general(
            pick,
            jnp.concatenate([top, rest_of], axis=1),
            (((1,), (1,)), ((), ())),
            preferred_element_type=F32,
        )


def norm_kernel(channels, conv_ref, own_ref, gain_ref, pool_ref, slot_ref, s0, s1, s2, s3, skip_ref, out_ref):
    tile_count = conv_ref.shape[0]
    total = jnp.concatenate([s0[...], s1[...], s2[...], s3[...]], axis=0)
    parts = []
    for _ in range(3):
        top = total.astype(BF)
        parts.append(top.astype(F32))
        total = total - top.astype(F32)
    parts = jnp.concatenate(parts, axis=0).astype(BF)
    count = parts.shape[0]
    spread = (lane_iota((count, 128)) // 64 == lax.broadcasted_iota(jnp.int32, (count, 128), 0) % 2).astype(BF)
    gain = gain_ref[...]
    for k in range(tile_count // 8):
        mean_square = lax.dot_general(
            parts[:, k * 256 : (k + 1) * 256],
            spread,
            (((0,), (0,)), ((), ())),
            preferred_element_type=F32,
        ) * (1.0 / channels)
        value = conv_ref[8 * k : 8 * k + 8].reshape(256, 128)
        v = gain * value * lax.rsqrt(mean_square + EPS)
        hidden = v / (1.0 + jnp.exp(-v))
        whole = (own_ref[8 * k : 8 * k + 8].reshape(256, 128) + hidden).astype(BF)
        cut = whole.reshape(8, HALF, 128)
        skip_ref[8 * k : 8 * k + 8, 0:HALF, :] = cut[:, :, 0:64]
        skip_ref[8 * k : 8 * k + 8, HALF:VOX, :] = cut[:, :, 64:128]
        pooled = jnp.dot(pool_ref[...], whole, preferred_element_type=F32)
        out_ref[slot_ref[0, k]] = pooled.astype(BF)


def place_kernel(place_ref, landed_ref, out_ref):
    parents = out_ref.shape[0]
    for i in range(landed_ref.shape[0]):
        where = place_ref[0, i]

        @pl.when(where < parents)
        def _(i=i, where=where):
            for ox in range(2):
                for px in range(2):
                    row = 16 * (2 * ox + px)
                    out_ref[where, row : row + 16, :] = landed_ref[i, 16 * ox : 16 * ox + 16, 64 * px : 64 * px + 64]


def pool_matrix():
    out = np.zeros((2, 4, 4, 2, 2, 2, 2, 4, 4), np.float32)
    for ox in range(2):
        for y in range(4):
            for z in range(4):
                out[ox, y, z, ox, y // 2, z // 2, :, 2 * (y % 2) : 2 * (y % 2) + 2, 2 * (z % 2) : 2 * (z % 2) + 2] = 0.125
    return out.reshape(32, 256)


VM = pl.BlockSpec(memory_space=pltpu.VMEM)
SM = pl.BlockSpec(memory_space=pltpu.SMEM)


def body(n, features, weights, gain, rulebook, recv_list, coarse_send, coarse_place):
    tile_count, _, channels = features.shape
    offsets, _, quarter = weights.shape
    rule_rows = rulebook.shape[0]
    ways = matchings(n)
    slots = tile_count // 4
    span = tile_count * VOX + 2 * PAD
    pairs = (offsets + 1) // 2
    params = pltpu.CompilerParams(vmem_limit_bytes=58 * 1024 * 1024)
    small = pltpu.CompilerParams(vmem_limit_bytes=24 * 1024 * 1024)

    flat_weights = weights.transpose(0, 2, 1).reshape(offsets * quarter, channels)
    block = jax.ShapeDtypeStruct((slots, HALF, 128), BF)
    made = pl.pallas_call(
        functools.partial(conv_kernel, n, ways, tile_count),
        out_shape=[block] * len(ways) + [jax.ShapeDtypeStruct((tile_count, HALF, 128), F32)],
        in_specs=[VM] * 3,
        out_specs=[VM] * (len(ways) + 1),
        scratch_shapes=[
            pltpu.VMEM((pairs * span, 128), F32),
            pltpu.VMEM((3 * tile_count, VOX, 128), F32),
            pltpu.VMEM((8, rule_rows), jnp.int32),
            pltpu.SMEM((8, rule_rows), jnp.int32),
            pltpu.SemaphoreType.DMA,
        ],
        compiler_params=params,
        name="rules",
    )(rulebook.T, features.reshape(tile_count * VOX, channels), flat_weights)
    sends, local = made[:-1], made[-1]
    arrivals = [lax.ppermute(x, "tiles", way[2]) for x, way in zip(sends, ways)]
    own = pl.pallas_call(
        own_kernel,
        out_shape=jax.ShapeDtypeStruct((tile_count, HALF, 128), F32),
        in_specs=[VM, pl.BlockSpec(memory_space=pl.ANY)],
        out_specs=VM,
        compiler_params=small,
        cost_estimate=pl.CostEstimate(flops=2000000, bytes_accessed=4000000, transcendentals=0),
        name="own",
    )(features, local)
    conv, sums = pl.pallas_call(
        functools.partial(combine_kernel, n, ways),
        out_shape=[
            jax.ShapeDtypeStruct((tile_count, HALF, 128), F32),
            jax.ShapeDtypeStruct((2, tile_count * HALF), F32),
        ],
        in_specs=[VM, SM] + [VM] * len(ways),
        out_specs=[VM, VM],
        compiler_params=small,
        name="combine",
    )(local, recv_list, *arrivals)
    wide = lax.axis_size("chan")
    others = [lax.ppermute(sums, "chan", [(i, i ^ m) for i in range(wide)]) for m in range(1, wide)]
    slot_count = coarse_place.shape[1]
    parent_count = tile_count // 8
    skip, outbound = pl.pallas_call(
        functools.partial(norm_kernel, channels),
        out_shape=[
            jax.ShapeDtypeStruct((tile_count, VOX, quarter), BF),
            jax.ShapeDtypeStruct((slot_count, HALF, 128), BF),
        ],
        in_specs=[VM] * 4 + [SM] + [VM] * 4,
        out_specs=[VM, VM],
        compiler_params=small,
        name="norm",
    )(
        conv,
        own,
        jnp.tile(gain.astype(F32), 2).reshape(1, 128),
        jnp.asarray(pool_matrix(), BF),
        coarse_send,
        sums,
        *others,
    )
    landed = lax.all_to_all(outbound, "tiles", split_axis=0, concat_axis=0, tiled=True)
    coarse = pl.pallas_call(
        place_kernel,
        out_shape=jax.ShapeDtypeStruct((parent_count, VOX, quarter), BF),
        in_specs=[SM, VM],
        out_specs=VM,
        compiler_params=small,
        name="place",
    )(coarse_place, landed)
    return (skip, coarse)


def solution(mesh):
    in_specs = (
        P("tiles", None, None),
        P(None, None, "chan"),
        P("chan"),
        P("tiles", None),
        P("tiles", None),
        P("tiles", None),
        P("tiles", None),
    )
    out_specs = (P("tiles", None, "chan"), P("tiles", None, "chan"))
    return jax.shard_map(
        functools.partial(body, mesh.shape["tiles"]),
        mesh=mesh,
        in_specs=in_specs,
        out_specs=out_specs,
        check_vma=False,
    )
```

time: 266 us -> 88.6 us (0.33)
  local copies, waits for them, and re-layouts: 101 us -> 2.36 us
  matrix products: 98.2 us -> 0 us
  Pallas kernels: 0 us -> 49.2 us
  waiting for transfers between devices: 25.2 us -> 9.72 us
  starting transfers between devices: 24.2 us -> 14.4 us
  other arithmetic: 4.43 us -> 0 us
    dot_general x21 -> x0, matrix products: 98.2 us -> none  [the longest x6 43.3 us: step_rules(): jnp.einsum('bvc,bcq->bvq', chosen, kernels, preferred_element_type=jnp.fl...]
    pallas_call x0 -> x5, Pallas kernels: none -> 49.2 us  [the longest x1 38 us: body(): pl.pallas_call(functools.partial(conv_kernel, n, ways, tile_count), out_s...]
    while x7 -> x0, local copies, waits for them, and re-layouts: 25.5 us -> none
    dot_general x7 -> x0, local copies, waits for them, and re-layouts: 24.1 us -> none  [the longest x6 22.7 us: step_rules(): jnp.einsum('bvc,bcq->bvq', chosen, kernels, preferred_element_type=jnp.fl...]
    unnamed x24 -> x20, local copies, waits for them, and re-layouts: 19.5 us -> 2.27 us
    gather x6 -> x0, local copies, waits for them, and re-layouts: 16.6 us -> none  [step_rules(): kernels = weights[jnp.minimum(group[:, 1], 26)]]
    all_to_all x0 -> x1, blocking collectives: none -> 12 us  [body(): lax.all_to_all(outbound, 'tiles', split_axis=0, concat_axis=0, tiled=True)]
    ppermute x8 -> x10, waiting for transfers between devices: 20.7 us -> 9.72 us  [the longest x7 9.71 us: body(): arrivals = [lax.ppermute(x, 'tiles', way[2]) for x, way in zip(sends, ways)]]
  transfers between devices with their start and end apart: 9 -> 10, of which waited for: 3 -> 3; matrix products, arithmetic and copies ran while one was open for 6% -> 0% of each run, Pallas kernels for 0% -> 5%
where the time goes in v1:
time: 88.6 us; the launch traced here: 88.5 us
  Pallas kernels  49.2 us (56%)
  starting transfers between devices  14.4 us (16%)
  blocking collectives  12 us (14%)
  waiting for transfers between devices  9.72 us (11%)
  local copies, waits for them, and re-layouts  2.36 us (3%)
    pallas_call x1, Pallas kernels, body(): pl.pallas_call(functools.partial(conv_kernel, n, ways, tile_count), out_s...  38 us
    ppermute x7, starting transfers between devices, body(): arrivals = [lax.ppermute(x, 'tiles', way[2]) for x, way in zip(sends, ways)]  12.6 us
    all_to_all x1, blocking collectives, body(): lax.all_to_all(outbound, 'tiles', split_axis=0, concat_axis=0, tiled=True)  12 us
    ppermute x7, waiting for transfers between devices, body(): arrivals = [lax.ppermute(x, 'tiles', way[2]) for x, way in zip(sends, ways)]  9.71 us
    pallas_call x1, Pallas kernels, body(): pl.pallas_call(own_kernel, out_shape=jax.ShapeDtypeStruct((tile_count, HA...  4.83 us
    pallas_call x1, Pallas kernels, body(): pl.pallas_call(functools.partial(norm_kernel, channels), out_shape=[jax.S...  3.26 us
    unnamed x20, local copies, waits for them, and re-layouts  2.27 us
    ppermute x3, starting transfers between devices, body(): lax.ppermute(sums, 'chan', [(i, i ^ m) for i in range(wide)])  1.86 us
  transfers between devices with their start and end apart: 10, of which 3 were waited for; matrix products, arithmetic and copies ran while one was open for 0% of the time, Pallas kernels for 5%

profile of v1, /device:TPU:0, one launch (start us, length us, event | category | flops | bytes accessed | tf_op | source)
XLA Modules:
  0.0 88.5 jit_solution(9720480376066432640)
XLA Ops:
  0.7 38.0 %rules.1 = (bf16[16,32,128]{2,1,0:T(8,128)(2,1)}, bf16[16,32,128]{2,1,0:T(8,128)(2,1)}, bf16[16,32,128]{2,1,0:T(8,128)(2,1)}, bf16[16,32,128]{2,1,0:T(8,128)(2,1...) custom-call(s32[4,768]{1,0:T(4,128)} %bitcast.7, ...), custom_call_target="tpu_custom_call" | custom-call | tf_op jit(solution)/shard_map/rules/pallas_call | solution.py:262
  38.7 4.2 %collective-permute-start = (bf16[16,32,128]{2,1,0:T(8,128)(2,1)}, bf16[16,32,128]{2,1,0:T(8,128)(2,1)S(1)}, u32[]{:S(2)}, u32[]{:S(2)}) collective-permute-start(bf16[16,32,128]{2,1,0:T(8,128)(2,1)} %get-tuple-element.15), channel_id=1, source_target_pairs={{0,16},{4,20},{8,24},{12,28},{16,0},{20,4},{24,8},{28,12},{1,17},{... | collective-permute-start | bytes 393224 | tf_op jit(solution)/shard_map/ppermute | solution.py:278
  42.9 2.3 %collective-permute-start.1 = (bf16[16,32,128]{2,1,0:T(8,128)(2,1)}, bf16[16,32,128]{2,1,0:T(8,128)(2,1)S(1)}, u32[]{:S(2)}, u32[]{:S(2)}) collective-permute-start(bf16[16,32,128]{2,1,0:T(8,128)(2,1)} %get-tuple-element.16), channel_id=1, source_target_pairs={{0,12},{4,16},{8,20},{24,28},{12,0},{16,4},{20,8},{28,24},{1,13},{... | collective-permute-start | bytes 393224 | tf_op jit(solution)/shard_map/ppermute | solution.py:278
  45.2 0.0 collective-permute-start.2
  45.2 2.0 %collective-permute-start.3 = (bf16[16,32,128]{2,1,0:T(8,128)(2,1)}, bf16[16,32,128]{2,1,0:T(8,128)(2,1)S(1)}, u32[]{:S(2)}, u32[]{:S(2)}) collective-permute-start(bf16[16,32,128]{2,1,0:T(8,128)(2,1)} %get-tuple-element.18), channel_id=1, source_target_pairs={{0,8},{4,12},{16,24},{20,28},{8,0},{12,4},{24,16},{28,20},{1,9},{5... | collective-permute-start | bytes 393224 | tf_op jit(solution)/shard_map/ppermute | solution.py:278
  47.2 0.5 collective-permute-start.4
  47.7 5.4 %collective-permute-done.rest_0_ = bf16[16,32,128]{2,1,0:T(8,128)(2,1)S(1)} collective-permute-done((bf16[16,32,128]{2,1,0:T(8,128)(2,1)}, bf16[16,32,128]{2,1,0:T(8,128)(2,1)S(1)}, u32[]{:S(2)}, u32[]{:S(2)}) %collective-permute-start) | collective-permute-done | bytes 131104 | tf_op jit(solution)/shard_map/ppermute | solution.py:278
  53.0 0.0 collective-permute-start.5
  53.0 0.0 collective-permute-done.1.rest_1_
  53.0 3.6 %collective-permute-start.6 = (bf16[16,32,128]{2,1,0:T(8,128)(2,1)}, bf16[16,32,128]{2,1,0:T(8,128)(2,1)S(1)}, u32[]{:S(2)}, u32[]{:S(2)}) collective-permute-start(bf16[16,32,128]{2,1,0:T(8,128)(2,1)} %get-tuple-element.21), channel_id=1, source_target_pairs={{4,8},{12,16},{20,24},{0,28},{8,4},{16,12},{24,20},{28,0},{5,9},{1... | collective-permute-start | bytes 393224 | tf_op jit(solution)/shard_map/ppermute | solution.py:278
  56.6 0.0 collective-permute-done.2.rest_2_
  56.7 0.0 collective-permute-done.3.rest_3_
  56.7 0.0 collective-permute-done.4.rest_4_
  56.7 3.8 %collective-permute-done.5.rest_5_ = bf16[16,32,128]{2,1,0:T(8,128)(2,1)S(1)} collective-permute-done((bf16[16,32,128]{2,1,0:T(8,128)(2,1)}, bf16[16,32,128]{2,1,0:T(8,128)(2,1)S(1)}, u32[]{:S(2)}, u32[]{:S(2)}) %collective-permute-start.5) | collective-permute-done | bytes 131104 | tf_op jit(solution)/shard_map/ppermute | solution.py:278
  60.5 0.5 collective-permute-done.6.rest_6_
  61.0 0.0 copy-done.6
  61.0 1.2 %copy-done.1 = f32[64,32,128]{2,1,0:T(8,128)S(1)} copy-done((f32[64,32,128]{2,1,0:T(8,128)S(1)}, f32[64,32,128]{2,1,0:T(8,128)}, u32[]{:S(2)}) %copy-start.1) | copy-done | bytes 1048600
  62.2 1.3 %combine.1 = (f32[64,32,128]{2,1,0:T(8,128)S(1)}, f32[2,2048]{1,0:T(2,128)S(1)}) custom-call(f32[64,32,128]{2,1,0:T(8,128)S(1)} %copy-done.1, s32[1,128]{1,0:T(1,128)S(1)} %copy-done.6, bf16[16,32,128]{2,1,0:T(8,128)(2,1)S(1)} %collective-permute-done.rest_0_, bf16[16,32,128]{2,1,0:T(8,128)(2,1)S(1)} %collective-permute-done.1.rest_1_, ...), custom_call_target="tpu_custom_call" | custom-call | tf_op jit(solution)/shard_map/combine/pallas_call | solution.py:288
  63.6 1.0 %copy-done.3 = f32[64,32,128]{2,1,0:T(8,128)} copy-done((f32[64,32,128]{2,1,0:T(8,128)}, f32[64,32,128]{2,1,0:T(8,128)S(1)}, u32[]{:S(2)}) %copy-start.3) | copy-done | bytes 1048600
  64.6 0.0 collective-permute-start.9
  64.6 1.7 %collective-permute-start.8 = (f32[2,2048]{1,0:T(2,128)S(1)}, f32[2,2048]{1,0:T(2,128)S(1)}, u32[]{:S(2)}, u32[]{:S(2)}) collective-permute-start(f32[2,2048]{1,0:T(2,128)S(1)} %get-tuple-element.23.s0), channel_id=1, source_target_pairs={{0,2},{1,3},{2,0},{3,1},{4,6},{5,7},{6,4},{7,5},{8,10},{9,11},{10,... | collective-permute-start | bytes 49160 | tf_op jit(solution)/shard_map/ppermute | solution.py:300
  66.2 0.2 collective-permute-start.7
  66.4 0.1 reshape_tile.3.gain_ref
  66.5 0.0 copy-done.2
  66.5 0.0 copy-start.8
  66.5 4.8 %own.1.own_ref = f32[64,32,128]{2,1,0:T(8,128)S(1)} custom-call(bf16[64,64,256]{2,1,0:T(8,128)(2,1)S(1)} %copy-done, f32[64,32,128]{2,1,0:T(8,128)S(1)} %copy-done.2), custom_call_target="tpu_custom_call" | custom-call | flops 2000000 | bytes 4000000 | tf_op jit(solution)/shard_map/own/pallas_call | solution.py:279
  71.4 0.0 collective-permute-done.9.s3
  71.4 0.0 collective-permute-done.8.s2
  71.4 0.0 collective-permute-done.7.s1
  71.4 3.3 %norm.1 = (bf16[64,64,64]{2,1,0:T(8,128)(2,1)}, bf16[8,32,128]{2,1,0:T(8,128)(2,1)S(1)}) custom-call(f32[64,32,128]{2,1,0:T(8,128)S(1)} %copy-done.4, f32[64,32,128]{2,1,0:T(8,128)S(1)} %own.1.own_ref, f32[1,128]{1,0:T(1,128)S(1)} %reshape_tile.3.gain_ref, bf16[32,256]{1,0:T(8,128)(2,1)S(1)} %copy-done.5, s32[1,8]{1,0:T(1,128)S(1)} %copy-done.8, ...), custom_call_target="tpu_custom_call" | custom-call | tf_op jit(solution)/shard_map/norm/pallas_call | solution.py:303
  74.7 12.0 %all_to_all.5.landed_ref = bf16[8,32,128]{2,1,0:T(8,128)(2,1)S(1)} all-to-all(bf16[8,32,128]{2,1,0:T(8,128)(2,1)S(1)} %get-tuple-element.25), channel_id=1, replica_groups=mesh['tiles'=8,'chan'=4] {'tiles'}, dimensions={0} | all-to-all | bytes 131072 | tf_op jit(solution)/shard_map/all_to_all | solution.py:322
  86.7 1.8 %place.1 = bf16[8,64,64]{2,1,0:T(8,128)(2,1)} custom-call(s32[1,8]{1,0:T(1,128)S(1)} %copy-done.7, bf16[8,32,128]{2,1,0:T(8,128)(2,1)S(1)} %all_to_all.5.landed_ref), custom_call_target="tpu_custom_call" | custom-call | tf_op jit(solution)/shard_map/place/pallas_call | solution.py:323
  (16 shorter events, 0.0 us)
Async XLA Ops:
  0.6 60.4 %copy-start.6 = (s32[1,128]{1,0:T(1,128)S(1)}, s32[1,128]{1,0:T(1,128)}, u32[]{:S(2)}) copy-start(s32[1,128]{1,0:T(1,128)} %list_ref.1) | copy-start | bytes 1540
  0.6 65.8 %copy-start.9 = (bf16[64]{0:T(256)(128)(2,1)S(1)}, bf16[64]{0:T(256)(128)(2,1)}, u32[]{:S(2)}) copy-start(bf16[64]{0:T(256)(128)(2,1)} %param.10) | copy-start | bytes 388
  0.7 65.9 %copy-start = (bf16[64,64,256]{2,1,0:T(8,128)(2,1)S(1)}, bf16[64,64,256]{2,1,0:T(8,128)(2,1)}, u32[]{:S(2)}) copy-start(bf16[64,64,256]{2,1,0:T(8,128)(2,1)} %f_ref.1) | copy-start | bytes 6291460
  38.7 14.3 %collective-permute-start = (bf16[16,32,128]{2,1,0:T(8,128)(2,1)}, bf16[16,32,128]{2,1,0:T(8,128)(2,1)S(1)}, u32[]{:S(2)}, u32[]{:S(2)}) collective-permute-start(bf16[16,32,128]{2,1,0:T(8,128)(2,1)} %get-tuple-element.15), channel_id=1, source_target_pairs={{0,16},{4,20},{8,24},{12,28},{16,0},{20,4},{24,8},{28,12},{1,17},{... | collective-permute-start | bytes 393224 | tf_op jit(solution)/shard_map/ppermute | solution.py:278
  42.9 10.1 %collective-permute-start.1 = (bf16[16,32,128]{2,1,0:T(8,128)(2,1)}, bf16[16,32,128]{2,1,0:T(8,128)(2,1)S(1)}, u32[]{:S(2)}, u32[]{:S(2)}) collective-permute-start(bf16[16,32,128]{2,1,0:T(8,128)(2,1)} %get-tuple-element.16), channel_id=1, source_target_pairs={{0,12},{4,16},{8,20},{24,28},{12,0},{16,4},{20,8},{28,24},{1,13},{... | collective-permute-start | bytes 393224 | tf_op jit(solution)/shard_map/ppermute | solution.py:278
  45.2 11.4 %collective-permute-start.2 = (bf16[16,32,128]{2,1,0:T(8,128)(2,1)}, bf16[16,32,128]{2,1,0:T(8,128)(2,1)S(1)}, u32[]{:S(2)}, u32[]{:S(2)}) collective-permute-start(bf16[16,32,128]{2,1,0:T(8,128)(2,1)} %get-tuple-element.17), channel_id=1, source_target_pairs={{12,24},{16,28},{0,4},{8,20},{24,12},{28,16},{4,0},{20,8},{13,25},... | collective-permute-start | bytes 393224 | tf_op jit(solution)/shard_map/ppermute | solution.py:278
  45.2 11.4 %collective-permute-start.3 = (bf16[16,32,128]{2,1,0:T(8,128)(2,1)}, bf16[16,32,128]{2,1,0:T(8,128)(2,1)S(1)}, u32[]{:S(2)}, u32[]{:S(2)}) collective-permute-start(bf16[16,32,128]{2,1,0:T(8,128)(2,1)} %get-tuple-element.18), channel_id=1, source_target_pairs={{0,8},{4,12},{16,24},{20,28},{8,0},{12,4},{24,16},{28,20},{1,9},{5... | collective-permute-start | bytes 393224 | tf_op jit(solution)/shard_map/ppermute | solution.py:278
  47.2 9.5 %collective-permute-start.4 = (bf16[16,32,128]{2,1,0:T(8,128)(2,1)}, bf16[16,32,128]{2,1,0:T(8,128)(2,1)S(1)}, u32[]{:S(2)}, u32[]{:S(2)}) collective-permute-start(bf16[16,32,128]{2,1,0:T(8,128)(2,1)} %get-tuple-element.19), channel_id=1, source_target_pairs={{8,16},{12,20},{0,4},{24,28},{16,8},{20,12},{4,0},{28,24},{9,17},{... | collective-permute-start | bytes 393224 | tf_op jit(solution)/shard_map/ppermute | solution.py:278
  53.0 7.5 %collective-permute-start.5 = (bf16[16,32,128]{2,1,0:T(8,128)(2,1)}, bf16[16,32,128]{2,1,0:T(8,128)(2,1)S(1)}, u32[]{:S(2)}, u32[]{:S(2)}) collective-permute-start(bf16[16,32,128]{2,1,0:T(8,128)(2,1)} %get-tuple-element.20), channel_id=1, source_target_pairs={{0,4},{8,12},{16,20},{24,28},{4,0},{12,8},{20,16},{28,24},{1,5},{9... | collective-permute-start | bytes 393224 | tf_op jit(solution)/shard_map/ppermute | solution.py:278
  53.0 8.0 %collective-permute-start.6 = (bf16[16,32,128]{2,1,0:T(8,128)(2,1)}, bf16[16,32,128]{2,1,0:T(8,128)(2,1)S(1)}, u32[]{:S(2)}, u32[]{:S(2)}) collective-permute-start(bf16[16,32,128]{2,1,0:T(8,128)(2,1)} %get-tuple-element.21), channel_id=1, source_target_pairs={{4,8},{12,16},{20,24},{0,28},{8,4},{16,12},{24,20},{28,0},{5,9},{1... | collective-permute-start | bytes 393224 | tf_op jit(solution)/shard_map/ppermute | solution.py:278
  61.0 1.2 %copy-start.1 = (f32[64,32,128]{2,1,0:T(8,128)S(1)}, f32[64,32,128]{2,1,0:T(8,128)}, u32[]{:S(2)}) copy-start(f32[64,32,128]{2,1,0:T(8,128)} %get-tuple-element.14.local_ref._after) | copy-start | bytes 3145732
  62.2 4.3 %copy-start.2 = (f32[64,32,128]{2,1,0:T(8,128)S(1)}, f32[64,32,128]{2,1,0:T(8,128)}, u32[]{:S(2)}) copy-start(f32[64,32,128]{2,1,0:T(8,128)} %get-tuple-element.14.local_ref._after) | copy-start | bytes 3145732
  63.6 1.0 %copy-start.3 = (f32[64,32,128]{2,1,0:T(8,128)}, f32[64,32,128]{2,1,0:T(8,128)S(1)}, u32[]{:S(2)}) copy-start(f32[64,32,128]{2,1,0:T(8,128)S(1)} %get-tuple-element.22.conv_ref) | copy-start | bytes 3145732
  64.6 6.8 %collective-permute-start.9 = (f32[2,2048]{1,0:T(2,128)S(1)}, f32[2,2048]{1,0:T(2,128)S(1)}, u32[]{:S(2)}, u32[]{:S(2)}) collective-permute-start(f32[2,2048]{1,0:T(2,128)S(1)} %get-tuple-element.23.s0), channel_id=1, source_target_pairs={{0,3},{1,2},{2,1},{3,0},{4,7},{5,6},{6,5},{7,4},{8,11},{9,10},{10,... | collective-permute-start | bytes 49160 | tf_op jit(solution)/shard_map/ppermute | solution.py:300
  64.6 6.8 %collective-permute-start.8 = (f32[2,2048]{1,0:T(2,128)S(1)}, f32[2,2048]{1,0:T(2,128)S(1)}, u32[]{:S(2)}, u32[]{:S(2)}) collective-permute-start(f32[2,2048]{1,0:T(2,128)S(1)} %get-tuple-element.23.s0), channel_id=1, source_target_pairs={{0,2},{1,3},{2,0},{3,1},{4,6},{5,7},{6,4},{7,5},{8,10},{9,11},{10,... | collective-permute-start | bytes 49160 | tf_op jit(solution)/shard_map/ppermute | solution.py:300
  66.2 5.2 %collective-permute-start.7 = (f32[2,2048]{1,0:T(2,128)S(1)}, f32[2,2048]{1,0:T(2,128)S(1)}, u32[]{:S(2)}, u32[]{:S(2)}) collective-permute-start(f32[2,2048]{1,0:T(2,128)S(1)} %get-tuple-element.23.s0), channel_id=1, source_target_pairs={{0,1},{1,0},{2,3},{3,2},{4,5},{5,4},{6,7},{7,6},{8,9},{9,8},{10,11... | collective-permute-start | bytes 49160 | tf_op jit(solution)/shard_map/ppermute | solution.py:300
  66.5 4.9 %copy-start.4 = (f32[64,32,128]{2,1,0:T(8,128)S(1)}, f32[64,32,128]{2,1,0:T(8,128)}, u32[]{:S(2)}) copy-start(f32[64,32,128]{2,1,0:T(8,128)} %copy-done.3) | copy-start | bytes 3145732
  66.5 4.9 %copy-start.5 = (bf16[32,256]{1,0:T(8,128)(2,1)S(1)}, bf16[32,256]{1,0:T(8,128)(2,1)}, u32[]{:S(2)}) copy-start(bf16[32,256]{1,0:T(8,128)(2,1)} %constant.2.clone.pool_ref) | copy-start | bytes 49156
  66.5 4.9 %copy-start.8 = (s32[1,8]{1,0:T(1,128)S(1)}, s32[1,8]{1,0:T(1,128)}, u32[]{:S(2)}) copy-start(s32[1,8]{1,0:T(1,128)} %slot_ref.1) | copy-start | bytes 100
  71.4 15.4 %copy-start.7 = (s32[1,8]{1,0:T(1,128)S(1)}, s32[1,8]{1,0:T(1,128)}, u32[]{:S(2)}) copy-start(s32[1,8]{1,0:T(1,128)} %place_ref.1) | copy-start | bytes 100

commit v2 on v1

--- a/solution.py
+++ b/solution.py
@@ -72,9 +72,9 @@
         acc_ref[i] = jnp.zeros((VOX, 128), F32)
         return c
 
-    lax.fori_loop(0, 3 * tile_count, zero, 0)
-
-    chunk = 512
+    lax.fori_loop(0, 3 * tile_count, zero, 0, unroll=8)
+
+    chunk = rows
     depth = w_ref.shape[0]
     for q in range(0, depth, 256):
         width = min(256, depth - q)
@@ -131,13 +131,13 @@
             send_ref[i] = folded(base + i).astype(BF)
             return c
 
-        lax.fori_loop(0, slots, emit, 0)
+        lax.fori_loop(0, slots, emit, 0, unroll=16)
 
     def keep(t, c):
         local_ref[t] = folded(t)
         return c
 
-    lax.fori_loop(0, tile_count, keep, 0)
+    lax.fori_loop(0, tile_count, keep, 0, unroll=16)
 
 
 def own_kernel(f_ref, _after, out_ref):
@@ -154,10 +154,10 @@
         out_ref[t] = jnp.where(odd == 1, odd_form, even_form)
         return s
 
-    lax.fori_loop(0, f_ref.shape[0], pack, 0)
-
-
-def combine_kernel(n, ways, local_ref, list_ref, *rest):
+    lax.fori_loop(0, f_ref.shape[0], pack, 0, unroll=8)
+
+
+def combine_kernel(n, ways, local_ref, list_ref, _own, *rest):
     blocks = rest[: len(ways)]
     conv_ref, sums_ref = rest[len(ways) :]
     e = lax.axis_index("tiles")
@@ -246,7 +246,7 @@
 SM = pl.BlockSpec(memory_space=pltpu.SMEM)
 
 
-def body(n, features, weights, gain, rulebook, recv_list, coarse_send, coarse_place):
+def call_rules(n, features, weights, rulebook):
     tile_count, _, channels = features.shape
     offsets, _, quarter = weights.shape
     rule_rows = rulebook.shape[0]
@@ -254,12 +254,9 @@
     slots = tile_count // 4
     span = tile_count * VOX + 2 * PAD
     pairs = (offsets + 1) // 2
-    params = pltpu.CompilerParams(vmem_limit_bytes=58 * 1024 * 1024)
-    small = pltpu.CompilerParams(vmem_limit_bytes=24 * 1024 * 1024)
-
     flat_weights = weights.transpose(0, 2, 1).reshape(offsets * quarter, channels)
     block = jax.ShapeDtypeStruct((slots, HALF, 128), BF)
-    made = pl.pallas_call(
+    return pl.pallas_call(
         functools.partial(conv_kernel, n, ways, tile_count),
         out_shape=[block] * len(ways) + [jax.ShapeDtypeStruct((tile_count, HALF, 128), F32)],
         in_specs=[VM] * 3,
@@ -271,9 +268,18 @@
             pltpu.SMEM((8, rule_rows), jnp.int32),
             pltpu.SemaphoreType.DMA,
         ],
-        compiler_params=params,
+        compiler_params=pltpu.CompilerParams(vmem_limit_bytes=48 * 1024 * 1024),
         name="rules",
     )(rulebook.T, features.reshape(tile_count * VOX, channels), flat_weights)
+
+
+def body(n, features, weights, gain, rulebook, recv_list, coarse_send, coarse_place):
+    tile_count, _, channels = features.shape
+    quarter = weights.shape[2]
+    ways = matchings(n)
+    small = pltpu.CompilerParams(vmem_limit_bytes=12 * 1024 * 1024)
+
+    made = call_rules(n, features, weights, rulebook)
     sends, local = made[:-1], made[-1]
     arrivals = [lax.ppermute(x, "tiles", way[2]) for x, way in zip(sends, ways)]
     own = pl.pallas_call(
@@ -291,11 +297,11 @@
             jax.ShapeDtypeStruct((tile_count, HALF, 128), F32),
             jax.ShapeDtypeStruct((2, tile_count * HALF), F32),
         ],
-        in_specs=[VM, SM] + [VM] * len(ways),
+        in_specs=[VM, SM, pl.BlockSpec(memory_space=pl.ANY)] + [VM] * len(ways),
         out_specs=[VM, VM],
         compiler_params=small,
         name="combine",
-    )(local, recv_list, *arrivals)
+    )(local, recv_list, own, *arrivals)
     wide = lax.axis_size("chan")
     others = [lax.ppermute(sums, "chan", [(i, i ^ m) for i in range(wide)]) for m in range(1, wide)]
     slot_count = coarse_place.shape[1]

time: 88.6 us -> 61.7 us (0.70)
  Pallas kernels: 49.2 us -> 19.2 us
  local copies, waits for them, and re-layouts: 2.36 us -> 3.57 us
  waiting for transfers between devices: 9.72 us -> 10.7 us
    pallas_call x1, Pallas kernels: 38 us -> 12 us  [call_rules(): pl.pallas_call(functools.partial(conv_kernel, n, ways, tile_count), out_s...]
    pallas_call x1, Pallas kernels: 4.83 us -> 0.84 us  [body(): pl.pallas_call(own_kernel, out_shape=jax.ShapeDtypeStruct((tile_count, HA...]
    ppermute x3, waiting for transfers between devices: 0.01 us -> 2.99 us  [body(): lax.ppermute(sums, 'chan', [(i, i ^ m) for i in range(wide)])]
    ppermute x7, waiting for transfers between devices: 9.71 us -> 7.74 us  [body(): arrivals = [lax.ppermute(x, 'tiles', way[2]) for x, way in zip(sends, ways)]]
    unnamed x20 -> x16, local copies, waits for them, and re-layouts: 2.27 us -> 3.49 us
  transfers between devices with their start and end apart: 10 -> 10, of which waited for: 3 -> 5; matrix products, arithmetic and copies ran while one was open for 0% -> 0% of each run, Pallas kernels for 5% -> 1%
where the time goes in v2:
time: 61.7 us; the launch traced here: 61.5 us
  Pallas kernels  19.2 us (31%)
  starting transfers between devices  15.1 us (24%)
  blocking collectives  12.1 us (20%)
  waiting for transfers between devices  10.7 us (17%)
  local copies, waits for them, and re-layouts  3.57 us (6%)
  between operations  0.73 us (1%)
    ppermute x7, starting transfers between devices, body(): arrivals = [lax.ppermute(x, 'tiles', way[2]) for x, way in zip(sends, ways)]  12.9 us
    all_to_all x1, blocking collectives, body(): lax.all_to_all(outbound, 'tiles', split_axis=0, concat_axis=0, tiled=True)  12.1 us
    pallas_call x1, Pallas kernels, call_rules(): pl.pallas_call(functools.partial(conv_kernel, n, ways, tile_count), out_s...  12 us
    ppermute x7, waiting for transfers between devices, body(): arrivals = [lax.ppermute(x, 'tiles', way[2]) for x, way in zip(sends, ways)]  7.74 us
    unnamed x16, local copies, waits for them, and re-layouts  3.49 us
    pallas_call x1, Pallas kernels, body(): pl.pallas_call(functools.partial(norm_kernel, channels), out_shape=[jax.S...  3.26 us
    ppermute x3, waiting for transfers between devices, body(): lax.ppermute(sums, 'chan', [(i, i ^ m) for i in range(wide)])  2.99 us
    ppermute x3, starting transfers between devices, body(): lax.ppermute(sums, 'chan', [(i, i ^ m) for i in range(wide)])  2.18 us
  transfers between devices with their start and end apart: 10, of which 5 were waited for; matrix products, arithmetic and copies ran while one was open for 0% of the time, Pallas kernels for 1%

profile of v2, /device:TPU:0, one launch (start us, length us, event | category | flops | bytes accessed | tf_op | source)
XLA Modules:
  0.0 61.5 jit_solution(13619287523176306812)
XLA Ops:
  0.6 1.6 %copy-done = bf16[64,64,256]{2,1,0:T(8,128)(2,1)S(1)} copy-done((bf16[64,64,256]{2,1,0:T(8,128)(2,1)S(1)}, bf16[64,64,256]{2,1,0:T(8,128)(2,1)}, u32[]{:S(2)}) %copy-start) | copy-done | bytes 2097176
  2.2 1.2 %copy-done.1 = bf16[27,256,64]{1,2,0:T(8,128)(2,1)S(1)} copy-done((bf16[27,256,64]{1,2,0:T(8,128)(2,1)S(1)}, bf16[27,256,64]{1,2,0:T(8,128)(2,1)}, u32[]{:S(2)}) %copy-start.1) | copy-done | bytes 884760
  3.4 0.7 %copy-done.3 = s32[768,4]{0,1:T(4,128)S(1)} copy-done((s32[768,4]{0,1:T(4,128)S(1)}, s32[768,4]{0,1:T(4,128)}, u32[]{:S(2)}) %copy-start.3) | copy-done | bytes 12312
  4.1 12.0 %rules.1 = (bf16[16,32,128]{2,1,0:T(8,128)(2,1)S(1)}, bf16[16,32,128]{2,1,0:T(8,128)(2,1)S(1)}, bf16[16,32,128]{2,1,0:T(8,128)(2,1)S(1)}, bf16[16,32,128]{2,1,0:...) custom-call(s32[4,768]{1,0:T(4,128)S(1)} %bitcast.7, ...), custom_call_target="tpu_custom_call" | custom-call | tf_op jit(solution)/shard_map/rules/pallas_call | solution.py:259
  16.1 3.9 %collective-permute-start = (bf16[16,32,128]{2,1,0:T(8,128)(2,1)S(1)}, bf16[16,32,128]{2,1,0:T(8,128)(2,1)S(1)}, u32[]{:S(2)}, u32[]{:S(2)}) collective-permute-start(bf16[16,32,128]{2,1,0:T(8,128)(2,1)S(1)} %get-tuple-element.15), channel_id=1, source_target_pairs={{0,16},{4,20},{8,24},{12,28},{16,0},{20,4},{24,8},{28,12},{1,17},{... | collective-permute-start | bytes 393224 | tf_op jit(solution)/shard_map/ppermute | solution.py:284
  20.0 2.6 %collective-permute-start.1 = (bf16[16,32,128]{2,1,0:T(8,128)(2,1)S(1)}, bf16[16,32,128]{2,1,0:T(8,128)(2,1)S(1)}, u32[]{:S(2)}, u32[]{:S(2)}) collective-permute-start(bf16[16,32,128]{2,1,0:T(8,128)(2,1)S(1)} %get-tuple-element.16), channel_id=1, source_target_pairs={{0,12},{4,16},{8,20},{24,28},{12,0},{16,4},{20,8},{28,24},{1,13},{... | collective-permute-start | bytes 393224 | tf_op jit(solution)/shard_map/ppermute | solution.py:284
  22.6 0.0 collective-permute-start.2
  22.6 1.6 %collective-permute-start.3 = (bf16[16,32,128]{2,1,0:T(8,128)(2,1)S(1)}, bf16[16,32,128]{2,1,0:T(8,128)(2,1)S(1)}, u32[]{:S(2)}, u32[]{:S(2)}) collective-permute-start(bf16[16,32,128]{2,1,0:T(8,128)(2,1)S(1)} %get-tuple-element.18), channel_id=1, source_target_pairs={{0,8},{4,12},{16,24},{20,28},{8,0},{12,4},{24,16},{28,20},{1,9},{5... | collective-permute-start | bytes 393224 | tf_op jit(solution)/shard_map/ppermute | solution.py:284
  24.3 0.8 %collective-permute-start.4 = (bf16[16,32,128]{2,1,0:T(8,128)(2,1)S(1)}, bf16[16,32,128]{2,1,0:T(8,128)(2,1)S(1)}, u32[]{:S(2)}, u32[]{:S(2)}) collective-permute-start(bf16[16,32,128]{2,1,0:T(8,128)(2,1)S(1)} %get-tuple-element.19), channel_id=1, source_target_pairs={{8,16},{12,20},{0,4},{24,28},{16,8},{20,12},{4,0},{28,24},{9,17},{... | collective-permute-start | bytes 393224 | tf_op jit(solution)/shard_map/ppermute | solution.py:284
  25.0 4.9 %collective-permute-done.rest_0_ = bf16[16,32,128]{2,1,0:T(8,128)(2,1)S(1)} collective-permute-done((bf16[16,32,128]{2,1,0:T(8,128)(2,1)S(1)}, bf16[16,32,128]{2,1,0:T(8,128)(2,1)S(1)}, u32[]{:S(2)}, u32[]{:S(2)}) %collective-permute-start) | collective-permute-done | bytes 131104 | tf_op jit(solution)/shard_map/ppermute | solution.py:284
  29.9 0.0 collective-permute-start.5
  29.9 0.0 collective-permute-done.1.rest_1_
  30.0 4.0 %collective-permute-start.6 = (bf16[16,32,128]{2,1,0:T(8,128)(2,1)S(1)}, bf16[16,32,128]{2,1,0:T(8,128)(2,1)S(1)}, u32[]{:S(2)}, u32[]{:S(2)}) collective-permute-start(bf16[16,32,128]{2,1,0:T(8,128)(2,1)S(1)} %get-tuple-element.21), channel_id=1, source_target_pairs={{4,8},{12,16},{20,24},{0,28},{8,4},{16,12},{24,20},{28,0},{5,9},{1... | collective-permute-start | bytes 393224 | tf_op jit(solution)/shard_map/ppermute | solution.py:284
  34.0 0.8 %own.1._own.own_ref = f32[64,32,128]{2,1,0:T(8,128)S(1)} custom-call(bf16[64,64,256]{2,1,0:T(8,128)(2,1)S(1)} %copy-done, f32[64,32,128]{2,1,0:T(8,128)S(1)} %get-tuple-element.14._after.local_ref), custom_call_target="tpu_custom_call" | custom-call | flops 2000000 | bytes 4000000 | tf_op jit(solution)/shard_map/own/pallas_call | solution.py:285
  34.8 0.0 copy-start.7
  34.8 0.0 copy-start.2
  34.8 0.0 copy-start.6
  34.9 0.0 copy-start.5
  34.9 0.0 collective-permute-done.2.rest_2_
  34.9 0.0 collective-permute-done.4.rest_4_
  34.9 2.0 %collective-permute-done.5.rest_5_ = bf16[16,32,128]{2,1,0:T(8,128)(2,1)S(1)} collective-permute-done((bf16[16,32,128]{2,1,0:T(8,128)(2,1)S(1)}, bf16[16,32,128]{2,1,0:T(8,128)(2,1)S(1)}, u32[]{:S(2)}, u32[]{:S(2)}) %collective-permute-start.5) | collective-permute-done | bytes 131104 | tf_op jit(solution)/shard_map/ppermute | solution.py:284
  36.9 0.8 %collective-permute-done.6.rest_6_ = bf16[16,32,128]{2,1,0:T(8,128)(2,1)S(1)} collective-permute-done((bf16[16,32,128]{2,1,0:T(8,128)(2,1)S(1)}, bf16[16,32,128]{2,1,0:T(8,128)(2,1)S(1)}, u32[]{:S(2)}, u32[]{:S(2)}) %collective-permute-start.6) | collective-permute-done | bytes 131104 | tf_op jit(solution)/shard_map/ppermute | solution.py:284
  37.7 1.3 %combine.1 = (f32[64,32,128]{2,1,0:T(8,128)S(1)}, f32[2,2048]{1,0:T(2,128)S(1)}) custom-call(f32[64,32,128]{2,1,0:T(8,128)S(1)} %get-tuple-element.14._after.local_ref, s32[1,128]{1,0:T(1,128)S(1)} %copy-done.4, f32[64,32,128]{2,1,0:T(8,128)S(1)} %own.1._own.own_ref, bf16[16,32,128]{2,1,0:T(8,128)(2,1)S(1)} %collective-permute-done.rest_0_, ...), custom_call_target="tpu_custom_call" | custom-call | tf_op jit(solution)/shard_map/combine/pallas_call | solution.py:294
  39.0 0.0 collective-permute-start.7
  39.1 2.1 %collective-permute-start.8 = (f32[2,2048]{1,0:T(2,128)S(1)}, f32[2,2048]{1,0:T(2,128)S(1)}, u32[]{:S(2)}, u32[]{:S(2)}) collective-permute-start(f32[2,2048]{1,0:T(2,128)S(1)} %get-tuple-element.23.s0), channel_id=1, source_target_pairs={{0,2},{1,3},{2,0},{3,1},{4,6},{5,7},{6,4},{7,5},{8,10},{9,11},{10,... | collective-permute-start | bytes 49160 | tf_op jit(solution)/shard_map/ppermute | solution.py:306
  41.1 0.1 collective-permute-start.9
  41.2 0.1 reshape_tile.3.gain_ref
  41.3 1.5 %collective-permute-done.8.s2 = f32[2,2048]{1,0:T(2,128)S(1)} collective-permute-done((f32[2,2048]{1,0:T(2,128)S(1)}, f32[2,2048]{1,0:T(2,128)S(1)}, u32[]{:S(2)}, u32[]{:S(2)}) %collective-permute-start.8) | collective-permute-done | bytes 16416 | tf_op jit(solution)/shard_map/ppermute | solution.py:306
  42.9 1.4 %collective-permute-done.9.s3 = f32[2,2048]{1,0:T(2,128)S(1)} collective-permute-done((f32[2,2048]{1,0:T(2,128)S(1)}, f32[2,2048]{1,0:T(2,128)S(1)}, u32[]{:S(2)}, u32[]{:S(2)}) %collective-permute-start.9) | collective-permute-done | bytes 16416 | tf_op jit(solution)/shard_map/ppermute | solution.py:306
  44.3 3.3 %norm.1 = (bf16[64,64,64]{2,1,0:T(8,128)(2,1)}, bf16[8,32,128]{2,1,0:T(8,128)(2,1)S(1)}) custom-call(f32[64,32,128]{2,1,0:T(8,128)S(1)} %get-tuple-element.22.conv_ref, f32[64,32,128]{2,1,0:T(8,128)S(1)} %own.1._own.own_ref, f32[1,128]{1,0:T(1,128)S(1)} %reshape_tile.3.gain_ref, bf16[32,256]{1,0:T(8,128)(2,1)S(1)} %copy-done.2, s32[1,8]{1,0:T(1,128)S(1)} %copy-done.6, ...), custom_call_target="tpu_custom_call" | custom-call | tf_op jit(solution)/shard_map/norm/pallas_call | solution.py:309
  47.6 12.1 %all_to_all.5.landed_ref = bf16[8,32,128]{2,1,0:T(8,128)(2,1)S(1)} all-to-all(bf16[8,32,128]{2,1,0:T(8,128)(2,1)S(1)} %get-tuple-element.25), channel_id=1, replica_groups=mesh['tiles'=8,'chan'=4] {'tiles'}, dimensions={0} | all-to-all | bytes 131072 | tf_op jit(solution)/shard_map/all_to_all | solution.py:328
  59.7 1.8 %place.1 = bf16[8,64,64]{2,1,0:T(8,128)(2,1)} custom-call(s32[1,8]{1,0:T(1,128)S(1)} %copy-done.5, bf16[8,32,128]{2,1,0:T(8,128)(2,1)S(1)} %all_to_all.5.landed_ref), custom_call_target="tpu_custom_call" | custom-call | tf_op jit(solution)/shard_map/place/pallas_call | solution.py:329
  (12 shorter events, 0.0 us)
Async XLA Ops:
  0.6 1.6 %copy-start = (bf16[64,64,256]{2,1,0:T(8,128)(2,1)S(1)}, bf16[64,64,256]{2,1,0:T(8,128)(2,1)}, u32[]{:S(2)}) copy-start(bf16[64,64,256]{2,1,0:T(8,128)(2,1)} %f_ref.1) | copy-start | bytes 6291460
  2.2 1.2 %copy-start.1 = (bf16[27,256,64]{1,2,0:T(8,128)(2,1)S(1)}, bf16[27,256,64]{1,2,0:T(8,128)(2,1)}, u32[]{:S(2)}) copy-start(bf16[27,256,64]{1,2,0:T(8,128)(2,1)} %param.9) | copy-start | bytes 2654212
  3.4 0.7 %copy-start.3 = (s32[768,4]{0,1:T(4,128)S(1)}, s32[768,4]{0,1:T(4,128)}, u32[]{:S(2)}) copy-start(s32[768,4]{0,1:T(4,128)} %param.11) | copy-start | bytes 36868
  16.1 13.8 %collective-permute-start = (bf16[16,32,128]{2,1,0:T(8,128)(2,1)S(1)}, bf16[16,32,128]{2,1,0:T(8,128)(2,1)S(1)}, u32[]{:S(2)}, u32[]{:S(2)}) collective-permute-start(bf16[16,32,128]{2,1,0:T(8,128)(2,1)S(1)} %get-tuple-element.15), channel_id=1, source_target_pairs={{0,16},{4,20},{8,24},{12,28},{16,0},{20,4},{24,8},{28,12},{1,17},{... | collective-permute-start | bytes 393224 | tf_op jit(solution)/shard_map/ppermute | solution.py:284
  20.0 10.0 %collective-permute-start.1 = (bf16[16,32,128]{2,1,0:T(8,128)(2,1)S(1)}, bf16[16,32,128]{2,1,0:T(8,128)(2,1)S(1)}, u32[]{:S(2)}, u32[]{:S(2)}) collective-permute-start(bf16[16,32,128]{2,1,0:T(8,128)(2,1)S(1)} %get-tuple-element.16), channel_id=1, source_target_pairs={{0,12},{4,16},{8,20},{24,28},{12,0},{16,4},{20,8},{28,24},{1,13},{... | collective-permute-start | bytes 393224 | tf_op jit(solution)/shard_map/ppermute | solution.py:284
  22.6 12.2 %collective-permute-start.2 = (bf16[16,32,128]{2,1,0:T(8,128)(2,1)S(1)}, bf16[16,32,128]{2,1,0:T(8,128)(2,1)S(1)}, u32[]{:S(2)}, u32[]{:S(2)}) collective-permute-start(bf16[16,32,128]{2,1,0:T(8,128)(2,1)S(1)} %get-tuple-element.17), channel_id=1, source_target_pairs={{12,24},{16,28},{0,4},{8,20},{24,12},{28,16},{4,0},{20,8},{13,25},... | collective-permute-start | bytes 393224 | tf_op jit(solution)/shard_map/ppermute | solution.py:284
  22.6 12.3 %collective-permute-start.3 = (bf16[16,32,128]{2,1,0:T(8,128)(2,1)S(1)}, bf16[16,32,128]{2,1,0:T(8,128)(2,1)S(1)}, u32[]{:S(2)}, u32[]{:S(2)}) collective-permute-start(bf16[16,32,128]{2,1,0:T(8,128)(2,1)S(1)} %get-tuple-element.18), channel_id=1, source_target_pairs={{0,8},{4,12},{16,24},{20,28},{8,0},{12,4},{24,16},{28,20},{1,9},{5... | collective-permute-start | bytes 393224 | tf_op jit(solution)/shard_map/ppermute | solution.py:284
  24.3 10.6 %collective-permute-start.4 = (bf16[16,32,128]{2,1,0:T(8,128)(2,1)S(1)}, bf16[16,32,128]{2,1,0:T(8,128)(2,1)S(1)}, u32[]{:S(2)}, u32[]{:S(2)}) collective-permute-start(bf16[16,32,128]{2,1,0:T(8,128)(2,1)S(1)} %get-tuple-element.19), channel_id=1, source_target_pairs={{8,16},{12,20},{0,4},{24,28},{16,8},{20,12},{4,0},{28,24},{9,17},{... | collective-permute-start | bytes 393224 | tf_op jit(solution)/shard_map/ppermute | solution.py:284
  29.9 7.0 %collective-permute-start.5 = (bf16[16,32,128]{2,1,0:T(8,128)(2,1)S(1)}, bf16[16,32,128]{2,1,0:T(8,128)(2,1)S(1)}, u32[]{:S(2)}, u32[]{:S(2)}) collective-permute-start(bf16[16,32,128]{2,1,0:T(8,128)(2,1)S(1)} %get-tuple-element.20), channel_id=1, source_target_pairs={{0,4},{8,12},{16,20},{24,28},{4,0},{12,8},{20,16},{28,24},{1,5},{9... | collective-permute-start | bytes 393224 | tf_op jit(solution)/shard_map/ppermute | solution.py:284
  30.0 7.8 %collective-permute-start.6 = (bf16[16,32,128]{2,1,0:T(8,128)(2,1)S(1)}, bf16[16,32,128]{2,1,0:T(8,128)(2,1)S(1)}, u32[]{:S(2)}, u32[]{:S(2)}) collective-permute-start(bf16[16,32,128]{2,1,0:T(8,128)(2,1)S(1)} %get-tuple-element.21), channel_id=1, source_target_pairs={{4,8},{12,16},{20,24},{0,28},{8,4},{16,12},{24,20},{28,0},{5,9},{1... | collective-permute-start | bytes 393224 | tf_op jit(solution)/shard_map/ppermute | solution.py:284
  34.0 3.8 %copy-start.4 = (s32[1,128]{1,0:T(1,128)S(1)}, s32[1,128]{1,0:T(1,128)}, u32[]{:S(2)}) copy-start(s32[1,128]{1,0:T(1,128)} %list_ref.1) | copy-start | bytes 1540
  34.8 6.4 %copy-start.7 = (bf16[64]{0:T(256)(128)(2,1)S(1)}, bf16[64]{0:T(256)(128)(2,1)}, u32[]{:S(2)}) copy-start(bf16[64]{0:T(256)(128)(2,1)} %param.10) | copy-start | bytes 388
  34.8 9.5 %copy-start.2 = (bf16[32,256]{1,0:T(8,128)(2,1)S(1)}, bf16[32,256]{1,0:T(8,128)(2,1)}, u32[]{:S(2)}) copy-start(bf16[32,256]{1,0:T(8,128)(2,1)} %constant.2.clone.pool_ref) | copy-start | bytes 49156
  34.8 9.5 %copy-start.6 = (s32[1,8]{1,0:T(1,128)S(1)}, s32[1,8]{1,0:T(1,128)}, u32[]{:S(2)}) copy-start(s32[1,8]{1,0:T(1,128)} %slot_ref.1) | copy-start | bytes 100
  34.9 24.9 %copy-start.5 = (s32[1,8]{1,0:T(1,128)S(1)}, s32[1,8]{1,0:T(1,128)}, u32[]{:S(2)}) copy-start(s32[1,8]{1,0:T(1,128)} %place_ref.1) | copy-start | bytes 100
  39.0 2.3 %collective-permute-start.7 = (f32[2,2048]{1,0:T(2,128)S(1)}, f32[2,2048]{1,0:T(2,128)S(1)}, u32[]{:S(2)}, u32[]{:S(2)}) collective-permute-start(f32[2,2048]{1,0:T(2,128)S(1)} %get-tuple-element.23.s0), channel_id=1, source_target_pairs={{0,1},{1,0},{2,3},{3,2},{4,5},{5,4},{6,7},{7,6},{8,9},{9,8},{10,11... | collective-permute-start | bytes 49160 | tf_op jit(solution)/shard_map/ppermute | solution.py:306
  39.1 3.8 %collective-permute-start.8 = (f32[2,2048]{1,0:T(2,128)S(1)}, f32[2,2048]{1,0:T(2,128)S(1)}, u32[]{:S(2)}, u32[]{:S(2)}) collective-permute-start(f32[2,2048]{1,0:T(2,128)S(1)} %get-tuple-element.23.s0), channel_id=1, source_target_pairs={{0,2},{1,3},{2,0},{3,1},{4,6},{5,7},{6,4},{7,5},{8,10},{9,11},{10,... | collective-permute-start | bytes 49160 | tf_op jit(solution)/shard_map/ppermute | solution.py:306
  41.1 3.2 %collective-permute-start.9 = (f32[2,2048]{1,0:T(2,128)S(1)}, f32[2,2048]{1,0:T(2,128)S(1)}, u32[]{:S(2)}, u32[]{:S(2)}) collective-permute-start(f32[2,2048]{1,0:T(2,128)S(1)} %get-tuple-element.23.s0), channel_id=1, source_target_pairs={{0,3},{1,2},{2,1},{3,0},{4,7},{5,6},{6,5},{7,4},{8,11},{9,10},{10,... | collective-permute-start | bytes 49160 | tf_op jit(solution)/shard_map/ppermute | solution.py:306

commit v3 on v2

--- a/solution.py
+++ b/solution.py
@@ -45,119 +45,176 @@
     return (lax.div(code, 9) - 1, lax.rem(lax.div(code, 3), 3) - 1, lax.rem(code, 3) - 1)
 
 
-def conv_kernel(n, ways, tile_count, rules_ref, f_ref, w_ref, *rest):
+def rules_matmul(f_ref, w_ref, y_ref, beside=None):
+    rows = f_ref.shape[0]
+    span = rows + 2 * PAD
+    depth = w_ref.shape[0]
+    steps = range(0, depth, 256)
+    for number, q in enumerate(steps):
+        width = min(256, depth - q)
+        part = lax.dot_general(
+            f_ref[...],
+            w_ref[q : q + width, :],
+            (((1,), (1,)), ((), ())),
+            preferred_element_type=F32,
+        )
+        for s in range(0, width, 128):
+            wide = min(128, width - s)
+            base = ((q + s) // 128) * span + PAD
+            y_ref[base : base + rows, 0:wide] = part[:, s : s + wide]
+        if beside is not None:
+            beside(number, len(steps))
+
+
+def rules_add(words, lists, start, count, y_ref, acc_ref):
+    voxel = lax.broadcasted_iota(jnp.int32, (VOX, 128), 0)
+    have = jnp.where(lane_iota((VOX, 128)) < 64, 1 << 21, 1 << 22)
+    for dim, place in enumerate((lax.div(voxel, 16), lax.rem(lax.div(voxel, 4), 4), lax.rem(voxel, 4))):
+        have = have + jnp.left_shift(jnp.full_like(place, 15), 3 - place + 7 * dim)
+
+    def several(i, c):
+        for u in range(UNROLL):
+            r = lists[start + i * UNROLL + u]
+            packed = words[0, r]
+            need = words[1, r]
+            taken = y_ref[pl.ds(lax.shift_right_logical(packed, 8), VOX), :]
+            t = packed & 255
+            acc_ref[t] = acc_ref[t] + jnp.where((have & need) == need, taken, 0.0)
+        return c
+
+    lax.fori_loop(0, lax.div(count + (UNROLL - 1), UNROLL), several, 0)
+
+
+def zero_blocks(acc_ref):
+    def zero(i, c):
+        acc_ref[i] = jnp.zeros((VOX, 128), F32)
+        return c
+
+    lax.fori_loop(0, acc_ref.shape[0], zero, 0, unroll=8)
+
+
+def folded(acc_ref, t):
+    first = lane_iota((HALF, 128)) < 64
+    low = acc_ref[t, 0:HALF, :]
+    high = acc_ref[t, HALF:VOX, :]
+    low = low + pltpu.roll(low, 64, 1)
+    high = high + pltpu.roll(high, 64, 1)
+    return jnp.where(first, low, high)
+
+
+def emit_sends(n, ways, acc_ref, sends):
+    e = lax.axis_index("tiles")
+    slots = sends[0].shape[0]
+    for (d, parity, _), send_ref in zip(ways, sends):
+        low, _high = role(e, n, d, parity)
+        base = slots * ((d - 1) % 2 + jnp.where(low, 0, 2))
+
+        def emit(i, c, send_ref=send_ref, base=base):
+            send_ref[i] = folded(acc_ref, base + i).astype(BF)
+            return c
+
+        lax.fori_loop(0, slots, emit, 0, unroll=16)
+
+
+def far_kernel(n, ways, tile_count, rules_hbm, f_hbm, w_hbm, *rest):
     sends = rest[: len(ways)]
-    local_ref, y_ref, acc_ref, words_v, words_s, sem = rest[len(ways) :]
+    words_v, lists, y_ref, acc_ref, f_ref, w_ref, rules_ref, words_s, sems = rest[len(ways) :]
     rows = tile_count * VOX
     span = rows + 2 * PAD
     rule_rows = rules_ref.shape[1]
-    e = lax.axis_index("tiles")
+    wide = words_v.shape[1]
+    slots = tile_count // 4
+    copies = [
+        pltpu.make_async_copy(src, dst, sems.at[i])
+        for i, (src, dst) in enumerate(((rules_hbm, rules_ref), (w_hbm, w_ref), (f_hbm, f_ref)))
+    ]
+    for copy in copies:
+        copy.start()
+    before = lax.broadcasted_iota(jnp.int32, (rule_rows, rule_rows), 0)
+    before = (before <= lane_iota((rule_rows, rule_rows))).astype(F32).astype(BF)
+    zero_blocks(acc_ref)
+    copies[0].wait()
     tile = rules_ref[0:1, :]
     kernel = rules_ref[1:2, :]
     heading = rules_ref[2:3, :]
+    target = rules_ref[3:4, :]
     code = jnp.minimum(kernel, 26)
     shift = jnp.zeros_like(code)
-    need = jnp.where(kernel < 27, 0, 1 << 23) + jnp.where(lax.rem(code, 2) == 0, 1 << 21, 1 << 22)
+    need = jnp.where(lax.rem(code, 2) == 0, 1 << 21, 1 << 22)
     for dim, (step, turn) in enumerate(zip(dims_of(code), dims_of(heading))):
         move = step - 4 * turn
         shift = shift + move * (16, 4, 1)[dim]
         need = need + jnp.left_shift(jnp.full_like(move, 1), move + (3 + 7 * dim))
-    words_v[0:1, :] = lax.div(code, 2) * span + PAD + tile * VOX + shift
-    words_v[1:2, :] = rules_ref[3:4, :]
-    words_v[2:3, :] = need
-    copy = pltpu.make_async_copy(words_v, words_s, sem)
-    copy.start()
-
-    def zero(i, c):
-        acc_ref[i] = jnp.zeros((VOX, 128), F32)
-        return c
-
-    lax.fori_loop(0, 3 * tile_count, zero, 0, unroll=8)
-
-    chunk = rows
-    depth = w_ref.shape[0]
-    for q in range(0, depth, 256):
-        width = min(256, depth - q)
-
-        def product(i, c, q=q, width=width):
-            at = pl.multiple_of(i * chunk, chunk)
-            part = lax.dot_general(
-                f_ref[pl.ds(at, chunk), :],
-                w_ref[q : q + width, :],
-                (((1,), (1,)), ((), ())),
-                preferred_element_type=F32,
-            )
-            for s in range(0, width, 128):
-                wide = min(128, width - s)
-                base = ((q + s) // 128) * span + PAD
-                y_ref[pl.ds(pl.multiple_of(base + at, 8), chunk), 0:wide] = part[:, s : s + wide]
-            return c
-
-        lax.fori_loop(0, rows // chunk, product, 0)
-
-    voxel = lax.broadcasted_iota(jnp.int32, (VOX, 128), 0)
-    lane = lane_iota((VOX, 128))
-    have = jnp.where(lane < 64, 1 << 21, 1 << 22)
-    for dim, place in enumerate((lax.div(voxel, 16), lax.rem(lax.div(voxel, 4), 4), lax.rem(voxel, 4))):
-        have = have + jnp.left_shift(jnp.full_like(place, 15), 3 - place + 7 * dim)
-    copy.wait()
-
-    def rule(i, c):
+    sent = jnp.maximum(target - tile_count, 0)
+    group = lax.div(sent, slots)
+    place = (lax.div(group, 4) * 2 + lax.rem(group, 2)) * slots + lax.rem(sent, slots)
+    near = lax.rem(group, 4) < 2
+    part = jnp.where(target < tile_count, 2, jnp.where(near, 1, 0))
+    part = jnp.where(kernel < 27, part, 3)
+    kind = lax.broadcasted_iota(jnp.int32, (8, rule_rows), 0)
+    flags = jnp.where(kind == part, 1.0, 0.0)
+    upto = jnp.dot(flags.astype(BF), before, preferred_element_type=F32)
+    at = jnp.sum(flags * (upto - 1.0 + (kind * wide).astype(F32)), axis=0, keepdims=True)
+    first_row = lax.div(code, 2) * span + PAD + tile * VOX + shift
+    words_v[...] = jnp.zeros(words_v.shape, jnp.int32)
+    words_v[0:1, 0:rule_rows] = first_row * 256 + jnp.where(target < tile_count, target, place)
+    words_v[1:2, 0:rule_rows] = need
+    words_v[2:3, 0:rule_rows] = at.astype(jnp.int32)
+    words_v[0:1, rule_rows:wide] = jnp.full((1, wide - rule_rows), PAD * 256, jnp.int32)
+    words_v[1:2, rule_rows:wide] = jnp.full((1, wide - rule_rows), 1 << 23, jnp.int32)
+    totals = jnp.broadcast_to(upto[0:3, rule_rows - 1 : rule_rows], (3, 128))
+    words_v[3:6, 0:128] = totals.astype(jnp.int32)
+    to_scalars = pltpu.make_async_copy(words_v, words_s, sems.at[3])
+    to_scalars.start()
+    to_scalars.wait()
+    copies[1].wait()
+    copies[2].wait()
+
+    def list_some(number, count):
+        share = -(-rule_rows // count)
+        for r in range(number * share, min(rule_rows, (number + 1) * share)):
+            lists[words_s[2, r]] = r
+
+    rules_matmul(f_ref, w_ref, y_ref, list_some)
+    for c in range(3):
         for u in range(UNROLL):
-            r = i * UNROLL + u
-            need_r = words_s[2, r]
-            taken = y_ref[pl.ds(words_s[0, r], VOX), :]
-            t = words_s[1, r]
-            acc_ref[t] = acc_ref[t] + jnp.where((have & need_r) == need_r, taken, 0.0)
-        return c
-
-    lax.fori_loop(0, rule_rows // UNROLL, rule, 0)
-
-    first = lane_iota((HALF, 128)) < 64
-
-    def folded(t):
-        low = acc_ref[t, 0:HALF, :]
-        high = acc_ref[t, HALF:VOX, :]
-        low = low + pltpu.roll(low, 64, 1)
-        high = high + pltpu.roll(high, 64, 1)
-        return jnp.where(first, low, high)
-
-    slots = 2 * tile_count // 8
-    for (d, parity, _), send_ref in zip(ways, sends):
-        low, _high = role(e, n, d, parity)
-        base = tile_count + slots * jnp.where(low, d - 1, d + 3)
-
-        def emit(i, c, send_ref=send_ref, base=base):
-            send_ref[i] = folded(base + i).astype(BF)
-            return c
-
-        lax.fori_loop(0, slots, emit, 0, unroll=16)
-
-    def keep(t, c):
-        local_ref[t] = folded(t)
-        return c
-
-    lax.fori_loop(0, tile_count, keep, 0, unroll=16)
-
-
-def own_kernel(f_ref, _after, out_ref):
+            lists[c * wide + words_s[3 + c, 0] + u] = rule_rows
+    rules_add(words_s, lists, 0, words_s[3, 0], y_ref, acc_ref)
+    emit_sends(n, ways, acc_ref, sends)
+
+
+def near_kernel(n, ways, words, lists, f_ref, w_ref, *rest):
+    sends = rest[: len(ways)]
+    y_ref, acc_ref = rest[len(ways) :]
+    zero_blocks(acc_ref)
+    rules_matmul(f_ref, w_ref, y_ref)
+    rules_add(words, lists, words.shape[1], words[4, 0], y_ref, acc_ref)
+    emit_sends(n, ways, acc_ref, sends)
+
+
+def local_kernel(words, lists, f_ref, w_ref, _after, local_ref, own_ref, y_ref, acc_ref):
+    tile_count = acc_ref.shape[0]
+    zero_blocks(acc_ref)
+    rules_matmul(f_ref, w_ref, y_ref)
+    rules_add(words, lists, 2 * words.shape[1], words[5, 0], y_ref, acc_ref)
     c = lax.axis_index("chan")
     at = pl.multiple_of(lax.div(c, 2) * 128, 128)
-    odd = lax.rem(c, 2)
+    odd = lax.rem(c, 2) == 1
     first = lane_iota((HALF, 128)) < 64
 
-    def pack(t, s):
-        block = f_ref[t, :, pl.ds(at, 128)].astype(F32)
+    def keep(t, c):
+        local_ref[t] = folded(acc_ref, t)
+        block = f_ref[pl.ds(pl.multiple_of(t * VOX, VOX), VOX), pl.ds(at, 128)].astype(F32)
         low, high = block[:HALF], block[HALF:]
         even_form = jnp.where(first, low, pltpu.roll(high, 64, 1))
         odd_form = jnp.where(first, pltpu.roll(low, 64, 1), high)
-        out_ref[t] = jnp.where(odd == 1, odd_form, even_form)
-        return s
-
-    lax.fori_loop(0, f_ref.shape[0], pack, 0, unroll=8)
-
-
-def combine_kernel(n, ways, local_ref, list_ref, _own, *rest):
+        own_ref[t] = jnp.where(odd, odd_form, even_form)
+        return c
+
+    lax.fori_loop(0, tile_count, keep, 0, unroll=8)
+
+
+def combine_kernel(n, ways, local_ref, list_ref, *rest):
     blocks = rest[: len(ways)]
     conv_ref, sums_ref = rest[len(ways) :]
     e = lax.axis_index("tiles")
@@ -244,6 +301,8 @@
 
 VM = pl.BlockSpec(memory_space=pltpu.VMEM)
 SM = pl.BlockSpec(memory_space=pltpu.SMEM)
+ANY = pl.BlockSpec(memory_space=pl.ANY)
+HBM = pl.BlockSpec(memory_space=pltpu.HBM)
 
 
 def call_rules(n, features, weights, rulebook):
@@ -251,26 +310,59 @@
     offsets, _, quarter = weights.shape
     rule_rows = rulebook.shape[0]
     ways = matchings(n)
+    far = [way for way in ways if way[0] > 2]
+    near = [way for way in ways if way[0] <= 2]
     slots = tile_count // 4
     span = tile_count * VOX + 2 * PAD
     pairs = (offsets + 1) // 2
+    wide = rule_rows + 128
+    flat = features.reshape(tile_count * VOX, channels)
     flat_weights = weights.transpose(0, 2, 1).reshape(offsets * quarter, channels)
     block = jax.ShapeDtypeStruct((slots, HALF, 128), BF)
-    return pl.pallas_call(
-        functools.partial(conv_kernel, n, ways, tile_count),
-        out_shape=[block] * len(ways) + [jax.ShapeDtypeStruct((tile_count, HALF, 128), F32)],
-        in_specs=[VM] * 3,
-        out_specs=[VM] * (len(ways) + 1),
-        scratch_shapes=[
-            pltpu.VMEM((pairs * span, 128), F32),
-            pltpu.VMEM((3 * tile_count, VOX, 128), F32),
-            pltpu.VMEM((8, rule_rows), jnp.int32),
-            pltpu.SMEM((8, rule_rows), jnp.int32),
-            pltpu.SemaphoreType.DMA,
+    whole = jax.ShapeDtypeStruct((tile_count, HALF, 128), F32)
+    work = [pltpu.VMEM((pairs * span, 128), F32), pltpu.VMEM((tile_count, VOX, 128), F32)]
+    flops = 2 * tile_count * VOX * channels * offsets * quarter
+    shared = dict(
+        compiler_params=pltpu.CompilerParams(vmem_limit_bytes=44 * 1024 * 1024),
+        cost_estimate=pl.CostEstimate(flops=flops, bytes_accessed=8 << 20, transcendentals=0),
+    )
+    made = pl.pallas_call(
+        functools.partial(far_kernel, n, far, tile_count),
+        out_shape=[block] * len(far)
+        + [jax.ShapeDtypeStruct((8, wide), jnp.int32), jax.ShapeDtypeStruct((4 * wide,), jnp.int32)],
+        in_specs=[HBM] * 3,
+        out_specs=[VM] * (len(far) + 1) + [SM],
+        scratch_shapes=work
+        + [
+            pltpu.VMEM(flat.shape, BF),
+            pltpu.VMEM(flat_weights.shape, BF),
+            pltpu.VMEM((4, rule_rows), jnp.int32),
+            pltpu.SMEM((8, wide), jnp.int32),
+            pltpu.SemaphoreType.DMA((4,)),
         ],
-        compiler_params=pltpu.CompilerParams(vmem_limit_bytes=48 * 1024 * 1024),
-        name="rules",
-    )(rulebook.T, features.reshape(tile_count * VOX, channels), flat_weights)
+        name="far",
+        **shared,
+    )(rulebook.T, flat, flat_weights)
+    far_sends, words, lists = made[: len(far)], made[-2], made[-1]
+    near_sends = pl.pallas_call(
+        functools.partial(near_kernel, n, near),
+        out_shape=[block] * len(near),
+        in_specs=[SM, SM, VM, VM],
+        out_specs=[VM] * len(near),
+        scratch_shapes=work,
+        name="near",
+        **shared,
+    )(words, lists, flat, flat_weights)
+    local, own = pl.pallas_call(
+        local_kernel,
+        out_shape=[whole, whole],
+        in_specs=[SM, SM, VM, VM, ANY],
+        out_specs=[VM, VM],
+        scratch_shapes=work,
+        name="local",
+        **shared,
+    )(words, lists, flat, flat_weights, near_sends[0])
+    return list(far_sends) + list(near_sends), local, own
 
 
 def body(n, features, weights, gain, rulebook, recv_list, coarse_send, coarse_place):
@@ -279,29 +371,19 @@
     ways = matchings(n)
     small = pltpu.CompilerParams(vmem_limit_bytes=12 * 1024 * 1024)
 
-    made = call_rules(n, features, weights, rulebook)
-    sends, local = made[:-1], made[-1]
+    sends, local, own = call_rules(n, features, weights, rulebook)
     arrivals = [lax.ppermute(x, "tiles", way[2]) for x, way in zip(sends, ways)]
-    own = pl.pallas_call(
-        own_kernel,
-        out_shape=jax.ShapeDtypeStruct((tile_count, HALF, 128), F32),
-        in_specs=[VM, pl.BlockSpec(memory_space=pl.ANY)],
-        out_specs=VM,
-        compiler_params=small,
-        cost_estimate=pl.CostEstimate(flops=2000000, bytes_accessed=4000000, transcendentals=0),
-        name="own",
-    )(features, local)
     conv, sums = pl.pallas_call(
         functools.partial(combine_kernel, n, ways),
         out_shape=[
             jax.ShapeDtypeStruct((tile_count, HALF, 128), F32),
             jax.ShapeDtypeStruct((2, tile_count * HALF), F32),
         ],
-        in_specs=[VM, SM, pl.BlockSpec(memory_space=pl.ANY)] + [VM] * len(ways),
+        in_specs=[VM, SM] + [VM] * len(ways),
         out_specs=[VM, VM],
         compiler_params=small,
         name="combine",
-    )(local, recv_list, own, *arrivals)
+    )(local, recv_list, *arrivals)
     wide = lax.axis_size("chan")
     others = [lax.ppermute(sums, "chan", [(i, i ^ m) for i in range(wide)]) for m in range(1, wide)]
     slot_count = coarse_place.shape[1]

time: 61.7 us -> 64.9 us (1.052)
  Pallas kernels: 19.2 us -> 31.3 us
  waiting for transfers between devices: 10.7 us -> 3.48 us
  blocking collectives: 12.1 us -> 10.5 us
    pallas_call x2 -> x3, Pallas kernels: 12.9 us -> 24.9 us  [the longest x1 10.3 us: call_rules(): pl.pallas_call(local_kernel, out_shape=[whole, whole], in_specs=[SM, SM,...]
    ppermute x7, waiting for transfers between devices: 7.74 us -> 0.68 us  [body(): arrivals = [lax.ppermute(x, 'tiles', way[2]) for x, way in zip(sends, ways)]]
    all_to_all x1, blocking collectives: 12.1 us -> 10.5 us  [body(): lax.all_to_all(outbound, 'tiles', split_axis=0, concat_axis=0, tiled=True)]
    unnamed x16 -> x20, local copies, waits for them, and re-layouts: 3.49 us -> 3.49 us
  transfers between devices with their start and end apart: 10 -> 10, of which waited for: 5 -> 3; matrix products, arithmetic and copies ran while one was open for 0% -> 0% of each run, Pallas kernels for 1% -> 16%
where the time goes in v3:
time: 64.9 us; the launch traced here: 64.8 us
  Pallas kernels  31.3 us (48%)
  starting transfers between devices  15.3 us (24%)
  blocking collectives  10.5 us (16%)
  local copies, waits for them, and re-layouts  3.57 us (6%)
  waiting for transfers between devices  3.48 us (5%)
  between operations  0.76 us (1%)
    ppermute x7, starting transfers between devices, body(): arrivals = [lax.ppermute(x, 'tiles', way[2]) for x, way in zip(sends, ways)]  13.4 us
    all_to_all x1, blocking collectives, body(): lax.all_to_all(outbound, 'tiles', split_axis=0, concat_axis=0, tiled=True)  10.5 us
    pallas_call x1, Pallas kernels, call_rules(): pl.pallas_call(local_kernel, out_shape=[whole, whole], in_specs=[SM, SM,...  10.3 us
    pallas_call x1, Pallas kernels, call_rules(): pl.pallas_call(functools.partial(far_kernel, n, far, tile_count), out_sha...  7.7 us
    pallas_call x1, Pallas kernels, call_rules(): pl.pallas_call(functools.partial(near_kernel, n, near), out_shape=[block]...  6.96 us
    unnamed x20, local copies, waits for them, and re-layouts  3.49 us
    pallas_call x1, Pallas kernels, body(): pl.pallas_call(functools.partial(norm_kernel, channels), out_shape=[jax.S...  3.26 us
    ppermute x3, waiting for transfers between devices, body(): lax.ppermute(sums, 'chan', [(i, i ^ m) for i in range(wide)])  2.79 us
  transfers between devices with their start and end apart: 10, of which 3 were waited for; matrix products, arithmetic and copies ran while one was open for 0% of the time, Pallas kernels for 16%

profile of v3, /device:TPU:0, one launch (start us, length us, event | category | flops | bytes accessed | tf_op | source)
XLA Modules:
  0.0 64.8 jit_solution(3187267089151798408)
XLA Ops:
  0.6 1.6 %copy-done.4 = bf16[64,64,256]{2,1,0:T(8,128)(2,1)S(1)} copy-done((bf16[64,64,256]{2,1,0:T(8,128)(2,1)S(1)}, bf16[64,64,256]{2,1,0:T(8,128)(2,1)}, u32[]{:S(2)}) %copy-start.4) | copy-done | bytes 2097176
  2.2 1.2 %copy-done.6 = bf16[27,256,64]{1,2,0:T(8,128)(2,1)S(1)} copy-done((bf16[27,256,64]{1,2,0:T(8,128)(2,1)S(1)}, bf16[27,256,64]{1,2,0:T(8,128)(2,1)}, u32[]{:S(2)}) %copy-start.6) | copy-done | bytes 884760
  3.4 0.7 %copy-done.8 = s32[768,4]{0,1:T(4,128)S(1)} copy-done((s32[768,4]{0,1:T(4,128)S(1)}, s32[768,4]{0,1:T(4,128)}, u32[]{:S(2)}) %copy-start.8) | copy-done | bytes 12312
  4.1 7.7 %far.1 = (bf16[16,32,128]{2,1,0:T(8,128)(2,1)S(1)}, bf16[16,32,128]{2,1,0:T(8,128)(2,1)S(1)}, bf16[16,32,128]{2,1,0:T(8,128)(2,1)S(1)}, s32[8,896]{1,0:T(8,128)S(1)}, s32[3584]{0:T(1024)S(1)}) custom-call(s32[4,768]{1,0:T(4,128)S(1)} %bitcast.11, bf16[4096,256]{1,0:T(8,128)(2,1)S(1)} %bitcast.5, bf16[1728,256]{1,0:T(8,128)(2,1)S(1)} %bitcast.8), custom_call_target="tpu_custom_call" | custom-call | flops 3623878656 | bytes 8388608 | tf_op jit(solution)/shard_map/far/pallas_call | solution.py:329
  11.8 7.0 %near.1 = (bf16[16,32,128]{2,1,0:T(8,128)(2,1)S(1)}, bf16[16,32,128]{2,1,0:T(8,128)(2,1)S(1)}, bf16[16,32,128]{2,1,0:T(8,128)(2,1)S(1)}, bf16[16,32,128]{2,1,0:T(8,128)(2,1)S(1)}) custom-call(s32[8,896]{1,0:T(8,128)S(1)} %get-tuple-element.17.words, s32[3584]{0:T(1024)S(1)} %get-tuple-element.18.lists, bf16[4096,256]{1,0:T(8,128)(2,1)S(1)} %bitcast.6, ...), custom_call_target="tpu_custom_call" | custom-call | flops 3623878656 | bytes 8388608 | tf_op jit(solution)/shard_map/near/pallas_call | solution.py:347
  18.8 3.3 %collective-permute-start.3 = (bf16[16,32,128]{2,1,0:T(8,128)(2,1)S(1)}, bf16[16,32,128]{2,1,0:T(8,128)(2,1)S(1)}, u32[]{:S(2)}, u32[]{:S(2)}) collective-permute-start(bf16[16,32,128]{2,1,0:T(8,128)(2,1)S(1)} %get-tuple-element.19._after), channel_id=1, source_target_pairs={{0,8},{4,12},{16,24},{20,28},{8,0},{12,4},{24,16},{28,20},{1,9},{5... | collective-permute-start | bytes 393224 | tf_op jit(solution)/shard_map/ppermute | solution.py:375
  22.1 1.3 %collective-permute-start.4 = (bf16[16,32,128]{2,1,0:T(8,128)(2,1)S(1)}, bf16[16,32,128]{2,1,0:T(8,128)(2,1)S(1)}, u32[]{:S(2)}, u32[]{:S(2)}) collective-permute-start(bf16[16,32,128]{2,1,0:T(8,128)(2,1)S(1)} %get-tuple-element.24), channel_id=1, source_target_pairs={{8,16},{12,20},{0,4},{24,28},{16,8},{20,12},{4,0},{28,24},{9,17},{... | collective-permute-start | bytes 393224 | tf_op jit(solution)/shard_map/ppermute | solution.py:375
  23.4 0.8 %collective-permute-start.5 = (bf16[16,32,128]{2,1,0:T(8,128)(2,1)S(1)}, bf16[16,32,128]{2,1,0:T(8,128)(2,1)S(1)}, u32[]{:S(2)}, u32[]{:S(2)}) collective-permute-start(bf16[16,32,128]{2,1,0:T(8,128)(2,1)S(1)} %get-tuple-element.25), channel_id=1, source_target_pairs={{0,4},{8,12},{16,20},{24,28},{4,0},{12,8},{20,16},{28,24},{1,5},{9... | collective-permute-start | bytes 393224 | tf_op jit(solution)/shard_map/ppermute | solution.py:375
  24.2 4.2 %collective-permute-start.6 = (bf16[16,32,128]{2,1,0:T(8,128)(2,1)S(1)}, bf16[16,32,128]{2,1,0:T(8,128)(2,1)S(1)}, u32[]{:S(2)}, u32[]{:S(2)}) collective-permute-start(bf16[16,32,128]{2,1,0:T(8,128)(2,1)S(1)} %get-tuple-element.26), channel_id=1, source_target_pairs={{4,8},{12,16},{20,24},{0,28},{8,4},{16,12},{24,20},{28,0},{5,9},{1... | collective-permute-start | bytes 393224 | tf_op jit(solution)/shard_map/ppermute | solution.py:375
  28.4 0.0 collective-permute-start
  28.4 0.0 collective-permute-done.3.rest_3_
  28.4 1.0 %collective-permute-start.1 = (bf16[16,32,128]{2,1,0:T(8,128)(2,1)S(1)}, bf16[16,32,128]{2,1,0:T(8,128)(2,1)S(1)}, u32[]{:S(2)}, u32[]{:S(2)}) collective-permute-start(bf16[16,32,128]{2,1,0:T(8,128)(2,1)S(1)} %get-tuple-element.22), channel_id=1, source_target_pairs={{0,12},{4,16},{8,20},{24,28},{12,0},{16,4},{20,8},{28,24},{1,13},{... | collective-permute-start | bytes 393224 | tf_op jit(solution)/shard_map/ppermute | solution.py:375
  29.5 0.7 %collective-permute-done.4.rest_4_ = bf16[16,32,128]{2,1,0:T(8,128)(2,1)S(1)} collective-permute-done((bf16[16,32,128]{2,1,0:T(8,128)(2,1)S(1)}, bf16[16,32,128]{2,1,0:T(8,128)(2,1)S(1)}, u32[]{:S(2)}, u32[]{:S(2)}) %collective-permute-start.4) | collective-permute-done | bytes 131104 | tf_op jit(solution)/shard_map/ppermute | solution.py:375
  30.1 2.8 %collective-permute-start.2 = (bf16[16,32,128]{2,1,0:T(8,128)(2,1)S(1)}, bf16[16,32,128]{2,1,0:T(8,128)(2,1)S(1)}, u32[]{:S(2)}, u32[]{:S(2)}) collective-permute-start(bf16[16,32,128]{2,1,0:T(8,128)(2,1)S(1)} %get-tuple-element.23), channel_id=1, source_target_pairs={{12,24},{16,28},{0,4},{8,20},{24,12},{28,16},{4,0},{20,8},{13,25},... | collective-permute-start | bytes 393224 | tf_op jit(solution)/shard_map/ppermute | solution.py:375
  32.9 10.3 %local.1 = (f32[64,32,128]{2,1,0:T(8,128)S(1)}, f32[64,32,128]{2,1,0:T(8,128)S(1)}) custom-call(s32[8,896]{1,0:T(8,128)S(1)} %get-tuple-element.17.words, s32[3584]{0:T(1024)S(1)} %get-tuple-element.18.lists, bf16[4096,256]{1,0:T(8,128)(2,1)S(1)} %bitcast.7, bf16[1728,256]{1,0:T(8,128)(2,1)S(1)} %bitcast.10, bf16[16,32,128]{2,1,0:T(8,128)(2,1)S(1)} %get-tuple-element.19._after), custom_call_target="tpu_custom_call" | custom-call | flops 3623878656 | bytes 8388608 | tf_op jit(solution)/shard_map/local/pallas_call | solution.py:356
  43.2 0.0 collective-permute-done.5.rest_5_
  43.2 0.0 collective-permute-done.6.rest_6_
  43.2 0.0 collective-permute-done.rest_0_
  43.2 0.0 collective-permute-done.1.rest_1_
  43.2 0.0 collective-permute-done.2.rest_2_
  43.2 0.0 copy-start.2
  43.2 1.3 %combine.1 = (f32[64,32,128]{2,1,0:T(8,128)S(1)}, f32[2,2048]{1,0:T(2,128)S(1)}) custom-call(f32[64,32,128]{2,1,0:T(8,128)S(1)} %get-tuple-element.20.local_ref, s32[1,128]{1,0:T(1,128)S(1)} %copy-done.1, bf16[16,32,128]{2,1,0:T(8,128)(2,1)S(1)} %collective-permute-done.rest_0_, bf16[16,32,128]{2,1,0:T(8,128)(2,1)S(1)} %collective-permute-done.1.rest_1_, ...), custom_call_target="tpu_custom_call" | custom-call | tf_op jit(solution)/shard_map/combine/pallas_call | solution.py:376
  44.6 0.0 collective-permute-start.7
  44.6 1.6 %collective-permute-start.8 = (f32[2,2048]{1,0:T(2,128)S(1)}, f32[2,2048]{1,0:T(2,128)S(1)}, u32[]{:S(2)}, u32[]{:S(2)}) collective-permute-start(f32[2,2048]{1,0:T(2,128)S(1)} %get-tuple-element.29.s0), channel_id=1, source_target_pairs={{0,2},{1,3},{2,0},{3,1},{4,6},{5,7},{6,4},{7,5},{8,10},{9,11},{10,... | collective-permute-start | bytes 49160 | tf_op jit(solution)/shard_map/ppermute | solution.py:388
  46.2 0.3 collective-permute-start.9
  46.4 0.1 reshape_tile.3.gain_ref
  46.5 0.0 collective-permute-done.7.s1
  46.5 1.8 %collective-permute-done.8.s2 = f32[2,2048]{1,0:T(2,128)S(1)} collective-permute-done((f32[2,2048]{1,0:T(2,128)S(1)}, f32[2,2048]{1,0:T(2,128)S(1)}, u32[]{:S(2)}, u32[]{:S(2)}) %collective-permute-start.8) | collective-permute-done | bytes 16416 | tf_op jit(solution)/shard_map/ppermute | solution.py:388
  48.4 0.9 %collective-permute-done.9.s3 = f32[2,2048]{1,0:T(2,128)S(1)} collective-permute-done((f32[2,2048]{1,0:T(2,128)S(1)}, f32[2,2048]{1,0:T(2,128)S(1)}, u32[]{:S(2)}, u32[]{:S(2)}) %collective-permute-start.9) | collective-permute-done | bytes 16416 | tf_op jit(solution)/shard_map/ppermute | solution.py:388
  49.3 3.3 %norm.1 = (bf16[64,64,64]{2,1,0:T(8,128)(2,1)}, bf16[8,32,128]{2,1,0:T(8,128)(2,1)S(1)}) custom-call(f32[64,32,128]{2,1,0:T(8,128)S(1)} %get-tuple-element.27.conv_ref, f32[64,32,128]{2,1,0:T(8,128)S(1)} %get-tuple-element.28.own_ref, f32[1,128]{1,0:T(1,128)S(1)} %reshape_tile.3.gain_ref, bf16[32,256]{1,0:T(8,128)(2,1)S(1)} %copy-done, ...), custom_call_target="tpu_custom_call" | custom-call | tf_op jit(solution)/shard_map/norm/pallas_call | solution.py:391
  52.6 10.5 %all_to_all.5.landed_ref = bf16[8,32,128]{2,1,0:T(8,128)(2,1)S(1)} all-to-all(bf16[8,32,128]{2,1,0:T(8,128)(2,1)S(1)} %get-tuple-element.31), channel_id=1, replica_groups=mesh['tiles'=8,'chan'=4] {'tiles'}, dimensions={0} | all-to-all | bytes 131072 | tf_op jit(solution)/shard_map/all_to_all | solution.py:410
  63.1 1.8 %place.1 = bf16[8,64,64]{2,1,0:T(8,128)(2,1)} custom-call(s32[1,8]{1,0:T(1,128)S(1)} %copy-done.2, bf16[8,32,128]{2,1,0:T(8,128)(2,1)S(1)} %all_to_all.5.landed_ref), custom_call_target="tpu_custom_call" | custom-call | tf_op jit(solution)/shard_map/place/pallas_call | solution.py:411
  (17 shorter events, 0.0 us)
Async XLA Ops:
  0.6 1.6 %copy-start.4 = (bf16[64,64,256]{2,1,0:T(8,128)(2,1)S(1)}, bf16[64,64,256]{2,1,0:T(8,128)(2,1)}, u32[]{:S(2)}) copy-start(bf16[64,64,256]{2,1,0:T(8,128)(2,1)} %param.8) | copy-start | bytes 6291460
  2.2 1.2 %copy-start.6 = (bf16[27,256,64]{1,2,0:T(8,128)(2,1)S(1)}, bf16[27,256,64]{1,2,0:T(8,128)(2,1)}, u32[]{:S(2)}) copy-start(bf16[27,256,64]{1,2,0:T(8,128)(2,1)} %param.9) | copy-start | bytes 2654212
  3.4 0.7 %copy-start.8 = (s32[768,4]{0,1:T(4,128)S(1)}, s32[768,4]{0,1:T(4,128)}, u32[]{:S(2)}) copy-start(s32[768,4]{0,1:T(4,128)} %param.11) | copy-start | bytes 36868
  4.1 7.7 %copy-start.5 = (bf16[64,64,256]{2,1,0:T(8,128)(2,1)S(1)}, bf16[64,64,256]{2,1,0:T(8,128)(2,1)}, u32[]{:S(2)}) copy-start(bf16[64,64,256]{2,1,0:T(8,128)(2,1)} %param.8) | copy-start | bytes 6291460
  4.1 7.7 %copy-start.7 = (bf16[27,256,64]{1,2,0:T(8,128)(2,1)S(1)}, bf16[27,256,64]{1,2,0:T(8,128)(2,1)}, u32[]{:S(2)}) copy-start(bf16[27,256,64]{1,2,0:T(8,128)(2,1)} %param.9) | copy-start | bytes 2654212
  18.8 9.6 %collective-permute-start.3 = (bf16[16,32,128]{2,1,0:T(8,128)(2,1)S(1)}, bf16[16,32,128]{2,1,0:T(8,128)(2,1)S(1)}, u32[]{:S(2)}, u32[]{:S(2)}) collective-permute-start(bf16[16,32,128]{2,1,0:T(8,128)(2,1)S(1)} %get-tuple-element.19._after), channel_id=1, source_target_pairs={{0,8},{4,12},{16,24},{20,28},{8,0},{12,4},{24,16},{28,20},{1,9},{5... | collective-permute-start | bytes 393224 | tf_op jit(solution)/shard_map/ppermute | solution.py:375
  22.1 8.0 %collective-permute-start.4 = (bf16[16,32,128]{2,1,0:T(8,128)(2,1)S(1)}, bf16[16,32,128]{2,1,0:T(8,128)(2,1)S(1)}, u32[]{:S(2)}, u32[]{:S(2)}) collective-permute-start(bf16[16,32,128]{2,1,0:T(8,128)(2,1)S(1)} %get-tuple-element.24), channel_id=1, source_target_pairs={{8,16},{12,20},{0,4},{24,28},{16,8},{20,12},{4,0},{28,24},{9,17},{... | collective-permute-start | bytes 393224 | tf_op jit(solution)/shard_map/ppermute | solution.py:375
  23.4 19.8 %collective-permute-start.5 = (bf16[16,32,128]{2,1,0:T(8,128)(2,1)S(1)}, bf16[16,32,128]{2,1,0:T(8,128)(2,1)S(1)}, u32[]{:S(2)}, u32[]{:S(2)}) collective-permute-start(bf16[16,32,128]{2,1,0:T(8,128)(2,1)S(1)} %get-tuple-element.25), channel_id=1, source_target_pairs={{0,4},{8,12},{16,20},{24,28},{4,0},{12,8},{20,16},{28,24},{1,5},{9... | collective-permute-start | bytes 393224 | tf_op jit(solution)/shard_map/ppermute | solution.py:375
  24.2 19.0 %collective-permute-start.6 = (bf16[16,32,128]{2,1,0:T(8,128)(2,1)S(1)}, bf16[16,32,128]{2,1,0:T(8,128)(2,1)S(1)}, u32[]{:S(2)}, u32[]{:S(2)}) collective-permute-start(bf16[16,32,128]{2,1,0:T(8,128)(2,1)S(1)} %get-tuple-element.26), channel_id=1, source_target_pairs={{4,8},{12,16},{20,24},{0,28},{8,4},{16,12},{24,20},{28,0},{5,9},{1... | collective-permute-start | bytes 393224 | tf_op jit(solution)/shard_map/ppermute | solution.py:375
  28.4 14.8 %collective-permute-start = (bf16[16,32,128]{2,1,0:T(8,128)(2,1)S(1)}, bf16[16,32,128]{2,1,0:T(8,128)(2,1)S(1)}, u32[]{:S(2)}, u32[]{:S(2)}) collective-permute-start(bf16[16,32,128]{2,1,0:T(8,128)(2,1)S(1)} %get-tuple-element.21), channel_id=1, source_target_pairs={{0,16},{4,20},{8,24},{12,28},{16,0},{20,4},{24,8},{28,12},{1,17},{... | collective-permute-start | bytes 393224 | tf_op jit(solution)/shard_map/ppermute | solution.py:375
  28.4 14.8 %collective-permute-start.1 = (bf16[16,32,128]{2,1,0:T(8,128)(2,1)S(1)}, bf16[16,32,128]{2,1,0:T(8,128)(2,1)S(1)}, u32[]{:S(2)}, u32[]{:S(2)}) collective-permute-start(bf16[16,32,128]{2,1,0:T(8,128)(2,1)S(1)} %get-tuple-element.22), channel_id=1, source_target_pairs={{0,12},{4,16},{8,20},{24,28},{12,0},{16,4},{20,8},{28,24},{1,13},{... | collective-permute-start | bytes 393224 | tf_op jit(solution)/shard_map/ppermute | solution.py:375
  30.1 13.1 %copy-start.1 = (s32[1,128]{1,0:T(1,128)S(1)}, s32[1,128]{1,0:T(1,128)}, u32[]{:S(2)}) copy-start(s32[1,128]{1,0:T(1,128)} %list_ref.1) | copy-start | bytes 1540
  30.1 16.3 %copy-start.9 = (bf16[64]{0:T(256)(128)(2,1)S(1)}, bf16[64]{0:T(256)(128)(2,1)}, u32[]{:S(2)}) copy-start(bf16[64]{0:T(256)(128)(2,1)} %param.10) | copy-start | bytes 388
  30.1 19.2 %copy-start = (bf16[32,256]{1,0:T(8,128)(2,1)S(1)}, bf16[32,256]{1,0:T(8,128)(2,1)}, u32[]{:S(2)}) copy-start(bf16[32,256]{1,0:T(8,128)(2,1)} %constant.2.clone.pool_ref) | copy-start | bytes 49156
  30.1 19.2 %copy-start.3 = (s32[1,8]{1,0:T(1,128)S(1)}, s32[1,8]{1,0:T(1,128)}, u32[]{:S(2)}) copy-start(s32[1,8]{1,0:T(1,128)} %slot_ref.1) | copy-start | bytes 100
  30.1 13.1 %collective-permute-start.2 = (bf16[16,32,128]{2,1,0:T(8,128)(2,1)S(1)}, bf16[16,32,128]{2,1,0:T(8,128)(2,1)S(1)}, u32[]{:S(2)}, u32[]{:S(2)}) collective-permute-start(bf16[16,32,128]{2,1,0:T(8,128)(2,1)S(1)} %get-tuple-element.23), channel_id=1, source_target_pairs={{12,24},{16,28},{0,4},{8,20},{24,12},{28,16},{4,0},{20,8},{13,25},... | collective-permute-start | bytes 393224 | tf_op jit(solution)/shard_map/ppermute | solution.py:375
  43.2 19.8 %copy-start.2 = (s32[1,8]{1,0:T(1,128)S(1)}, s32[1,8]{1,0:T(1,128)}, u32[]{:S(2)}) copy-start(s32[1,8]{1,0:T(1,128)} %place_ref.1) | copy-start | bytes 100
  44.6 2.0 %collective-permute-start.7 = (f32[2,2048]{1,0:T(2,128)S(1)}, f32[2,2048]{1,0:T(2,128)S(1)}, u32[]{:S(2)}, u32[]{:S(2)}) collective-permute-start(f32[2,2048]{1,0:T(2,128)S(1)} %get-tuple-element.29.s0), channel_id=1, source_target_pairs={{0,1},{1,0},{2,3},{3,2},{4,5},{5,4},{6,7},{7,6},{8,9},{9,8},{10,11... | collective-permute-start | bytes 49160 | tf_op jit(solution)/shard_map/ppermute | solution.py:388
  44.6 3.8 %collective-permute-start.8 = (f32[2,2048]{1,0:T(2,128)S(1)}, f32[2,2048]{1,0:T(2,128)S(1)}, u32[]{:S(2)}, u32[]{:S(2)}) collective-permute-start(f32[2,2048]{1,0:T(2,128)S(1)} %get-tuple-element.29.s0), channel_id=1, source_target_pairs={{0,2},{1,3},{2,0},{3,1},{4,6},{5,7},{6,4},{7,5},{8,10},{9,11},{10,... | collective-permute-start | bytes 49160 | tf_op jit(solution)/shard_map/ppermute | solution.py:388
  46.2 3.2 %collective-permute-start.9 = (f32[2,2048]{1,0:T(2,128)S(1)}, f32[2,2048]{1,0:T(2,128)S(1)}, u32[]{:S(2)}, u32[]{:S(2)}) collective-permute-start(f32[2,2048]{1,0:T(2,128)S(1)} %get-tuple-element.29.s0), channel_id=1, source_target_pairs={{0,3},{1,2},{2,1},{3,0},{4,7},{5,6},{6,5},{7,4},{8,11},{9,10},{10,... | collective-permute-start | bytes 49160 | tf_op jit(solution)/shard_map/ppermute | solution.py:388

commit v4 on v3

--- a/solution.py
+++ b/solution.py
@@ -118,7 +118,7 @@
 
 def far_kernel(n, ways, tile_count, rules_hbm, f_hbm, w_hbm, *rest):
     sends = rest[: len(ways)]
-    words_v, lists, y_ref, acc_ref, f_ref, w_ref, rules_ref, words_s, sems = rest[len(ways) :]
+    f_ref, w_ref, words_v, lists, y_ref, acc_ref, rules_ref, words_s, sems = rest[len(ways) :]
     rows = tile_count * VOX
     span = rows + 2 * PAD
     rule_rows = rules_ref.shape[1]
@@ -192,7 +192,23 @@
     emit_sends(n, ways, acc_ref, sends)
 
 
-def local_kernel(words, lists, f_ref, w_ref, _after, local_ref, own_ref, y_ref, acc_ref):
+def add_arrivals(n, ways, blocks, list_ref, out_ref):
+    e = lax.axis_index("tiles")
+    slots = blocks[0].shape[0]
+    for (d, parity, _), block in zip(ways, blocks):
+        low, high = role(e, n, d, parity)
+        base = slots * jnp.where(low, d + 3, d - 1)
+
+        @pl.when(jnp.logical_or(low, high))
+        def _(block=block, base=base):
+            for i in range(slots):
+                t = list_ref[0, base + i]
+                out_ref[t] = out_ref[t] + block[i].astype(F32)
+
+
+def local_kernel(n, ways, words, lists, list_ref, f_ref, w_ref, *rest):
+    blocks = rest[: len(ways)]
+    local_ref, own_ref, y_ref, acc_ref = rest[len(ways) :]
     tile_count = acc_ref.shape[0]
     zero_blocks(acc_ref)
     rules_matmul(f_ref, w_ref, y_ref)
@@ -212,25 +228,15 @@
         return c
 
     lax.fori_loop(0, tile_count, keep, 0, unroll=8)
+    add_arrivals(n, ways, blocks, list_ref, local_ref)
 
 
 def combine_kernel(n, ways, local_ref, list_ref, *rest):
     blocks = rest[: len(ways)]
     conv_ref, sums_ref = rest[len(ways) :]
-    e = lax.axis_index("tiles")
     tile_count = local_ref.shape[0]
-    slots = blocks[0].shape[0]
     conv_ref[...] = local_ref[...]
-    for (d, parity, _), block in zip(ways, blocks):
-        low, high = role(e, n, d, parity)
-        base = slots * jnp.where(low, d + 3, d - 1)
-
-        @pl.when(jnp.logical_or(low, high))
-        def _(block=block, base=base):
-            for i in range(slots):
-                t = list_ref[0, base + i]
-                conv_ref[t] = conv_ref[t] + block[i].astype(F32)
-
+    add_arrivals(n, ways, blocks, list_ref, conv_ref)
     rows = tile_count * HALF
     pick = (lane_iota((2, 256)) // 64 % 2 == lax.broadcasted_iota(jnp.int32, (2, 256), 0)).astype(BF)
     step = 512
@@ -305,7 +311,7 @@
 HBM = pl.BlockSpec(memory_space=pltpu.HBM)
 
 
-def call_rules(n, features, weights, rulebook):
+def call_rules(n, features, weights, rulebook, recv_list):
     tile_count, _, channels = features.shape
     offsets, _, quarter = weights.shape
     rule_rows = rulebook.shape[0]
@@ -329,21 +335,22 @@
     made = pl.pallas_call(
         functools.partial(far_kernel, n, far, tile_count),
         out_shape=[block] * len(far)
+        + [jax.ShapeDtypeStruct(flat.shape, BF), jax.ShapeDtypeStruct(flat_weights.shape, BF)]
         + [jax.ShapeDtypeStruct((8, wide), jnp.int32), jax.ShapeDtypeStruct((4 * wide,), jnp.int32)],
         in_specs=[HBM] * 3,
-        out_specs=[VM] * (len(far) + 1) + [SM],
+        out_specs=[VM] * (len(far) + 3) + [SM],
         scratch_shapes=work
         + [
-            pltpu.VMEM(flat.shape, BF),
-            pltpu.VMEM(flat_weights.shape, BF),
             pltpu.VMEM((4, rule_rows), jnp.int32),
             pltpu.SMEM((8, wide), jnp.int32),
             pltpu.SemaphoreType.DMA((4,)),
         ],
         name="far",
         **shared,
-    )(rulebook.T, flat, flat_weights)
-    far_sends, words, lists = made[: len(far)], made[-2], made[-1]
+    )(*(pltpu.with_memory_space_constraint(x, pltpu.HBM) for x in (rulebook.T, flat, flat_weights)))
+    far_sends = made[: len(far)]
+    held, held_weights, words, lists = made[len(far) :]
+    arrivals = [lax.ppermute(x, "tiles", way[2]) for x, way in zip(far_sends, far)]
     near_sends = pl.pallas_call(
         functools.partial(near_kernel, n, near),
         out_shape=[block] * len(near),
@@ -352,34 +359,33 @@
         scratch_shapes=work,
         name="near",
         **shared,
-    )(words, lists, flat, flat_weights)
+    )(words, lists, held, held_weights)
+    near_arrivals = [lax.ppermute(x, "tiles", way[2]) for x, way in zip(near_sends, near)]
     local, own = pl.pallas_call(
-        local_kernel,
+        functools.partial(local_kernel, n, far),
         out_shape=[whole, whole],
-        in_specs=[SM, SM, VM, VM, ANY],
+        in_specs=[SM, SM, SM, VM, VM] + [VM] * len(far),
         out_specs=[VM, VM],
         scratch_shapes=work,
         name="local",
         **shared,
-    )(words, lists, flat, flat_weights, near_sends[0])
-    return list(far_sends) + list(near_sends), local, own
+    )(words, lists, recv_list, held, held_weights, *arrivals)
+    return near, near_arrivals, local, own
 
 
 def body(n, features, weights, gain, rulebook, recv_list, coarse_send, coarse_place):
     tile_count, _, channels = features.shape
     quarter = weights.shape[2]
-    ways = matchings(n)
     small = pltpu.CompilerParams(vmem_limit_bytes=12 * 1024 * 1024)
 
-    sends, local, own = call_rules(n, features, weights, rulebook)
-    arrivals = [lax.ppermute(x, "tiles", way[2]) for x, way in zip(sends, ways)]
+    near, arrivals, local, own = call_rules(n, features, weights, rulebook, recv_list)
     conv, sums = pl.pallas_call(
-        functools.partial(combine_kernel, n, ways),
+        functools.partial(combine_kernel, n, near),
         out_shape=[
             jax.ShapeDtypeStruct((tile_count, HALF, 128), F32),
             jax.ShapeDtypeStruct((2, tile_count * HALF), F32),
         ],
-        in_specs=[VM, SM] + [VM] * len(ways),
+        in_specs=[VM, SM] + [VM] * len(near),
         out_specs=[VM, VM],
         compiler_params=small,
         name="combine",

time: 64.9 us -> 61 us (0.940)
  local copies, waits for them, and re-layouts: 3.57 us -> 0.11 us
  blocking collectives: 10.5 us -> 12.2 us
  Pallas kernels: 31.3 us -> 30 us
  waiting for transfers between devices: 3.48 us -> 2.8 us
    unnamed x20 -> x10, local copies, waits for them, and re-layouts: 3.49 us -> 0.02 us
    all_to_all x1, blocking collectives: 10.5 us -> 12.2 us  [body(): lax.all_to_all(outbound, 'tiles', split_axis=0, concat_axis=0, tiled=True)]
    pallas_call x2, Pallas kernels: 11.6 us -> 10.6 us  [the longest x1 9.4 us: call_rules(): pl.pallas_call(functools.partial(local_kernel, n, far), out_shape=[whole,...]
    ppermute x7, waiting for transfers between devices: 0.68 us -> 0.02 us  [call_rules(): lax.ppermute(x, 'tiles', way[2])]
  transfers between devices with their start and end apart: 10 -> 10, of which waited for: 3 -> 2; matrix products, arithmetic and copies ran while one was open for 0% -> 0% of each run, Pallas kernels for 16% -> 27%
where the time goes in v4:
time: 61 us; the launch traced here: 60.6 us
  Pallas kernels  30 us (49%)
  starting transfers between devices  14.8 us (24%)
  blocking collectives  12.2 us (20%)
  waiting for transfers between devices  2.8 us (5%)
  between operations  0.72 us (1%)
    ppermute x7, starting transfers between devices, call_rules(): lax.ppermute(x, 'tiles', way[2])  13 us
    all_to_all x1, blocking collectives, body(): lax.all_to_all(outbound, 'tiles', split_axis=0, concat_axis=0, tiled=True)  12.2 us
    pallas_call x1, Pallas kernels, call_rules(): pl.pallas_call(functools.partial(local_kernel, n, far), out_shape=[whole,...  9.4 us
    pallas_call x1, Pallas kernels, call_rules(): pl.pallas_call(functools.partial(far_kernel, n, far, tile_count), out_sha...  7.61 us
    pallas_call x1, Pallas kernels, call_rules(): pl.pallas_call(functools.partial(near_kernel, n, near), out_shape=[block]...  6.79 us
    pallas_call x1, Pallas kernels, body(): pl.pallas_call(functools.partial(norm_kernel, channels), out_shape=[jax.S...  3.26 us
    ppermute x3, waiting for transfers between devices, body(): lax.ppermute(sums, 'chan', [(i, i ^ m) for i in range(wide)])  2.78 us
    ppermute x3, starting transfers between devices, body(): lax.ppermute(sums, 'chan', [(i, i ^ m) for i in range(wide)])  1.87 us
  transfers between devices with their start and end apart: 10, of which 2 were waited for; matrix products, arithmetic and copies ran while one was open for 0% of the time, Pallas kernels for 27%

profile of v4, /device:TPU:0, one launch (start us, length us, event | category | flops | bytes accessed | tf_op | source)
XLA Modules:
  0.0 60.6 jit_solution(7765369109331958728)
XLA Ops:
  0.6 7.6 %far.1 = (bf16[16,32,128]{2,1,0:T(8,128)(2,1)S(1)}, bf16[16,32,128]{2,1,0:T(8,128)(2,1)S(1)}, bf16[16,32,128]{2,1,0:T(8,128)(2,1)S(1)}, bf16[4096,256]{1,0:T(8,1...) custom-call(s32[4,768]{1,0:T(4,128)} %bitcast.7, bf16[4096,256]{1,0:T(8,128)(2,1)} %bitcast.5, ...), custom_call_target="tpu_custom_call" | custom-call | flops 3623878656 | bytes 8388608 | tf_op jit(solution)/shard_map/far/pallas_call | solution.py:335
  8.3 4.1 %collective-permute-start = (bf16[16,32,128]{2,1,0:T(8,128)(2,1)S(1)}, bf16[16,32,128]{2,1,0:T(8,128)(2,1)S(1)}, u32[]{:S(2)}, u32[]{:S(2)}) collective-permute-start(bf16[16,32,128]{2,1,0:T(8,128)(2,1)S(1)} %get-tuple-element.23), channel_id=1, source_target_pairs={{0,16},{4,20},{8,24},{12,28},{16,0},{20,4},{24,8},{28,12},{1,17},{... | collective-permute-start | bytes 393224 | tf_op jit(solution)/shard_map/ppermute | solution.py:353
  12.3 2.6 %collective-permute-start.1 = (bf16[16,32,128]{2,1,0:T(8,128)(2,1)S(1)}, bf16[16,32,128]{2,1,0:T(8,128)(2,1)S(1)}, u32[]{:S(2)}, u32[]{:S(2)}) collective-permute-start(bf16[16,32,128]{2,1,0:T(8,128)(2,1)S(1)} %get-tuple-element.24), channel_id=1, source_target_pairs={{0,12},{4,16},{8,20},{24,28},{12,0},{16,4},{20,8},{28,24},{1,13},{... | collective-permute-start | bytes 393224 | tf_op jit(solution)/shard_map/ppermute | solution.py:353
  14.9 0.0 collective-permute-start.2
  14.9 6.8 %near.1 = (bf16[16,32,128]{2,1,0:T(8,128)(2,1)S(1)}, bf16[16,32,128]{2,1,0:T(8,128)(2,1)S(1)}, bf16[16,32,128]{2,1,0:T(8,128)(2,1)S(1)}, bf16[16,32,128]{2,1,0:T(8,128)(2,1)S(1)}) custom-call(s32[8,896]{1,0:T(8,128)S(1)} %get-tuple-element.19.words, s32[3584]{0:T(1024)S(1)} %get-tuple-element.20.lists, bf16[4096,256]{1,0:T(8,128)(2,1)S(1)} %get-tuple-element.21.f_ref, ...), custom_call_target="tpu_custom_call" | custom-call | flops 3623878656 | bytes 8388608 | tf_op jit(solution)/shard_map/near/pallas_call | solution.py:354
  21.7 2.9 %collective-permute-start.3 = (bf16[16,32,128]{2,1,0:T(8,128)(2,1)S(1)}, bf16[16,32,128]{2,1,0:T(8,128)(2,1)S(1)}, u32[]{:S(2)}, u32[]{:S(2)}) collective-permute-start(bf16[16,32,128]{2,1,0:T(8,128)(2,1)S(1)} %get-tuple-element.27), channel_id=1, source_target_pairs={{0,8},{4,12},{16,24},{20,28},{8,0},{12,4},{24,16},{28,20},{1,9},{5... | collective-permute-start | bytes 393224 | tf_op jit(solution)/shard_map/ppermute | solution.py:363
  24.6 1.5 %collective-permute-start.4 = (bf16[16,32,128]{2,1,0:T(8,128)(2,1)S(1)}, bf16[16,32,128]{2,1,0:T(8,128)(2,1)S(1)}, u32[]{:S(2)}, u32[]{:S(2)}) collective-permute-start(bf16[16,32,128]{2,1,0:T(8,128)(2,1)S(1)} %get-tuple-element.28), channel_id=1, source_target_pairs={{8,16},{12,20},{0,4},{24,28},{16,8},{20,12},{4,0},{28,24},{9,17},{... | collective-permute-start | bytes 393224 | tf_op jit(solution)/shard_map/ppermute | solution.py:363
  26.0 0.0 collective-permute-done.rest_0_
  26.0 0.6 collective-permute-start.5
  26.6 0.0 collective-permute-done.1.rest_1_
  26.6 1.4 %collective-permute-start.6 = (bf16[16,32,128]{2,1,0:T(8,128)(2,1)S(1)}, bf16[16,32,128]{2,1,0:T(8,128)(2,1)S(1)}, u32[]{:S(2)}, u32[]{:S(2)}) collective-permute-start(bf16[16,32,128]{2,1,0:T(8,128)(2,1)S(1)} %get-tuple-element.30), channel_id=1, source_target_pairs={{4,8},{12,16},{20,24},{0,28},{8,4},{16,12},{24,20},{28,0},{5,9},{1... | collective-permute-start | bytes 393224 | tf_op jit(solution)/shard_map/ppermute | solution.py:363
  28.0 0.0 collective-permute-done.2.rest_2_
  28.0 0.0 copy-done.1
  28.0 9.4 %local.1 = (f32[64,32,128]{2,1,0:T(8,128)S(1)}, f32[64,32,128]{2,1,0:T(8,128)S(1)}) custom-call(s32[8,896]{1,0:T(8,128)S(1)} %get-tuple-element.19.words, s32[3584]{0:T(1024)S(1)} %get-tuple-element.20.lists, s32[1,128]{1,0:T(1,128)S(1)} %copy-done.1, bf16[4096,256]{1,0:T(8,128)(2,1)S(1)} %get-tuple-element.21.f_ref, ...), custom_call_target="tpu_custom_call" | custom-call | flops 3623878656 | bytes 8388608 | tf_op jit(solution)/shard_map/local/pallas_call | solution.py:364
  37.4 0.0 copy-start.2
  37.5 0.0 collective-permute-done.3.rest_0_
  37.5 0.0 collective-permute-done.4.rest_1_
  37.5 0.0 collective-permute-done.5.rest_2_
  37.5 0.0 collective-permute-done.6.rest_3_
  37.5 1.2 %combine.1 = (f32[64,32,128]{2,1,0:T(8,128)S(1)}, f32[2,2048]{1,0:T(2,128)S(1)}) custom-call(f32[64,32,128]{2,1,0:T(8,128)S(1)} %get-tuple-element.26.local_ref, s32[1,128]{1,0:T(1,128)S(1)} %copy-done.1, bf16[16,32,128]{2,1,0:T(8,128)(2,1)S(1)} %collective-permute-done.3.rest_0_, bf16[16,32,128]{2,1,0:T(8,128)(2,1)S(1)} %collective-permute-done.4.rest_1_, ...), custom_call_target="tpu_custom_call" | custom-call | tf_op jit(solution)/shard_map/combine/pallas_call | solution.py:382
  38.7 0.0 collective-permute-start.7
  38.7 1.6 %collective-permute-start.8 = (f32[2,2048]{1,0:T(2,128)S(1)}, f32[2,2048]{1,0:T(2,128)S(1)}, u32[]{:S(2)}, u32[]{:S(2)}) collective-permute-start(f32[2,2048]{1,0:T(2,128)S(1)} %get-tuple-element.33.s0), channel_id=1, source_target_pairs={{0,2},{1,3},{2,0},{3,1},{4,6},{5,7},{6,4},{7,5},{8,10},{9,11},{10,... | collective-permute-start | bytes 49160 | tf_op jit(solution)/shard_map/ppermute | solution.py:394
  40.2 0.3 collective-permute-start.9
  40.5 0.1 reshape_tile.3.gain_ref
  40.6 0.0 collective-permute-done.7.s1
  40.6 1.8 %collective-permute-done.8.s2 = f32[2,2048]{1,0:T(2,128)S(1)} collective-permute-done((f32[2,2048]{1,0:T(2,128)S(1)}, f32[2,2048]{1,0:T(2,128)S(1)}, u32[]{:S(2)}, u32[]{:S(2)}) %collective-permute-start.8) | collective-permute-done | bytes 16416 | tf_op jit(solution)/shard_map/ppermute | solution.py:394
  42.5 0.9 %collective-permute-done.9.s3 = f32[2,2048]{1,0:T(2,128)S(1)} collective-permute-done((f32[2,2048]{1,0:T(2,128)S(1)}, f32[2,2048]{1,0:T(2,128)S(1)}, u32[]{:S(2)}, u32[]{:S(2)}) %collective-permute-start.9) | collective-permute-done | bytes 16416 | tf_op jit(solution)/shard_map/ppermute | solution.py:394
  43.4 0.0 copy-done.3
  43.4 3.3 %norm.1 = (bf16[64,64,64]{2,1,0:T(8,128)(2,1)}, bf16[8,32,128]{2,1,0:T(8,128)(2,1)S(1)}) custom-call(f32[64,32,128]{2,1,0:T(8,128)S(1)} %get-tuple-element.31.conv_ref, f32[64,32,128]{2,1,0:T(8,128)S(1)} %get-tuple-element.32.own_ref, f32[1,128]{1,0:T(1,128)S(1)} %reshape_tile.3.gain_ref, bf16[32,256]{1,0:T(8,128)(2,1)S(1)} %copy-done, ...), custom_call_target="tpu_custom_call" | custom-call | tf_op jit(solution)/shard_map/norm/pallas_call | solution.py:397
  46.7 12.2 %all_to_all.5.landed_ref = bf16[8,32,128]{2,1,0:T(8,128)(2,1)S(1)} all-to-all(bf16[8,32,128]{2,1,0:T(8,128)(2,1)S(1)} %get-tuple-element.35), channel_id=1, replica_groups=mesh['tiles'=8,'chan'=4] {'tiles'}, dimensions={0} | all-to-all | bytes 131072 | tf_op jit(solution)/shard_map/all_to_all | solution.py:416
  58.9 0.0 copy-done.2
  58.9 1.8 %place.1 = bf16[8,64,64]{2,1,0:T(8,128)(2,1)} custom-call(s32[1,8]{1,0:T(1,128)S(1)} %copy-done.2, bf16[8,32,128]{2,1,0:T(8,128)(2,1)S(1)} %all_to_all.5.landed_ref), custom_call_target="tpu_custom_call" | custom-call | tf_op jit(solution)/shard_map/place/pallas_call | solution.py:417
  (7 shorter events, 0.0 us)
Async XLA Ops:
  8.3 17.8 %collective-permute-start = (bf16[16,32,128]{2,1,0:T(8,128)(2,1)S(1)}, bf16[16,32,128]{2,1,0:T(8,128)(2,1)S(1)}, u32[]{:S(2)}, u32[]{:S(2)}) collective-permute-start(bf16[16,32,128]{2,1,0:T(8,128)(2,1)S(1)} %get-tuple-element.23), channel_id=1, source_target_pairs={{0,16},{4,20},{8,24},{12,28},{16,0},{20,4},{24,8},{28,12},{1,17},{... | collective-permute-start | bytes 393224 | tf_op jit(solution)/shard_map/ppermute | solution.py:353
  12.3 14.3 %collective-permute-start.1 = (bf16[16,32,128]{2,1,0:T(8,128)(2,1)S(1)}, bf16[16,32,128]{2,1,0:T(8,128)(2,1)S(1)}, u32[]{:S(2)}, u32[]{:S(2)}) collective-permute-start(bf16[16,32,128]{2,1,0:T(8,128)(2,1)S(1)} %get-tuple-element.24), channel_id=1, source_target_pairs={{0,12},{4,16},{8,20},{24,28},{12,0},{16,4},{20,8},{28,24},{1,13},{... | collective-permute-start | bytes 393224 | tf_op jit(solution)/shard_map/ppermute | solution.py:353
  14.9 13.1 %collective-permute-start.2 = (bf16[16,32,128]{2,1,0:T(8,128)(2,1)S(1)}, bf16[16,32,128]{2,1,0:T(8,128)(2,1)S(1)}, u32[]{:S(2)}, u32[]{:S(2)}) collective-permute-start(bf16[16,32,128]{2,1,0:T(8,128)(2,1)S(1)} %get-tuple-element.25), channel_id=1, source_target_pairs={{12,24},{16,28},{0,4},{8,20},{24,12},{28,16},{4,0},{20,8},{13,25},... | collective-permute-start | bytes 393224 | tf_op jit(solution)/shard_map/ppermute | solution.py:353
  14.9 13.1 %copy-start.1 = (s32[1,128]{1,0:T(1,128)S(1)}, s32[1,128]{1,0:T(1,128)}, u32[]{:S(2)}) copy-start(s32[1,128]{1,0:T(1,128)} %list_ref.3) | copy-start | bytes 1540
  21.7 15.7 %collective-permute-start.3 = (bf16[16,32,128]{2,1,0:T(8,128)(2,1)S(1)}, bf16[16,32,128]{2,1,0:T(8,128)(2,1)S(1)}, u32[]{:S(2)}, u32[]{:S(2)}) collective-permute-start(bf16[16,32,128]{2,1,0:T(8,128)(2,1)S(1)} %get-tuple-element.27), channel_id=1, source_target_pairs={{0,8},{4,12},{16,24},{20,28},{8,0},{12,4},{24,16},{28,20},{1,9},{5... | collective-permute-start | bytes 393224 | tf_op jit(solution)/shard_map/ppermute | solution.py:363
  24.6 12.9 %collective-permute-start.4 = (bf16[16,32,128]{2,1,0:T(8,128)(2,1)S(1)}, bf16[16,32,128]{2,1,0:T(8,128)(2,1)S(1)}, u32[]{:S(2)}, u32[]{:S(2)}) collective-permute-start(bf16[16,32,128]{2,1,0:T(8,128)(2,1)S(1)} %get-tuple-element.28), channel_id=1, source_target_pairs={{8,16},{12,20},{0,4},{24,28},{16,8},{20,12},{4,0},{28,24},{9,17},{... | collective-permute-start | bytes 393224 | tf_op jit(solution)/shard_map/ppermute | solution.py:363
  26.0 11.4 %collective-permute-start.5 = (bf16[16,32,128]{2,1,0:T(8,128)(2,1)S(1)}, bf16[16,32,128]{2,1,0:T(8,128)(2,1)S(1)}, u32[]{:S(2)}, u32[]{:S(2)}) collective-permute-start(bf16[16,32,128]{2,1,0:T(8,128)(2,1)S(1)} %get-tuple-element.29), channel_id=1, source_target_pairs={{0,4},{8,12},{16,20},{24,28},{4,0},{12,8},{20,16},{28,24},{1,5},{9... | collective-permute-start | bytes 393224 | tf_op jit(solution)/shard_map/ppermute | solution.py:363
  26.6 13.9 %copy-start.4 = (bf16[64]{0:T(256)(128)(2,1)S(1)}, bf16[64]{0:T(256)(128)(2,1)}, u32[]{:S(2)}) copy-start(bf16[64]{0:T(256)(128)(2,1)} %param.10) | copy-start | bytes 388
  26.6 16.8 %copy-start = (bf16[32,256]{1,0:T(8,128)(2,1)S(1)}, bf16[32,256]{1,0:T(8,128)(2,1)}, u32[]{:S(2)}) copy-start(bf16[32,256]{1,0:T(8,128)(2,1)} %constant.2.clone.pool_ref) | copy-start | bytes 49156
  26.6 16.8 %copy-start.3 = (s32[1,8]{1,0:T(1,128)S(1)}, s32[1,8]{1,0:T(1,128)}, u32[]{:S(2)}) copy-start(s32[1,8]{1,0:T(1,128)} %slot_ref.1) | copy-start | bytes 100
  26.6 10.9 %collective-permute-start.6 = (bf16[16,32,128]{2,1,0:T(8,128)(2,1)S(1)}, bf16[16,32,128]{2,1,0:T(8,128)(2,1)S(1)}, u32[]{:S(2)}, u32[]{:S(2)}) collective-permute-start(bf16[16,32,128]{2,1,0:T(8,128)(2,1)S(1)} %get-tuple-element.30), channel_id=1, source_target_pairs={{4,8},{12,16},{20,24},{0,28},{8,4},{16,12},{24,20},{28,0},{5,9},{1... | collective-permute-start | bytes 393224 | tf_op jit(solution)/shard_map/ppermute | solution.py:363
  37.4 21.4 %copy-start.2 = (s32[1,8]{1,0:T(1,128)S(1)}, s32[1,8]{1,0:T(1,128)}, u32[]{:S(2)}) copy-start(s32[1,8]{1,0:T(1,128)} %place_ref.1) | copy-start | bytes 100
  38.7 2.0 %collective-permute-start.7 = (f32[2,2048]{1,0:T(2,128)S(1)}, f32[2,2048]{1,0:T(2,128)S(1)}, u32[]{:S(2)}, u32[]{:S(2)}) collective-permute-start(f32[2,2048]{1,0:T(2,128)S(1)} %get-tuple-element.33.s0), channel_id=1, source_target_pairs={{0,1},{1,0},{2,3},{3,2},{4,5},{5,4},{6,7},{7,6},{8,9},{9,8},{10,11... | collective-permute-start | bytes 49160 | tf_op jit(solution)/shard_map/ppermute | solution.py:394
  38.7 3.8 %collective-permute-start.8 = (f32[2,2048]{1,0:T(2,128)S(1)}, f32[2,2048]{1,0:T(2,128)S(1)}, u32[]{:S(2)}, u32[]{:S(2)}) collective-permute-start(f32[2,2048]{1,0:T(2,128)S(1)} %get-tuple-element.33.s0), channel_id=1, source_target_pairs={{0,2},{1,3},{2,0},{3,1},{4,6},{5,7},{6,4},{7,5},{8,10},{9,11},{10,... | collective-permute-start | bytes 49160 | tf_op jit(solution)/shard_map/ppermute | solution.py:394
  40.2 3.2 %collective-permute-start.9 = (f32[2,2048]{1,0:T(2,128)S(1)}, f32[2,2048]{1,0:T(2,128)S(1)}, u32[]{:S(2)}, u32[]{:S(2)}) collective-permute-start(f32[2,2048]{1,0:T(2,128)S(1)} %get-tuple-element.33.s0), channel_id=1, source_target_pairs={{0,3},{1,2},{2,1},{3,0},{4,7},{5,6},{6,5},{7,4},{8,11},{9,10},{10,... | collective-permute-start | bytes 49160 | tf_op jit(solution)/shard_map/ppermute | solution.py:394

commit v5 on v4

--- a/solution.py
+++ b/solution.py
@@ -16,6 +16,8 @@
 F32 = jnp.float32
 PAD = 64
 UNROLL = 8
+PARTS = 2
+PER_PART = 7
 
 
 def matchings(n):
@@ -45,7 +47,7 @@
     return (lax.div(code, 9) - 1, lax.rem(lax.div(code, 3), 3) - 1, lax.rem(code, 3) - 1)
 
 
-def rules_matmul(f_ref, w_ref, y_ref, beside=None):
+def rules_matmul(f_ref, w_ref, y_refs, beside=None):
     rows = f_ref.shape[0]
     span = rows + 2 * PAD
     depth = w_ref.shape[0]
@@ -60,18 +62,25 @@
         )
         for s in range(0, width, 128):
             wide = min(128, width - s)
-            base = ((q + s) // 128) * span + PAD
+            y_ref = y_refs[(q + s) // 128 // PER_PART]
+            base = ((q + s) // 128 % PER_PART) * span + PAD
             y_ref[base : base + rows, 0:wide] = part[:, s : s + wide]
         if beside is not None:
             beside(number, len(steps))
 
 
-def rules_add(words, lists, start, count, y_ref, acc_ref):
+def rules_add(words, lists, part, y_refs, acc_ref):
     voxel = lax.broadcasted_iota(jnp.int32, (VOX, 128), 0)
     have = jnp.where(lane_iota((VOX, 128)) < 64, 1 << 21, 1 << 22)
     for dim, place in enumerate((lax.div(voxel, 16), lax.rem(lax.div(voxel, 4), 4), lax.rem(voxel, 4))):
         have = have + jnp.left_shift(jnp.full_like(place, 15), 3 - place + 7 * dim)
 
+    for which, y_ref in enumerate(y_refs):
+        kind = part * PARTS + which
+        add_listed(words, lists, kind * words.shape[1], words[3, 128 * kind], have, y_ref, acc_ref)
+
+
+def add_listed(words, lists, start, count, have, y_ref, acc_ref):
     def several(i, c):
         for u in range(UNROLL):
             r = lists[start + i * UNROLL + u]
@@ -118,7 +127,9 @@
 
 def far_kernel(n, ways, tile_count, rules_hbm, f_hbm, w_hbm, *rest):
     sends = rest[: len(ways)]
-    f_ref, w_ref, words_v, lists, y_ref, acc_ref, rules_ref, words_s, sems = rest[len(ways) :]
+    f_ref = rest[len(ways)]
+    y_refs = rest[len(ways) + 1 : len(ways) + 1 + PARTS]
+    words_v, lists, acc_ref, w_ref, rules_ref, words_s, sems = rest[len(ways) + 1 + PARTS :]
     rows = tile_count * VOX
     span = rows + 2 * PAD
     rule_rows = rules_ref.shape[1]
@@ -150,20 +161,22 @@
     place = (lax.div(group, 4) * 2 + lax.rem(group, 2)) * slots + lax.rem(sent, slots)
     near = lax.rem(group, 4) < 2
     part = jnp.where(target < tile_count, 2, jnp.where(near, 1, 0))
-    part = jnp.where(kernel < 27, part, 3)
+    pair = lax.div(code, 2)
+    part = jnp.where(kernel < 27, part * PARTS + lax.div(pair, PER_PART), 3 * PARTS)
     kind = lax.broadcasted_iota(jnp.int32, (8, rule_rows), 0)
     flags = jnp.where(kind == part, 1.0, 0.0)
     upto = jnp.dot(flags.astype(BF), before, preferred_element_type=F32)
     at = jnp.sum(flags * (upto - 1.0 + (kind * wide).astype(F32)), axis=0, keepdims=True)
-    first_row = lax.div(code, 2) * span + PAD + tile * VOX + shift
+    first_row = lax.rem(pair, PER_PART) * span + PAD + tile * VOX + shift
     words_v[...] = jnp.zeros(words_v.shape, jnp.int32)
     words_v[0:1, 0:rule_rows] = first_row * 256 + jnp.where(target < tile_count, target, place)
     words_v[1:2, 0:rule_rows] = need
     words_v[2:3, 0:rule_rows] = at.astype(jnp.int32)
     words_v[0:1, rule_rows:wide] = jnp.full((1, wide - rule_rows), PAD * 256, jnp.int32)
     words_v[1:2, rule_rows:wide] = jnp.full((1, wide - rule_rows), 1 << 23, jnp.int32)
-    totals = jnp.broadcast_to(upto[0:3, rule_rows - 1 : rule_rows], (3, 128))
-    words_v[3:6, 0:128] = totals.astype(jnp.int32)
+    for c in range(3 * PARTS):
+        total = upto[c : c + 1, rule_rows - 1 : rule_rows]
+        words_v[3:4, 128 * c : 128 * c + 128] = jnp.broadcast_to(total, (1, 128)).astype(jnp.int32)
     to_scalars = pltpu.make_async_copy(words_v, words_s, sems.at[3])
     to_scalars.start()
     to_scalars.wait()
@@ -175,20 +188,20 @@
         for r in range(number * share, min(rule_rows, (number + 1) * share)):
             lists[words_s[2, r]] = r
 
-    rules_matmul(f_ref, w_ref, y_ref, list_some)
-    for c in range(3):
+    rules_matmul(f_ref, w_ref, y_refs, list_some)
+    for c in range(3 * PARTS):
         for u in range(UNROLL):
-            lists[c * wide + words_s[3 + c, 0] + u] = rule_rows
-    rules_add(words_s, lists, 0, words_s[3, 0], y_ref, acc_ref)
+            lists[c * wide + words_s[3, 128 * c] + u] = rule_rows
+    rules_add(words_s, lists, 0, y_refs, acc_ref)
     emit_sends(n, ways, acc_ref, sends)
 
 
-def near_kernel(n, ways, words, lists, f_ref, w_ref, *rest):
+def near_kernel(n, ways, words, lists, *rest):
+    y_refs, rest = rest[:PARTS], rest[PARTS:]
     sends = rest[: len(ways)]
-    y_ref, acc_ref = rest[len(ways) :]
+    acc_ref = rest[len(ways)]
     zero_blocks(acc_ref)
-    rules_matmul(f_ref, w_ref, y_ref)
-    rules_add(words, lists, words.shape[1], words[4, 0], y_ref, acc_ref)
+    rules_add(words, lists, 1, y_refs, acc_ref)
     emit_sends(n, ways, acc_ref, sends)
 
 
@@ -206,13 +219,13 @@
                 out_ref[t] = out_ref[t] + block[i].astype(F32)
 
 
-def local_kernel(n, ways, words, lists, list_ref, f_ref, w_ref, *rest):
+def local_kernel(n, ways, words, lists, list_ref, f_ref, *rest):
+    y_refs, rest = rest[:PARTS], rest[PARTS:]
     blocks = rest[: len(ways)]
-    local_ref, own_ref, y_ref, acc_ref = rest[len(ways) :]
+    local_ref, own_ref, acc_ref = rest[len(ways) :]
     tile_count = acc_ref.shape[0]
     zero_blocks(acc_ref)
-    rules_matmul(f_ref, w_ref, y_ref)
-    rules_add(words, lists, 2 * words.shape[1], words[5, 0], y_ref, acc_ref)
+    rules_add(words, lists, 2, y_refs, acc_ref)
     c = lax.axis_index("chan")
     at = pl.multiple_of(lax.div(c, 2) * 128, 128)
     odd = lax.rem(c, 2) == 1
@@ -320,27 +333,28 @@
     near = [way for way in ways if way[0] <= 2]
     slots = tile_count // 4
     span = tile_count * VOX + 2 * PAD
-    pairs = (offsets + 1) // 2
     wide = rule_rows + 128
     flat = features.reshape(tile_count * VOX, channels)
     flat_weights = weights.transpose(0, 2, 1).reshape(offsets * quarter, channels)
     block = jax.ShapeDtypeStruct((slots, HALF, 128), BF)
     whole = jax.ShapeDtypeStruct((tile_count, HALF, 128), F32)
-    work = [pltpu.VMEM((pairs * span, 128), F32), pltpu.VMEM((tile_count, VOX, 128), F32)]
+    work = [pltpu.VMEM((tile_count, VOX, 128), F32)]
     flops = 2 * tile_count * VOX * channels * offsets * quarter
     shared = dict(
-        compiler_params=pltpu.CompilerParams(vmem_limit_bytes=44 * 1024 * 1024),
+        compiler_params=pltpu.CompilerParams(vmem_limit_bytes=16 * 1024 * 1024),
         cost_estimate=pl.CostEstimate(flops=flops, bytes_accessed=8 << 20, transcendentals=0),
     )
     made = pl.pallas_call(
         functools.partial(far_kernel, n, far, tile_count),
         out_shape=[block] * len(far)
-        + [jax.ShapeDtypeStruct(flat.shape, BF), jax.ShapeDtypeStruct(flat_weights.shape, BF)]
-        + [jax.ShapeDtypeStruct((8, wide), jnp.int32), jax.ShapeDtypeStruct((4 * wide,), jnp.int32)],
+        + [jax.ShapeDtypeStruct(flat.shape, BF), jax.ShapeDtypeStruct((PER_PART * span, 128), F32)]
+        + [jax.ShapeDtypeStruct((PER_PART * span, 128), F32)] * (PARTS - 1)
+        + [jax.ShapeDtypeStruct((8, wide), jnp.int32), jax.ShapeDtypeStruct(((3 * PARTS + 1) * wide,), jnp.int32)],
         in_specs=[HBM] * 3,
-        out_specs=[VM] * (len(far) + 3) + [SM],
+        out_specs=[VM] * (len(far) + 2 + PARTS) + [SM],
         scratch_shapes=work
         + [
+            pltpu.VMEM(flat_weights.shape, BF),
             pltpu.VMEM((4, rule_rows), jnp.int32),
             pltpu.SMEM((8, wide), jnp.int32),
             pltpu.SemaphoreType.DMA((4,)),
@@ -349,27 +363,27 @@
         **shared,
     )(*(pltpu.with_memory_space_constraint(x, pltpu.HBM) for x in (rulebook.T, flat, flat_weights)))
     far_sends = made[: len(far)]
-    held, held_weights, words, lists = made[len(far) :]
+    held, *products, words, lists = made[len(far) :]
     arrivals = [lax.ppermute(x, "tiles", way[2]) for x, way in zip(far_sends, far)]
     near_sends = pl.pallas_call(
         functools.partial(near_kernel, n, near),
         out_shape=[block] * len(near),
-        in_specs=[SM, SM, VM, VM],
+        in_specs=[SM, SM] + [VM] * PARTS,
         out_specs=[VM] * len(near),
         scratch_shapes=work,
         name="near",
         **shared,
-    )(words, lists, held, held_weights)
+    )(words, lists, *products)
     near_arrivals = [lax.ppermute(x, "tiles", way[2]) for x, way in zip(near_sends, near)]
     local, own = pl.pallas_call(
         functools.partial(local_kernel, n, far),
         out_shape=[whole, whole],
-        in_specs=[SM, SM, SM, VM, VM] + [VM] * len(far),
+        in_specs=[SM, SM, SM, VM] + [VM] * (PARTS + len(far)),
         out_specs=[VM, VM],
         scratch_shapes=work,
         name="local",
         **shared,
-    )(words, lists, recv_list, held, held_weights, *arrivals)
+    )(words, lists, recv_list, held, *products, *arrivals)
     return near, near_arrivals, local, own
 
 

time: 61 us -> 55 us (0.902)
  Pallas kernels: 30 us -> 23.4 us
  blocking collectives: 12.2 us -> 9.93 us
  local copies, waits for them, and re-layouts: 0.11 us -> 1.34 us
  waiting for transfers between devices: 2.8 us -> 3.83 us
  starting transfers between devices: 14.8 us -> 15.7 us
    pallas_call x1, Pallas kernels: 6.79 us -> 3.01 us  [call_rules(): pl.pallas_call(functools.partial(near_kernel, n, near), out_shape=[block]...]
    pallas_call x1, Pallas kernels: 9.4 us -> 6.34 us  [call_rules(): pl.pallas_call(functools.partial(local_kernel, n, far), out_shape=[whole,...]
    all_to_all x1, blocking collectives: 12.2 us -> 9.93 us  [body(): lax.all_to_all(outbound, 'tiles', split_axis=0, concat_axis=0, tiled=True)]
    unnamed x10 -> x14, local copies, waits for them, and re-layouts: 0.02 us -> 1.26 us
    ppermute x7, waiting for transfers between devices: 0.02 us -> 1.04 us  [call_rules(): lax.ppermute(x, 'tiles', way[2])]
    ppermute x7, starting transfers between devices: 13 us -> 13.8 us  [call_rules(): lax.ppermute(x, 'tiles', way[2])]
  transfers between devices with their start and end apart: 10 -> 10, of which waited for: 2 -> 3; matrix products, arithmetic and copies ran while one was open for 0% -> 0% of each run, Pallas kernels for 27% -> 17%
where the time goes in v5:
time: 55 us; the launch traced here: 54.9 us
  Pallas kernels  23.4 us (43%)
  starting transfers between devices  15.7 us (29%)
  blocking collectives  9.93 us (18%)
  waiting for transfers between devices  3.83 us (7%)
  local copies, waits for them, and re-layouts  1.34 us (2%)
  between operations  0.74 us (1%)
    ppermute x7, starting transfers between devices, call_rules(): lax.ppermute(x, 'tiles', way[2])  13.8 us
    all_to_all x1, blocking collectives, body(): lax.all_to_all(outbound, 'tiles', split_axis=0, concat_axis=0, tiled=True)  9.93 us
    pallas_call x1, Pallas kernels, call_rules(): pl.pallas_call(functools.partial(far_kernel, n, far, tile_count), out_sha...  7.83 us
    pallas_call x1, Pallas kernels, call_rules(): pl.pallas_call(functools.partial(local_kernel, n, far), out_shape=[whole,...  6.34 us
    pallas_call x1, Pallas kernels, body(): pl.pallas_call(functools.partial(norm_kernel, channels), out_shape=[jax.S...  3.26 us
    pallas_call x1, Pallas kernels, call_rules(): pl.pallas_call(functools.partial(near_kernel, n, near), out_shape=[block]...  3.01 us
    ppermute x3, waiting for transfers between devices, body(): lax.ppermute(sums, 'chan', [(i, i ^ m) for i in range(wide)])  2.79 us
    ppermute x3, starting transfers between devices, body(): lax.ppermute(sums, 'chan', [(i, i ^ m) for i in range(wide)])  1.88 us
  transfers between devices with their start and end apart: 10, of which 3 were waited for; matrix products, arithmetic and copies ran while one was open for 0% of the time, Pallas kernels for 17%

profile of v5, /device:TPU:0, one launch (start us, length us, event | category | flops | bytes accessed | tf_op | source)
XLA Modules:
  0.0 54.9 jit_solution(15540046070309619137)
XLA Ops:
  0.6 7.8 %far.1 = (bf16[16,32,128]{2,1,0:T(8,128)(2,1)S(1)}, bf16[16,32,128]{2,1,0:T(8,128)(2,1)S(1)}, bf16[16,32,128]{2,1,0:T(8,128)(2,1)S(1)}, bf16[4096,256]{1,0:T(8,1...) custom-call(s32[4,768]{1,0:T(4,128)} %bitcast.7, ...), custom_call_target="tpu_custom_call" | custom-call | flops 3623878656 | bytes 8388608 | tf_op jit(solution)/shard_map/far/pallas_call | solution.py:347
  8.5 3.9 %collective-permute-start = (bf16[16,32,128]{2,1,0:T(8,128)(2,1)S(1)}, bf16[16,32,128]{2,1,0:T(8,128)(2,1)S(1)}, u32[]{:S(2)}, u32[]{:S(2)}) collective-permute-start(bf16[16,32,128]{2,1,0:T(8,128)(2,1)S(1)} %get-tuple-element.25), channel_id=1, source_target_pairs={{0,16},{4,20},{8,24},{12,28},{16,0},{20,4},{24,8},{28,12},{1,17},{... | collective-permute-start | bytes 393224 | tf_op jit(solution)/shard_map/ppermute | solution.py:367
  12.4 2.7 %collective-permute-start.1 = (bf16[16,32,128]{2,1,0:T(8,128)(2,1)S(1)}, bf16[16,32,128]{2,1,0:T(8,128)(2,1)S(1)}, u32[]{:S(2)}, u32[]{:S(2)}) collective-permute-start(bf16[16,32,128]{2,1,0:T(8,128)(2,1)S(1)} %get-tuple-element.26), channel_id=1, source_target_pairs={{0,12},{4,16},{8,20},{24,28},{12,0},{16,4},{20,8},{28,24},{1,13},{... | collective-permute-start | bytes 393224 | tf_op jit(solution)/shard_map/ppermute | solution.py:367
  15.1 0.0 collective-permute-start.2
  15.1 3.0 %near.1 = (bf16[16,32,128]{2,1,0:T(8,128)(2,1)S(1)}, bf16[16,32,128]{2,1,0:T(8,128)(2,1)S(1)}, bf16[16,32,128]{2,1,0:T(8,128)(2,1)S(1)}, bf16[16,32,128]{2,1,0:T(8,128)(2,1)S(1)}) custom-call(s32[8,896]{1,0:T(8,128)S(1)} %get-tuple-element.20.words, s32[6272]{0:T(1024)S(1)} %get-tuple-element.21.lists, f32[29568,128]{1,0:T(8,128)S(1)} %get-tuple-element.23.rest_0_, ...), custom_call_target="tpu_custom_call" | custom-call | flops 3623878656 | bytes 8388608 | tf_op jit(solution)/shard_map/near/pallas_call | solution.py:368
  18.1 2.4 %collective-permute-start.3 = (bf16[16,32,128]{2,1,0:T(8,128)(2,1)S(1)}, bf16[16,32,128]{2,1,0:T(8,128)(2,1)S(1)}, u32[]{:S(2)}, u32[]{:S(2)}) collective-permute-start(bf16[16,32,128]{2,1,0:T(8,128)(2,1)S(1)} %get-tuple-element.29), channel_id=1, source_target_pairs={{0,8},{4,12},{16,24},{20,28},{8,0},{12,4},{24,16},{28,20},{1,9},{5... | collective-permute-start | bytes 393224 | tf_op jit(solution)/shard_map/ppermute | solution.py:377
  20.5 0.8 %collective-permute-start.4 = (bf16[16,32,128]{2,1,0:T(8,128)(2,1)S(1)}, bf16[16,32,128]{2,1,0:T(8,128)(2,1)S(1)}, u32[]{:S(2)}, u32[]{:S(2)}) collective-permute-start(bf16[16,32,128]{2,1,0:T(8,128)(2,1)S(1)} %get-tuple-element.30), channel_id=1, source_target_pairs={{8,16},{12,20},{0,4},{24,28},{16,8},{20,12},{4,0},{28,24},{9,17},{... | collective-permute-start | bytes 393224 | tf_op jit(solution)/shard_map/ppermute | solution.py:377
  21.3 1.0 %collective-permute-done.rest_2_ = bf16[16,32,128]{2,1,0:T(8,128)(2,1)S(1)} collective-permute-done((bf16[16,32,128]{2,1,0:T(8,128)(2,1)S(1)}, bf16[16,32,128]{2,1,0:T(8,128)(2,1)S(1)}, u32[]{:S(2)}, u32[]{:S(2)}) %collective-permute-start) | collective-permute-done | bytes 131104 | tf_op jit(solution)/shard_map/ppermute | solution.py:367
  22.4 0.2 collective-permute-start.5
  22.5 0.0 collective-permute-done.1.rest_3_
  22.5 3.8 %collective-permute-start.6 = (bf16[16,32,128]{2,1,0:T(8,128)(2,1)S(1)}, bf16[16,32,128]{2,1,0:T(8,128)(2,1)S(1)}, u32[]{:S(2)}, u32[]{:S(2)}) collective-permute-start(bf16[16,32,128]{2,1,0:T(8,128)(2,1)S(1)} %get-tuple-element.32), channel_id=1, source_target_pairs={{4,8},{12,16},{20,24},{0,28},{8,4},{16,12},{24,20},{28,0},{5,9},{1... | collective-permute-start | bytes 393224 | tf_op jit(solution)/shard_map/ppermute | solution.py:377
  26.3 0.0 collective-permute-done.2.rest_4_
  26.3 0.0 copy-start.5
  26.3 0.0 copy-start.4
  26.3 6.3 %local.1 = (f32[64,32,128]{2,1,0:T(8,128)S(1)}, f32[64,32,128]{2,1,0:T(8,128)S(1)}) custom-call(s32[8,896]{1,0:T(8,128)S(1)} %get-tuple-element.20.words, s32[6272]{0:T(1024)S(1)} %get-tuple-element.21.lists, s32[1,128]{1,0:T(1,128)S(1)} %copy-done.3, bf16[4096,256]{1,0:T(8,128)(2,1)S(1)} %get-tuple-element.22.f_ref, ...), custom_call_target="tpu_custom_call" | custom-call | flops 3623878656 | bytes 8388608 | tf_op jit(solution)/shard_map/local/pallas_call | solution.py:378
  32.7 0.0 copy-start
  32.7 0.0 collective-permute-done.3.rest_0_
  32.7 0.0 collective-permute-done.4.rest_1_
  32.7 0.0 collective-permute-done.5.rest_2_
  32.7 0.0 collective-permute-done.6.rest_3_
  32.7 1.2 %combine.1 = (f32[64,32,128]{2,1,0:T(8,128)S(1)}, f32[2,2048]{1,0:T(2,128)S(1)}) custom-call(f32[64,32,128]{2,1,0:T(8,128)S(1)} %get-tuple-element.28.local_ref, s32[1,128]{1,0:T(1,128)S(1)} %copy-done.3, bf16[16,32,128]{2,1,0:T(8,128)(2,1)S(1)} %collective-permute-done.3.rest_0_, bf16[16,32,128]{2,1,0:T(8,128)(2,1)S(1)} %collective-permute-done.4.rest_1_, ...), custom_call_target="tpu_custom_call" | custom-call | tf_op jit(solution)/shard_map/combine/pallas_call | solution.py:396
  33.9 0.0 collective-permute-start.7
  33.9 1.6 %collective-permute-start.8 = (f32[2,2048]{1,0:T(2,128)S(1)}, f32[2,2048]{1,0:T(2,128)S(1)}, u32[]{:S(2)}, u32[]{:S(2)}) collective-permute-start(f32[2,2048]{1,0:T(2,128)S(1)} %get-tuple-element.35.s0), channel_id=1, source_target_pairs={{0,2},{1,3},{2,0},{3,1},{4,6},{5,7},{6,4},{7,5},{8,10},{9,11},{10,... | collective-permute-start | bytes 49160 | tf_op jit(solution)/shard_map/ppermute | solution.py:408
  35.5 0.3 collective-permute-start.9
  35.8 0.1 reshape_tile.3.gain_ref
  35.9 0.0 collective-permute-done.7.s1
  35.9 1.8 %collective-permute-done.8.s2 = f32[2,2048]{1,0:T(2,128)S(1)} collective-permute-done((f32[2,2048]{1,0:T(2,128)S(1)}, f32[2,2048]{1,0:T(2,128)S(1)}, u32[]{:S(2)}, u32[]{:S(2)}) %collective-permute-start.8) | collective-permute-done | bytes 16416 | tf_op jit(solution)/shard_map/ppermute | solution.py:408
  37.7 0.9 %collective-permute-done.9.s3 = f32[2,2048]{1,0:T(2,128)S(1)} collective-permute-done((f32[2,2048]{1,0:T(2,128)S(1)}, f32[2,2048]{1,0:T(2,128)S(1)}, u32[]{:S(2)}, u32[]{:S(2)}) %collective-permute-start.9) | collective-permute-done | bytes 16416 | tf_op jit(solution)/shard_map/ppermute | solution.py:408
  38.7 1.2 %copy-done.1 = f32[64,32,128]{2,1,0:T(8,128)S(1)} copy-done((f32[64,32,128]{2,1,0:T(8,128)S(1)}, f32[64,32,128]{2,1,0:T(8,128)}, u32[]{:S(2)}) %copy-start.1) | copy-done | bytes 1048600
  39.9 3.3 %norm.1 = (bf16[64,64,64]{2,1,0:T(8,128)(2,1)}, bf16[8,32,128]{2,1,0:T(8,128)(2,1)S(1)}) custom-call(f32[64,32,128]{2,1,0:T(8,128)S(1)} %get-tuple-element.33.conv_ref, f32[64,32,128]{2,1,0:T(8,128)S(1)} %copy-done.1, f32[1,128]{1,0:T(1,128)S(1)} %reshape_tile.3.gain_ref, bf16[32,256]{1,0:T(8,128)(2,1)S(1)} %copy-done.2, s32[1,8]{1,0:T(1,128)S(1)} %copy-done.5, ...), custom_call_target="tpu_custom_call" | custom-call | tf_op jit(solution)/shard_map/norm/pallas_call | solution.py:411
  43.2 9.9 %all_to_all.5.landed_ref = bf16[8,32,128]{2,1,0:T(8,128)(2,1)S(1)} all-to-all(bf16[8,32,128]{2,1,0:T(8,128)(2,1)S(1)} %get-tuple-element.37), channel_id=1, replica_groups=mesh['tiles'=8,'chan'=4] {'tiles'}, dimensions={0} | all-to-all | bytes 131072 | tf_op jit(solution)/shard_map/all_to_all | solution.py:430
  53.1 1.8 %place.1 = bf16[8,64,64]{2,1,0:T(8,128)(2,1)} custom-call(s32[1,8]{1,0:T(1,128)S(1)} %copy-done.4, bf16[8,32,128]{2,1,0:T(8,128)(2,1)S(1)} %all_to_all.5.landed_ref), custom_call_target="tpu_custom_call" | custom-call | tf_op jit(solution)/shard_map/place/pallas_call | solution.py:431
  (11 shorter events, 0.0 us)
Async XLA Ops:
  8.5 13.9 %collective-permute-start = (bf16[16,32,128]{2,1,0:T(8,128)(2,1)S(1)}, bf16[16,32,128]{2,1,0:T(8,128)(2,1)S(1)}, u32[]{:S(2)}, u32[]{:S(2)}) collective-permute-start(bf16[16,32,128]{2,1,0:T(8,128)(2,1)S(1)} %get-tuple-element.25), channel_id=1, source_target_pairs={{0,16},{4,20},{8,24},{12,28},{16,0},{20,4},{24,8},{28,12},{1,17},{... | collective-permute-start | bytes 393224 | tf_op jit(solution)/shard_map/ppermute | solution.py:367
  12.4 10.1 %collective-permute-start.1 = (bf16[16,32,128]{2,1,0:T(8,128)(2,1)S(1)}, bf16[16,32,128]{2,1,0:T(8,128)(2,1)S(1)}, u32[]{:S(2)}, u32[]{:S(2)}) collective-permute-start(bf16[16,32,128]{2,1,0:T(8,128)(2,1)S(1)} %get-tuple-element.26), channel_id=1, source_target_pairs={{0,12},{4,16},{8,20},{24,28},{12,0},{16,4},{20,8},{28,24},{1,13},{... | collective-permute-start | bytes 393224 | tf_op jit(solution)/shard_map/ppermute | solution.py:367
  15.1 11.2 %collective-permute-start.2 = (bf16[16,32,128]{2,1,0:T(8,128)(2,1)S(1)}, bf16[16,32,128]{2,1,0:T(8,128)(2,1)S(1)}, u32[]{:S(2)}, u32[]{:S(2)}) collective-permute-start(bf16[16,32,128]{2,1,0:T(8,128)(2,1)S(1)} %get-tuple-element.27), channel_id=1, source_target_pairs={{12,24},{16,28},{0,4},{8,20},{24,12},{28,16},{4,0},{20,8},{13,25},... | collective-permute-start | bytes 393224 | tf_op jit(solution)/shard_map/ppermute | solution.py:367
  15.1 11.2 %copy-start.3 = (s32[1,128]{1,0:T(1,128)S(1)}, s32[1,128]{1,0:T(1,128)}, u32[]{:S(2)}) copy-start(s32[1,128]{1,0:T(1,128)} %list_ref.3) | copy-start | bytes 1540
  18.1 14.6 %collective-permute-start.3 = (bf16[16,32,128]{2,1,0:T(8,128)(2,1)S(1)}, bf16[16,32,128]{2,1,0:T(8,128)(2,1)S(1)}, u32[]{:S(2)}, u32[]{:S(2)}) collective-permute-start(bf16[16,32,128]{2,1,0:T(8,128)(2,1)S(1)} %get-tuple-element.29), channel_id=1, source_target_pairs={{0,8},{4,12},{16,24},{20,28},{8,0},{12,4},{24,16},{28,20},{1,9},{5... | collective-permute-start | bytes 393224 | tf_op jit(solution)/shard_map/ppermute | solution.py:377
  20.5 12.2 %collective-permute-start.4 = (bf16[16,32,128]{2,1,0:T(8,128)(2,1)S(1)}, bf16[16,32,128]{2,1,0:T(8,128)(2,1)S(1)}, u32[]{:S(2)}, u32[]{:S(2)}) collective-permute-start(bf16[16,32,128]{2,1,0:T(8,128)(2,1)S(1)} %get-tuple-element.30), channel_id=1, source_target_pairs={{8,16},{12,20},{0,4},{24,28},{16,8},{20,12},{4,0},{28,24},{9,17},{... | collective-permute-start | bytes 393224 | tf_op jit(solution)/shard_map/ppermute | solution.py:377
  22.4 10.4 %collective-permute-start.5 = (bf16[16,32,128]{2,1,0:T(8,128)(2,1)S(1)}, bf16[16,32,128]{2,1,0:T(8,128)(2,1)S(1)}, u32[]{:S(2)}, u32[]{:S(2)}) collective-permute-start(bf16[16,32,128]{2,1,0:T(8,128)(2,1)S(1)} %get-tuple-element.31), channel_id=1, source_target_pairs={{0,4},{8,12},{16,20},{24,28},{4,0},{12,8},{20,16},{28,24},{1,5},{9... | collective-permute-start | bytes 393224 | tf_op jit(solution)/shard_map/ppermute | solution.py:377
  22.5 10.2 %collective-permute-start.6 = (bf16[16,32,128]{2,1,0:T(8,128)(2,1)S(1)}, bf16[16,32,128]{2,1,0:T(8,128)(2,1)S(1)}, u32[]{:S(2)}, u32[]{:S(2)}) collective-permute-start(bf16[16,32,128]{2,1,0:T(8,128)(2,1)S(1)} %get-tuple-element.32), channel_id=1, source_target_pairs={{4,8},{12,16},{20,24},{0,28},{8,4},{16,12},{24,20},{28,0},{5,9},{1... | collective-permute-start | bytes 393224 | tf_op jit(solution)/shard_map/ppermute | solution.py:377
  26.3 9.5 %copy-start.6 = (bf16[64]{0:T(256)(128)(2,1)S(1)}, bf16[64]{0:T(256)(128)(2,1)}, u32[]{:S(2)}) copy-start(bf16[64]{0:T(256)(128)(2,1)} %param.10) | copy-start | bytes 388
  26.3 12.4 %copy-start.2 = (bf16[32,256]{1,0:T(8,128)(2,1)S(1)}, bf16[32,256]{1,0:T(8,128)(2,1)}, u32[]{:S(2)}) copy-start(bf16[32,256]{1,0:T(8,128)(2,1)} %constant.2.clone.pool_ref) | copy-start | bytes 49156
  26.3 12.4 %copy-start.5 = (s32[1,8]{1,0:T(1,128)S(1)}, s32[1,8]{1,0:T(1,128)}, u32[]{:S(2)}) copy-start(s32[1,8]{1,0:T(1,128)} %slot_ref.1) | copy-start | bytes 100
  26.3 26.8 %copy-start.4 = (s32[1,8]{1,0:T(1,128)S(1)}, s32[1,8]{1,0:T(1,128)}, u32[]{:S(2)}) copy-start(s32[1,8]{1,0:T(1,128)} %place_ref.1) | copy-start | bytes 100
  32.7 1.2 %copy-start = (f32[64,32,128]{2,1,0:T(8,128)}, f32[64,32,128]{2,1,0:T(8,128)S(1)}, u32[]{:S(2)}) copy-start(f32[64,32,128]{2,1,0:T(8,128)S(1)} %get-tuple-element.34.own_ref) | copy-start | bytes 3145732
  33.9 2.0 %collective-permute-start.7 = (f32[2,2048]{1,0:T(2,128)S(1)}, f32[2,2048]{1,0:T(2,128)S(1)}, u32[]{:S(2)}, u32[]{:S(2)}) collective-permute-start(f32[2,2048]{1,0:T(2,128)S(1)} %get-tuple-element.35.s0), channel_id=1, source_target_pairs={{0,1},{1,0},{2,3},{3,2},{4,5},{5,4},{6,7},{7,6},{8,9},{9,8},{10,11... | collective-permute-start | bytes 49160 | tf_op jit(solution)/shard_map/ppermute | solution.py:408
  33.9 3.8 %collective-permute-start.8 = (f32[2,2048]{1,0:T(2,128)S(1)}, f32[2,2048]{1,0:T(2,128)S(1)}, u32[]{:S(2)}, u32[]{:S(2)}) collective-permute-start(f32[2,2048]{1,0:T(2,128)S(1)} %get-tuple-element.35.s0), channel_id=1, source_target_pairs={{0,2},{1,3},{2,0},{3,1},{4,6},{5,7},{6,4},{7,5},{8,10},{9,11},{10,... | collective-permute-start | bytes 49160 | tf_op jit(solution)/shard_map/ppermute | solution.py:408
  35.5 3.2 %collective-permute-start.9 = (f32[2,2048]{1,0:T(2,128)S(1)}, f32[2,2048]{1,0:T(2,128)S(1)}, u32[]{:S(2)}, u32[]{:S(2)}) collective-permute-start(f32[2,2048]{1,0:T(2,128)S(1)} %get-tuple-element.35.s0), channel_id=1, source_target_pairs={{0,3},{1,2},{2,1},{3,0},{4,7},{5,6},{6,5},{7,4},{8,11},{9,10},{10,... | collective-permute-start | bytes 49160 | tf_op jit(solution)/shard_map/ppermute | solution.py:408
  38.7 1.2 %copy-start.1 = (f32[64,32,128]{2,1,0:T(8,128)S(1)}, f32[64,32,128]{2,1,0:T(8,128)}, u32[]{:S(2)}) copy-start(f32[64,32,128]{2,1,0:T(8,128)} %copy-done) | copy-start | bytes 3145732

commit v6 on v5

--- a/solution.py
+++ b/solution.py
@@ -20,23 +20,68 @@
 PER_PART = 7
 
 
+def perfect(n):
+    real = [(i, j) for i in range(n) for j in range(i + 1, n) if j - i <= REACH]
+    fill = [(0, 1), (0, 1), (0, 2), (6, 7), (6, 7), (5, 7)]
+    first = [(i, i + REACH) for i in range(n - REACH)]
+    start = [(p, True) for p in real if p not in first] + [(p, False) for p in fill]
+
+    def crossing(found):
+        return -sum(i < n // 2 <= j for (i, j), _ in found)
+
+    def split(left):
+        if not left:
+            return []
+        here = left[0]
+
+        def grow(chosen, rest):
+            used = {i for p, _ in chosen for i in p}
+            if len(used) == n:
+                yield chosen, rest
+                return
+            low = min(set(range(n)) - used)
+            for k, item in enumerate(rest):
+                if low in item[0] and not used & set(item[0]):
+                    yield from grow(chosen + [item], rest[:k] + rest[k + 1 :])
+
+        for chosen, rest in grow([here], left[1:]):
+            more = split(rest)
+            if more is not None:
+                return [chosen] + more
+        return None
+
+    found = split(start)
+    return None if found is None else [[(p, True) for p in first]] + sorted(found, key=crossing)
+
+
 def matchings(n):
-    found = []
-    for d in range(REACH, 0, -1):
-        for parity in (0, 1):
-            pairs = [(i, i + d) for i in range(n - d) if (i // d) % 2 == parity]
-            if pairs:
+    found = perfect(n) if n == 2 * REACH else None
+    if found is None:
+        found = []
+        for d in range(REACH, 0, -1):
+            for parity in (0, 1):
+                pairs = [(i, i + d) for i in range(n - d) if (i // d) % 2 == parity]
                 rest = [i for i in range(n) if all(i not in p for p in pairs)]
-                fill = list(zip(rest[::2], rest[1::2]))
-                both = pairs + fill
-                found.append((d, parity, both + [(b, a) for a, b in both]))
+                if pairs:
+                    found.append([(p, True) for p in pairs] + [(p, False) for p in zip(rest[::2], rest[1::2])])
+    routes = [[q for p, _ in way for q in (p, p[::-1])] for way in found]
+    table = np.full((n, 16), -1, np.int32)
+    table[:, 15] = 0
+    for m, way in enumerate(found):
+        for pair, is_real in way:
+            for e, other in (pair, pair[::-1]):
+                if is_real:
+                    gap = other - e
+                    table[e, m] = REACH - 1 + gap if gap > 0 else -gap - 1
+                    table[e, 15] += m << (4 * (gap - 1 if gap > 0 else REACH - 1 - gap))
+    return routes, table
+
+
+def pick(e, values):
+    found = jnp.int32(int(values[0]))
+    for i in range(1, len(values)):
+        found = jnp.where(e == i, jnp.int32(int(values[i])), found)
     return found
-
-
-def role(e, n, d, parity):
-    low = jnp.logical_and(lax.rem(lax.div(e, d), 2) == parity, e + d < n)
-    high = jnp.logical_and(e >= d, lax.rem(lax.div(jnp.maximum(e - d, 0), d), 2) == parity)
-    return low, high
 
 
 def lane_iota(shape):
@@ -111,25 +156,21 @@
     return jnp.where(first, low, high)
 
 
-def emit_sends(n, ways, acc_ref, sends):
-    e = lax.axis_index("tiles")
+def emit_sends(acc_ref, sends):
     slots = sends[0].shape[0]
-    for (d, parity, _), send_ref in zip(ways, sends):
-        low, _high = role(e, n, d, parity)
-        base = slots * ((d - 1) % 2 + jnp.where(low, 0, 2))
-
-        def emit(i, c, send_ref=send_ref, base=base):
+    for m, send_ref in enumerate(sends):
+
+        def emit(i, c, send_ref=send_ref, base=slots * m):
             send_ref[i] = folded(acc_ref, base + i).astype(BF)
             return c
 
         lax.fori_loop(0, slots, emit, 0, unroll=16)
 
 
-def far_kernel(n, ways, tile_count, rules_hbm, f_hbm, w_hbm, *rest):
-    sends = rest[: len(ways)]
-    f_ref = rest[len(ways)]
-    y_refs = rest[len(ways) + 1 : len(ways) + 1 + PARTS]
-    words_v, lists, acc_ref, w_ref, rules_ref, words_s, sems = rest[len(ways) + 1 + PARTS :]
+def far_kernel(count, table, tile_count, rules_hbm, f_hbm, w_hbm, *rest):
+    sends, rest = rest[:count], rest[count:]
+    f_ref, y_refs, rest = rest[0], rest[1 : 1 + PARTS], rest[1 + PARTS :]
+    words_v, lists, acc_ref, w_ref, rules_ref, words_s, sems = rest
     rows = tile_count * VOX
     span = rows + 2 * PAD
     rule_rows = rules_ref.shape[1]
@@ -158,8 +199,10 @@
         need = need + jnp.left_shift(jnp.full_like(move, 1), move + (3 + 7 * dim))
     sent = jnp.maximum(target - tile_count, 0)
     group = lax.div(sent, slots)
-    place = (lax.div(group, 4) * 2 + lax.rem(group, 2)) * slots + lax.rem(sent, slots)
-    near = lax.rem(group, 4) < 2
+    coded = jnp.full_like(group, pick(lax.axis_index("tiles"), table[:, 15]))
+    way = lax.shift_right_logical(coded, 4 * group) & 15
+    near = way >= count
+    place = jnp.where(near, way - count, way) * slots + lax.rem(sent, slots)
     part = jnp.where(target < tile_count, 2, jnp.where(near, 1, 0))
     pair = lax.div(code, 2)
     part = jnp.where(kernel < 27, part * PARTS + lax.div(pair, PER_PART), 3 * PARTS)
@@ -179,12 +222,13 @@
         words_v[3:4, 128 * c : 128 * c + 128] = jnp.broadcast_to(total, (1, 128)).astype(jnp.int32)
     to_scalars = pltpu.make_async_copy(words_v, words_s, sems.at[3])
     to_scalars.start()
-    to_scalars.wait()
     copies[1].wait()
     copies[2].wait()
 
-    def list_some(number, count):
-        share = -(-rule_rows // count)
+    def list_some(number, steps):
+        if number == 0:
+            to_scalars.wait()
+        share = -(-rule_rows // (steps - 1))
         for r in range(number * share, min(rule_rows, (number + 1) * share)):
             lists[words_s[2, r]] = r
 
@@ -193,46 +237,50 @@
         for u in range(UNROLL):
             lists[c * wide + words_s[3, 128 * c] + u] = rule_rows
     rules_add(words_s, lists, 0, y_refs, acc_ref)
-    emit_sends(n, ways, acc_ref, sends)
-
-
-def near_kernel(n, ways, words, lists, *rest):
-    y_refs, rest = rest[:PARTS], rest[PARTS:]
-    sends = rest[: len(ways)]
-    acc_ref = rest[len(ways)]
+    emit_sends(acc_ref, sends)
+
+
+def near_kernel(words, lists, *rest):
+    y_refs, sends, acc_ref = rest[:PARTS], rest[PARTS:-1], rest[-1]
     zero_blocks(acc_ref)
     rules_add(words, lists, 1, y_refs, acc_ref)
-    emit_sends(n, ways, acc_ref, sends)
-
-
-def add_arrivals(n, ways, blocks, list_ref, out_ref):
+    emit_sends(acc_ref, sends)
+
+
+def add_arrivals(first, table, blocks, list_ref, out_ref):
     e = lax.axis_index("tiles")
     slots = blocks[0].shape[0]
-    for (d, parity, _), block in zip(ways, blocks):
-        low, high = role(e, n, d, parity)
-        base = slots * jnp.where(low, d + 3, d - 1)
-
-        @pl.when(jnp.logical_or(low, high))
-        def _(block=block, base=base):
+    for m, block in enumerate(blocks):
+        group = pick(e, table[:, first + m])
+
+        @pl.when(group >= 0)
+        def _(block=block, group=group):
             for i in range(slots):
-                t = list_ref[0, base + i]
+                t = list_ref[0, group * slots + i]
                 out_ref[t] = out_ref[t] + block[i].astype(F32)
 
 
-def local_kernel(n, ways, words, lists, list_ref, f_ref, *rest):
-    y_refs, rest = rest[:PARTS], rest[PARTS:]
-    blocks = rest[: len(ways)]
-    local_ref, own_ref, acc_ref = rest[len(ways) :]
-    tile_count = acc_ref.shape[0]
+def local_kernel(table, words, lists, list_ref, *rest):
+    y_refs, blocks = rest[:PARTS], rest[PARTS:-2]
+    local_ref, acc_ref = rest[-2:]
     zero_blocks(acc_ref)
     rules_add(words, lists, 2, y_refs, acc_ref)
+
+    def keep(t, c):
+        local_ref[t] = folded(acc_ref, t)
+        return c
+
+    lax.fori_loop(0, acc_ref.shape[0], keep, 0, unroll=16)
+    add_arrivals(0, table, blocks, list_ref, local_ref)
+
+
+def own_kernel(f_ref, _after, own_ref):
     c = lax.axis_index("chan")
     at = pl.multiple_of(lax.div(c, 2) * 128, 128)
     odd = lax.rem(c, 2) == 1
     first = lane_iota((HALF, 128)) < 64
 
-    def keep(t, c):
-        local_ref[t] = folded(acc_ref, t)
+    def pack(t, c):
         block = f_ref[pl.ds(pl.multiple_of(t * VOX, VOX), VOX), pl.ds(at, 128)].astype(F32)
         low, high = block[:HALF], block[HALF:]
         even_form = jnp.where(first, low, pltpu.roll(high, 64, 1))
@@ -240,16 +288,15 @@
         own_ref[t] = jnp.where(odd, odd_form, even_form)
         return c
 
-    lax.fori_loop(0, tile_count, keep, 0, unroll=8)
-    add_arrivals(n, ways, blocks, list_ref, local_ref)
-
-
-def combine_kernel(n, ways, local_ref, list_ref, *rest):
-    blocks = rest[: len(ways)]
-    conv_ref, sums_ref = rest[len(ways) :]
+    lax.fori_loop(0, own_ref.shape[0], pack, 0, unroll=8)
+
+
+def combine_kernel(first, table, list_ref, local_ref, *rest):
+    blocks = rest[:-2]
+    conv_ref, sums_ref = rest[-2:]
     tile_count = local_ref.shape[0]
     conv_ref[...] = local_ref[...]
-    add_arrivals(n, ways, blocks, list_ref, conv_ref)
+    add_arrivals(first, table, blocks, list_ref, conv_ref)
     rows = tile_count * HALF
     pick = (lane_iota((2, 256)) // 64 % 2 == lax.broadcasted_iota(jnp.int32, (2, 256), 0)).astype(BF)
     step = 512
@@ -266,7 +313,7 @@
         )
 
 
-def norm_kernel(channels, conv_ref, own_ref, gain_ref, pool_ref, slot_ref, s0, s1, s2, s3, skip_ref, out_ref):
+def norm_kernel(channels, conv_ref, own_ref, gain_ref, pool_ref, slot_ref, s0, s1, s2, s3, whole_ref, out_ref):
     tile_count = conv_ref.shape[0]
     total = jnp.concatenate([s0[...], s1[...], s2[...], s3[...]], axis=0)
     parts = []
@@ -287,13 +334,17 @@
         ) * (1.0 / channels)
         value = conv_ref[8 * k : 8 * k + 8].reshape(256, 128)
         v = gain * value * lax.rsqrt(mean_square + EPS)
-        hidden = v / (1.0 + jnp.exp(-v))
+        half = 0.5 * v
+        hidden = half + half * jnp.tanh(half)
         whole = (own_ref[8 * k : 8 * k + 8].reshape(256, 128) + hidden).astype(BF)
-        cut = whole.reshape(8, HALF, 128)
-        skip_ref[8 * k : 8 * k + 8, 0:HALF, :] = cut[:, :, 0:64]
-        skip_ref[8 * k : 8 * k + 8, HALF:VOX, :] = cut[:, :, 64:128]
+        whole_ref[8 * k : 8 * k + 8] = whole.reshape(8, HALF, 128)
         pooled = jnp.dot(pool_ref[...], whole, preferred_element_type=F32)
         out_ref[slot_ref[0, k]] = pooled.astype(BF)
+
+
+def unpack_kernel(whole_ref, skip_ref):
+    skip_ref[:, 0:HALF, :] = whole_ref[:, :, 0:64]
+    skip_ref[:, HALF:VOX, :] = whole_ref[:, :, 64:128]
 
 
 def place_kernel(place_ref, landed_ref, out_ref):
@@ -328,9 +379,8 @@
     tile_count, _, channels = features.shape
     offsets, _, quarter = weights.shape
     rule_rows = rulebook.shape[0]
-    ways = matchings(n)
-    far = [way for way in ways if way[0] > 2]
-    near = [way for way in ways if way[0] <= 2]
+    routes, table = matchings(n)
+    count = len(routes) // 2
     slots = tile_count // 4
     span = tile_count * VOX + 2 * PAD
     wide = rule_rows + 128
@@ -345,13 +395,13 @@
         cost_estimate=pl.CostEstimate(flops=flops, bytes_accessed=8 << 20, transcendentals=0),
     )
     made = pl.pallas_call(
-        functools.partial(far_kernel, n, far, tile_count),
-        out_shape=[block] * len(far)
+        functools.partial(far_kernel, count, table, tile_count),
+        out_shape=[block] * count
         + [jax.ShapeDtypeStruct(flat.shape, BF), jax.ShapeDtypeStruct((PER_PART * span, 128), F32)]
         + [jax.ShapeDtypeStruct((PER_PART * span, 128), F32)] * (PARTS - 1)
         + [jax.ShapeDtypeStruct((8, wide), jnp.int32), jax.ShapeDtypeStruct(((3 * PARTS + 1) * wide,), jnp.int32)],
         in_specs=[HBM] * 3,
-        out_specs=[VM] * (len(far) + 2 + PARTS) + [SM],
+        out_specs=[VM] * (count + 2 + PARTS) + [SM],
         scratch_shapes=work
         + [
             pltpu.VMEM(flat_weights.shape, BF),
@@ -362,29 +412,29 @@
         name="far",
         **shared,
     )(*(pltpu.with_memory_space_constraint(x, pltpu.HBM) for x in (rulebook.T, flat, flat_weights)))
-    far_sends = made[: len(far)]
-    held, *products, words, lists = made[len(far) :]
-    arrivals = [lax.ppermute(x, "tiles", way[2]) for x, way in zip(far_sends, far)]
+    far_sends = made[:count]
+    held, *products, words, lists = made[count:]
+    arrivals = [lax.ppermute(x, "tiles", route) for x, route in zip(far_sends, routes[:count])]
     near_sends = pl.pallas_call(
-        functools.partial(near_kernel, n, near),
-        out_shape=[block] * len(near),
+        near_kernel,
+        out_shape=[block] * (len(routes) - count),
         in_specs=[SM, SM] + [VM] * PARTS,
-        out_specs=[VM] * len(near),
+        out_specs=[VM] * (len(routes) - count),
         scratch_shapes=work,
         name="near",
         **shared,
     )(words, lists, *products)
-    near_arrivals = [lax.ppermute(x, "tiles", way[2]) for x, way in zip(near_sends, near)]
-    local, own = pl.pallas_call(
-        functools.partial(local_kernel, n, far),
-        out_shape=[whole, whole],
-        in_specs=[SM, SM, SM, VM] + [VM] * (PARTS + len(far)),
-        out_specs=[VM, VM],
+    near_arrivals = [lax.ppermute(x, "tiles", route) for x, route in zip(near_sends, routes[count:])]
+    local = pl.pallas_call(
+        functools.partial(local_kernel, table),
+        out_shape=whole,
+        in_specs=[SM] * 3 + [VM] * (PARTS + count),
+        out_specs=VM,
         scratch_shapes=work,
         name="local",
         **shared,
-    )(words, lists, recv_list, held, *products, *arrivals)
-    return near, near_arrivals, local, own
+    )(words, lists, recv_list, *products, *arrivals)
+    return count, table, held, local, near_arrivals
 
 
 def body(n, features, weights, gain, rulebook, recv_list, coarse_send, coarse_place):
@@ -392,26 +442,34 @@
     quarter = weights.shape[2]
     small = pltpu.CompilerParams(vmem_limit_bytes=12 * 1024 * 1024)
 
-    near, arrivals, local, own = call_rules(n, features, weights, rulebook, recv_list)
+    count, table, held, local, arrivals = call_rules(n, features, weights, rulebook, recv_list)
     conv, sums = pl.pallas_call(
-        functools.partial(combine_kernel, n, near),
+        functools.partial(combine_kernel, count, table),
         out_shape=[
             jax.ShapeDtypeStruct((tile_count, HALF, 128), F32),
             jax.ShapeDtypeStruct((2, tile_count * HALF), F32),
         ],
-        in_specs=[VM, SM] + [VM] * len(near),
+        in_specs=[SM] + [VM] * (1 + len(arrivals)),
         out_specs=[VM, VM],
         compiler_params=small,
         name="combine",
-    )(local, recv_list, *arrivals)
+    )(recv_list, local, *arrivals)
+    own = pl.pallas_call(
+        own_kernel,
+        out_shape=jax.ShapeDtypeStruct((tile_count, HALF, 128), F32),
+        in_specs=[VM, ANY],
+        out_specs=VM,
+        compiler_params=small,
+        name="own",
+    )(held, sums)
     wide = lax.axis_size("chan")
     others = [lax.ppermute(sums, "chan", [(i, i ^ m) for i in range(wide)]) for m in range(1, wide)]
     slot_count = coarse_place.shape[1]
     parent_count = tile_count // 8
-    skip, outbound = pl.pallas_call(
+    packed, outbound = pl.pallas_call(
         functools.partial(norm_kernel, channels),
         out_shape=[
-            jax.ShapeDtypeStruct((tile_count, VOX, quarter), BF),
+            jax.ShapeDtypeStruct((tile_count, HALF, 128), BF),
             jax.ShapeDtypeStruct((slot_count, HALF, 128), BF),
         ],
         in_specs=[VM] * 4 + [SM] + [VM] * 4,
@@ -428,6 +486,14 @@
         *others,
     )
     landed = lax.all_to_all(outbound, "tiles", split_axis=0, concat_axis=0, tiled=True)
+    skip = pl.pallas_call(
+        unpack_kernel,
+        out_shape=jax.ShapeDtypeStruct((tile_count, VOX, quarter), BF),
+        in_specs=[VM],
+        out_specs=VM,
+        compiler_params=small,
+        name="unpack",
+    )(packed)
     coarse = pl.pallas_call(
         place_kernel,
         out_shape=jax.ShapeDtypeStruct((parent_count, VOX, quarter), BF),

time: 55 us -> 56.6 us (1.029)
  blocking collectives: 9.93 us -> 0 us
  waiting for transfers between devices: 3.83 us -> 10.4 us
  starting transfers between devices: 15.7 us -> 21.3 us
  local copies, waits for them, and re-layouts: 1.34 us -> 0.11 us
    all_to_all x1 -> x0, blocking collectives: 9.93 us -> none  [body(): lax.all_to_all(outbound, 'tiles', split_axis=0, concat_axis=0, tiled=True)]
    all_to_all x0 -> x1, starting transfers between devices: none -> 7.68 us  [body(): lax.all_to_all(outbound, 'tiles', split_axis=0, concat_axis=0, tiled=True)]
    all_to_all x0 -> x1, waiting for transfers between devices: none -> 5.6 us  [body(): lax.all_to_all(outbound, 'tiles', split_axis=0, concat_axis=0, tiled=True)]
    ppermute x7, starting transfers between devices: 13.8 us -> 11.7 us  [call_rules(): lax.ppermute(x, 'tiles', route)]
    ppermute x7, waiting for transfers between devices: 1.04 us -> 2.91 us  [call_rules(): lax.ppermute(x, 'tiles', route)]
    unnamed x14 -> x10, local copies, waits for them, and re-layouts: 1.26 us -> 0.03 us
    pallas_call x4 -> x6, Pallas kernels: 18.3 us -> 19.2 us  [the longest x1 7.57 us: call_rules(): pl.pallas_call(functools.partial(far_kernel, count, table, tile_count), o...]
    ppermute x3, waiting for transfers between devices: 2.79 us -> 1.94 us  [body(): lax.ppermute(sums, 'chan', [(i, i ^ m) for i in range(wide)])]
  transfers between devices with their start and end apart: 10 -> 11, of which waited for: 3 -> 4; matrix products, arithmetic and copies ran while one was open for 0% -> 0% of each run, Pallas kernels for 17% -> 18%
where the time goes in v6:
time: 56.6 us; the launch traced here: 56.3 us
  Pallas kernels  23.8 us (42%)
  starting transfers between devices  21.3 us (38%)
  waiting for transfers between devices  10.4 us (18%)
  between operations  0.75 us (1%)
    ppermute x7, starting transfers between devices, call_rules(): lax.ppermute(x, 'tiles', route)  11.7 us
    all_to_all x1, starting transfers between devices, body(): lax.all_to_all(outbound, 'tiles', split_axis=0, concat_axis=0, tiled=True)  7.68 us
    pallas_call x1, Pallas kernels, call_rules(): pl.pallas_call(functools.partial(far_kernel, count, table, tile_count), o...  7.57 us
    all_to_all x1, waiting for transfers between devices, body(): lax.all_to_all(outbound, 'tiles', split_axis=0, concat_axis=0, tiled=True)  5.6 us
    pallas_call x1, Pallas kernels, call_rules(): pl.pallas_call(functools.partial(local_kernel, table), out_shape=whole, i...  5.08 us
    pallas_call x1, Pallas kernels, call_rules(): pl.pallas_call(near_kernel, out_shape=[block] * (len(routes) - count), in...  3.19 us
    ppermute x7, waiting for transfers between devices, call_rules(): lax.ppermute(x, 'tiles', route)  2.91 us
    pallas_call x1, Pallas kernels, body(): pl.pallas_call(functools.partial(norm_kernel, channels), out_shape=[jax.S...  2.82 us
  transfers between devices with their start and end apart: 11, of which 4 were waited for; matrix products, arithmetic and copies ran while one was open for 0% of the time, Pallas kernels for 18%

profile of v6, /device:TPU:0, one launch (start us, length us, event | category | flops | bytes accessed | tf_op | source)
XLA Modules:
  0.0 56.3 jit_solution(8098898185541638291)
XLA Ops:
  0.6 7.6 %far.1 = (bf16[16,32,128]{2,1,0:T(8,128)(2,1)S(1)}, bf16[16,32,128]{2,1,0:T(8,128)(2,1)S(1)}, bf16[16,32,128]{2,1,0:T(8,128)(2,1)S(1)}, bf16[4096,256]{1,0:T(8,1...) custom-call(s32[4,768]{1,0:T(4,128)} %bitcast.7, ...), custom_call_target="tpu_custom_call" | custom-call | flops 3623878656 | bytes 8388608 | tf_op jit(solution)/shard_map/far/pallas_call | solution.py:397
  8.2 4.6 %collective-permute-start = (bf16[16,32,128]{2,1,0:T(8,128)(2,1)S(1)}, bf16[16,32,128]{2,1,0:T(8,128)(2,1)S(1)}, u32[]{:S(2)}, u32[]{:S(2)}) collective-permute-start(bf16[16,32,128]{2,1,0:T(8,128)(2,1)S(1)} %get-tuple-element.22), channel_id=1, source_target_pairs={{0,16},{16,0},{4,20},{20,4},{8,24},{24,8},{12,28},{28,12},{1,17},{... | collective-permute-start | bytes 393224 | tf_op jit(solution)/shard_map/ppermute | solution.py:417
  12.8 1.8 %collective-permute-start.1 = (bf16[16,32,128]{2,1,0:T(8,128)(2,1)S(1)}, bf16[16,32,128]{2,1,0:T(8,128)(2,1)S(1)}, u32[]{:S(2)}, u32[]{:S(2)}) collective-permute-start(bf16[16,32,128]{2,1,0:T(8,128)(2,1)S(1)} %get-tuple-element.23), channel_id=1, source_target_pairs={{4,16},{16,4},{0,8},{8,0},{12,20},{20,12},{24,28},{28,24},{5,17},{... | collective-permute-start | bytes 393224 | tf_op jit(solution)/shard_map/ppermute | solution.py:417
  14.5 0.0 collective-permute-start.2
  14.5 3.2 %near.1 = (bf16[16,32,128]{2,1,0:T(8,128)(2,1)S(1)}, bf16[16,32,128]{2,1,0:T(8,128)(2,1)S(1)}, bf16[16,32,128]{2,1,0:T(8,128)(2,1)S(1)}, bf16[16,32,128]{2,1,0:T(8,128)(2,1)S(1)}) custom-call(s32[8,896]{1,0:T(8,128)S(1)} %get-tuple-element.18.words, s32[6272]{0:T(1024)S(1)} %get-tuple-element.19.lists, f32[29568,128]{1,0:T(8,128)S(1)} %get-tuple-element.20.rest_0_, ...), custom_call_target="tpu_custom_call" | custom-call | flops 3623878656 | bytes 8388608 | tf_op jit(solution)/shard_map/near/pallas_call | solution.py:418
  17.7 1.5 %collective-permute-start.3 = (bf16[16,32,128]{2,1,0:T(8,128)(2,1)S(1)}, bf16[16,32,128]{2,1,0:T(8,128)(2,1)S(1)}, u32[]{:S(2)}, u32[]{:S(2)}) collective-permute-start(bf16[16,32,128]{2,1,0:T(8,128)(2,1)S(1)} %get-tuple-element.25), channel_id=1, source_target_pairs={{8,20},{20,8},{0,4},{4,0},{12,16},{16,12},{24,28},{28,24},{9,21},{... | collective-permute-start | bytes 393224 | tf_op jit(solution)/shard_map/ppermute | solution.py:427
  19.2 0.6 %collective-permute-start.4 = (bf16[16,32,128]{2,1,0:T(8,128)(2,1)S(1)}, bf16[16,32,128]{2,1,0:T(8,128)(2,1)S(1)}, u32[]{:S(2)}, u32[]{:S(2)}) collective-permute-start(bf16[16,32,128]{2,1,0:T(8,128)(2,1)S(1)} %get-tuple-element.26), channel_id=1, source_target_pairs={{0,4},{4,0},{8,12},{12,8},{16,20},{20,16},{24,28},{28,24},{1,5},{5... | collective-permute-start | bytes 393224 | tf_op jit(solution)/shard_map/ppermute | solution.py:427
  19.8 2.9 %collective-permute-done.rest_2_ = bf16[16,32,128]{2,1,0:T(8,128)(2,1)S(1)} collective-permute-done((bf16[16,32,128]{2,1,0:T(8,128)(2,1)S(1)}, bf16[16,32,128]{2,1,0:T(8,128)(2,1)S(1)}, u32[]{:S(2)}, u32[]{:S(2)}) %collective-permute-start) | collective-permute-done | bytes 131104 | tf_op jit(solution)/shard_map/ppermute | solution.py:417
  22.7 0.0 collective-permute-start.5
  22.7 0.0 collective-permute-done.1.rest_3_
  22.7 0.0 copy-start
  22.8 0.0 copy-start.3
  22.8 0.0 copy-start.2
  22.8 3.3 %collective-permute-start.6 = (bf16[16,32,128]{2,1,0:T(8,128)(2,1)S(1)}, bf16[16,32,128]{2,1,0:T(8,128)(2,1)S(1)}, u32[]{:S(2)}, u32[]{:S(2)}) collective-permute-start(bf16[16,32,128]{2,1,0:T(8,128)(2,1)S(1)} %get-tuple-element.28), channel_id=1, source_target_pairs={{0,12},{12,0},{4,8},{8,4},{16,28},{28,16},{20,24},{24,20},{1,13},{... | collective-permute-start | bytes 393224 | tf_op jit(solution)/shard_map/ppermute | solution.py:427
  26.1 0.0 collective-permute-done.2.rest_4_
  26.1 5.1 %local.1.local_ref = f32[64,32,128]{2,1,0:T(8,128)S(1)} custom-call(s32[8,896]{1,0:T(8,128)S(1)} %get-tuple-element.18.words, s32[6272]{0:T(1024)S(1)} %get-tuple-element.19.lists, s32[1,128]{1,0:T(1,128)S(1)} %copy-done.1, f32[29568,128]{1,0:T(8,128)S(1)} %get-tuple-element.20.rest_0_, f32[29568,128]{1,0:T(8,128)S(1)} %get-tuple-element.21.rest_1_, ...), custom_call_target="tpu_custom_call" | custom-call | flops 3623878656 | bytes 8388608 | tf_op jit(solution)/shard_map/local/pallas_call | solution.py:428
  31.1 0.0 collective-permute-done.3.rest_0_
  31.2 0.0 collective-permute-done.4.rest_1_
  31.2 0.0 collective-permute-done.6.rest_3_
  31.2 1.2 %combine.1 = (f32[64,32,128]{2,1,0:T(8,128)S(1)}, f32[2,2048]{1,0:T(2,128)S(1)}) custom-call(s32[1,128]{1,0:T(1,128)S(1)} %copy-done.1, f32[64,32,128]{2,1,0:T(8,128)S(1)} %local.1.local_ref, bf16[16,32,128]{2,1,0:T(8,128)(2,1)S(1)} %collective-permute-done.3.rest_0_, bf16[16,32,128]{2,1,0:T(8,128)(2,1)S(1)} %collective-permute-done.4.rest_1_, ...), custom_call_target="tpu_custom_call" | custom-call | tf_op jit(solution)/shard_map/combine/pallas_call | solution.py:446
  32.4 0.0 collective-permute-start.7
  32.4 1.6 %collective-permute-start.8 = (f32[2,2048]{1,0:T(2,128)S(1)}, f32[2,2048]{1,0:T(2,128)S(1)}, u32[]{:S(2)}, u32[]{:S(2)}) collective-permute-start(f32[2,2048]{1,0:T(2,128)S(1)} %get-tuple-element.31._after.s0), channel_id=1, source_target_pairs={{0,2},{1,3},{2,0},{3,1},{4,6},{5,7},{6,4},{7,5},{8,10},{9,11},{10,... | collective-permute-start | bytes 49160 | tf_op jit(solution)/shard_map/ppermute | solution.py:466
  34.0 0.3 collective-permute-start.9
  34.3 0.1 reshape_tile.3.gain_ref
  34.4 0.8 %own.1.own_ref = f32[64,32,128]{2,1,0:T(8,128)S(1)} custom-call(bf16[4096,256]{1,0:T(8,128)(2,1)S(1)} %get-tuple-element.30.f_ref, f32[2,2048]{1,0:T(2,128)S(1)} %get-tuple-element.31._after.s0), custom_call_target="tpu_custom_call" | custom-call | tf_op jit(solution)/shard_map/own/pallas_call | solution.py:457
  35.2 1.0 %collective-permute-done.8.s2 = f32[2,2048]{1,0:T(2,128)S(1)} collective-permute-done((f32[2,2048]{1,0:T(2,128)S(1)}, f32[2,2048]{1,0:T(2,128)S(1)}, u32[]{:S(2)}, u32[]{:S(2)}) %collective-permute-start.8) | collective-permute-done | bytes 16416 | tf_op jit(solution)/shard_map/ppermute | solution.py:466
  36.2 0.9 %collective-permute-done.9.s3 = f32[2,2048]{1,0:T(2,128)S(1)} collective-permute-done((f32[2,2048]{1,0:T(2,128)S(1)}, f32[2,2048]{1,0:T(2,128)S(1)}, u32[]{:S(2)}, u32[]{:S(2)}) %collective-permute-start.9) | collective-permute-done | bytes 16416 | tf_op jit(solution)/shard_map/ppermute | solution.py:466
  37.2 2.8 %norm.1 = (bf16[64,32,128]{2,1,0:T(8,128)(2,1)S(1)}, bf16[8,32,128]{2,1,0:T(8,128)(2,1)}) custom-call(f32[64,32,128]{2,1,0:T(8,128)S(1)} %get-tuple-element.29.conv_ref, f32[64,32,128]{2,1,0:T(8,128)S(1)} %own.1.own_ref, f32[1,128]{1,0:T(1,128)S(1)} %reshape_tile.3.gain_ref, bf16[32,256]{1,0:T(8,128)(2,1)S(1)} %copy-done, s32[1,8]{1,0:T(1,128)S(1)} %copy-done.3, ...), custom_call_target="tpu_custom_call" | custom-call | tf_op jit(solution)/shard_map/norm/pallas_call | solution.py:469
  40.0 7.7 %all-to-all-start = ((bf16[8,32,128]{2,1,0:T(8,128)(2,1)}), bf16[8,32,128]{2,1,0:T(8,128)(2,1)S(1)}, u32[]{:S(2)}, u32[]{:S(2)}) async-start(bf16[8,32,128]{2,1,0:T(8,128)(2,1)} %get-tuple-element.33), calls=%async_computation | async-start | bytes 131072 | tf_op jit(solution)/shard_map/all_to_all | solution.py:488
  47.7 1.3 %unpack.1 = bf16[64,64,64]{2,1,0:T(8,128)(2,1)} custom-call(bf16[64,32,128]{2,1,0:T(8,128)(2,1)S(1)} %get-tuple-element.32.whole_ref), custom_call_target="tpu_custom_call" | custom-call | tf_op jit(solution)/shard_map/unpack/pallas_call | solution.py:489
  49.0 5.6 %all-to-all-done.landed_ref = bf16[8,32,128]{2,1,0:T(8,128)(2,1)S(1)} async-done(((bf16[8,32,128]{2,1,0:T(8,128)(2,1)}), bf16[8,32,128]{2,1,0:T(8,128)(2,1)S(1)}, u32[]{:S(2)}, u32[]{:S(2)}) %all-to-all-start) | async-done | bytes 65568 | tf_op jit(solution)/shard_map/all_to_all | solution.py:488
  54.6 1.8 %place.1 = bf16[8,64,64]{2,1,0:T(8,128)(2,1)} custom-call(s32[1,8]{1,0:T(1,128)S(1)} %copy-done.2, bf16[8,32,128]{2,1,0:T(8,128)(2,1)S(1)} %all-to-all-done.landed_ref), custom_call_target="tpu_custom_call" | custom-call | tf_op jit(solution)/shard_map/place/pallas_call | solution.py:497
  (10 shorter events, 0.0 us)
Async XLA Ops:
  8.2 14.5 %collective-permute-start = (bf16[16,32,128]{2,1,0:T(8,128)(2,1)S(1)}, bf16[16,32,128]{2,1,0:T(8,128)(2,1)S(1)}, u32[]{:S(2)}, u32[]{:S(2)}) collective-permute-start(bf16[16,32,128]{2,1,0:T(8,128)(2,1)S(1)} %get-tuple-element.22), channel_id=1, source_target_pairs={{0,16},{16,0},{4,20},{20,4},{8,24},{24,8},{12,28},{28,12},{1,17},{... | collective-permute-start | bytes 393224 | tf_op jit(solution)/shard_map/ppermute | solution.py:417
  12.8 9.9 %collective-permute-start.1 = (bf16[16,32,128]{2,1,0:T(8,128)(2,1)S(1)}, bf16[16,32,128]{2,1,0:T(8,128)(2,1)S(1)}, u32[]{:S(2)}, u32[]{:S(2)}) collective-permute-start(bf16[16,32,128]{2,1,0:T(8,128)(2,1)S(1)} %get-tuple-element.23), channel_id=1, source_target_pairs={{4,16},{16,4},{0,8},{8,0},{12,20},{20,12},{24,28},{28,24},{5,17},{... | collective-permute-start | bytes 393224 | tf_op jit(solution)/shard_map/ppermute | solution.py:417
  14.5 11.5 %collective-permute-start.2 = (bf16[16,32,128]{2,1,0:T(8,128)(2,1)S(1)}, bf16[16,32,128]{2,1,0:T(8,128)(2,1)S(1)}, u32[]{:S(2)}, u32[]{:S(2)}) collective-permute-start(bf16[16,32,128]{2,1,0:T(8,128)(2,1)S(1)} %get-tuple-element.24), channel_id=1, source_target_pairs={{8,16},{16,8},{0,4},{4,0},{12,24},{24,12},{20,28},{28,20},{9,17},{... | collective-permute-start | bytes 393224 | tf_op jit(solution)/shard_map/ppermute | solution.py:417
  14.5 11.5 %copy-start.1 = (s32[1,128]{1,0:T(1,128)S(1)}, s32[1,128]{1,0:T(1,128)}, u32[]{:S(2)}) copy-start(s32[1,128]{1,0:T(1,128)} %list_ref.3) | copy-start | bytes 1540
  17.7 13.4 %collective-permute-start.3 = (bf16[16,32,128]{2,1,0:T(8,128)(2,1)S(1)}, bf16[16,32,128]{2,1,0:T(8,128)(2,1)S(1)}, u32[]{:S(2)}, u32[]{:S(2)}) collective-permute-start(bf16[16,32,128]{2,1,0:T(8,128)(2,1)S(1)} %get-tuple-element.25), channel_id=1, source_target_pairs={{8,20},{20,8},{0,4},{4,0},{12,16},{16,12},{24,28},{28,24},{9,21},{... | collective-permute-start | bytes 393224 | tf_op jit(solution)/shard_map/ppermute | solution.py:427
  19.2 11.9 %collective-permute-start.4 = (bf16[16,32,128]{2,1,0:T(8,128)(2,1)S(1)}, bf16[16,32,128]{2,1,0:T(8,128)(2,1)S(1)}, u32[]{:S(2)}, u32[]{:S(2)}) collective-permute-start(bf16[16,32,128]{2,1,0:T(8,128)(2,1)S(1)} %get-tuple-element.26), channel_id=1, source_target_pairs={{0,4},{4,0},{8,12},{12,8},{16,20},{20,16},{24,28},{28,24},{1,5},{5... | collective-permute-start | bytes 393224 | tf_op jit(solution)/shard_map/ppermute | solution.py:427
  22.7 8.4 %collective-permute-start.5 = (bf16[16,32,128]{2,1,0:T(8,128)(2,1)S(1)}, bf16[16,32,128]{2,1,0:T(8,128)(2,1)S(1)}, u32[]{:S(2)}, u32[]{:S(2)}) collective-permute-start(bf16[16,32,128]{2,1,0:T(8,128)(2,1)S(1)} %get-tuple-element.27), channel_id=1, source_target_pairs={{0,8},{8,0},{4,12},{12,4},{16,24},{24,16},{20,28},{28,20},{1,9},{9... | collective-permute-start | bytes 393224 | tf_op jit(solution)/shard_map/ppermute | solution.py:427
  22.7 11.6 %copy-start.4 = (bf16[64]{0:T(256)(128)(2,1)S(1)}, bf16[64]{0:T(256)(128)(2,1)}, u32[]{:S(2)}) copy-start(bf16[64]{0:T(256)(128)(2,1)} %param.10) | copy-start | bytes 388
  22.7 14.4 %copy-start = (bf16[32,256]{1,0:T(8,128)(2,1)S(1)}, bf16[32,256]{1,0:T(8,128)(2,1)}, u32[]{:S(2)}) copy-start(bf16[32,256]{1,0:T(8,128)(2,1)} %constant.2.clone.pool_ref) | copy-start | bytes 49156
  22.8 14.4 %copy-start.3 = (s32[1,8]{1,0:T(1,128)S(1)}, s32[1,8]{1,0:T(1,128)}, u32[]{:S(2)}) copy-start(s32[1,8]{1,0:T(1,128)} %slot_ref.1) | copy-start | bytes 100
  22.8 31.8 %copy-start.2 = (s32[1,8]{1,0:T(1,128)S(1)}, s32[1,8]{1,0:T(1,128)}, u32[]{:S(2)}) copy-start(s32[1,8]{1,0:T(1,128)} %place_ref.1) | copy-start | bytes 100
  22.8 8.4 %collective-permute-start.6 = (bf16[16,32,128]{2,1,0:T(8,128)(2,1)S(1)}, bf16[16,32,128]{2,1,0:T(8,128)(2,1)S(1)}, u32[]{:S(2)}, u32[]{:S(2)}) collective-permute-start(bf16[16,32,128]{2,1,0:T(8,128)(2,1)S(1)} %get-tuple-element.28), channel_id=1, source_target_pairs={{0,12},{12,0},{4,8},{8,4},{16,28},{28,16},{20,24},{24,20},{1,13},{... | collective-permute-start | bytes 393224 | tf_op jit(solution)/shard_map/ppermute | solution.py:427
  32.4 2.8 %collective-permute-start.7 = (f32[2,2048]{1,0:T(2,128)S(1)}, f32[2,2048]{1,0:T(2,128)S(1)}, u32[]{:S(2)}, u32[]{:S(2)}) collective-permute-start(f32[2,2048]{1,0:T(2,128)S(1)} %get-tuple-element.31._after.s0), channel_id=1, source_target_pairs={{0,1},{1,0},{2,3},{3,2},{4,5},{5,4},{6,7},{7,6},{8,9},{9,8},{10,11... | collective-permute-start | bytes 49160 | tf_op jit(solution)/shard_map/ppermute | solution.py:466
  32.4 3.8 %collective-permute-start.8 = (f32[2,2048]{1,0:T(2,128)S(1)}, f32[2,2048]{1,0:T(2,128)S(1)}, u32[]{:S(2)}, u32[]{:S(2)}) collective-permute-start(f32[2,2048]{1,0:T(2,128)S(1)} %get-tuple-element.31._after.s0), channel_id=1, source_target_pairs={{0,2},{1,3},{2,0},{3,1},{4,6},{5,7},{6,4},{7,5},{8,10},{9,11},{10,... | collective-permute-start | bytes 49160 | tf_op jit(solution)/shard_map/ppermute | solution.py:466
  34.0 3.2 %collective-permute-start.9 = (f32[2,2048]{1,0:T(2,128)S(1)}, f32[2,2048]{1,0:T(2,128)S(1)}, u32[]{:S(2)}, u32[]{:S(2)}) collective-permute-start(f32[2,2048]{1,0:T(2,128)S(1)} %get-tuple-element.31._after.s0), channel_id=1, source_target_pairs={{0,3},{1,2},{2,1},{3,0},{4,7},{5,6},{6,5},{7,4},{8,11},{9,10},{10,... | collective-permute-start | bytes 49160 | tf_op jit(solution)/shard_map/ppermute | solution.py:466
  40.0 14.6 %all-to-all-start = ((bf16[8,32,128]{2,1,0:T(8,128)(2,1)}), bf16[8,32,128]{2,1,0:T(8,128)(2,1)S(1)}, u32[]{:S(2)}, u32[]{:S(2)}) async-start(bf16[8,32,128]{2,1,0:T(8,128)(2,1)} %get-tuple-element.33), calls=%async_computation | async-start | bytes 131072 | tf_op jit(solution)/shard_map/all_to_all | solution.py:488

commit v7 on v6

--- a/solution.py
+++ b/solution.py
@@ -170,7 +170,7 @@
 def far_kernel(count, table, tile_count, rules_hbm, f_hbm, w_hbm, *rest):
     sends, rest = rest[:count], rest[count:]
     f_ref, y_refs, rest = rest[0], rest[1 : 1 + PARTS], rest[1 + PARTS :]
-    words_v, lists, acc_ref, w_ref, rules_ref, words_s, sems = rest
+    words_v, lists_v, acc_ref, w_ref, rules_ref, words_s, lists, sems = rest
     rows = tile_count * VOX
     span = rows + 2 * PAD
     rule_rows = rules_ref.shape[1]
@@ -236,13 +236,25 @@
     for c in range(3 * PARTS):
         for u in range(UNROLL):
             lists[c * wide + words_s[3, 128 * c] + u] = rule_rows
+    hand_on = pltpu.make_async_copy(lists, lists_v, sems.at[4])
+    hand_on.start()
     rules_add(words_s, lists, 0, y_refs, acc_ref)
     emit_sends(acc_ref, sends)
-
-
-def near_kernel(words, lists, *rest):
-    y_refs, sends, acc_ref = rest[:PARTS], rest[PARTS:-1], rest[-1]
+    hand_on.wait()
+
+
+def near_kernel(words_v, lists_v, *rest):
+    y_refs, sends = rest[:PARTS], rest[PARTS:-4]
+    acc_ref, words, lists, sems = rest[-4:]
+    copies = [
+        pltpu.make_async_copy(words_v, words, sems.at[0]),
+        pltpu.make_async_copy(lists_v, lists, sems.at[1]),
+    ]
+    for copy in copies:
+        copy.start()
     zero_blocks(acc_ref)
+    for copy in copies:
+        copy.wait()
     rules_add(words, lists, 1, y_refs, acc_ref)
     emit_sends(acc_ref, sends)
 
@@ -260,10 +272,17 @@
                 out_ref[t] = out_ref[t] + block[i].astype(F32)
 
 
-def local_kernel(table, words, lists, list_ref, *rest):
-    y_refs, blocks = rest[:PARTS], rest[PARTS:-2]
-    local_ref, acc_ref = rest[-2:]
+def local_kernel(words_v, lists_v, _after, *rest):
+    y_refs, (local_ref, acc_ref, words, lists, sems) = rest[:PARTS], rest[PARTS:]
+    copies = [
+        pltpu.make_async_copy(words_v, words, sems.at[0]),
+        pltpu.make_async_copy(lists_v, lists, sems.at[1]),
+    ]
+    for copy in copies:
+        copy.start()
     zero_blocks(acc_ref)
+    for copy in copies:
+        copy.wait()
     rules_add(words, lists, 2, y_refs, acc_ref)
 
     def keep(t, c):
@@ -271,7 +290,16 @@
         return c
 
     lax.fori_loop(0, acc_ref.shape[0], keep, 0, unroll=16)
-    add_arrivals(0, table, blocks, list_ref, local_ref)
+
+
+def arrive_kernel(first, table, list_v, local_ref, *rest):
+    blocks = rest[:-3]
+    out_ref, list_ref, sem = rest[-3:]
+    copy = pltpu.make_async_copy(list_v, list_ref, sem)
+    copy.start()
+    out_ref[...] = local_ref[...]
+    copy.wait()
+    add_arrivals(first, table, blocks, list_ref, out_ref)
 
 
 def own_kernel(f_ref, _after, own_ref):
@@ -291,11 +319,14 @@
     lax.fori_loop(0, own_ref.shape[0], pack, 0, unroll=8)
 
 
-def combine_kernel(first, table, list_ref, local_ref, *rest):
-    blocks = rest[:-2]
-    conv_ref, sums_ref = rest[-2:]
+def combine_kernel(first, table, list_v, local_ref, *rest):
+    blocks = rest[:-4]
+    conv_ref, sums_ref, list_ref, sem = rest[-4:]
+    copy = pltpu.make_async_copy(list_v, list_ref, sem)
+    copy.start()
     tile_count = local_ref.shape[0]
     conv_ref[...] = local_ref[...]
+    copy.wait()
     add_arrivals(first, table, blocks, list_ref, conv_ref)
     rows = tile_count * HALF
     pick = (lane_iota((2, 256)) // 64 % 2 == lax.broadcasted_iota(jnp.int32, (2, 256), 0)).astype(BF)
@@ -313,7 +344,9 @@
         )
 
 
-def norm_kernel(channels, conv_ref, own_ref, gain_ref, pool_ref, slot_ref, s0, s1, s2, s3, whole_ref, out_ref):
+def norm_kernel(channels, conv_ref, own_ref, gain_ref, pool_ref, slot_v, s0, s1, s2, s3, whole_ref, out_ref, slot_ref, sem):
+    copy = pltpu.make_async_copy(slot_v, slot_ref, sem)
+    copy.start()
     tile_count = conv_ref.shape[0]
     total = jnp.concatenate([s0[...], s1[...], s2[...], s3[...]], axis=0)
     parts = []
@@ -339,6 +372,8 @@
         whole = (own_ref[8 * k : 8 * k + 8].reshape(256, 128) + hidden).astype(BF)
         whole_ref[8 * k : 8 * k + 8] = whole.reshape(8, HALF, 128)
         pooled = jnp.dot(pool_ref[...], whole, preferred_element_type=F32)
+        if k == 0:
+            copy.wait()
         out_ref[slot_ref[0, k]] = pooled.astype(BF)
 
 
@@ -348,16 +383,17 @@
 
 
 def place_kernel(place_ref, landed_ref, out_ref):
-    parents = out_ref.shape[0]
-    for i in range(landed_ref.shape[0]):
-        where = place_ref[0, i]
-
-        @pl.when(where < parents)
-        def _(i=i, where=where):
-            for ox in range(2):
-                for px in range(2):
-                    row = 16 * (2 * ox + px)
-                    out_ref[where, row : row + 16, :] = landed_ref[i, 16 * ox : 16 * ox + 16, 64 * px : 64 * px + 64]
+    slots = landed_ref.shape[0]
+    where = [jnp.broadcast_to(place_ref[:, i : i + 1], (HALF, 128)) for i in range(slots)]
+    for p in range(out_ref.shape[0]):
+        block = landed_ref[0].astype(F32)
+        for i in range(1, slots):
+            block = jnp.where(where[i] == p, landed_ref[i].astype(F32), block)
+        block = block.astype(BF)
+        for ox in range(2):
+            for px in range(2):
+                row = 16 * (2 * ox + px)
+                out_ref[p, row : row + 16, :] = block[16 * ox : 16 * ox + 16, 64 * px : 64 * px + 64]
 
 
 def pool_matrix():
@@ -384,6 +420,8 @@
     slots = tile_count // 4
     span = tile_count * VOX + 2 * PAD
     wide = rule_rows + 128
+    lists_shape = ((3 * PARTS + 1) * wide,)
+    scalars = [pltpu.SMEM((8, wide), jnp.int32), pltpu.SMEM(lists_shape, jnp.int32)]
     flat = features.reshape(tile_count * VOX, channels)
     flat_weights = weights.transpose(0, 2, 1).reshape(offsets * quarter, channels)
     block = jax.ShapeDtypeStruct((slots, HALF, 128), BF)
@@ -399,15 +437,15 @@
         out_shape=[block] * count
         + [jax.ShapeDtypeStruct(flat.shape, BF), jax.ShapeDtypeStruct((PER_PART * span, 128), F32)]
         + [jax.ShapeDtypeStruct((PER_PART * span, 128), F32)] * (PARTS - 1)
-        + [jax.ShapeDtypeStruct((8, wide), jnp.int32), jax.ShapeDtypeStruct(((3 * PARTS + 1) * wide,), jnp.int32)],
+        + [jax.ShapeDtypeStruct((8, wide), jnp.int32), jax.ShapeDtypeStruct(lists_shape, jnp.int32)],
         in_specs=[HBM] * 3,
-        out_specs=[VM] * (count + 2 + PARTS) + [SM],
+        out_specs=[VM] * (count + 3 + PARTS),
         scratch_shapes=work
         + [
             pltpu.VMEM(flat_weights.shape, BF),
             pltpu.VMEM((4, rule_rows), jnp.int32),
-            pltpu.SMEM((8, wide), jnp.int32),
-            pltpu.SemaphoreType.DMA((4,)),
+            *scalars,
+            pltpu.SemaphoreType.DMA((5,)),
         ],
         name="far",
         **shared,
@@ -418,22 +456,31 @@
     near_sends = pl.pallas_call(
         near_kernel,
         out_shape=[block] * (len(routes) - count),
-        in_specs=[SM, SM] + [VM] * PARTS,
+        in_specs=[VM] * (2 + PARTS),
         out_specs=[VM] * (len(routes) - count),
-        scratch_shapes=work,
+        scratch_shapes=work + scalars + [pltpu.SemaphoreType.DMA((2,))],
         name="near",
         **shared,
     )(words, lists, *products)
     near_arrivals = [lax.ppermute(x, "tiles", route) for x, route in zip(near_sends, routes[count:])]
     local = pl.pallas_call(
-        functools.partial(local_kernel, table),
+        local_kernel,
         out_shape=whole,
-        in_specs=[SM] * 3 + [VM] * (PARTS + count),
+        in_specs=[VM, VM, ANY] + [VM] * PARTS,
         out_specs=VM,
-        scratch_shapes=work,
+        scratch_shapes=work + scalars + [pltpu.SemaphoreType.DMA((2,))],
         name="local",
         **shared,
-    )(words, lists, recv_list, *products, *arrivals)
+    )(words, lists, near_sends[0], *products)
+    local = pl.pallas_call(
+        functools.partial(arrive_kernel, 0, table),
+        out_shape=whole,
+        in_specs=[VM] * (2 + count),
+        out_specs=VM,
+        scratch_shapes=[pltpu.SMEM(recv_list.shape, jnp.int32), pltpu.SemaphoreType.DMA],
+        compiler_params=pltpu.CompilerParams(vmem_limit_bytes=12 * 1024 * 1024),
+        name="arrive",
+    )(recv_list, local, *arrivals)
     return count, table, held, local, near_arrivals
 
 
@@ -449,8 +496,9 @@
             jax.ShapeDtypeStruct((tile_count, HALF, 128), F32),
             jax.ShapeDtypeStruct((2, tile_count * HALF), F32),
         ],
-        in_specs=[SM] + [VM] * (1 + len(arrivals)),
+        in_specs=[VM] * (2 + len(arrivals)),
         out_specs=[VM, VM],
+        scratch_shapes=[pltpu.SMEM(recv_list.shape, jnp.int32), pltpu.SemaphoreType.DMA],
         compiler_params=small,
         name="combine",
     )(recv_list, local, *arrivals)
@@ -472,8 +520,9 @@
             jax.ShapeDtypeStruct((tile_count, HALF, 128), BF),
             jax.ShapeDtypeStruct((slot_count, HALF, 128), BF),
         ],
-        in_specs=[VM] * 4 + [SM] + [VM] * 4,
+        in_specs=[VM] * 9,
         out_specs=[VM, VM],
+        scratch_shapes=[pltpu.SMEM(coarse_send.shape, jnp.int32), pltpu.SemaphoreType.DMA],
         compiler_params=small,
         name="norm",
     )(
@@ -497,7 +546,7 @@
     coarse = pl.pallas_call(
         place_kernel,
         out_shape=jax.ShapeDtypeStruct((parent_count, VOX, quarter), BF),
-        in_specs=[SM, VM],
+        in_specs=[VM, VM],
         out_specs=VM,
         compiler_params=small,
         name="place",

time: 56.6 us -> 54.8 us (0.968)
  Pallas kernels: 23.8 us -> 21.4 us
    pallas_call x1, Pallas kernels: 1.76 us -> 0.84 us  [body(): pl.pallas_call(place_kernel, out_shape=jax.ShapeDtypeStruct((parent_count...]
    all_to_all x1, starting transfers between devices: 7.68 us -> 6.82 us  [body(): lax.all_to_all(outbound, 'tiles', split_axis=0, concat_axis=0, tiled=True)]
    pallas_call x1 -> x2, Pallas kernels: 5.08 us -> 4.47 us  [the longest x1 3.82 us: call_rules(): pl.pallas_call(local_kernel, out_shape=whole, in_specs=[VM, VM, ANY] + [V...]
    ppermute x7, starting transfers between devices: 11.7 us -> 12.3 us  [call_rules(): lax.ppermute(x, 'tiles', route)]
  transfers between devices with their start and end apart: 11 -> 11, of which waited for: 4 -> 4; matrix products, arithmetic and copies ran while one was open for 0% -> 0% of each run, Pallas kernels for 18% -> 17%
where the time goes in v7:
time: 54.8 us; the launch traced here: 54.3 us
  Pallas kernels  21.4 us (39%)
  starting transfers between devices  21 us (38%)
  waiting for transfers between devices  10.9 us (20%)
  between operations  0.8 us (1%)
    ppermute x7, starting transfers between devices, call_rules(): lax.ppermute(x, 'tiles', route)  12.3 us
    pallas_call x1, Pallas kernels, call_rules(): pl.pallas_call(functools.partial(far_kernel, count, table, tile_count), o...  7.47 us
    all_to_all x1, starting transfers between devices, body(): lax.all_to_all(outbound, 'tiles', split_axis=0, concat_axis=0, tiled=True)  6.82 us
    all_to_all x1, waiting for transfers between devices, body(): lax.all_to_all(outbound, 'tiles', split_axis=0, concat_axis=0, tiled=True)  5.6 us
    pallas_call x1, Pallas kernels, call_rules(): pl.pallas_call(local_kernel, out_shape=whole, in_specs=[VM, VM, ANY] + [V...  3.82 us
    ppermute x7, waiting for transfers between devices, call_rules(): lax.ppermute(x, 'tiles', route)  3.37 us
    pallas_call x1, Pallas kernels, call_rules(): pl.pallas_call(near_kernel, out_shape=[block] * (len(routes) - count), in...  2.66 us
    pallas_call x1, Pallas kernels, body(): pl.pallas_call(functools.partial(norm_kernel, channels), out_shape=[jax.S...  2.64 us
  transfers between devices with their start and end apart: 11, of which 4 were waited for; matrix products, arithmetic and copies ran while one was open for 0% of the time, Pallas kernels for 17%

profile of v7, /device:TPU:0, one launch (start us, length us, event | category | flops | bytes accessed | tf_op | source)
XLA Modules:
  0.0 54.3 jit_solution(1759963391245869458)
XLA Ops:
  0.6 7.5 %far.1 = (bf16[16,32,128]{2,1,0:T(8,128)(2,1)S(1)}, bf16[16,32,128]{2,1,0:T(8,128)(2,1)S(1)}, bf16[16,32,128]{2,1,0:T(8,128)(2,1)S(1)}, bf16[4096,256]{1,0:T(8,1...) custom-call(s32[4,768]{1,0:T(4,128)} %bitcast.7, ...), custom_call_target="tpu_custom_call" | custom-call | flops 3623878656 | bytes 8388608 | tf_op jit(solution)/shard_map/far/pallas_call | solution.py:435
  8.1 5.0 %collective-permute-start = (bf16[16,32,128]{2,1,0:T(8,128)(2,1)S(1)}, bf16[16,32,128]{2,1,0:T(8,128)(2,1)S(1)}, u32[]{:S(2)}, u32[]{:S(2)}) collective-permute-start(bf16[16,32,128]{2,1,0:T(8,128)(2,1)S(1)} %get-tuple-element.23), channel_id=1, source_target_pairs={{0,16},{16,0},{4,20},{20,4},{8,24},{24,8},{12,28},{28,12},{1,17},{... | collective-permute-start | bytes 393224 | tf_op jit(solution)/shard_map/ppermute | solution.py:455
  13.1 1.0 %collective-permute-start.1 = (bf16[16,32,128]{2,1,0:T(8,128)(2,1)S(1)}, bf16[16,32,128]{2,1,0:T(8,128)(2,1)S(1)}, u32[]{:S(2)}, u32[]{:S(2)}) collective-permute-start(bf16[16,32,128]{2,1,0:T(8,128)(2,1)S(1)} %get-tuple-element.24), channel_id=1, source_target_pairs={{4,16},{16,4},{0,8},{8,0},{12,20},{20,12},{24,28},{28,24},{5,17},{... | collective-permute-start | bytes 393224 | tf_op jit(solution)/shard_map/ppermute | solution.py:455
  14.2 0.5 collective-permute-start.2
  14.7 2.7 %near.1 = (bf16[16,32,128]{2,1,0:T(8,128)(2,1)S(1)}, bf16[16,32,128]{2,1,0:T(8,128)(2,1)S(1)}, bf16[16,32,128]{2,1,0:T(8,128)(2,1)S(1)}, bf16[16,32,128]{2,1,0:T(8,128)(2,1)S(1)}) custom-call(s32[8,896]{1,0:T(8,128)S(1)} %get-tuple-element.18.words_v, s32[6272]{0:T(1024)S(1)} %get-tuple-element.19.lists_v, f32[29568,128]{1,0:T(8,128)S(1)} %get-tuple-element.20.rest_0_, ...), custom_call_target="tpu_custom_call" | custom-call | flops 3623878656 | bytes 8388608 | tf_op jit(solution)/shard_map/near/pallas_call | solution.py:456
  17.3 1.7 %collective-permute-start.3 = (bf16[16,32,128]{2,1,0:T(8,128)(2,1)S(1)}, bf16[16,32,128]{2,1,0:T(8,128)(2,1)S(1)}, u32[]{:S(2)}, u32[]{:S(2)}) collective-permute-start(bf16[16,32,128]{2,1,0:T(8,128)(2,1)S(1)} %get-tuple-element.22._after), channel_id=1, source_target_pairs={{8,20},{20,8},{0,4},{4,0},{12,16},{16,12},{24,28},{28,24},{9,21},{... | collective-permute-start | bytes 393224 | tf_op jit(solution)/shard_map/ppermute | solution.py:465
  19.1 0.4 collective-permute-start.4
  19.4 3.4 %collective-permute-done.rest_0_ = bf16[16,32,128]{2,1,0:T(8,128)(2,1)S(1)} collective-permute-done((bf16[16,32,128]{2,1,0:T(8,128)(2,1)S(1)}, bf16[16,32,128]{2,1,0:T(8,128)(2,1)S(1)}, u32[]{:S(2)}, u32[]{:S(2)}) %collective-permute-start) | collective-permute-done | bytes 131104 | tf_op jit(solution)/shard_map/ppermute | solution.py:455
  22.8 0.0 collective-permute-done.1.rest_1_
  22.8 0.0 copy-start.4
  22.8 0.0 copy-start
  22.8 0.0 copy-start.3
  22.8 0.0 copy-start.2
  22.9 3.6 %collective-permute-start.6 = (bf16[16,32,128]{2,1,0:T(8,128)(2,1)S(1)}, bf16[16,32,128]{2,1,0:T(8,128)(2,1)S(1)}, u32[]{:S(2)}, u32[]{:S(2)}) collective-permute-start(bf16[16,32,128]{2,1,0:T(8,128)(2,1)S(1)} %get-tuple-element.28), channel_id=1, source_target_pairs={{0,12},{12,0},{4,8},{8,4},{16,28},{28,16},{20,24},{24,20},{1,13},{... | collective-permute-start | bytes 393224 | tf_op jit(solution)/shard_map/ppermute | solution.py:465
  26.5 3.8 %local.1.local_ref = f32[64,32,128]{2,1,0:T(8,128)S(1)} custom-call(s32[8,896]{1,0:T(8,128)S(1)} %get-tuple-element.18.words_v, s32[6272]{0:T(1024)S(1)} %get-tuple-element.19.lists_v, bf16[16,32,128]{2,1,0:T(8,128)(2,1)S(1)} %get-tuple-element.22._after, f32[29568,128]{1,0:T(8,128)S(1)} %get-tuple-element.20.rest_0_, f32[29568,128]{1,0:T(8,128)S(1)} %get-tuple-element.21.rest_1_), custom_call_target="tpu_custom_call" | custom-call | flops 3623878656 | bytes 8388608 | tf_op jit(solution)/shard_map/local/pallas_call | solution.py:466
  30.3 0.0 collective-permute-done.2.rest_2_
  30.3 0.7 %arrive.1.local_ref = f32[64,32,128]{2,1,0:T(8,128)S(1)} custom-call(s32[1,128]{1,0:T(1,128)S(1)} %copy-done.1, f32[64,32,128]{2,1,0:T(8,128)S(1)} %local.1.local_ref, bf16[16,32,128]{2,1,0:T(8,128)(2,1)S(1)} %collective-permute-done.rest_0_, bf16[16,32,128]{2,1,0:T(8,128)(2,1)S(1)} %collective-permute-done.1.rest_1_, ...), custom_call_target="tpu_custom_call" | custom-call | tf_op jit(solution)/shard_map/arrive/pallas_call | solution.py:475
  31.0 0.0 collective-permute-done.3.rest_0_
  31.0 0.0 collective-permute-done.5.rest_2_
  31.0 1.2 %combine.1 = (f32[64,32,128]{2,1,0:T(8,128)S(1)}, f32[2,2048]{1,0:T(2,128)S(1)}) custom-call(s32[1,128]{1,0:T(1,128)S(1)} %copy-done.1, f32[64,32,128]{2,1,0:T(8,128)S(1)} %arrive.1.local_ref, bf16[16,32,128]{2,1,0:T(8,128)(2,1)S(1)} %collective-permute-done.3.rest_0_, bf16[16,32,128]{2,1,0:T(8,128)(2,1)S(1)} %collective-permute-done.4.rest_1_, ...), custom_call_target="tpu_custom_call" | custom-call | tf_op jit(solution)/shard_map/combine/pallas_call | solution.py:493
  32.2 0.1 collective-permute-start.7
  32.3 1.6 %collective-permute-start.8 = (f32[2,2048]{1,0:T(2,128)S(1)}, f32[2,2048]{1,0:T(2,128)S(1)}, u32[]{:S(2)}, u32[]{:S(2)}) collective-permute-start(f32[2,2048]{1,0:T(2,128)S(1)} %get-tuple-element.31._after.s0), channel_id=1, source_target_pairs={{0,2},{1,3},{2,0},{3,1},{4,6},{5,7},{6,4},{7,5},{8,10},{9,11},{10,... | collective-permute-start | bytes 49160 | tf_op jit(solution)/shard_map/ppermute | solution.py:514
  33.9 0.3 collective-permute-start.9
  34.2 0.1 reshape_tile.3.gain_ref
  34.3 0.8 %own.1.own_ref = f32[64,32,128]{2,1,0:T(8,128)S(1)} custom-call(bf16[4096,256]{1,0:T(8,128)(2,1)S(1)} %get-tuple-element.30.f_ref, f32[2,2048]{1,0:T(2,128)S(1)} %get-tuple-element.31._after.s0), custom_call_target="tpu_custom_call" | custom-call | tf_op jit(solution)/shard_map/own/pallas_call | solution.py:505
  35.1 1.0 %collective-permute-done.8.s2 = f32[2,2048]{1,0:T(2,128)S(1)} collective-permute-done((f32[2,2048]{1,0:T(2,128)S(1)}, f32[2,2048]{1,0:T(2,128)S(1)}, u32[]{:S(2)}, u32[]{:S(2)}) %collective-permute-start.8) | collective-permute-done | bytes 16416 | tf_op jit(solution)/shard_map/ppermute | solution.py:514
  36.1 0.9 %collective-permute-done.9.s3 = f32[2,2048]{1,0:T(2,128)S(1)} collective-permute-done((f32[2,2048]{1,0:T(2,128)S(1)}, f32[2,2048]{1,0:T(2,128)S(1)}, u32[]{:S(2)}, u32[]{:S(2)}) %collective-permute-start.9) | collective-permute-done | bytes 16416 | tf_op jit(solution)/shard_map/ppermute | solution.py:514
  37.0 2.6 %norm.1 = (bf16[64,32,128]{2,1,0:T(8,128)(2,1)S(1)}, bf16[8,32,128]{2,1,0:T(8,128)(2,1)}) custom-call(f32[64,32,128]{2,1,0:T(8,128)S(1)} %get-tuple-element.29.conv_ref, f32[64,32,128]{2,1,0:T(8,128)S(1)} %own.1.own_ref, f32[1,128]{1,0:T(1,128)S(1)} %reshape_tile.3.gain_ref, bf16[32,256]{1,0:T(8,128)(2,1)S(1)} %copy-done, s32[1,8]{1,0:T(1,128)S(1)} %copy-done.3, ...), custom_call_target="tpu_custom_call" | custom-call | tf_op jit(solution)/shard_map/norm/pallas_call | solution.py:517
  39.7 6.8 %all-to-all-start = ((bf16[8,32,128]{2,1,0:T(8,128)(2,1)}), bf16[8,32,128]{2,1,0:T(8,128)(2,1)S(1)}, u32[]{:S(2)}, u32[]{:S(2)}) async-start(bf16[8,32,128]{2,1,0:T(8,128)(2,1)} %get-tuple-element.33), calls=%async_computation | async-start | bytes 131072 | tf_op jit(solution)/shard_map/all_to_all | solution.py:537
  46.5 1.3 %unpack.1 = bf16[64,64,64]{2,1,0:T(8,128)(2,1)} custom-call(bf16[64,32,128]{2,1,0:T(8,128)(2,1)S(1)} %get-tuple-element.32.whole_ref), custom_call_target="tpu_custom_call" | custom-call | tf_op jit(solution)/shard_map/unpack/pallas_call | solution.py:538
  47.8 5.6 %all-to-all-done.landed_ref = bf16[8,32,128]{2,1,0:T(8,128)(2,1)S(1)} async-done(((bf16[8,32,128]{2,1,0:T(8,128)(2,1)}), bf16[8,32,128]{2,1,0:T(8,128)(2,1)S(1)}, u32[]{:S(2)}, u32[]{:S(2)}) %all-to-all-start) | async-done | bytes 65568 | tf_op jit(solution)/shard_map/all_to_all | solution.py:537
  53.4 0.8 %place.1 = bf16[8,64,64]{2,1,0:T(8,128)(2,1)} custom-call(s32[1,8]{1,0:T(1,128)S(1)} %copy-done.2, bf16[8,32,128]{2,1,0:T(8,128)(2,1)S(1)} %all-to-all-done.landed_ref), custom_call_target="tpu_custom_call" | custom-call | tf_op jit(solution)/shard_map/place/pallas_call | solution.py:546
  (11 shorter events, 0.0 us)
Async XLA Ops:
  8.1 14.7 %collective-permute-start = (bf16[16,32,128]{2,1,0:T(8,128)(2,1)S(1)}, bf16[16,32,128]{2,1,0:T(8,128)(2,1)S(1)}, u32[]{:S(2)}, u32[]{:S(2)}) collective-permute-start(bf16[16,32,128]{2,1,0:T(8,128)(2,1)S(1)} %get-tuple-element.23), channel_id=1, source_target_pairs={{0,16},{16,0},{4,20},{20,4},{8,24},{24,8},{12,28},{28,12},{1,17},{... | collective-permute-start | bytes 393224 | tf_op jit(solution)/shard_map/ppermute | solution.py:455
  13.1 9.7 %collective-permute-start.1 = (bf16[16,32,128]{2,1,0:T(8,128)(2,1)S(1)}, bf16[16,32,128]{2,1,0:T(8,128)(2,1)S(1)}, u32[]{:S(2)}, u32[]{:S(2)}) collective-permute-start(bf16[16,32,128]{2,1,0:T(8,128)(2,1)S(1)} %get-tuple-element.24), channel_id=1, source_target_pairs={{4,16},{16,4},{0,8},{8,0},{12,20},{20,12},{24,28},{28,24},{5,17},{... | collective-permute-start | bytes 393224 | tf_op jit(solution)/shard_map/ppermute | solution.py:455
  14.2 16.1 %collective-permute-start.2 = (bf16[16,32,128]{2,1,0:T(8,128)(2,1)S(1)}, bf16[16,32,128]{2,1,0:T(8,128)(2,1)S(1)}, u32[]{:S(2)}, u32[]{:S(2)}) collective-permute-start(bf16[16,32,128]{2,1,0:T(8,128)(2,1)S(1)} %get-tuple-element.25), channel_id=1, source_target_pairs={{8,16},{16,8},{0,4},{4,0},{12,24},{24,12},{20,28},{28,20},{9,17},{... | collective-permute-start | bytes 393224 | tf_op jit(solution)/shard_map/ppermute | solution.py:455
  17.3 13.6 %collective-permute-start.3 = (bf16[16,32,128]{2,1,0:T(8,128)(2,1)S(1)}, bf16[16,32,128]{2,1,0:T(8,128)(2,1)S(1)}, u32[]{:S(2)}, u32[]{:S(2)}) collective-permute-start(bf16[16,32,128]{2,1,0:T(8,128)(2,1)S(1)} %get-tuple-element.22._after), channel_id=1, source_target_pairs={{8,20},{20,8},{0,4},{4,0},{12,16},{16,12},{24,28},{28,24},{9,21},{... | collective-permute-start | bytes 393224 | tf_op jit(solution)/shard_map/ppermute | solution.py:465
  19.1 11.9 %collective-permute-start.4 = (bf16[16,32,128]{2,1,0:T(8,128)(2,1)S(1)}, bf16[16,32,128]{2,1,0:T(8,128)(2,1)S(1)}, u32[]{:S(2)}, u32[]{:S(2)}) collective-permute-start(bf16[16,32,128]{2,1,0:T(8,128)(2,1)S(1)} %get-tuple-element.26), channel_id=1, source_target_pairs={{0,4},{4,0},{8,12},{12,8},{16,20},{20,16},{24,28},{28,24},{1,5},{5... | collective-permute-start | bytes 393224 | tf_op jit(solution)/shard_map/ppermute | solution.py:465
  22.8 8.2 %collective-permute-start.5 = (bf16[16,32,128]{2,1,0:T(8,128)(2,1)S(1)}, bf16[16,32,128]{2,1,0:T(8,128)(2,1)S(1)}, u32[]{:S(2)}, u32[]{:S(2)}) collective-permute-start(bf16[16,32,128]{2,1,0:T(8,128)(2,1)S(1)} %get-tuple-element.27), channel_id=1, source_target_pairs={{0,8},{8,0},{4,12},{12,4},{16,24},{24,16},{20,28},{28,20},{1,9},{9... | collective-permute-start | bytes 393224 | tf_op jit(solution)/shard_map/ppermute | solution.py:465
  22.8 7.5 %copy-start.1 = (s32[1,128]{1,0:T(1,128)S(1)}, s32[1,128]{1,0:T(1,128)}, u32[]{:S(2)}) copy-start(s32[1,128]{1,0:T(1,128)} %list_v.3) | copy-start | bytes 1540
  22.8 11.4 %copy-start.4 = (bf16[64]{0:T(256)(128)(2,1)S(1)}, bf16[64]{0:T(256)(128)(2,1)}, u32[]{:S(2)}) copy-start(bf16[64]{0:T(256)(128)(2,1)} %param.10) | copy-start | bytes 388
  22.8 14.2 %copy-start = (bf16[32,256]{1,0:T(8,128)(2,1)S(1)}, bf16[32,256]{1,0:T(8,128)(2,1)}, u32[]{:S(2)}) copy-start(bf16[32,256]{1,0:T(8,128)(2,1)} %constant.2.clone.pool_ref) | copy-start | bytes 49156
  22.8 14.2 %copy-start.3 = (s32[1,8]{1,0:T(1,128)S(1)}, s32[1,8]{1,0:T(1,128)}, u32[]{:S(2)}) copy-start(s32[1,8]{1,0:T(1,128)} %slot_v.1) | copy-start | bytes 100
  22.8 30.6 %copy-start.2 = (s32[1,8]{1,0:T(1,128)S(1)}, s32[1,8]{1,0:T(1,128)}, u32[]{:S(2)}) copy-start(s32[1,8]{1,0:T(1,128)} %place_ref.1) | copy-start | bytes 100
  22.9 8.2 %collective-permute-start.6 = (bf16[16,32,128]{2,1,0:T(8,128)(2,1)S(1)}, bf16[16,32,128]{2,1,0:T(8,128)(2,1)S(1)}, u32[]{:S(2)}, u32[]{:S(2)}) collective-permute-start(bf16[16,32,128]{2,1,0:T(8,128)(2,1)S(1)} %get-tuple-element.28), channel_id=1, source_target_pairs={{0,12},{12,0},{4,8},{8,4},{16,28},{28,16},{20,24},{24,20},{1,13},{... | collective-permute-start | bytes 393224 | tf_op jit(solution)/shard_map/ppermute | solution.py:465
  32.2 2.9 %collective-permute-start.7 = (f32[2,2048]{1,0:T(2,128)S(1)}, f32[2,2048]{1,0:T(2,128)S(1)}, u32[]{:S(2)}, u32[]{:S(2)}) collective-permute-start(f32[2,2048]{1,0:T(2,128)S(1)} %get-tuple-element.31._after.s0), channel_id=1, source_target_pairs={{0,1},{1,0},{2,3},{3,2},{4,5},{5,4},{6,7},{7,6},{8,9},{9,8},{10,11... | collective-permute-start | bytes 49160 | tf_op jit(solution)/shard_map/ppermute | solution.py:514
  32.3 3.8 %collective-permute-start.8 = (f32[2,2048]{1,0:T(2,128)S(1)}, f32[2,2048]{1,0:T(2,128)S(1)}, u32[]{:S(2)}, u32[]{:S(2)}) collective-permute-start(f32[2,2048]{1,0:T(2,128)S(1)} %get-tuple-element.31._after.s0), channel_id=1, source_target_pairs={{0,2},{1,3},{2,0},{3,1},{4,6},{5,7},{6,4},{7,5},{8,10},{9,11},{10,... | collective-permute-start | bytes 49160 | tf_op jit(solution)/shard_map/ppermute | solution.py:514
  33.9 3.2 %collective-permute-start.9 = (f32[2,2048]{1,0:T(2,128)S(1)}, f32[2,2048]{1,0:T(2,128)S(1)}, u32[]{:S(2)}, u32[]{:S(2)}) collective-permute-start(f32[2,2048]{1,0:T(2,128)S(1)} %get-tuple-element.31._after.s0), channel_id=1, source_target_pairs={{0,3},{1,2},{2,1},{3,0},{4,7},{5,6},{6,5},{7,4},{8,11},{9,10},{10,... | collective-permute-start | bytes 49160 | tf_op jit(solution)/shard_map/ppermute | solution.py:514
  39.7 13.7 %all-to-all-start = ((bf16[8,32,128]{2,1,0:T(8,128)(2,1)}), bf16[8,32,128]{2,1,0:T(8,128)(2,1)S(1)}, u32[]{:S(2)}, u32[]{:S(2)}) async-start(bf16[8,32,128]{2,1,0:T(8,128)(2,1)} %get-tuple-element.33), calls=%async_computation | async-start | bytes 131072 | tf_op jit(solution)/shard_map/all_to_all | solution.py:537

commit v8 on v7

--- a/solution.py
+++ b/solution.py
@@ -18,6 +18,7 @@
 UNROLL = 8
 PARTS = 2
 PER_PART = 7
+ORDER = (0, 4, 5, 1, 2, 6, 3)
 
 
 def perfect(n):
@@ -56,6 +57,8 @@
 
 def matchings(n):
     found = perfect(n) if n == 2 * REACH else None
+    if found is not None:
+        found = [found[i] for i in ORDER]
     if found is None:
         found = []
         for d in range(REACH, 0, -1):
@@ -348,33 +351,32 @@
     copy = pltpu.make_async_copy(slot_v, slot_ref, sem)
     copy.start()
     tile_count = conv_ref.shape[0]
-    total = jnp.concatenate([s0[...], s1[...], s2[...], s3[...]], axis=0)
+    total = (s0[...] + s1[...]) + (s2[...] + s3[...])
+    rest = lax.rsqrt(total * (1.0 / channels) + EPS)
     parts = []
     for _ in range(3):
-        top = total.astype(BF)
-        parts.append(top.astype(F32))
-        total = total - top.astype(F32)
+        top = rest.astype(BF).astype(F32)
+        parts.append(top)
+        rest = rest - top
     parts = jnp.concatenate(parts, axis=0).astype(BF)
     count = parts.shape[0]
     spread = (lane_iota((count, 128)) // 64 == lax.broadcasted_iota(jnp.int32, (count, 128), 0) % 2).astype(BF)
-    gain = gain_ref[...]
+    gain = 0.5 * gain_ref[...]
     for k in range(tile_count // 8):
-        mean_square = lax.dot_general(
+        part = lax.dot_general(
             parts[:, k * 256 : (k + 1) * 256],
             spread,
             (((0,), (0,)), ((), ())),
             preferred_element_type=F32,
-        ) * (1.0 / channels)
-        value = conv_ref[8 * k : 8 * k + 8].reshape(256, 128)
-        v = gain * value * lax.rsqrt(mean_square + EPS)
-        half = 0.5 * v
+        )
+        half = gain * conv_ref[8 * k : 8 * k + 8].reshape(256, 128) * part
         hidden = half + half * jnp.tanh(half)
         whole = (own_ref[8 * k : 8 * k + 8].reshape(256, 128) + hidden).astype(BF)
         whole_ref[8 * k : 8 * k + 8] = whole.reshape(8, HALF, 128)
-        pooled = jnp.dot(pool_ref[...], whole, preferred_element_type=F32)
-        if k == 0:
-            copy.wait()
-        out_ref[slot_ref[0, k]] = pooled.astype(BF)
+    copy.wait()
+    for k in range(tile_count // 8):
+        whole = whole_ref[8 * k : 8 * k + 8].reshape(256, 128)
+        out_ref[slot_ref[0, k]] = jnp.dot(pool_ref[...], whole, preferred_element_type=F32).astype(BF)
 
 
 def unpack_kernel(whole_ref, skip_ref):

time: 54.8 us -> 50.8 us (0.927)
  starting transfers between devices: 21 us -> 19.3 us
  Pallas kernels: 21.4 us -> 20.1 us
  waiting for transfers between devices: 10.9 us -> 10.2 us
    all_to_all x1, starting transfers between devices: 6.82 us -> 4.34 us  [body(): lax.all_to_all(outbound, 'tiles', split_axis=0, concat_axis=0, tiled=True)]
    pallas_call x1, Pallas kernels: 2.64 us -> 1.39 us  [body(): pl.pallas_call(functools.partial(norm_kernel, channels), out_shape=[jax.S...]
    ppermute x7, starting transfers between devices: 12.3 us -> 13.1 us  [call_rules(): lax.ppermute(x, 'tiles', route)]
    ppermute x7, waiting for transfers between devices: 3.37 us -> 2.62 us  [call_rules(): lax.ppermute(x, 'tiles', route)]
  transfers between devices with their start and end apart: 11 -> 11, of which waited for: 4 -> 5; matrix products, arithmetic and copies ran while one was open for 0% -> 0% of each run, Pallas kernels for 17% -> 18%
where the time goes in v8:
time: 50.8 us; the launch traced here: 50.5 us
  Pallas kernels  20.1 us (40%)
  starting transfers between devices  19.3 us (38%)
  waiting for transfers between devices  10.2 us (20%)
  between operations  0.76 us (1%)
    ppermute x7, starting transfers between devices, call_rules(): lax.ppermute(x, 'tiles', route)  13.1 us
    pallas_call x1, Pallas kernels, call_rules(): pl.pallas_call(functools.partial(far_kernel, count, table, tile_count), o...  7.67 us
    all_to_all x1, waiting for transfers between devices, body(): lax.all_to_all(outbound, 'tiles', split_axis=0, concat_axis=0, tiled=True)  5.6 us
    all_to_all x1, starting transfers between devices, body(): lax.all_to_all(outbound, 'tiles', split_axis=0, concat_axis=0, tiled=True)  4.34 us
    pallas_call x1, Pallas kernels, call_rules(): pl.pallas_call(local_kernel, out_shape=whole, in_specs=[VM, VM, ANY] + [V...  3.93 us
    ppermute x7, waiting for transfers between devices, call_rules(): lax.ppermute(x, 'tiles', route)  2.62 us
    pallas_call x1, Pallas kernels, call_rules(): pl.pallas_call(near_kernel, out_shape=[block] * (len(routes) - count), in...  2.3 us
    ppermute x3, waiting for transfers between devices, body(): lax.ppermute(sums, 'chan', [(i, i ^ m) for i in range(wide)])  1.94 us
  transfers between devices with their start and end apart: 11, of which 5 were waited for; matrix products, arithmetic and copies ran while one was open for 0% of the time, Pallas kernels for 18%

profile of v8, /device:TPU:0, one launch (start us, length us, event | category | flops | bytes accessed | tf_op | source)
XLA Modules:
  0.0 50.5 jit_solution(17309924586562386872)
XLA Ops:
  0.6 7.7 %far.1 = (bf16[16,32,128]{2,1,0:T(8,128)(2,1)S(1)}, bf16[16,32,128]{2,1,0:T(8,128)(2,1)S(1)}, bf16[16,32,128]{2,1,0:T(8,128)(2,1)S(1)}, bf16[4096,256]{1,0:T(8,1...) custom-call(s32[4,768]{1,0:T(4,128)} %bitcast.7, ...), custom_call_target="tpu_custom_call" | custom-call | flops 3623878656 | bytes 8388608 | tf_op jit(solution)/shard_map/far/pallas_call | solution.py:437
  8.3 4.1 %collective-permute-start = (bf16[16,32,128]{2,1,0:T(8,128)(2,1)S(1)}, bf16[16,32,128]{2,1,0:T(8,128)(2,1)S(1)}, u32[]{:S(2)}, u32[]{:S(2)}) collective-permute-start(bf16[16,32,128]{2,1,0:T(8,128)(2,1)S(1)} %get-tuple-element.23), channel_id=1, source_target_pairs={{0,16},{16,0},{4,20},{20,4},{8,24},{24,8},{12,28},{28,12},{1,17},{... | collective-permute-start | bytes 393224 | tf_op jit(solution)/shard_map/ppermute | solution.py:457
  12.4 2.1 %collective-permute-start.1 = (bf16[16,32,128]{2,1,0:T(8,128)(2,1)S(1)}, bf16[16,32,128]{2,1,0:T(8,128)(2,1)S(1)}, u32[]{:S(2)}, u32[]{:S(2)}) collective-permute-start(bf16[16,32,128]{2,1,0:T(8,128)(2,1)S(1)} %get-tuple-element.24), channel_id=1, source_target_pairs={{0,4},{4,0},{8,12},{12,8},{16,20},{20,16},{24,28},{28,24},{1,5},{5... | collective-permute-start | bytes 393224 | tf_op jit(solution)/shard_map/ppermute | solution.py:457
  14.6 1.2 %collective-permute-start.2 = (bf16[16,32,128]{2,1,0:T(8,128)(2,1)S(1)}, bf16[16,32,128]{2,1,0:T(8,128)(2,1)S(1)}, u32[]{:S(2)}, u32[]{:S(2)}) collective-permute-start(bf16[16,32,128]{2,1,0:T(8,128)(2,1)S(1)} %get-tuple-element.25), channel_id=1, source_target_pairs={{0,8},{8,0},{4,12},{12,4},{16,24},{24,16},{20,28},{28,20},{1,9},{9... | collective-permute-start | bytes 393224 | tf_op jit(solution)/shard_map/ppermute | solution.py:457
  15.8 2.3 %near.1 = (bf16[16,32,128]{2,1,0:T(8,128)(2,1)S(1)}, bf16[16,32,128]{2,1,0:T(8,128)(2,1)S(1)}, bf16[16,32,128]{2,1,0:T(8,128)(2,1)S(1)}, bf16[16,32,128]{2,1,0:T(8,128)(2,1)S(1)}) custom-call(s32[8,896]{1,0:T(8,128)S(1)} %get-tuple-element.18.words_v, s32[6272]{0:T(1024)S(1)} %get-tuple-element.19.lists_v, f32[29568,128]{1,0:T(8,128)S(1)} %get-tuple-element.20.rest_0_, ...), custom_call_target="tpu_custom_call" | custom-call | flops 3623878656 | bytes 8388608 | tf_op jit(solution)/shard_map/near/pallas_call | solution.py:458
  18.1 2.0 %collective-permute-start.3 = (bf16[16,32,128]{2,1,0:T(8,128)(2,1)S(1)}, bf16[16,32,128]{2,1,0:T(8,128)(2,1)S(1)}, u32[]{:S(2)}, u32[]{:S(2)}) collective-permute-start(bf16[16,32,128]{2,1,0:T(8,128)(2,1)S(1)} %get-tuple-element.22._after), channel_id=1, source_target_pairs={{4,16},{16,4},{0,8},{8,0},{12,20},{20,12},{24,28},{28,24},{5,17},{... | collective-permute-start | bytes 393224 | tf_op jit(solution)/shard_map/ppermute | solution.py:467
  20.1 0.9 %collective-permute-start.4 = (bf16[16,32,128]{2,1,0:T(8,128)(2,1)S(1)}, bf16[16,32,128]{2,1,0:T(8,128)(2,1)S(1)}, u32[]{:S(2)}, u32[]{:S(2)}) collective-permute-start(bf16[16,32,128]{2,1,0:T(8,128)(2,1)S(1)} %get-tuple-element.26), channel_id=1, source_target_pairs={{8,16},{16,8},{0,4},{4,0},{12,24},{24,12},{20,28},{28,20},{9,17},{... | collective-permute-start | bytes 393224 | tf_op jit(solution)/shard_map/ppermute | solution.py:467
  21.0 0.0 collective-permute-done.rest_0_
  21.0 0.1 collective-permute-start.5
  21.1 0.0 collective-permute-done.1.rest_1_
  21.1 0.0 copy-start.3
  21.1 0.0 copy-start.2
  21.2 2.6 %collective-permute-start.6 = (bf16[16,32,128]{2,1,0:T(8,128)(2,1)S(1)}, bf16[16,32,128]{2,1,0:T(8,128)(2,1)S(1)}, u32[]{:S(2)}, u32[]{:S(2)}) collective-permute-start(bf16[16,32,128]{2,1,0:T(8,128)(2,1)S(1)} %get-tuple-element.28), channel_id=1, source_target_pairs={{8,20},{20,8},{0,4},{4,0},{12,16},{16,12},{24,28},{28,24},{9,21},{... | collective-permute-start | bytes 393224 | tf_op jit(solution)/shard_map/ppermute | solution.py:467
  23.7 3.9 %local.1.local_ref = f32[64,32,128]{2,1,0:T(8,128)S(1)} custom-call(s32[8,896]{1,0:T(8,128)S(1)} %get-tuple-element.18.words_v, s32[6272]{0:T(1024)S(1)} %get-tuple-element.19.lists_v, bf16[16,32,128]{2,1,0:T(8,128)(2,1)S(1)} %get-tuple-element.22._after, f32[29568,128]{1,0:T(8,128)S(1)} %get-tuple-element.20.rest_0_, f32[29568,128]{1,0:T(8,128)S(1)} %get-tuple-element.21.rest_1_), custom_call_target="tpu_custom_call" | custom-call | flops 3623878656 | bytes 8388608 | tf_op jit(solution)/shard_map/local/pallas_call | solution.py:468
  27.7 0.0 collective-permute-done.2.rest_2_
  27.7 0.8 %arrive.1.local_ref = f32[64,32,128]{2,1,0:T(8,128)S(1)} custom-call(s32[1,128]{1,0:T(1,128)S(1)} %copy-done.1, f32[64,32,128]{2,1,0:T(8,128)S(1)} %local.1.local_ref, bf16[16,32,128]{2,1,0:T(8,128)(2,1)S(1)} %collective-permute-done.rest_0_, bf16[16,32,128]{2,1,0:T(8,128)(2,1)S(1)} %collective-permute-done.1.rest_1_, ...), custom_call_target="tpu_custom_call" | custom-call | tf_op jit(solution)/shard_map/arrive/pallas_call | solution.py:477
  28.5 0.8 %collective-permute-done.4.rest_1_ = bf16[16,32,128]{2,1,0:T(8,128)(2,1)S(1)} collective-permute-done((bf16[16,32,128]{2,1,0:T(8,128)(2,1)S(1)}, bf16[16,32,128]{2,1,0:T(8,128)(2,1)S(1)}, u32[]{:S(2)}, u32[]{:S(2)}) %collective-permute-start.4) | collective-permute-done | bytes 131104 | tf_op jit(solution)/shard_map/ppermute | solution.py:467
  29.3 0.0 collective-permute-done.5.rest_2_
  29.3 1.8 %collective-permute-done.6.rest_3_ = bf16[16,32,128]{2,1,0:T(8,128)(2,1)S(1)} collective-permute-done((bf16[16,32,128]{2,1,0:T(8,128)(2,1)S(1)}, bf16[16,32,128]{2,1,0:T(8,128)(2,1)S(1)}, u32[]{:S(2)}, u32[]{:S(2)}) %collective-permute-start.6) | collective-permute-done | bytes 131104 | tf_op jit(solution)/shard_map/ppermute | solution.py:467
  31.1 1.1 %combine.1 = (f32[64,32,128]{2,1,0:T(8,128)S(1)}, f32[2,2048]{1,0:T(2,128)S(1)}) custom-call(s32[1,128]{1,0:T(1,128)S(1)} %copy-done.1, f32[64,32,128]{2,1,0:T(8,128)S(1)} %arrive.1.local_ref, bf16[16,32,128]{2,1,0:T(8,128)(2,1)S(1)} %collective-permute-done.3.rest_0_, bf16[16,32,128]{2,1,0:T(8,128)(2,1)S(1)} %collective-permute-done.4.rest_1_, ...), custom_call_target="tpu_custom_call" | custom-call | tf_op jit(solution)/shard_map/combine/pallas_call | solution.py:495
  32.1 0.1 collective-permute-start.7
  32.2 1.6 %collective-permute-start.8 = (f32[2,2048]{1,0:T(2,128)S(1)}, f32[2,2048]{1,0:T(2,128)S(1)}, u32[]{:S(2)}, u32[]{:S(2)}) collective-permute-start(f32[2,2048]{1,0:T(2,128)S(1)} %get-tuple-element.31._after.s0), channel_id=1, source_target_pairs={{0,2},{1,3},{2,0},{3,1},{4,6},{5,7},{6,4},{7,5},{8,10},{9,11},{10,... | collective-permute-start | bytes 49160 | tf_op jit(solution)/shard_map/ppermute | solution.py:516
  33.8 0.3 collective-permute-start.9
  34.1 0.1 reshape_tile.3.gain_ref
  34.2 0.8 %own.1.own_ref = f32[64,32,128]{2,1,0:T(8,128)S(1)} custom-call(bf16[4096,256]{1,0:T(8,128)(2,1)S(1)} %get-tuple-element.30.f_ref, f32[2,2048]{1,0:T(2,128)S(1)} %get-tuple-element.31._after.s0), custom_call_target="tpu_custom_call" | custom-call | tf_op jit(solution)/shard_map/own/pallas_call | solution.py:507
  35.0 1.0 %collective-permute-done.8.s2 = f32[2,2048]{1,0:T(2,128)S(1)} collective-permute-done((f32[2,2048]{1,0:T(2,128)S(1)}, f32[2,2048]{1,0:T(2,128)S(1)}, u32[]{:S(2)}, u32[]{:S(2)}) %collective-permute-start.8) | collective-permute-done | bytes 16416 | tf_op jit(solution)/shard_map/ppermute | solution.py:516
  36.0 0.9 %collective-permute-done.9.s3 = f32[2,2048]{1,0:T(2,128)S(1)} collective-permute-done((f32[2,2048]{1,0:T(2,128)S(1)}, f32[2,2048]{1,0:T(2,128)S(1)}, u32[]{:S(2)}, u32[]{:S(2)}) %collective-permute-start.9) | collective-permute-done | bytes 16416 | tf_op jit(solution)/shard_map/ppermute | solution.py:516
  37.0 1.4 %norm.1 = (bf16[64,32,128]{2,1,0:T(8,128)(2,1)S(1)}, bf16[8,32,128]{2,1,0:T(8,128)(2,1)}) custom-call(f32[64,32,128]{2,1,0:T(8,128)S(1)} %get-tuple-element.29.conv_ref, f32[64,32,128]{2,1,0:T(8,128)S(1)} %own.1.own_ref, f32[1,128]{1,0:T(1,128)S(1)} %reshape_tile.3.gain_ref, bf16[32,256]{1,0:T(8,128)(2,1)S(1)} %copy-done, s32[1,8]{1,0:T(1,128)S(1)} %copy-done.3, ...), custom_call_target="tpu_custom_call" | custom-call | tf_op jit(solution)/shard_map/norm/pallas_call | solution.py:519
  38.4 4.3 %all-to-all-start = ((bf16[8,32,128]{2,1,0:T(8,128)(2,1)}), bf16[8,32,128]{2,1,0:T(8,128)(2,1)S(1)}, u32[]{:S(2)}, u32[]{:S(2)}) async-start(bf16[8,32,128]{2,1,0:T(8,128)(2,1)} %get-tuple-element.33), calls=%async_computation | async-start | bytes 131072 | tf_op jit(solution)/shard_map/all_to_all | solution.py:539
  42.7 1.3 %unpack.1 = bf16[64,64,64]{2,1,0:T(8,128)(2,1)} custom-call(bf16[64,32,128]{2,1,0:T(8,128)(2,1)S(1)} %get-tuple-element.32.whole_ref), custom_call_target="tpu_custom_call" | custom-call | tf_op jit(solution)/shard_map/unpack/pallas_call | solution.py:540
  44.0 5.6 %all-to-all-done.landed_ref = bf16[8,32,128]{2,1,0:T(8,128)(2,1)S(1)} async-done(((bf16[8,32,128]{2,1,0:T(8,128)(2,1)}), bf16[8,32,128]{2,1,0:T(8,128)(2,1)S(1)}, u32[]{:S(2)}, u32[]{:S(2)}) %all-to-all-start) | async-done | bytes 65568 | tf_op jit(solution)/shard_map/all_to_all | solution.py:539
  49.6 0.8 %place.1 = bf16[8,64,64]{2,1,0:T(8,128)(2,1)} custom-call(s32[1,8]{1,0:T(1,128)S(1)} %copy-done.2, bf16[8,32,128]{2,1,0:T(8,128)(2,1)S(1)} %all-to-all-done.landed_ref), custom_call_target="tpu_custom_call" | custom-call | tf_op jit(solution)/shard_map/place/pallas_call | solution.py:548
  (11 shorter events, 0.0 us)
Async XLA Ops:
  8.3 12.7 %collective-permute-start = (bf16[16,32,128]{2,1,0:T(8,128)(2,1)S(1)}, bf16[16,32,128]{2,1,0:T(8,128)(2,1)S(1)}, u32[]{:S(2)}, u32[]{:S(2)}) collective-permute-start(bf16[16,32,128]{2,1,0:T(8,128)(2,1)S(1)} %get-tuple-element.23), channel_id=1, source_target_pairs={{0,16},{16,0},{4,20},{20,4},{8,24},{24,8},{12,28},{28,12},{1,17},{... | collective-permute-start | bytes 393224 | tf_op jit(solution)/shard_map/ppermute | solution.py:457
  12.4 8.7 %collective-permute-start.1 = (bf16[16,32,128]{2,1,0:T(8,128)(2,1)S(1)}, bf16[16,32,128]{2,1,0:T(8,128)(2,1)S(1)}, u32[]{:S(2)}, u32[]{:S(2)}) collective-permute-start(bf16[16,32,128]{2,1,0:T(8,128)(2,1)S(1)} %get-tuple-element.24), channel_id=1, source_target_pairs={{0,4},{4,0},{8,12},{12,8},{16,20},{20,16},{24,28},{28,24},{1,5},{5... | collective-permute-start | bytes 393224 | tf_op jit(solution)/shard_map/ppermute | solution.py:457
  14.6 13.1 %collective-permute-start.2 = (bf16[16,32,128]{2,1,0:T(8,128)(2,1)S(1)}, bf16[16,32,128]{2,1,0:T(8,128)(2,1)S(1)}, u32[]{:S(2)}, u32[]{:S(2)}) collective-permute-start(bf16[16,32,128]{2,1,0:T(8,128)(2,1)S(1)} %get-tuple-element.25), channel_id=1, source_target_pairs={{0,8},{8,0},{4,12},{12,4},{16,24},{24,16},{20,28},{28,20},{1,9},{9... | collective-permute-start | bytes 393224 | tf_op jit(solution)/shard_map/ppermute | solution.py:457
  18.1 10.4 %collective-permute-start.3 = (bf16[16,32,128]{2,1,0:T(8,128)(2,1)S(1)}, bf16[16,32,128]{2,1,0:T(8,128)(2,1)S(1)}, u32[]{:S(2)}, u32[]{:S(2)}) collective-permute-start(bf16[16,32,128]{2,1,0:T(8,128)(2,1)S(1)} %get-tuple-element.22._after), channel_id=1, source_target_pairs={{4,16},{16,4},{0,8},{8,0},{12,20},{20,12},{24,28},{28,24},{5,17},{... | collective-permute-start | bytes 393224 | tf_op jit(solution)/shard_map/ppermute | solution.py:467
  20.1 9.1 %collective-permute-start.4 = (bf16[16,32,128]{2,1,0:T(8,128)(2,1)S(1)}, bf16[16,32,128]{2,1,0:T(8,128)(2,1)S(1)}, u32[]{:S(2)}, u32[]{:S(2)}) collective-permute-start(bf16[16,32,128]{2,1,0:T(8,128)(2,1)S(1)} %get-tuple-element.26), channel_id=1, source_target_pairs={{8,16},{16,8},{0,4},{4,0},{12,24},{24,12},{20,28},{28,20},{9,17},{... | collective-permute-start | bytes 393224 | tf_op jit(solution)/shard_map/ppermute | solution.py:467
  21.0 8.3 %collective-permute-start.5 = (bf16[16,32,128]{2,1,0:T(8,128)(2,1)S(1)}, bf16[16,32,128]{2,1,0:T(8,128)(2,1)S(1)}, u32[]{:S(2)}, u32[]{:S(2)}) collective-permute-start(bf16[16,32,128]{2,1,0:T(8,128)(2,1)S(1)} %get-tuple-element.27), channel_id=1, source_target_pairs={{0,12},{12,0},{4,8},{8,4},{16,28},{28,16},{20,24},{24,20},{1,13},{... | collective-permute-start | bytes 393224 | tf_op jit(solution)/shard_map/ppermute | solution.py:467
  21.1 6.5 %copy-start.1 = (s32[1,128]{1,0:T(1,128)S(1)}, s32[1,128]{1,0:T(1,128)}, u32[]{:S(2)}) copy-start(s32[1,128]{1,0:T(1,128)} %list_v.3) | copy-start | bytes 1540
  21.1 13.0 %copy-start.4 = (bf16[64]{0:T(256)(128)(2,1)S(1)}, bf16[64]{0:T(256)(128)(2,1)}, u32[]{:S(2)}) copy-start(bf16[64]{0:T(256)(128)(2,1)} %param.10) | copy-start | bytes 388
  21.1 15.8 %copy-start = (bf16[32,256]{1,0:T(8,128)(2,1)S(1)}, bf16[32,256]{1,0:T(8,128)(2,1)}, u32[]{:S(2)}) copy-start(bf16[32,256]{1,0:T(8,128)(2,1)} %constant.2.clone.pool_ref) | copy-start | bytes 49156
  21.1 15.8 %copy-start.3 = (s32[1,8]{1,0:T(1,128)S(1)}, s32[1,8]{1,0:T(1,128)}, u32[]{:S(2)}) copy-start(s32[1,8]{1,0:T(1,128)} %slot_v.1) | copy-start | bytes 100
  21.1 28.5 %copy-start.2 = (s32[1,8]{1,0:T(1,128)S(1)}, s32[1,8]{1,0:T(1,128)}, u32[]{:S(2)}) copy-start(s32[1,8]{1,0:T(1,128)} %place_ref.1) | copy-start | bytes 100
  21.2 9.9 %collective-permute-start.6 = (bf16[16,32,128]{2,1,0:T(8,128)(2,1)S(1)}, bf16[16,32,128]{2,1,0:T(8,128)(2,1)S(1)}, u32[]{:S(2)}, u32[]{:S(2)}) collective-permute-start(bf16[16,32,128]{2,1,0:T(8,128)(2,1)S(1)} %get-tuple-element.28), channel_id=1, source_target_pairs={{8,20},{20,8},{0,4},{4,0},{12,16},{16,12},{24,28},{28,24},{9,21},{... | collective-permute-start | bytes 393224 | tf_op jit(solution)/shard_map/ppermute | solution.py:467
  32.1 2.9 %collective-permute-start.7 = (f32[2,2048]{1,0:T(2,128)S(1)}, f32[2,2048]{1,0:T(2,128)S(1)}, u32[]{:S(2)}, u32[]{:S(2)}) collective-permute-start(f32[2,2048]{1,0:T(2,128)S(1)} %get-tuple-element.31._after.s0), channel_id=1, source_target_pairs={{0,1},{1,0},{2,3},{3,2},{4,5},{5,4},{6,7},{7,6},{8,9},{9,8},{10,11... | collective-permute-start | bytes 49160 | tf_op jit(solution)/shard_map/ppermute | solution.py:516
  32.2 3.8 %collective-permute-start.8 = (f32[2,2048]{1,0:T(2,128)S(1)}, f32[2,2048]{1,0:T(2,128)S(1)}, u32[]{:S(2)}, u32[]{:S(2)}) collective-permute-start(f32[2,2048]{1,0:T(2,128)S(1)} %get-tuple-element.31._after.s0), channel_id=1, source_target_pairs={{0,2},{1,3},{2,0},{3,1},{4,6},{5,7},{6,4},{7,5},{8,10},{9,11},{10,... | collective-permute-start | bytes 49160 | tf_op jit(solution)/shard_map/ppermute | solution.py:516
  33.8 3.2 %collective-permute-start.9 = (f32[2,2048]{1,0:T(2,128)S(1)}, f32[2,2048]{1,0:T(2,128)S(1)}, u32[]{:S(2)}, u32[]{:S(2)}) collective-permute-start(f32[2,2048]{1,0:T(2,128)S(1)} %get-tuple-element.31._after.s0), channel_id=1, source_target_pairs={{0,3},{1,2},{2,1},{3,0},{4,7},{5,6},{6,5},{7,4},{8,11},{9,10},{10,... | collective-permute-start | bytes 49160 | tf_op jit(solution)/shard_map/ppermute | solution.py:516
  38.4 11.2 %all-to-all-start = ((bf16[8,32,128]{2,1,0:T(8,128)(2,1)}), bf16[8,32,128]{2,1,0:T(8,128)(2,1)S(1)}, u32[]{:S(2)}, u32[]{:S(2)}) async-start(bf16[8,32,128]{2,1,0:T(8,128)(2,1)} %get-tuple-element.33), calls=%async_computation | async-start | bytes 131072 | tf_op jit(solution)/shard_map/all_to_all | solution.py:539

commit v9 on v8

--- a/solution.py
+++ b/solution.py
@@ -16,9 +16,10 @@
 F32 = jnp.float32
 PAD = 64
 UNROLL = 8
+F_PARTS = 1
 PARTS = 2
 PER_PART = 7
-ORDER = (0, 4, 5, 1, 2, 6, 3)
+ORDER = (0, 5, 4, 1, 2, 6, 3)
 
 
 def perfect(n):
@@ -95,26 +96,29 @@
     return (lax.div(code, 9) - 1, lax.rem(lax.div(code, 3), 3) - 1, lax.rem(code, 3) - 1)
 
 
-def rules_matmul(f_ref, w_ref, y_refs, beside=None):
+def rules_matmul(f_ref, w_ref, y_refs, ready, beside):
     rows = f_ref.shape[0]
     span = rows + 2 * PAD
     depth = w_ref.shape[0]
     steps = range(0, depth, 256)
     for number, q in enumerate(steps):
         width = min(256, depth - q)
-        part = lax.dot_general(
-            f_ref[...],
-            w_ref[q : q + width, :],
-            (((1,), (1,)), ((), ())),
-            preferred_element_type=F32,
-        )
-        for s in range(0, width, 128):
-            wide = min(128, width - s)
-            y_ref = y_refs[(q + s) // 128 // PER_PART]
-            base = ((q + s) // 128 % PER_PART) * span + PAD
-            y_ref[base : base + rows, 0:wide] = part[:, s : s + wide]
-        if beside is not None:
-            beside(number, len(steps))
+        cuts = F_PARTS if number == 0 else 1
+        size = rows // cuts
+        for h in range(cuts):
+            ready(number, h)
+            part = lax.dot_general(
+                f_ref[h * size : (h + 1) * size, :],
+                w_ref[q : q + width, :],
+                (((1,), (1,)), ((), ())),
+                preferred_element_type=F32,
+            )
+            for s in range(0, width, 128):
+                wide = min(128, width - s)
+                y_ref = y_refs[(q + s) // 128 // PER_PART]
+                base = ((q + s) // 128 % PER_PART) * span + PAD + h * size
+                y_ref[base : base + size, 0:wide] = part[:, s : s + wide]
+        beside(number, len(steps))
 
 
 def rules_add(words, lists, part, y_refs, acc_ref):
@@ -136,7 +140,8 @@
             need = words[1, r]
             taken = y_ref[pl.ds(lax.shift_right_logical(packed, 8), VOX), :]
             t = packed & 255
-            acc_ref[t] = acc_ref[t] + jnp.where((have & need) == need, taken, 0.0)
+            half = acc_ref[u % 2]
+            half[t] = half[t] + jnp.where((have & need) == need, taken, 0.0)
         return c
 
     lax.fori_loop(0, lax.div(count + (UNROLL - 1), UNROLL), several, 0)
@@ -144,16 +149,17 @@
 
 def zero_blocks(acc_ref):
     def zero(i, c):
-        acc_ref[i] = jnp.zeros((VOX, 128), F32)
+        for half in acc_ref:
+            half[i] = jnp.zeros((VOX, 128), F32)
         return c
 
-    lax.fori_loop(0, acc_ref.shape[0], zero, 0, unroll=8)
+    lax.fori_loop(0, acc_ref[0].shape[0], zero, 0, unroll=8)
 
 
 def folded(acc_ref, t):
     first = lane_iota((HALF, 128)) < 64
-    low = acc_ref[t, 0:HALF, :]
-    high = acc_ref[t, HALF:VOX, :]
+    low = acc_ref[0][t, 0:HALF, :] + acc_ref[1][t, 0:HALF, :]
+    high = acc_ref[0][t, HALF:VOX, :] + acc_ref[1][t, HALF:VOX, :]
     low = low + pltpu.roll(low, 64, 1)
     high = high + pltpu.roll(high, 64, 1)
     return jnp.where(first, low, high)
@@ -173,22 +179,29 @@
 def far_kernel(count, table, tile_count, rules_hbm, f_hbm, w_hbm, *rest):
     sends, rest = rest[:count], rest[count:]
     f_ref, y_refs, rest = rest[0], rest[1 : 1 + PARTS], rest[1 + PARTS :]
-    words_v, lists_v, acc_ref, w_ref, rules_ref, words_s, lists, sems = rest
+    words_v, lists_v, *acc_ref, w_ref, rules_ref, words_s, lists, sems = rest
     rows = tile_count * VOX
     span = rows + 2 * PAD
     rule_rows = rules_ref.shape[1]
     wide = words_v.shape[1]
     slots = tile_count // 4
-    copies = [
-        pltpu.make_async_copy(src, dst, sems.at[i])
-        for i, (src, dst) in enumerate(((rules_hbm, rules_ref), (w_hbm, w_ref), (f_hbm, f_ref)))
+    depth = w_ref.shape[0]
+    size = rows // F_PARTS
+    rules_copy = pltpu.make_async_copy(rules_hbm, rules_ref, sems.at[0])
+    f_copies = [
+        pltpu.make_async_copy(f_hbm.at[pl.ds(h * size, size)], f_ref.at[pl.ds(h * size, size)], sems.at[3 + h])
+        for h in range(F_PARTS)
     ]
-    for copy in copies:
+    w_copies = [
+        pltpu.make_async_copy(w_hbm.at[pl.ds(q, width)], w_ref.at[pl.ds(q, width)], sems.at[3 + F_PARTS + i])
+        for i, (q, width) in enumerate([(0, 256), (256, depth - 256)])
+    ]
+    for copy in [rules_copy, w_copies[0], *f_copies, w_copies[1]]:
         copy.start()
     before = lax.broadcasted_iota(jnp.int32, (rule_rows, rule_rows), 0)
     before = (before <= lane_iota((rule_rows, rule_rows))).astype(F32).astype(BF)
     zero_blocks(acc_ref)
-    copies[0].wait()
+    rules_copy.wait()
     tile = rules_ref[0:1, :]
     kernel = rules_ref[1:2, :]
     heading = rules_ref[2:3, :]
@@ -223,10 +236,16 @@
     for c in range(3 * PARTS):
         total = upto[c : c + 1, rule_rows - 1 : rule_rows]
         words_v[3:4, 128 * c : 128 * c + 128] = jnp.broadcast_to(total, (1, 128)).astype(jnp.int32)
-    to_scalars = pltpu.make_async_copy(words_v, words_s, sems.at[3])
+    to_scalars = pltpu.make_async_copy(words_v, words_s, sems.at[1])
     to_scalars.start()
-    copies[1].wait()
-    copies[2].wait()
+
+    def ready(number, h):
+        if number == 0:
+            if h == 0:
+                w_copies[0].wait()
+            f_copies[h].wait()
+        if number == 1:
+            w_copies[1].wait()
 
     def list_some(number, steps):
         if number == 0:
@@ -235,11 +254,11 @@
         for r in range(number * share, min(rule_rows, (number + 1) * share)):
             lists[words_s[2, r]] = r
 
-    rules_matmul(f_ref, w_ref, y_refs, list_some)
+    rules_matmul(f_ref, w_ref, y_refs, ready, list_some)
     for c in range(3 * PARTS):
         for u in range(UNROLL):
             lists[c * wide + words_s[3, 128 * c] + u] = rule_rows
-    hand_on = pltpu.make_async_copy(lists, lists_v, sems.at[4])
+    hand_on = pltpu.make_async_copy(lists, lists_v, sems.at[2])
     hand_on.start()
     rules_add(words_s, lists, 0, y_refs, acc_ref)
     emit_sends(acc_ref, sends)
@@ -247,8 +266,8 @@
 
 
 def near_kernel(words_v, lists_v, *rest):
-    y_refs, sends = rest[:PARTS], rest[PARTS:-4]
-    acc_ref, words, lists, sems = rest[-4:]
+    y_refs, sends = rest[:PARTS], rest[PARTS:-5]
+    *acc_ref, words, lists, sems = rest[-5:]
     copies = [
         pltpu.make_async_copy(words_v, words, sems.at[0]),
         pltpu.make_async_copy(lists_v, lists, sems.at[1]),
@@ -276,7 +295,7 @@
 
 
 def local_kernel(words_v, lists_v, _after, *rest):
-    y_refs, (local_ref, acc_ref, words, lists, sems) = rest[:PARTS], rest[PARTS:]
+    y_refs, (local_ref, *acc_ref, words, lists, sems) = rest[:PARTS], rest[PARTS:]
     copies = [
         pltpu.make_async_copy(words_v, words, sems.at[0]),
         pltpu.make_async_copy(lists_v, lists, sems.at[1]),
@@ -292,7 +311,7 @@
         local_ref[t] = folded(acc_ref, t)
         return c
 
-    lax.fori_loop(0, acc_ref.shape[0], keep, 0, unroll=16)
+    lax.fori_loop(0, acc_ref[0].shape[0], keep, 0, unroll=16)
 
 
 def arrive_kernel(first, table, list_v, local_ref, *rest):
@@ -333,7 +352,7 @@
     add_arrivals(first, table, blocks, list_ref, conv_ref)
     rows = tile_count * HALF
     pick = (lane_iota((2, 256)) // 64 % 2 == lax.broadcasted_iota(jnp.int32, (2, 256), 0)).astype(BF)
-    step = 512
+    step = rows
     for at in range(0, rows, step):
         value = conv_ref[at // HALF : (at + step) // HALF].reshape(step, 128)
         square = value * value
@@ -428,7 +447,7 @@
     flat_weights = weights.transpose(0, 2, 1).reshape(offsets * quarter, channels)
     block = jax.ShapeDtypeStruct((slots, HALF, 128), BF)
     whole = jax.ShapeDtypeStruct((tile_count, HALF, 128), F32)
-    work = [pltpu.VMEM((tile_count, VOX, 128), F32)]
+    work = [pltpu.VMEM((tile_count, VOX, 128), F32)] * 2
     flops = 2 * tile_count * VOX * channels * offsets * quarter
     shared = dict(
         compiler_params=pltpu.CompilerParams(vmem_limit_bytes=16 * 1024 * 1024),
@@ -447,7 +466,7 @@
             pltpu.VMEM(flat_weights.shape, BF),
             pltpu.VMEM((4, rule_rows), jnp.int32),
             *scalars,
-            pltpu.SemaphoreType.DMA((5,)),
+            pltpu.SemaphoreType.DMA((5 + F_PARTS,)),
         ],
         name="far",
         **shared,

time: 50.8 us -> 50.7 us (level)
  Pallas kernels: 20.1 us -> 21.1 us
  waiting for transfers between devices: 10.2 us -> 9.61 us
    ppermute x7, starting transfers between devices: 13.1 us -> 12.1 us  [call_rules(): lax.ppermute(x, 'tiles', route)]
    pallas_call x1, Pallas kernels: 3.93 us -> 4.68 us  [call_rules(): pl.pallas_call(local_kernel, out_shape=whole, in_specs=[VM, VM, ANY] + [V...]
    ppermute x7, waiting for transfers between devices: 2.62 us -> 2.07 us  [call_rules(): lax.ppermute(x, 'tiles', route)]
  transfers between devices with their start and end apart: 11 -> 11, of which waited for: 5 -> 5; matrix products, arithmetic and copies ran while one was open for 0% -> 0% of each run, Pallas kernels for 18% -> 20%
where the time goes in v9:
time: 50.7 us; the launch traced here: 50.5 us
  Pallas kernels  21.1 us (42%)
  starting transfers between devices  18.9 us (37%)
  waiting for transfers between devices  9.61 us (19%)
  between operations  0.76 us (1%)
    ppermute x7, starting transfers between devices, call_rules(): lax.ppermute(x, 'tiles', route)  12.1 us
    pallas_call x1, Pallas kernels, call_rules(): pl.pallas_call(functools.partial(far_kernel, count, table, tile_count), o...  7.74 us
    all_to_all x1, waiting for transfers between devices, body(): lax.all_to_all(outbound, 'tiles', split_axis=0, concat_axis=0, tiled=True)  5.6 us
    all_to_all x1, starting transfers between devices, body(): lax.all_to_all(outbound, 'tiles', split_axis=0, concat_axis=0, tiled=True)  4.84 us
    pallas_call x1, Pallas kernels, call_rules(): pl.pallas_call(local_kernel, out_shape=whole, in_specs=[VM, VM, ANY] + [V...  4.68 us
    pallas_call x1, Pallas kernels, call_rules(): pl.pallas_call(near_kernel, out_shape=[block] * (len(routes) - count), in...  2.47 us
    ppermute x7, waiting for transfers between devices, call_rules(): lax.ppermute(x, 'tiles', route)  2.07 us
    ppermute x3, waiting for transfers between devices, body(): lax.ppermute(sums, 'chan', [(i, i ^ m) for i in range(wide)])  1.94 us
  transfers between devices with their start and end apart: 11, of which 5 were waited for; matrix products, arithmetic and copies ran while one was open for 0% of the time, Pallas kernels for 20%

profile of v9, /device:TPU:0, one launch (start us, length us, event | category | flops | bytes accessed | tf_op | source)
XLA Modules:
  0.0 50.5 jit_solution(2817420524613492065)
XLA Ops:
  0.6 7.7 %far.1 = (bf16[16,32,128]{2,1,0:T(8,128)(2,1)S(1)}, bf16[16,32,128]{2,1,0:T(8,128)(2,1)S(1)}, bf16[16,32,128]{2,1,0:T(8,128)(2,1)S(1)}, bf16[4096,256]{1,0:T(8,1...) custom-call(s32[4,768]{1,0:T(4,128)} %bitcast.7, ...), custom_call_target="tpu_custom_call" | custom-call | flops 3623878656 | bytes 8388608 | tf_op jit(solution)/shard_map/far/pallas_call | solution.py:456
  8.4 3.7 %collective-permute-start = (bf16[16,32,128]{2,1,0:T(8,128)(2,1)S(1)}, bf16[16,32,128]{2,1,0:T(8,128)(2,1)S(1)}, u32[]{:S(2)}, u32[]{:S(2)}) collective-permute-start(bf16[16,32,128]{2,1,0:T(8,128)(2,1)S(1)} %get-tuple-element.23), channel_id=1, source_target_pairs={{0,16},{16,0},{4,20},{20,4},{8,24},{24,8},{12,28},{28,12},{1,17},{... | collective-permute-start | bytes 393224 | tf_op jit(solution)/shard_map/ppermute | solution.py:476
  12.1 1.7 %collective-permute-start.1 = (bf16[16,32,128]{2,1,0:T(8,128)(2,1)S(1)}, bf16[16,32,128]{2,1,0:T(8,128)(2,1)S(1)}, u32[]{:S(2)}, u32[]{:S(2)}) collective-permute-start(bf16[16,32,128]{2,1,0:T(8,128)(2,1)S(1)} %get-tuple-element.24), channel_id=1, source_target_pairs={{0,8},{8,0},{4,12},{12,4},{16,24},{24,16},{20,28},{28,20},{1,9},{9... | collective-permute-start | bytes 393224 | tf_op jit(solution)/shard_map/ppermute | solution.py:476
  13.8 1.9 %collective-permute-start.2 = (bf16[16,32,128]{2,1,0:T(8,128)(2,1)S(1)}, bf16[16,32,128]{2,1,0:T(8,128)(2,1)S(1)}, u32[]{:S(2)}, u32[]{:S(2)}) collective-permute-start(bf16[16,32,128]{2,1,0:T(8,128)(2,1)S(1)} %get-tuple-element.25), channel_id=1, source_target_pairs={{0,4},{4,0},{8,12},{12,8},{16,20},{20,16},{24,28},{28,24},{1,5},{5... | collective-permute-start | bytes 393224 | tf_op jit(solution)/shard_map/ppermute | solution.py:476
  15.8 2.5 %near.1 = (bf16[16,32,128]{2,1,0:T(8,128)(2,1)S(1)}, bf16[16,32,128]{2,1,0:T(8,128)(2,1)S(1)}, bf16[16,32,128]{2,1,0:T(8,128)(2,1)S(1)}, bf16[16,32,128]{2,1,0:T(8,128)(2,1)S(1)}) custom-call(s32[8,896]{1,0:T(8,128)S(1)} %get-tuple-element.18.words_v, s32[6272]{0:T(1024)S(1)} %get-tuple-element.19.lists_v, f32[29568,128]{1,0:T(8,128)S(1)} %get-tuple-element.20.rest_0_, ...), custom_call_target="tpu_custom_call" | custom-call | flops 3623878656 | bytes 8388608 | tf_op jit(solution)/shard_map/near/pallas_call | solution.py:477
  18.3 1.3 %collective-permute-start.3 = (bf16[16,32,128]{2,1,0:T(8,128)(2,1)S(1)}, bf16[16,32,128]{2,1,0:T(8,128)(2,1)S(1)}, u32[]{:S(2)}, u32[]{:S(2)}) collective-permute-start(bf16[16,32,128]{2,1,0:T(8,128)(2,1)S(1)} %get-tuple-element.22._after), channel_id=1, source_target_pairs={{4,16},{16,4},{0,8},{8,0},{12,20},{20,12},{24,28},{28,24},{5,17},{... | collective-permute-start | bytes 393224 | tf_op jit(solution)/shard_map/ppermute | solution.py:486
  19.6 0.6 %collective-permute-start.4 = (bf16[16,32,128]{2,1,0:T(8,128)(2,1)S(1)}, bf16[16,32,128]{2,1,0:T(8,128)(2,1)S(1)}, u32[]{:S(2)}, u32[]{:S(2)}) collective-permute-start(bf16[16,32,128]{2,1,0:T(8,128)(2,1)S(1)} %get-tuple-element.26), channel_id=1, source_target_pairs={{8,16},{16,8},{0,4},{4,0},{12,24},{24,12},{20,28},{28,20},{9,17},{... | collective-permute-start | bytes 393224 | tf_op jit(solution)/shard_map/ppermute | solution.py:486
  20.2 0.0 collective-permute-done.rest_0_
  20.2 0.6 %collective-permute-start.5 = (bf16[16,32,128]{2,1,0:T(8,128)(2,1)S(1)}, bf16[16,32,128]{2,1,0:T(8,128)(2,1)S(1)}, u32[]{:S(2)}, u32[]{:S(2)}) collective-permute-start(bf16[16,32,128]{2,1,0:T(8,128)(2,1)S(1)} %get-tuple-element.27), channel_id=1, source_target_pairs={{0,12},{12,0},{4,8},{8,4},{16,28},{28,16},{20,24},{24,20},{1,13},{... | collective-permute-start | bytes 393224 | tf_op jit(solution)/shard_map/ppermute | solution.py:486
  20.8 0.0 collective-permute-done.1.rest_1_
  20.8 0.0 copy-start.3
  20.8 0.0 copy-start.2
  20.9 2.2 %collective-permute-start.6 = (bf16[16,32,128]{2,1,0:T(8,128)(2,1)S(1)}, bf16[16,32,128]{2,1,0:T(8,128)(2,1)S(1)}, u32[]{:S(2)}, u32[]{:S(2)}) collective-permute-start(bf16[16,32,128]{2,1,0:T(8,128)(2,1)S(1)} %get-tuple-element.28), channel_id=1, source_target_pairs={{8,20},{20,8},{0,4},{4,0},{12,16},{16,12},{24,28},{28,24},{9,21},{... | collective-permute-start | bytes 393224 | tf_op jit(solution)/shard_map/ppermute | solution.py:486
  23.0 4.7 %local.1.local_ref = f32[64,32,128]{2,1,0:T(8,128)S(1)} custom-call(s32[8,896]{1,0:T(8,128)S(1)} %get-tuple-element.18.words_v, s32[6272]{0:T(1024)S(1)} %get-tuple-element.19.lists_v, bf16[16,32,128]{2,1,0:T(8,128)(2,1)S(1)} %get-tuple-element.22._after, f32[29568,128]{1,0:T(8,128)S(1)} %get-tuple-element.20.rest_0_, f32[29568,128]{1,0:T(8,128)S(1)} %get-tuple-element.21.rest_1_), custom_call_target="tpu_custom_call" | custom-call | flops 3623878656 | bytes 8388608 | tf_op jit(solution)/shard_map/local/pallas_call | solution.py:487
  27.7 0.8 %arrive.1.local_ref = f32[64,32,128]{2,1,0:T(8,128)S(1)} custom-call(s32[1,128]{1,0:T(1,128)S(1)} %copy-done.1, f32[64,32,128]{2,1,0:T(8,128)S(1)} %local.1.local_ref, bf16[16,32,128]{2,1,0:T(8,128)(2,1)S(1)} %collective-permute-done.rest_0_, bf16[16,32,128]{2,1,0:T(8,128)(2,1)S(1)} %collective-permute-done.1.rest_1_, ...), custom_call_target="tpu_custom_call" | custom-call | tf_op jit(solution)/shard_map/arrive/pallas_call | solution.py:496
  28.5 0.0 collective-permute-done.3.rest_0_
  28.5 0.2 collective-permute-done.4.rest_1_
  28.7 0.0 collective-permute-done.5.rest_2_
  28.7 1.9 %collective-permute-done.6.rest_3_ = bf16[16,32,128]{2,1,0:T(8,128)(2,1)S(1)} collective-permute-done((bf16[16,32,128]{2,1,0:T(8,128)(2,1)S(1)}, bf16[16,32,128]{2,1,0:T(8,128)(2,1)S(1)}, u32[]{:S(2)}, u32[]{:S(2)}) %collective-permute-start.6) | collective-permute-done | bytes 131104 | tf_op jit(solution)/shard_map/ppermute | solution.py:486
  30.6 1.1 %combine.1 = (f32[64,32,128]{2,1,0:T(8,128)S(1)}, f32[2,2048]{1,0:T(2,128)S(1)}) custom-call(s32[1,128]{1,0:T(1,128)S(1)} %copy-done.1, f32[64,32,128]{2,1,0:T(8,128)S(1)} %arrive.1.local_ref, bf16[16,32,128]{2,1,0:T(8,128)(2,1)S(1)} %collective-permute-done.3.rest_0_, bf16[16,32,128]{2,1,0:T(8,128)(2,1)S(1)} %collective-permute-done.4.rest_1_, ...), custom_call_target="tpu_custom_call" | custom-call | tf_op jit(solution)/shard_map/combine/pallas_call | solution.py:514
  31.6 0.1 collective-permute-start.7
  31.7 1.6 %collective-permute-start.8 = (f32[2,2048]{1,0:T(2,128)S(1)}, f32[2,2048]{1,0:T(2,128)S(1)}, u32[]{:S(2)}, u32[]{:S(2)}) collective-permute-start(f32[2,2048]{1,0:T(2,128)S(1)} %get-tuple-element.31._after.s0), channel_id=1, source_target_pairs={{0,2},{1,3},{2,0},{3,1},{4,6},{5,7},{6,4},{7,5},{8,10},{9,11},{10,... | collective-permute-start | bytes 49160 | tf_op jit(solution)/shard_map/ppermute | solution.py:535
  33.3 0.3 collective-permute-start.9
  33.6 0.1 reshape_tile.3.gain_ref
  33.7 0.8 %own.1.own_ref = f32[64,32,128]{2,1,0:T(8,128)S(1)} custom-call(bf16[4096,256]{1,0:T(8,128)(2,1)S(1)} %get-tuple-element.30.f_ref, f32[2,2048]{1,0:T(2,128)S(1)} %get-tuple-element.31._after.s0), custom_call_target="tpu_custom_call" | custom-call | tf_op jit(solution)/shard_map/own/pallas_call | solution.py:526
  34.5 1.0 %collective-permute-done.8.s2 = f32[2,2048]{1,0:T(2,128)S(1)} collective-permute-done((f32[2,2048]{1,0:T(2,128)S(1)}, f32[2,2048]{1,0:T(2,128)S(1)}, u32[]{:S(2)}, u32[]{:S(2)}) %collective-permute-start.8) | collective-permute-done | bytes 16416 | tf_op jit(solution)/shard_map/ppermute | solution.py:535
  35.5 0.9 %collective-permute-done.9.s3 = f32[2,2048]{1,0:T(2,128)S(1)} collective-permute-done((f32[2,2048]{1,0:T(2,128)S(1)}, f32[2,2048]{1,0:T(2,128)S(1)}, u32[]{:S(2)}, u32[]{:S(2)}) %collective-permute-start.9) | collective-permute-done | bytes 16416 | tf_op jit(solution)/shard_map/ppermute | solution.py:535
  36.5 1.4 %norm.1 = (bf16[64,32,128]{2,1,0:T(8,128)(2,1)S(1)}, bf16[8,32,128]{2,1,0:T(8,128)(2,1)}) custom-call(f32[64,32,128]{2,1,0:T(8,128)S(1)} %get-tuple-element.29.conv_ref, f32[64,32,128]{2,1,0:T(8,128)S(1)} %own.1.own_ref, f32[1,128]{1,0:T(1,128)S(1)} %reshape_tile.3.gain_ref, bf16[32,256]{1,0:T(8,128)(2,1)S(1)} %copy-done, s32[1,8]{1,0:T(1,128)S(1)} %copy-done.3, ...), custom_call_target="tpu_custom_call" | custom-call | tf_op jit(solution)/shard_map/norm/pallas_call | solution.py:538
  37.9 4.8 %all-to-all-start = ((bf16[8,32,128]{2,1,0:T(8,128)(2,1)}), bf16[8,32,128]{2,1,0:T(8,128)(2,1)S(1)}, u32[]{:S(2)}, u32[]{:S(2)}) async-start(bf16[8,32,128]{2,1,0:T(8,128)(2,1)} %get-tuple-element.33), calls=%async_computation | async-start | bytes 131072 | tf_op jit(solution)/shard_map/all_to_all | solution.py:558
  42.7 1.3 %unpack.1 = bf16[64,64,64]{2,1,0:T(8,128)(2,1)} custom-call(bf16[64,32,128]{2,1,0:T(8,128)(2,1)S(1)} %get-tuple-element.32.whole_ref), custom_call_target="tpu_custom_call" | custom-call | tf_op jit(solution)/shard_map/unpack/pallas_call | solution.py:559
  44.0 5.6 %all-to-all-done.landed_ref = bf16[8,32,128]{2,1,0:T(8,128)(2,1)S(1)} async-done(((bf16[8,32,128]{2,1,0:T(8,128)(2,1)}), bf16[8,32,128]{2,1,0:T(8,128)(2,1)S(1)}, u32[]{:S(2)}, u32[]{:S(2)}) %all-to-all-start) | async-done | bytes 65568 | tf_op jit(solution)/shard_map/all_to_all | solution.py:558
  49.6 0.8 %place.1 = bf16[8,64,64]{2,1,0:T(8,128)(2,1)} custom-call(s32[1,8]{1,0:T(1,128)S(1)} %copy-done.2, bf16[8,32,128]{2,1,0:T(8,128)(2,1)S(1)} %all-to-all-done.landed_ref), custom_call_target="tpu_custom_call" | custom-call | tf_op jit(solution)/shard_map/place/pallas_call | solution.py:567
  (11 shorter events, 0.0 us)
Async XLA Ops:
  8.4 11.8 %collective-permute-start = (bf16[16,32,128]{2,1,0:T(8,128)(2,1)S(1)}, bf16[16,32,128]{2,1,0:T(8,128)(2,1)S(1)}, u32[]{:S(2)}, u32[]{:S(2)}) collective-permute-start(bf16[16,32,128]{2,1,0:T(8,128)(2,1)S(1)} %get-tuple-element.23), channel_id=1, source_target_pairs={{0,16},{16,0},{4,20},{20,4},{8,24},{24,8},{12,28},{28,12},{1,17},{... | collective-permute-start | bytes 393224 | tf_op jit(solution)/shard_map/ppermute | solution.py:476
  12.1 8.7 %collective-permute-start.1 = (bf16[16,32,128]{2,1,0:T(8,128)(2,1)S(1)}, bf16[16,32,128]{2,1,0:T(8,128)(2,1)S(1)}, u32[]{:S(2)}, u32[]{:S(2)}) collective-permute-start(bf16[16,32,128]{2,1,0:T(8,128)(2,1)S(1)} %get-tuple-element.24), channel_id=1, source_target_pairs={{0,8},{8,0},{4,12},{12,4},{16,24},{24,16},{20,28},{28,20},{1,9},{9... | collective-permute-start | bytes 393224 | tf_op jit(solution)/shard_map/ppermute | solution.py:476
  13.8 13.9 %collective-permute-start.2 = (bf16[16,32,128]{2,1,0:T(8,128)(2,1)S(1)}, bf16[16,32,128]{2,1,0:T(8,128)(2,1)S(1)}, u32[]{:S(2)}, u32[]{:S(2)}) collective-permute-start(bf16[16,32,128]{2,1,0:T(8,128)(2,1)S(1)} %get-tuple-element.25), channel_id=1, source_target_pairs={{0,4},{4,0},{8,12},{12,8},{16,20},{20,16},{24,28},{28,24},{1,5},{5... | collective-permute-start | bytes 393224 | tf_op jit(solution)/shard_map/ppermute | solution.py:476
  18.3 10.2 %collective-permute-start.3 = (bf16[16,32,128]{2,1,0:T(8,128)(2,1)S(1)}, bf16[16,32,128]{2,1,0:T(8,128)(2,1)S(1)}, u32[]{:S(2)}, u32[]{:S(2)}) collective-permute-start(bf16[16,32,128]{2,1,0:T(8,128)(2,1)S(1)} %get-tuple-element.22._after), channel_id=1, source_target_pairs={{4,16},{16,4},{0,8},{8,0},{12,20},{20,12},{24,28},{28,24},{5,17},{... | collective-permute-start | bytes 393224 | tf_op jit(solution)/shard_map/ppermute | solution.py:486
  19.6 9.1 %collective-permute-start.4 = (bf16[16,32,128]{2,1,0:T(8,128)(2,1)S(1)}, bf16[16,32,128]{2,1,0:T(8,128)(2,1)S(1)}, u32[]{:S(2)}, u32[]{:S(2)}) collective-permute-start(bf16[16,32,128]{2,1,0:T(8,128)(2,1)S(1)} %get-tuple-element.26), channel_id=1, source_target_pairs={{8,16},{16,8},{0,4},{4,0},{12,24},{24,12},{20,28},{28,20},{9,17},{... | collective-permute-start | bytes 393224 | tf_op jit(solution)/shard_map/ppermute | solution.py:486
  20.2 8.5 %collective-permute-start.5 = (bf16[16,32,128]{2,1,0:T(8,128)(2,1)S(1)}, bf16[16,32,128]{2,1,0:T(8,128)(2,1)S(1)}, u32[]{:S(2)}, u32[]{:S(2)}) collective-permute-start(bf16[16,32,128]{2,1,0:T(8,128)(2,1)S(1)} %get-tuple-element.27), channel_id=1, source_target_pairs={{0,12},{12,0},{4,8},{8,4},{16,28},{28,16},{20,24},{24,20},{1,13},{... | collective-permute-start | bytes 393224 | tf_op jit(solution)/shard_map/ppermute | solution.py:486
  20.8 6.9 %copy-start.1 = (s32[1,128]{1,0:T(1,128)S(1)}, s32[1,128]{1,0:T(1,128)}, u32[]{:S(2)}) copy-start(s32[1,128]{1,0:T(1,128)} %list_v.3) | copy-start | bytes 1540
  20.8 12.7 %copy-start.4 = (bf16[64]{0:T(256)(128)(2,1)S(1)}, bf16[64]{0:T(256)(128)(2,1)}, u32[]{:S(2)}) copy-start(bf16[64]{0:T(256)(128)(2,1)} %param.10) | copy-start | bytes 388
  20.8 15.6 %copy-start = (bf16[32,256]{1,0:T(8,128)(2,1)S(1)}, bf16[32,256]{1,0:T(8,128)(2,1)}, u32[]{:S(2)}) copy-start(bf16[32,256]{1,0:T(8,128)(2,1)} %constant.2.clone.pool_ref) | copy-start | bytes 49156
  20.8 15.6 %copy-start.3 = (s32[1,8]{1,0:T(1,128)S(1)}, s32[1,8]{1,0:T(1,128)}, u32[]{:S(2)}) copy-start(s32[1,8]{1,0:T(1,128)} %slot_v.1) | copy-start | bytes 100
  20.8 28.8 %copy-start.2 = (s32[1,8]{1,0:T(1,128)S(1)}, s32[1,8]{1,0:T(1,128)}, u32[]{:S(2)}) copy-start(s32[1,8]{1,0:T(1,128)} %place_ref.1) | copy-start | bytes 100
  20.9 9.7 %collective-permute-start.6 = (bf16[16,32,128]{2,1,0:T(8,128)(2,1)S(1)}, bf16[16,32,128]{2,1,0:T(8,128)(2,1)S(1)}, u32[]{:S(2)}, u32[]{:S(2)}) collective-permute-start(bf16[16,32,128]{2,1,0:T(8,128)(2,1)S(1)} %get-tuple-element.28), channel_id=1, source_target_pairs={{8,20},{20,8},{0,4},{4,0},{12,16},{16,12},{24,28},{28,24},{9,21},{... | collective-permute-start | bytes 393224 | tf_op jit(solution)/shard_map/ppermute | solution.py:486
  31.6 2.9 %collective-permute-start.7 = (f32[2,2048]{1,0:T(2,128)S(1)}, f32[2,2048]{1,0:T(2,128)S(1)}, u32[]{:S(2)}, u32[]{:S(2)}) collective-permute-start(f32[2,2048]{1,0:T(2,128)S(1)} %get-tuple-element.31._after.s0), channel_id=1, source_target_pairs={{0,1},{1,0},{2,3},{3,2},{4,5},{5,4},{6,7},{7,6},{8,9},{9,8},{10,11... | collective-permute-start | bytes 49160 | tf_op jit(solution)/shard_map/ppermute | solution.py:535
  31.7 3.8 %collective-permute-start.8 = (f32[2,2048]{1,0:T(2,128)S(1)}, f32[2,2048]{1,0:T(2,128)S(1)}, u32[]{:S(2)}, u32[]{:S(2)}) collective-permute-start(f32[2,2048]{1,0:T(2,128)S(1)} %get-tuple-element.31._after.s0), channel_id=1, source_target_pairs={{0,2},{1,3},{2,0},{3,1},{4,6},{5,7},{6,4},{7,5},{8,10},{9,11},{10,... | collective-permute-start | bytes 49160 | tf_op jit(solution)/shard_map/ppermute | solution.py:535
  33.3 3.2 %collective-permute-start.9 = (f32[2,2048]{1,0:T(2,128)S(1)}, f32[2,2048]{1,0:T(2,128)S(1)}, u32[]{:S(2)}, u32[]{:S(2)}) collective-permute-start(f32[2,2048]{1,0:T(2,128)S(1)} %get-tuple-element.31._after.s0), channel_id=1, source_target_pairs={{0,3},{1,2},{2,1},{3,0},{4,7},{5,6},{6,5},{7,4},{8,11},{9,10},{10,... | collective-permute-start | bytes 49160 | tf_op jit(solution)/shard_map/ppermute | solution.py:535
  37.9 11.7 %all-to-all-start = ((bf16[8,32,128]{2,1,0:T(8,128)(2,1)}), bf16[8,32,128]{2,1,0:T(8,128)(2,1)S(1)}, u32[]{:S(2)}, u32[]{:S(2)}) async-start(bf16[8,32,128]{2,1,0:T(8,128)(2,1)} %get-tuple-element.33), calls=%async_computation | async-start | bytes 131072 | tf_op jit(solution)/shard_map/all_to_all | solution.py:558

commit v10 on v9

--- a/solution.py
+++ b/solution.py
@@ -9,6 +9,7 @@
 from jax.sharding import PartitionSpec as P
 
 EPS = 1e-05
+BF_MAX = float(jnp.finfo(jnp.bfloat16).max)
 REACH = 4
 VOX = 64
 HALF = 32
@@ -356,7 +357,7 @@
     for at in range(0, rows, step):
         value = conv_ref[at // HALF : (at + step) // HALF].reshape(step, 128)
         square = value * value
-        top = square.astype(BF)
+        top = jnp.minimum(square, BF_MAX).astype(BF)
         rest_of = (square - top.astype(F32)).astype(BF)
         sums_ref[:, at : at + step] = lax.dot_general(
             pick,

time: 50.7 us -> 50.2 us (level)
  starting transfers between devices: 18.9 us -> 17.7 us
  Pallas kernels: 21.1 us -> 22 us
    all_to_all x1, starting transfers between devices: 4.84 us -> 4.08 us  [body(): lax.all_to_all(outbound, 'tiles', split_axis=0, concat_axis=0, tiled=True)]
    pallas_call x1, Pallas kernels: 4.68 us -> 5.28 us  [call_rules(): pl.pallas_call(local_kernel, out_shape=whole, in_specs=[VM, VM, ANY] + [V...]
  transfers between devices with their start and end apart: 11 -> 11, of which waited for: 5 -> 5; matrix products, arithmetic and copies ran while one was open for 0% -> 0% of each run, Pallas kernels for 20% -> 21%
where the time goes in v10:
time: 50.2 us; the launch traced here: 49.7 us
  Pallas kernels  22 us (44%)
  starting transfers between devices  17.7 us (35%)
  waiting for transfers between devices  9.2 us (18%)
  between operations  0.78 us (2%)
    ppermute x7, starting transfers between devices, call_rules(): lax.ppermute(x, 'tiles', route)  11.6 us
    pallas_call x1, Pallas kernels, call_rules(): pl.pallas_call(functools.partial(far_kernel, count, table, tile_count), o...  8.03 us
    all_to_all x1, waiting for transfers between devices, body(): lax.all_to_all(outbound, 'tiles', split_axis=0, concat_axis=0, tiled=True)  5.6 us
    pallas_call x1, Pallas kernels, call_rules(): pl.pallas_call(local_kernel, out_shape=whole, in_specs=[VM, VM, ANY] + [V...  5.28 us
    all_to_all x1, starting transfers between devices, body(): lax.all_to_all(outbound, 'tiles', split_axis=0, concat_axis=0, tiled=True)  4.08 us
    pallas_call x1, Pallas kernels, call_rules(): pl.pallas_call(near_kernel, out_shape=[block] * (len(routes) - count), in...  2.47 us
    ppermute x3, starting transfers between devices, body(): lax.ppermute(sums, 'chan', [(i, i ^ m) for i in range(wide)])  1.93 us
    ppermute x3, waiting for transfers between devices, body(): lax.ppermute(sums, 'chan', [(i, i ^ m) for i in range(wide)])  1.93 us
  transfers between devices with their start and end apart: 11, of which 5 were waited for; matrix products, arithmetic and copies ran while one was open for 0% of the time, Pallas kernels for 21%

profile of v10, /device:TPU:0, one launch (start us, length us, event | category | flops | bytes accessed | tf_op | source)
XLA Modules:
  0.0 49.7 jit_solution(15177001715413598177)
XLA Ops:
  0.6 8.0 %far.1 = (bf16[16,32,128]{2,1,0:T(8,128)(2,1)S(1)}, bf16[16,32,128]{2,1,0:T(8,128)(2,1)S(1)}, bf16[16,32,128]{2,1,0:T(8,128)(2,1)S(1)}, bf16[4096,256]{1,0:T(8,1...) custom-call(s32[4,768]{1,0:T(4,128)} %bitcast.7, ...), custom_call_target="tpu_custom_call" | custom-call | flops 3623878656 | bytes 8388608 | tf_op jit(solution)/shard_map/far/pallas_call | solution.py:457
  8.7 4.1 %collective-permute-start = (bf16[16,32,128]{2,1,0:T(8,128)(2,1)S(1)}, bf16[16,32,128]{2,1,0:T(8,128)(2,1)S(1)}, u32[]{:S(2)}, u32[]{:S(2)}) collective-permute-start(bf16[16,32,128]{2,1,0:T(8,128)(2,1)S(1)} %get-tuple-element.23), channel_id=1, source_target_pairs={{0,16},{16,0},{4,20},{20,4},{8,24},{24,8},{12,28},{28,12},{1,17},{... | collective-permute-start | bytes 393224 | tf_op jit(solution)/shard_map/ppermute | solution.py:477
  12.8 1.0 %collective-permute-start.1 = (bf16[16,32,128]{2,1,0:T(8,128)(2,1)S(1)}, bf16[16,32,128]{2,1,0:T(8,128)(2,1)S(1)}, u32[]{:S(2)}, u32[]{:S(2)}) collective-permute-start(bf16[16,32,128]{2,1,0:T(8,128)(2,1)S(1)} %get-tuple-element.24), channel_id=1, source_target_pairs={{0,8},{8,0},{4,12},{12,4},{16,24},{24,16},{20,28},{28,20},{1,9},{9... | collective-permute-start | bytes 393224 | tf_op jit(solution)/shard_map/ppermute | solution.py:477
  13.7 1.4 %collective-permute-start.2 = (bf16[16,32,128]{2,1,0:T(8,128)(2,1)S(1)}, bf16[16,32,128]{2,1,0:T(8,128)(2,1)S(1)}, u32[]{:S(2)}, u32[]{:S(2)}) collective-permute-start(bf16[16,32,128]{2,1,0:T(8,128)(2,1)S(1)} %get-tuple-element.25), channel_id=1, source_target_pairs={{0,4},{4,0},{8,12},{12,8},{16,20},{20,16},{24,28},{28,24},{1,5},{5... | collective-permute-start | bytes 393224 | tf_op jit(solution)/shard_map/ppermute | solution.py:477
  15.2 2.5 %near.1 = (bf16[16,32,128]{2,1,0:T(8,128)(2,1)S(1)}, bf16[16,32,128]{2,1,0:T(8,128)(2,1)S(1)}, bf16[16,32,128]{2,1,0:T(8,128)(2,1)S(1)}, bf16[16,32,128]{2,1,0:T(8,128)(2,1)S(1)}) custom-call(s32[8,896]{1,0:T(8,128)S(1)} %get-tuple-element.18.words_v, s32[6272]{0:T(1024)S(1)} %get-tuple-element.19.lists_v, f32[29568,128]{1,0:T(8,128)S(1)} %get-tuple-element.20.rest_0_, ...), custom_call_target="tpu_custom_call" | custom-call | flops 3623878656 | bytes 8388608 | tf_op jit(solution)/shard_map/near/pallas_call | solution.py:478
  17.7 1.3 %collective-permute-start.3 = (bf16[16,32,128]{2,1,0:T(8,128)(2,1)S(1)}, bf16[16,32,128]{2,1,0:T(8,128)(2,1)S(1)}, u32[]{:S(2)}, u32[]{:S(2)}) collective-permute-start(bf16[16,32,128]{2,1,0:T(8,128)(2,1)S(1)} %get-tuple-element.22._after), channel_id=1, source_target_pairs={{4,16},{16,4},{0,8},{8,0},{12,20},{20,12},{24,28},{28,24},{5,17},{... | collective-permute-start | bytes 393224 | tf_op jit(solution)/shard_map/ppermute | solution.py:487
  19.0 2.3 %collective-permute-start.4 = (bf16[16,32,128]{2,1,0:T(8,128)(2,1)S(1)}, bf16[16,32,128]{2,1,0:T(8,128)(2,1)S(1)}, u32[]{:S(2)}, u32[]{:S(2)}) collective-permute-start(bf16[16,32,128]{2,1,0:T(8,128)(2,1)S(1)} %get-tuple-element.26), channel_id=1, source_target_pairs={{8,16},{16,8},{0,4},{4,0},{12,24},{24,12},{20,28},{28,20},{9,17},{... | collective-permute-start | bytes 393224 | tf_op jit(solution)/shard_map/ppermute | solution.py:487
  21.3 0.0 collective-permute-done.1.rest_1_
  21.3 0.0 copy-start.1
  21.3 0.0 copy-start.4
  21.3 0.0 copy-start
  21.3 0.0 copy-start.3
  21.3 0.0 copy-start.2
  21.4 1.5 %collective-permute-start.6 = (bf16[16,32,128]{2,1,0:T(8,128)(2,1)S(1)}, bf16[16,32,128]{2,1,0:T(8,128)(2,1)S(1)}, u32[]{:S(2)}, u32[]{:S(2)}) collective-permute-start(bf16[16,32,128]{2,1,0:T(8,128)(2,1)S(1)} %get-tuple-element.28), channel_id=1, source_target_pairs={{8,20},{20,8},{0,4},{4,0},{12,16},{16,12},{24,28},{28,24},{9,21},{... | collective-permute-start | bytes 393224 | tf_op jit(solution)/shard_map/ppermute | solution.py:487
  22.9 5.3 %local.1.local_ref = f32[64,32,128]{2,1,0:T(8,128)S(1)} custom-call(s32[8,896]{1,0:T(8,128)S(1)} %get-tuple-element.18.words_v, s32[6272]{0:T(1024)S(1)} %get-tuple-element.19.lists_v, bf16[16,32,128]{2,1,0:T(8,128)(2,1)S(1)} %get-tuple-element.22._after, f32[29568,128]{1,0:T(8,128)S(1)} %get-tuple-element.20.rest_0_, f32[29568,128]{1,0:T(8,128)S(1)} %get-tuple-element.21.rest_1_), custom_call_target="tpu_custom_call" | custom-call | flops 3623878656 | bytes 8388608 | tf_op jit(solution)/shard_map/local/pallas_call | solution.py:488
  28.1 0.0 collective-permute-done.2.rest_2_
  28.2 0.8 %arrive.1.local_ref = f32[64,32,128]{2,1,0:T(8,128)S(1)} custom-call(s32[1,128]{1,0:T(1,128)S(1)} %copy-done.1, f32[64,32,128]{2,1,0:T(8,128)S(1)} %local.1.local_ref, bf16[16,32,128]{2,1,0:T(8,128)(2,1)S(1)} %collective-permute-done.rest_0_, bf16[16,32,128]{2,1,0:T(8,128)(2,1)S(1)} %collective-permute-done.1.rest_1_, ...), custom_call_target="tpu_custom_call" | custom-call | tf_op jit(solution)/shard_map/arrive/pallas_call | solution.py:497
  29.0 0.1 collective-permute-done.4.rest_1_
  29.0 1.6 %collective-permute-done.6.rest_3_ = bf16[16,32,128]{2,1,0:T(8,128)(2,1)S(1)} collective-permute-done((bf16[16,32,128]{2,1,0:T(8,128)(2,1)S(1)}, bf16[16,32,128]{2,1,0:T(8,128)(2,1)S(1)}, u32[]{:S(2)}, u32[]{:S(2)}) %collective-permute-start.6) | collective-permute-done | bytes 131104 | tf_op jit(solution)/shard_map/ppermute | solution.py:487
  30.6 1.1 %combine.1 = (f32[64,32,128]{2,1,0:T(8,128)S(1)}, f32[2,2048]{1,0:T(2,128)S(1)}) custom-call(s32[1,128]{1,0:T(1,128)S(1)} %copy-done.1, f32[64,32,128]{2,1,0:T(8,128)S(1)} %arrive.1.local_ref, bf16[16,32,128]{2,1,0:T(8,128)(2,1)S(1)} %collective-permute-done.3.rest_0_, bf16[16,32,128]{2,1,0:T(8,128)(2,1)S(1)} %collective-permute-done.4.rest_1_, ...), custom_call_target="tpu_custom_call" | custom-call | tf_op jit(solution)/shard_map/combine/pallas_call | solution.py:515
  31.7 0.1 collective-permute-start.7
  31.8 1.6 %collective-permute-start.8 = (f32[2,2048]{1,0:T(2,128)S(1)}, f32[2,2048]{1,0:T(2,128)S(1)}, u32[]{:S(2)}, u32[]{:S(2)}) collective-permute-start(f32[2,2048]{1,0:T(2,128)S(1)} %get-tuple-element.31._after.s0), channel_id=1, source_target_pairs={{0,2},{1,3},{2,0},{3,1},{4,6},{5,7},{6,4},{7,5},{8,10},{9,11},{10,... | collective-permute-start | bytes 49160 | tf_op jit(solution)/shard_map/ppermute | solution.py:536
  33.3 0.3 collective-permute-start.9
  33.6 0.1 reshape_tile.3.gain_ref
  33.7 0.8 %own.1.own_ref = f32[64,32,128]{2,1,0:T(8,128)S(1)} custom-call(bf16[4096,256]{1,0:T(8,128)(2,1)S(1)} %get-tuple-element.30.f_ref, f32[2,2048]{1,0:T(2,128)S(1)} %get-tuple-element.31._after.s0), custom_call_target="tpu_custom_call" | custom-call | tf_op jit(solution)/shard_map/own/pallas_call | solution.py:527
  34.6 1.0 %collective-permute-done.8.s2 = f32[2,2048]{1,0:T(2,128)S(1)} collective-permute-done((f32[2,2048]{1,0:T(2,128)S(1)}, f32[2,2048]{1,0:T(2,128)S(1)}, u32[]{:S(2)}, u32[]{:S(2)}) %collective-permute-start.8) | collective-permute-done | bytes 16416 | tf_op jit(solution)/shard_map/ppermute | solution.py:536
  35.6 0.9 %collective-permute-done.9.s3 = f32[2,2048]{1,0:T(2,128)S(1)} collective-permute-done((f32[2,2048]{1,0:T(2,128)S(1)}, f32[2,2048]{1,0:T(2,128)S(1)}, u32[]{:S(2)}, u32[]{:S(2)}) %collective-permute-start.9) | collective-permute-done | bytes 16416 | tf_op jit(solution)/shard_map/ppermute | solution.py:536
  36.5 1.4 %norm.1 = (bf16[64,32,128]{2,1,0:T(8,128)(2,1)S(1)}, bf16[8,32,128]{2,1,0:T(8,128)(2,1)}) custom-call(f32[64,32,128]{2,1,0:T(8,128)S(1)} %get-tuple-element.29.conv_ref, f32[64,32,128]{2,1,0:T(8,128)S(1)} %own.1.own_ref, f32[1,128]{1,0:T(1,128)S(1)} %reshape_tile.3.gain_ref, bf16[32,256]{1,0:T(8,128)(2,1)S(1)} %copy-done, s32[1,8]{1,0:T(1,128)S(1)} %copy-done.3, ...), custom_call_target="tpu_custom_call" | custom-call | tf_op jit(solution)/shard_map/norm/pallas_call | solution.py:539
  37.9 4.1 %all-to-all-start = ((bf16[8,32,128]{2,1,0:T(8,128)(2,1)}), bf16[8,32,128]{2,1,0:T(8,128)(2,1)S(1)}, u32[]{:S(2)}, u32[]{:S(2)}) async-start(bf16[8,32,128]{2,1,0:T(8,128)(2,1)} %get-tuple-element.33), calls=%async_computation | async-start | bytes 131072 | tf_op jit(solution)/shard_map/all_to_all | solution.py:559
  42.0 1.3 %unpack.1 = bf16[64,64,64]{2,1,0:T(8,128)(2,1)} custom-call(bf16[64,32,128]{2,1,0:T(8,128)(2,1)S(1)} %get-tuple-element.32.whole_ref), custom_call_target="tpu_custom_call" | custom-call | tf_op jit(solution)/shard_map/unpack/pallas_call | solution.py:560
  43.3 5.6 %all-to-all-done.landed_ref = bf16[8,32,128]{2,1,0:T(8,128)(2,1)S(1)} async-done(((bf16[8,32,128]{2,1,0:T(8,128)(2,1)}), bf16[8,32,128]{2,1,0:T(8,128)(2,1)S(1)}, u32[]{:S(2)}, u32[]{:S(2)}) %all-to-all-start) | async-done | bytes 65568 | tf_op jit(solution)/shard_map/all_to_all | solution.py:559
  48.9 0.8 %place.1 = bf16[8,64,64]{2,1,0:T(8,128)(2,1)} custom-call(s32[1,8]{1,0:T(1,128)S(1)} %copy-done.2, bf16[8,32,128]{2,1,0:T(8,128)(2,1)S(1)} %all-to-all-done.landed_ref), custom_call_target="tpu_custom_call" | custom-call | tf_op jit(solution)/shard_map/place/pallas_call | solution.py:568
  (11 shorter events, 0.0 us)
Async XLA Ops:
  8.7 12.6 %collective-permute-start = (bf16[16,32,128]{2,1,0:T(8,128)(2,1)S(1)}, bf16[16,32,128]{2,1,0:T(8,128)(2,1)S(1)}, u32[]{:S(2)}, u32[]{:S(2)}) collective-permute-start(bf16[16,32,128]{2,1,0:T(8,128)(2,1)S(1)} %get-tuple-element.23), channel_id=1, source_target_pairs={{0,16},{16,0},{4,20},{20,4},{8,24},{24,8},{12,28},{28,12},{1,17},{... | collective-permute-start | bytes 393224 | tf_op jit(solution)/shard_map/ppermute | solution.py:477
  12.8 8.5 %collective-permute-start.1 = (bf16[16,32,128]{2,1,0:T(8,128)(2,1)S(1)}, bf16[16,32,128]{2,1,0:T(8,128)(2,1)S(1)}, u32[]{:S(2)}, u32[]{:S(2)}) collective-permute-start(bf16[16,32,128]{2,1,0:T(8,128)(2,1)S(1)} %get-tuple-element.24), channel_id=1, source_target_pairs={{0,8},{8,0},{4,12},{12,4},{16,24},{24,16},{20,28},{28,20},{1,9},{9... | collective-permute-start | bytes 393224 | tf_op jit(solution)/shard_map/ppermute | solution.py:477
  13.7 14.4 %collective-permute-start.2 = (bf16[16,32,128]{2,1,0:T(8,128)(2,1)S(1)}, bf16[16,32,128]{2,1,0:T(8,128)(2,1)S(1)}, u32[]{:S(2)}, u32[]{:S(2)}) collective-permute-start(bf16[16,32,128]{2,1,0:T(8,128)(2,1)S(1)} %get-tuple-element.25), channel_id=1, source_target_pairs={{0,4},{4,0},{8,12},{12,8},{16,20},{20,16},{24,28},{28,24},{1,5},{5... | collective-permute-start | bytes 393224 | tf_op jit(solution)/shard_map/ppermute | solution.py:477
  17.7 11.3 %collective-permute-start.3 = (bf16[16,32,128]{2,1,0:T(8,128)(2,1)S(1)}, bf16[16,32,128]{2,1,0:T(8,128)(2,1)S(1)}, u32[]{:S(2)}, u32[]{:S(2)}) collective-permute-start(bf16[16,32,128]{2,1,0:T(8,128)(2,1)S(1)} %get-tuple-element.22._after), channel_id=1, source_target_pairs={{4,16},{16,4},{0,8},{8,0},{12,20},{20,12},{24,28},{28,24},{5,17},{... | collective-permute-start | bytes 393224 | tf_op jit(solution)/shard_map/ppermute | solution.py:487
  19.0 10.0 %collective-permute-start.4 = (bf16[16,32,128]{2,1,0:T(8,128)(2,1)S(1)}, bf16[16,32,128]{2,1,0:T(8,128)(2,1)S(1)}, u32[]{:S(2)}, u32[]{:S(2)}) collective-permute-start(bf16[16,32,128]{2,1,0:T(8,128)(2,1)S(1)} %get-tuple-element.26), channel_id=1, source_target_pairs={{8,16},{16,8},{0,4},{4,0},{12,24},{24,12},{20,28},{28,20},{9,17},{... | collective-permute-start | bytes 393224 | tf_op jit(solution)/shard_map/ppermute | solution.py:487
  21.3 7.7 %collective-permute-start.5 = (bf16[16,32,128]{2,1,0:T(8,128)(2,1)S(1)}, bf16[16,32,128]{2,1,0:T(8,128)(2,1)S(1)}, u32[]{:S(2)}, u32[]{:S(2)}) collective-permute-start(bf16[16,32,128]{2,1,0:T(8,128)(2,1)S(1)} %get-tuple-element.27), channel_id=1, source_target_pairs={{0,12},{12,0},{4,8},{8,4},{16,28},{28,16},{20,24},{24,20},{1,13},{... | collective-permute-start | bytes 393224 | tf_op jit(solution)/shard_map/ppermute | solution.py:487
  21.3 6.9 %copy-start.1 = (s32[1,128]{1,0:T(1,128)S(1)}, s32[1,128]{1,0:T(1,128)}, u32[]{:S(2)}) copy-start(s32[1,128]{1,0:T(1,128)} %list_v.3) | copy-start | bytes 1540
  21.3 12.3 %copy-start.4 = (bf16[64]{0:T(256)(128)(2,1)S(1)}, bf16[64]{0:T(256)(128)(2,1)}, u32[]{:S(2)}) copy-start(bf16[64]{0:T(256)(128)(2,1)} %param.10) | copy-start | bytes 388
  21.3 15.2 %copy-start = (bf16[32,256]{1,0:T(8,128)(2,1)S(1)}, bf16[32,256]{1,0:T(8,128)(2,1)}, u32[]{:S(2)}) copy-start(bf16[32,256]{1,0:T(8,128)(2,1)} %constant.2.clone.pool_ref) | copy-start | bytes 49156
  21.3 15.2 %copy-start.3 = (s32[1,8]{1,0:T(1,128)S(1)}, s32[1,8]{1,0:T(1,128)}, u32[]{:S(2)}) copy-start(s32[1,8]{1,0:T(1,128)} %slot_v.1) | copy-start | bytes 100
  21.3 27.5 %copy-start.2 = (s32[1,8]{1,0:T(1,128)S(1)}, s32[1,8]{1,0:T(1,128)}, u32[]{:S(2)}) copy-start(s32[1,8]{1,0:T(1,128)} %place_ref.1) | copy-start | bytes 100
  21.4 9.3 %collective-permute-start.6 = (bf16[16,32,128]{2,1,0:T(8,128)(2,1)S(1)}, bf16[16,32,128]{2,1,0:T(8,128)(2,1)S(1)}, u32[]{:S(2)}, u32[]{:S(2)}) collective-permute-start(bf16[16,32,128]{2,1,0:T(8,128)(2,1)S(1)} %get-tuple-element.28), channel_id=1, source_target_pairs={{8,20},{20,8},{0,4},{4,0},{12,16},{16,12},{24,28},{28,24},{9,21},{... | collective-permute-start | bytes 393224 | tf_op jit(solution)/shard_map/ppermute | solution.py:487
  31.7 2.9 %collective-permute-start.7 = (f32[2,2048]{1,0:T(2,128)S(1)}, f32[2,2048]{1,0:T(2,128)S(1)}, u32[]{:S(2)}, u32[]{:S(2)}) collective-permute-start(f32[2,2048]{1,0:T(2,128)S(1)} %get-tuple-element.31._after.s0), channel_id=1, source_target_pairs={{0,1},{1,0},{2,3},{3,2},{4,5},{5,4},{6,7},{7,6},{8,9},{9,8},{10,11... | collective-permute-start | bytes 49160 | tf_op jit(solution)/shard_map/ppermute | solution.py:536
  31.8 3.8 %collective-permute-start.8 = (f32[2,2048]{1,0:T(2,128)S(1)}, f32[2,2048]{1,0:T(2,128)S(1)}, u32[]{:S(2)}, u32[]{:S(2)}) collective-permute-start(f32[2,2048]{1,0:T(2,128)S(1)} %get-tuple-element.31._after.s0), channel_id=1, source_target_pairs={{0,2},{1,3},{2,0},{3,1},{4,6},{5,7},{6,4},{7,5},{8,10},{9,11},{10,... | collective-permute-start | bytes 49160 | tf_op jit(solution)/shard_map/ppermute | solution.py:536
  33.3 3.2 %collective-permute-start.9 = (f32[2,2048]{1,0:T(2,128)S(1)}, f32[2,2048]{1,0:T(2,128)S(1)}, u32[]{:S(2)}, u32[]{:S(2)}) collective-permute-start(f32[2,2048]{1,0:T(2,128)S(1)} %get-tuple-element.31._after.s0), channel_id=1, source_target_pairs={{0,3},{1,2},{2,1},{3,0},{4,7},{5,6},{6,5},{7,4},{8,11},{9,10},{10,... | collective-permute-start | bytes 49160 | tf_op jit(solution)/shard_map/ppermute | solution.py:536
  37.9 11.0 %all-to-all-start = ((bf16[8,32,128]{2,1,0:T(8,128)(2,1)}), bf16[8,32,128]{2,1,0:T(8,128)(2,1)S(1)}, u32[]{:S(2)}, u32[]{:S(2)}) async-start(bf16[8,32,128]{2,1,0:T(8,128)(2,1)} %get-tuple-element.33), calls=%async_computation | async-start | bytes 131072 | tf_op jit(solution)/shard_map/all_to_all | solution.py:559

commit v11 on v10

--- a/solution.py
+++ b/solution.py
@@ -20,7 +20,7 @@
 F_PARTS = 1
 PARTS = 2
 PER_PART = 7
-ORDER = (0, 5, 4, 1, 2, 6, 3)
+ORDER = (0, 5, 4, 2, 1, 6, 3)
 
 
 def perfect(n):

time: 50.2 us -> 50.7 us (level)
  Pallas kernels: 22 us -> 20.3 us
  starting transfers between devices: 17.7 us -> 19.3 us
  waiting for transfers between devices: 9.2 us -> 9.91 us
    all_to_all x1, starting transfers between devices: 4.08 us -> 5.27 us  [body(): lax.all_to_all(outbound, 'tiles', split_axis=0, concat_axis=0, tiled=True)]
    pallas_call x1, Pallas kernels: 5.28 us -> 4.13 us  [call_rules(): pl.pallas_call(local_kernel, out_shape=whole, in_specs=[VM, VM, ANY] + [V...]
    ppermute x7, waiting for transfers between devices: 1.66 us -> 2.36 us  [call_rules(): lax.ppermute(x, 'tiles', route)]
  transfers between devices with their start and end apart: 11 -> 11, of which waited for: 5 -> 4; matrix products, arithmetic and copies ran while one was open for 0% -> 0% of each run, Pallas kernels for 21% -> 19%
where the time goes in v11:
time: 50.7 us; the launch traced here: 50.4 us
  Pallas kernels  20.3 us (40%)
  starting transfers between devices  19.3 us (38%)
  waiting for transfers between devices  9.91 us (20%)
  between operations  0.78 us (2%)
    ppermute x7, starting transfers between devices, call_rules(): lax.ppermute(x, 'tiles', route)  12.1 us
    pallas_call x1, Pallas kernels, call_rules(): pl.pallas_call(functools.partial(far_kernel, count, table, tile_count), o...  7.64 us
    all_to_all x1, waiting for transfers between devices, body(): lax.all_to_all(outbound, 'tiles', split_axis=0, concat_axis=0, tiled=True)  5.6 us
    all_to_all x1, starting transfers between devices, body(): lax.all_to_all(outbound, 'tiles', split_axis=0, concat_axis=0, tiled=True)  5.27 us
    pallas_call x1, Pallas kernels, call_rules(): pl.pallas_call(local_kernel, out_shape=whole, in_specs=[VM, VM, ANY] + [V...  4.13 us
    ppermute x7, waiting for transfers between devices, call_rules(): lax.ppermute(x, 'tiles', route)  2.36 us
    pallas_call x1, Pallas kernels, call_rules(): pl.pallas_call(near_kernel, out_shape=[block] * (len(routes) - count), in...  2.32 us
    ppermute x3, waiting for transfers between devices, body(): lax.ppermute(sums, 'chan', [(i, i ^ m) for i in range(wide)])  1.95 us
  transfers between devices with their start and end apart: 11, of which 4 were waited for; matrix products, arithmetic and copies ran while one was open for 0% of the time, Pallas kernels for 19%

profile of v11, /device:TPU:0, one launch (start us, length us, event | category | flops | bytes accessed | tf_op | source)
XLA Modules:
  0.0 50.4 jit_solution(17503491815611351338)
XLA Ops:
  0.6 7.6 %far.1 = (bf16[16,32,128]{2,1,0:T(8,128)(2,1)S(1)}, bf16[16,32,128]{2,1,0:T(8,128)(2,1)S(1)}, bf16[16,32,128]{2,1,0:T(8,128)(2,1)S(1)}, bf16[4096,256]{1,0:T(8,1...) custom-call(s32[4,768]{1,0:T(4,128)} %bitcast.7, ...), custom_call_target="tpu_custom_call" | custom-call | flops 3623878656 | bytes 8388608 | tf_op jit(solution)/shard_map/far/pallas_call | solution.py:457
  8.3 4.0 %collective-permute-start = (bf16[16,32,128]{2,1,0:T(8,128)(2,1)S(1)}, bf16[16,32,128]{2,1,0:T(8,128)(2,1)S(1)}, u32[]{:S(2)}, u32[]{:S(2)}) collective-permute-start(bf16[16,32,128]{2,1,0:T(8,128)(2,1)S(1)} %get-tuple-element.23), channel_id=1, source_target_pairs={{0,16},{16,0},{4,20},{20,4},{8,24},{24,8},{12,28},{28,12},{1,17},{... | collective-permute-start | bytes 393224 | tf_op jit(solution)/shard_map/ppermute | solution.py:477
  12.3 1.7 %collective-permute-start.1 = (bf16[16,32,128]{2,1,0:T(8,128)(2,1)S(1)}, bf16[16,32,128]{2,1,0:T(8,128)(2,1)S(1)}, u32[]{:S(2)}, u32[]{:S(2)}) collective-permute-start(bf16[16,32,128]{2,1,0:T(8,128)(2,1)S(1)} %get-tuple-element.24), channel_id=1, source_target_pairs={{0,8},{8,0},{4,12},{12,4},{16,24},{24,16},{20,28},{28,20},{1,9},{9... | collective-permute-start | bytes 393224 | tf_op jit(solution)/shard_map/ppermute | solution.py:477
  14.0 1.1 %collective-permute-start.2 = (bf16[16,32,128]{2,1,0:T(8,128)(2,1)S(1)}, bf16[16,32,128]{2,1,0:T(8,128)(2,1)S(1)}, u32[]{:S(2)}, u32[]{:S(2)}) collective-permute-start(bf16[16,32,128]{2,1,0:T(8,128)(2,1)S(1)} %get-tuple-element.25), channel_id=1, source_target_pairs={{0,4},{4,0},{8,12},{12,8},{16,20},{20,16},{24,28},{28,24},{1,5},{5... | collective-permute-start | bytes 393224 | tf_op jit(solution)/shard_map/ppermute | solution.py:477
  15.2 2.3 %near.1 = (bf16[16,32,128]{2,1,0:T(8,128)(2,1)S(1)}, bf16[16,32,128]{2,1,0:T(8,128)(2,1)S(1)}, bf16[16,32,128]{2,1,0:T(8,128)(2,1)S(1)}, bf16[16,32,128]{2,1,0:T(8,128)(2,1)S(1)}) custom-call(s32[8,896]{1,0:T(8,128)S(1)} %get-tuple-element.18.words_v, s32[6272]{0:T(1024)S(1)} %get-tuple-element.19.lists_v, f32[29568,128]{1,0:T(8,128)S(1)} %get-tuple-element.20.rest_0_, ...), custom_call_target="tpu_custom_call" | custom-call | flops 3623878656 | bytes 8388608 | tf_op jit(solution)/shard_map/near/pallas_call | solution.py:478
  17.5 1.7 %collective-permute-start.3 = (bf16[16,32,128]{2,1,0:T(8,128)(2,1)S(1)}, bf16[16,32,128]{2,1,0:T(8,128)(2,1)S(1)}, u32[]{:S(2)}, u32[]{:S(2)}) collective-permute-start(bf16[16,32,128]{2,1,0:T(8,128)(2,1)S(1)} %get-tuple-element.22._after), channel_id=1, source_target_pairs={{8,16},{16,8},{0,4},{4,0},{12,24},{24,12},{20,28},{28,20},{9,17},{... | collective-permute-start | bytes 393224 | tf_op jit(solution)/shard_map/ppermute | solution.py:487
  19.2 0.4 collective-permute-start.4
  19.6 0.0 collective-permute-done.rest_0_
  19.6 0.9 %collective-permute-start.5 = (bf16[16,32,128]{2,1,0:T(8,128)(2,1)S(1)}, bf16[16,32,128]{2,1,0:T(8,128)(2,1)S(1)}, u32[]{:S(2)}, u32[]{:S(2)}) collective-permute-start(bf16[16,32,128]{2,1,0:T(8,128)(2,1)S(1)} %get-tuple-element.27), channel_id=1, source_target_pairs={{0,12},{12,0},{4,8},{8,4},{16,28},{28,16},{20,24},{24,20},{1,13},{... | collective-permute-start | bytes 393224 | tf_op jit(solution)/shard_map/ppermute | solution.py:487
  20.5 0.0 collective-permute-done.1.rest_1_
  20.5 0.0 copy-start.3
  20.5 0.0 copy-start.2
  20.5 2.2 %collective-permute-start.6 = (bf16[16,32,128]{2,1,0:T(8,128)(2,1)S(1)}, bf16[16,32,128]{2,1,0:T(8,128)(2,1)S(1)}, u32[]{:S(2)}, u32[]{:S(2)}) collective-permute-start(bf16[16,32,128]{2,1,0:T(8,128)(2,1)S(1)} %get-tuple-element.28), channel_id=1, source_target_pairs={{8,20},{20,8},{0,4},{4,0},{12,16},{16,12},{24,28},{28,24},{9,21},{... | collective-permute-start | bytes 393224 | tf_op jit(solution)/shard_map/ppermute | solution.py:487
  22.8 4.1 %local.1.local_ref = f32[64,32,128]{2,1,0:T(8,128)S(1)} custom-call(s32[8,896]{1,0:T(8,128)S(1)} %get-tuple-element.18.words_v, s32[6272]{0:T(1024)S(1)} %get-tuple-element.19.lists_v, bf16[16,32,128]{2,1,0:T(8,128)(2,1)S(1)} %get-tuple-element.22._after, f32[29568,128]{1,0:T(8,128)S(1)} %get-tuple-element.20.rest_0_, f32[29568,128]{1,0:T(8,128)S(1)} %get-tuple-element.21.rest_1_), custom_call_target="tpu_custom_call" | custom-call | flops 3623878656 | bytes 8388608 | tf_op jit(solution)/shard_map/local/pallas_call | solution.py:488
  26.9 0.0 collective-permute-done.2.rest_2_
  26.9 0.8 %arrive.1.local_ref = f32[64,32,128]{2,1,0:T(8,128)S(1)} custom-call(s32[1,128]{1,0:T(1,128)S(1)} %copy-done.1, f32[64,32,128]{2,1,0:T(8,128)S(1)} %local.1.local_ref, bf16[16,32,128]{2,1,0:T(8,128)(2,1)S(1)} %collective-permute-done.rest_0_, bf16[16,32,128]{2,1,0:T(8,128)(2,1)S(1)} %collective-permute-done.1.rest_1_, ...), custom_call_target="tpu_custom_call" | custom-call | tf_op jit(solution)/shard_map/arrive/pallas_call | solution.py:497
  27.7 0.0 collective-permute-done.4.rest_1_
  27.7 2.3 %collective-permute-done.6.rest_3_ = bf16[16,32,128]{2,1,0:T(8,128)(2,1)S(1)} collective-permute-done((bf16[16,32,128]{2,1,0:T(8,128)(2,1)S(1)}, bf16[16,32,128]{2,1,0:T(8,128)(2,1)S(1)}, u32[]{:S(2)}, u32[]{:S(2)}) %collective-permute-start.6) | collective-permute-done | bytes 131104 | tf_op jit(solution)/shard_map/ppermute | solution.py:487
  30.1 1.1 %combine.1 = (f32[64,32,128]{2,1,0:T(8,128)S(1)}, f32[2,2048]{1,0:T(2,128)S(1)}) custom-call(s32[1,128]{1,0:T(1,128)S(1)} %copy-done.1, f32[64,32,128]{2,1,0:T(8,128)S(1)} %arrive.1.local_ref, bf16[16,32,128]{2,1,0:T(8,128)(2,1)S(1)} %collective-permute-done.3.rest_0_, bf16[16,32,128]{2,1,0:T(8,128)(2,1)S(1)} %collective-permute-done.4.rest_1_, ...), custom_call_target="tpu_custom_call" | custom-call | tf_op jit(solution)/shard_map/combine/pallas_call | solution.py:515
  31.1 0.1 collective-permute-start.7
  31.2 1.6 %collective-permute-start.8 = (f32[2,2048]{1,0:T(2,128)S(1)}, f32[2,2048]{1,0:T(2,128)S(1)}, u32[]{:S(2)}, u32[]{:S(2)}) collective-permute-start(f32[2,2048]{1,0:T(2,128)S(1)} %get-tuple-element.31._after.s0), channel_id=1, source_target_pairs={{0,2},{1,3},{2,0},{3,1},{4,6},{5,7},{6,4},{7,5},{8,10},{9,11},{10,... | collective-permute-start | bytes 49160 | tf_op jit(solution)/shard_map/ppermute | solution.py:536
  32.8 0.3 collective-permute-start.9
  33.1 0.1 reshape_tile.3.gain_ref
  33.2 0.8 %own.1.own_ref = f32[64,32,128]{2,1,0:T(8,128)S(1)} custom-call(bf16[4096,256]{1,0:T(8,128)(2,1)S(1)} %get-tuple-element.30.f_ref, f32[2,2048]{1,0:T(2,128)S(1)} %get-tuple-element.31._after.s0), custom_call_target="tpu_custom_call" | custom-call | tf_op jit(solution)/shard_map/own/pallas_call | solution.py:527
  34.0 0.0 collective-permute-done.7.s1
  34.0 1.0 %collective-permute-done.8.s2 = f32[2,2048]{1,0:T(2,128)S(1)} collective-permute-done((f32[2,2048]{1,0:T(2,128)S(1)}, f32[2,2048]{1,0:T(2,128)S(1)}, u32[]{:S(2)}, u32[]{:S(2)}) %collective-permute-start.8) | collective-permute-done | bytes 16416 | tf_op jit(solution)/shard_map/ppermute | solution.py:536
  35.0 0.9 %collective-permute-done.9.s3 = f32[2,2048]{1,0:T(2,128)S(1)} collective-permute-done((f32[2,2048]{1,0:T(2,128)S(1)}, f32[2,2048]{1,0:T(2,128)S(1)}, u32[]{:S(2)}, u32[]{:S(2)}) %collective-permute-start.9) | collective-permute-done | bytes 16416 | tf_op jit(solution)/shard_map/ppermute | solution.py:536
  36.0 1.4 %norm.1 = (bf16[64,32,128]{2,1,0:T(8,128)(2,1)S(1)}, bf16[8,32,128]{2,1,0:T(8,128)(2,1)}) custom-call(f32[64,32,128]{2,1,0:T(8,128)S(1)} %get-tuple-element.29.conv_ref, f32[64,32,128]{2,1,0:T(8,128)S(1)} %own.1.own_ref, f32[1,128]{1,0:T(1,128)S(1)} %reshape_tile.3.gain_ref, bf16[32,256]{1,0:T(8,128)(2,1)S(1)} %copy-done, s32[1,8]{1,0:T(1,128)S(1)} %copy-done.3, ...), custom_call_target="tpu_custom_call" | custom-call | tf_op jit(solution)/shard_map/norm/pallas_call | solution.py:539
  37.4 5.3 %all-to-all-start = ((bf16[8,32,128]{2,1,0:T(8,128)(2,1)}), bf16[8,32,128]{2,1,0:T(8,128)(2,1)S(1)}, u32[]{:S(2)}, u32[]{:S(2)}) async-start(bf16[8,32,128]{2,1,0:T(8,128)(2,1)} %get-tuple-element.33), calls=%async_computation | async-start | bytes 131072 | tf_op jit(solution)/shard_map/all_to_all | solution.py:559
  42.6 1.3 %unpack.1 = bf16[64,64,64]{2,1,0:T(8,128)(2,1)} custom-call(bf16[64,32,128]{2,1,0:T(8,128)(2,1)S(1)} %get-tuple-element.32.whole_ref), custom_call_target="tpu_custom_call" | custom-call | tf_op jit(solution)/shard_map/unpack/pallas_call | solution.py:560
  44.0 5.6 %all-to-all-done.landed_ref = bf16[8,32,128]{2,1,0:T(8,128)(2,1)S(1)} async-done(((bf16[8,32,128]{2,1,0:T(8,128)(2,1)}), bf16[8,32,128]{2,1,0:T(8,128)(2,1)S(1)}, u32[]{:S(2)}, u32[]{:S(2)}) %all-to-all-start) | async-done | bytes 65568 | tf_op jit(solution)/shard_map/all_to_all | solution.py:559
  49.6 0.8 %place.1 = bf16[8,64,64]{2,1,0:T(8,128)(2,1)} custom-call(s32[1,8]{1,0:T(1,128)S(1)} %copy-done.2, bf16[8,32,128]{2,1,0:T(8,128)(2,1)S(1)} %all-to-all-done.landed_ref), custom_call_target="tpu_custom_call" | custom-call | tf_op jit(solution)/shard_map/place/pallas_call | solution.py:568
  (11 shorter events, 0.0 us)
Async XLA Ops:
  8.3 11.3 %collective-permute-start = (bf16[16,32,128]{2,1,0:T(8,128)(2,1)S(1)}, bf16[16,32,128]{2,1,0:T(8,128)(2,1)S(1)}, u32[]{:S(2)}, u32[]{:S(2)}) collective-permute-start(bf16[16,32,128]{2,1,0:T(8,128)(2,1)S(1)} %get-tuple-element.23), channel_id=1, source_target_pairs={{0,16},{16,0},{4,20},{20,4},{8,24},{24,8},{12,28},{28,12},{1,17},{... | collective-permute-start | bytes 393224 | tf_op jit(solution)/shard_map/ppermute | solution.py:477
  12.3 8.2 %collective-permute-start.1 = (bf16[16,32,128]{2,1,0:T(8,128)(2,1)S(1)}, bf16[16,32,128]{2,1,0:T(8,128)(2,1)S(1)}, u32[]{:S(2)}, u32[]{:S(2)}) collective-permute-start(bf16[16,32,128]{2,1,0:T(8,128)(2,1)S(1)} %get-tuple-element.24), channel_id=1, source_target_pairs={{0,8},{8,0},{4,12},{12,4},{16,24},{24,16},{20,28},{28,20},{1,9},{9... | collective-permute-start | bytes 393224 | tf_op jit(solution)/shard_map/ppermute | solution.py:477
  14.0 12.9 %collective-permute-start.2 = (bf16[16,32,128]{2,1,0:T(8,128)(2,1)S(1)}, bf16[16,32,128]{2,1,0:T(8,128)(2,1)S(1)}, u32[]{:S(2)}, u32[]{:S(2)}) collective-permute-start(bf16[16,32,128]{2,1,0:T(8,128)(2,1)S(1)} %get-tuple-element.25), channel_id=1, source_target_pairs={{0,4},{4,0},{8,12},{12,8},{16,20},{20,16},{24,28},{28,24},{1,5},{5... | collective-permute-start | bytes 393224 | tf_op jit(solution)/shard_map/ppermute | solution.py:477
  17.5 10.2 %collective-permute-start.3 = (bf16[16,32,128]{2,1,0:T(8,128)(2,1)S(1)}, bf16[16,32,128]{2,1,0:T(8,128)(2,1)S(1)}, u32[]{:S(2)}, u32[]{:S(2)}) collective-permute-start(bf16[16,32,128]{2,1,0:T(8,128)(2,1)S(1)} %get-tuple-element.22._after), channel_id=1, source_target_pairs={{8,16},{16,8},{0,4},{4,0},{12,24},{24,12},{20,28},{28,20},{9,17},{... | collective-permute-start | bytes 393224 | tf_op jit(solution)/shard_map/ppermute | solution.py:487
  19.2 8.5 %collective-permute-start.4 = (bf16[16,32,128]{2,1,0:T(8,128)(2,1)S(1)}, bf16[16,32,128]{2,1,0:T(8,128)(2,1)S(1)}, u32[]{:S(2)}, u32[]{:S(2)}) collective-permute-start(bf16[16,32,128]{2,1,0:T(8,128)(2,1)S(1)} %get-tuple-element.26), channel_id=1, source_target_pairs={{4,16},{16,4},{0,8},{8,0},{12,20},{20,12},{24,28},{28,24},{5,17},{... | collective-permute-start | bytes 393224 | tf_op jit(solution)/shard_map/ppermute | solution.py:487
  19.6 8.1 %collective-permute-start.5 = (bf16[16,32,128]{2,1,0:T(8,128)(2,1)S(1)}, bf16[16,32,128]{2,1,0:T(8,128)(2,1)S(1)}, u32[]{:S(2)}, u32[]{:S(2)}) collective-permute-start(bf16[16,32,128]{2,1,0:T(8,128)(2,1)S(1)} %get-tuple-element.27), channel_id=1, source_target_pairs={{0,12},{12,0},{4,8},{8,4},{16,28},{28,16},{20,24},{24,20},{1,13},{... | collective-permute-start | bytes 393224 | tf_op jit(solution)/shard_map/ppermute | solution.py:487
  20.5 6.4 %copy-start.1 = (s32[1,128]{1,0:T(1,128)S(1)}, s32[1,128]{1,0:T(1,128)}, u32[]{:S(2)}) copy-start(s32[1,128]{1,0:T(1,128)} %list_v.3) | copy-start | bytes 1540
  20.5 12.6 %copy-start.4 = (bf16[64]{0:T(256)(128)(2,1)S(1)}, bf16[64]{0:T(256)(128)(2,1)}, u32[]{:S(2)}) copy-start(bf16[64]{0:T(256)(128)(2,1)} %param.10) | copy-start | bytes 388
  20.5 15.5 %copy-start = (bf16[32,256]{1,0:T(8,128)(2,1)S(1)}, bf16[32,256]{1,0:T(8,128)(2,1)}, u32[]{:S(2)}) copy-start(bf16[32,256]{1,0:T(8,128)(2,1)} %constant.2.clone.pool_ref) | copy-start | bytes 49156
  20.5 15.5 %copy-start.3 = (s32[1,8]{1,0:T(1,128)S(1)}, s32[1,8]{1,0:T(1,128)}, u32[]{:S(2)}) copy-start(s32[1,8]{1,0:T(1,128)} %slot_v.1) | copy-start | bytes 100
  20.5 29.1 %copy-start.2 = (s32[1,8]{1,0:T(1,128)S(1)}, s32[1,8]{1,0:T(1,128)}, u32[]{:S(2)}) copy-start(s32[1,8]{1,0:T(1,128)} %place_ref.1) | copy-start | bytes 100
  20.5 9.6 %collective-permute-start.6 = (bf16[16,32,128]{2,1,0:T(8,128)(2,1)S(1)}, bf16[16,32,128]{2,1,0:T(8,128)(2,1)S(1)}, u32[]{:S(2)}, u32[]{:S(2)}) collective-permute-start(bf16[16,32,128]{2,1,0:T(8,128)(2,1)S(1)} %get-tuple-element.28), channel_id=1, source_target_pairs={{8,20},{20,8},{0,4},{4,0},{12,16},{16,12},{24,28},{28,24},{9,21},{... | collective-permute-start | bytes 393224 | tf_op jit(solution)/shard_map/ppermute | solution.py:487
  31.1 2.9 %collective-permute-start.7 = (f32[2,2048]{1,0:T(2,128)S(1)}, f32[2,2048]{1,0:T(2,128)S(1)}, u32[]{:S(2)}, u32[]{:S(2)}) collective-permute-start(f32[2,2048]{1,0:T(2,128)S(1)} %get-tuple-element.31._after.s0), channel_id=1, source_target_pairs={{0,1},{1,0},{2,3},{3,2},{4,5},{5,4},{6,7},{7,6},{8,9},{9,8},{10,11... | collective-permute-start | bytes 49160 | tf_op jit(solution)/shard_map/ppermute | solution.py:536
  31.2 3.8 %collective-permute-start.8 = (f32[2,2048]{1,0:T(2,128)S(1)}, f32[2,2048]{1,0:T(2,128)S(1)}, u32[]{:S(2)}, u32[]{:S(2)}) collective-permute-start(f32[2,2048]{1,0:T(2,128)S(1)} %get-tuple-element.31._after.s0), channel_id=1, source_target_pairs={{0,2},{1,3},{2,0},{3,1},{4,6},{5,7},{6,4},{7,5},{8,10},{9,11},{10,... | collective-permute-start | bytes 49160 | tf_op jit(solution)/shard_map/ppermute | solution.py:536
  32.8 3.2 %collective-permute-start.9 = (f32[2,2048]{1,0:T(2,128)S(1)}, f32[2,2048]{1,0:T(2,128)S(1)}, u32[]{:S(2)}, u32[]{:S(2)}) collective-permute-start(f32[2,2048]{1,0:T(2,128)S(1)} %get-tuple-element.31._after.s0), channel_id=1, source_target_pairs={{0,3},{1,2},{2,1},{3,0},{4,7},{5,6},{6,5},{7,4},{8,11},{9,10},{10,... | collective-permute-start | bytes 49160 | tf_op jit(solution)/shard_map/ppermute | solution.py:536
  37.4 12.2 %all-to-all-start = ((bf16[8,32,128]{2,1,0:T(8,128)(2,1)}), bf16[8,32,128]{2,1,0:T(8,128)(2,1)S(1)}, u32[]{:S(2)}, u32[]{:S(2)}) async-start(bf16[8,32,128]{2,1,0:T(8,128)(2,1)} %get-tuple-element.33), calls=%async_computation | async-start | bytes 131072 | tf_op jit(solution)/shard_map/all_to_all | solution.py:559

commit v12 on v10

--- a/solution.py
+++ b/solution.py
@@ -16,7 +16,7 @@
 BF = jnp.bfloat16
 F32 = jnp.float32
 PAD = 64
-UNROLL = 8
+UNROLL = 16
 F_PARTS = 1
 PARTS = 2
 PER_PART = 7

time: 50.2 us -> 50.5 us (level)
  no operation moved by 1% of the time
where the time goes in v12:
time: 50.5 us; the launch traced here: 50.2 us
  Pallas kernels  21.6 us (43%)
  starting transfers between devices  18.2 us (36%)
  waiting for transfers between devices  9.52 us (19%)
  between operations  0.76 us (2%)
    ppermute x7, starting transfers between devices, call_rules(): lax.ppermute(x, 'tiles', route)  12 us
    pallas_call x1, Pallas kernels, call_rules(): pl.pallas_call(functools.partial(far_kernel, count, table, tile_count), o...  7.91 us
    all_to_all x1, waiting for transfers between devices, body(): lax.all_to_all(outbound, 'tiles', split_axis=0, concat_axis=0, tiled=True)  5.6 us
    pallas_call x1, Pallas kernels, call_rules(): pl.pallas_call(local_kernel, out_shape=whole, in_specs=[VM, VM, ANY] + [V...  4.95 us
    all_to_all x1, starting transfers between devices, body(): lax.all_to_all(outbound, 'tiles', split_axis=0, concat_axis=0, tiled=True)  4.23 us
    pallas_call x1, Pallas kernels, call_rules(): pl.pallas_call(near_kernel, out_shape=[block] * (len(routes) - count), in...  2.51 us
    ppermute x7, waiting for transfers between devices, call_rules(): lax.ppermute(x, 'tiles', route)  1.98 us
    ppermute x3, waiting for transfers between devices, body(): lax.ppermute(sums, 'chan', [(i, i ^ m) for i in range(wide)])  1.94 us
  transfers between devices with their start and end apart: 11, of which 5 were waited for; matrix products, arithmetic and copies ran while one was open for 0% of the time, Pallas kernels for 21%

profile of v12, /device:TPU:0, one launch (start us, length us, event | category | flops | bytes accessed | tf_op | source)
XLA Modules:
  0.0 50.2 jit_solution(16137632267986066563)
XLA Ops:
  0.6 7.9 %far.1 = (bf16[16,32,128]{2,1,0:T(8,128)(2,1)S(1)}, bf16[16,32,128]{2,1,0:T(8,128)(2,1)S(1)}, bf16[16,32,128]{2,1,0:T(8,128)(2,1)S(1)}, bf16[4096,256]{1,0:T(8,1...) custom-call(s32[4,768]{1,0:T(4,128)} %bitcast.7, ...), custom_call_target="tpu_custom_call" | custom-call | flops 3623878656 | bytes 8388608 | tf_op jit(solution)/shard_map/far/pallas_call | solution.py:457
  8.6 4.2 %collective-permute-start = (bf16[16,32,128]{2,1,0:T(8,128)(2,1)S(1)}, bf16[16,32,128]{2,1,0:T(8,128)(2,1)S(1)}, u32[]{:S(2)}, u32[]{:S(2)}) collective-permute-start(bf16[16,32,128]{2,1,0:T(8,128)(2,1)S(1)} %get-tuple-element.23), channel_id=1, source_target_pairs={{0,16},{16,0},{4,20},{20,4},{8,24},{24,8},{12,28},{28,12},{1,17},{... | collective-permute-start | bytes 393224 | tf_op jit(solution)/shard_map/ppermute | solution.py:477
  12.7 1.4 %collective-permute-start.1 = (bf16[16,32,128]{2,1,0:T(8,128)(2,1)S(1)}, bf16[16,32,128]{2,1,0:T(8,128)(2,1)S(1)}, u32[]{:S(2)}, u32[]{:S(2)}) collective-permute-start(bf16[16,32,128]{2,1,0:T(8,128)(2,1)S(1)} %get-tuple-element.24), channel_id=1, source_target_pairs={{0,8},{8,0},{4,12},{12,4},{16,24},{24,16},{20,28},{28,20},{1,9},{9... | collective-permute-start | bytes 393224 | tf_op jit(solution)/shard_map/ppermute | solution.py:477
  14.1 1.3 %collective-permute-start.2 = (bf16[16,32,128]{2,1,0:T(8,128)(2,1)S(1)}, bf16[16,32,128]{2,1,0:T(8,128)(2,1)S(1)}, u32[]{:S(2)}, u32[]{:S(2)}) collective-permute-start(bf16[16,32,128]{2,1,0:T(8,128)(2,1)S(1)} %get-tuple-element.25), channel_id=1, source_target_pairs={{0,4},{4,0},{8,12},{12,8},{16,20},{20,16},{24,28},{28,24},{1,5},{5... | collective-permute-start | bytes 393224 | tf_op jit(solution)/shard_map/ppermute | solution.py:477
  15.4 2.5 %near.1 = (bf16[16,32,128]{2,1,0:T(8,128)(2,1)S(1)}, bf16[16,32,128]{2,1,0:T(8,128)(2,1)S(1)}, bf16[16,32,128]{2,1,0:T(8,128)(2,1)S(1)}, bf16[16,32,128]{2,1,0:T(8,128)(2,1)S(1)}) custom-call(s32[8,896]{1,0:T(8,128)S(1)} %get-tuple-element.18.words_v, s32[6272]{0:T(1024)S(1)} %get-tuple-element.19.lists_v, f32[29568,128]{1,0:T(8,128)S(1)} %get-tuple-element.20.rest_0_, ...), custom_call_target="tpu_custom_call" | custom-call | flops 3623878656 | bytes 8388608 | tf_op jit(solution)/shard_map/near/pallas_call | solution.py:478
  18.0 1.2 %collective-permute-start.3 = (bf16[16,32,128]{2,1,0:T(8,128)(2,1)S(1)}, bf16[16,32,128]{2,1,0:T(8,128)(2,1)S(1)}, u32[]{:S(2)}, u32[]{:S(2)}) collective-permute-start(bf16[16,32,128]{2,1,0:T(8,128)(2,1)S(1)} %get-tuple-element.22._after), channel_id=1, source_target_pairs={{4,16},{16,4},{0,8},{8,0},{12,20},{20,12},{24,28},{28,24},{5,17},{... | collective-permute-start | bytes 393224 | tf_op jit(solution)/shard_map/ppermute | solution.py:487
  19.2 1.5 %collective-permute-start.4 = (bf16[16,32,128]{2,1,0:T(8,128)(2,1)S(1)}, bf16[16,32,128]{2,1,0:T(8,128)(2,1)S(1)}, u32[]{:S(2)}, u32[]{:S(2)}) collective-permute-start(bf16[16,32,128]{2,1,0:T(8,128)(2,1)S(1)} %get-tuple-element.26), channel_id=1, source_target_pairs={{8,16},{16,8},{0,4},{4,0},{12,24},{24,12},{20,28},{28,20},{9,17},{... | collective-permute-start | bytes 393224 | tf_op jit(solution)/shard_map/ppermute | solution.py:487
  20.7 0.1 collective-permute-start.5
  20.8 0.0 copy-start.3
  20.9 0.0 copy-start.2
  20.9 2.3 %collective-permute-start.6 = (bf16[16,32,128]{2,1,0:T(8,128)(2,1)S(1)}, bf16[16,32,128]{2,1,0:T(8,128)(2,1)S(1)}, u32[]{:S(2)}, u32[]{:S(2)}) collective-permute-start(bf16[16,32,128]{2,1,0:T(8,128)(2,1)S(1)} %get-tuple-element.28), channel_id=1, source_target_pairs={{8,20},{20,8},{0,4},{4,0},{12,16},{16,12},{24,28},{28,24},{9,21},{... | collective-permute-start | bytes 393224 | tf_op jit(solution)/shard_map/ppermute | solution.py:487
  23.1 5.0 %local.1.local_ref = f32[64,32,128]{2,1,0:T(8,128)S(1)} custom-call(s32[8,896]{1,0:T(8,128)S(1)} %get-tuple-element.18.words_v, s32[6272]{0:T(1024)S(1)} %get-tuple-element.19.lists_v, bf16[16,32,128]{2,1,0:T(8,128)(2,1)S(1)} %get-tuple-element.22._after, f32[29568,128]{1,0:T(8,128)S(1)} %get-tuple-element.20.rest_0_, f32[29568,128]{1,0:T(8,128)S(1)} %get-tuple-element.21.rest_1_), custom_call_target="tpu_custom_call" | custom-call | flops 3623878656 | bytes 8388608 | tf_op jit(solution)/shard_map/local/pallas_call | solution.py:488
  28.1 0.0 collective-permute-done.2.rest_2_
  28.1 0.8 %arrive.1.local_ref = f32[64,32,128]{2,1,0:T(8,128)S(1)} custom-call(s32[1,128]{1,0:T(1,128)S(1)} %copy-done.1, f32[64,32,128]{2,1,0:T(8,128)S(1)} %local.1.local_ref, bf16[16,32,128]{2,1,0:T(8,128)(2,1)S(1)} %collective-permute-done.rest_0_, bf16[16,32,128]{2,1,0:T(8,128)(2,1)S(1)} %collective-permute-done.1.rest_1_, ...), custom_call_target="tpu_custom_call" | custom-call | tf_op jit(solution)/shard_map/arrive/pallas_call | solution.py:497
  28.9 0.0 collective-permute-done.3.rest_0_
  28.9 0.1 collective-permute-done.4.rest_1_
  29.0 0.0 collective-permute-done.5.rest_2_
  29.0 1.9 %collective-permute-done.6.rest_3_ = bf16[16,32,128]{2,1,0:T(8,128)(2,1)S(1)} collective-permute-done((bf16[16,32,128]{2,1,0:T(8,128)(2,1)S(1)}, bf16[16,32,128]{2,1,0:T(8,128)(2,1)S(1)}, u32[]{:S(2)}, u32[]{:S(2)}) %collective-permute-start.6) | collective-permute-done | bytes 131104 | tf_op jit(solution)/shard_map/ppermute | solution.py:487
  30.9 1.1 %combine.1 = (f32[64,32,128]{2,1,0:T(8,128)S(1)}, f32[2,2048]{1,0:T(2,128)S(1)}) custom-call(s32[1,128]{1,0:T(1,128)S(1)} %copy-done.1, f32[64,32,128]{2,1,0:T(8,128)S(1)} %arrive.1.local_ref, bf16[16,32,128]{2,1,0:T(8,128)(2,1)S(1)} %collective-permute-done.3.rest_0_, bf16[16,32,128]{2,1,0:T(8,128)(2,1)S(1)} %collective-permute-done.4.rest_1_, ...), custom_call_target="tpu_custom_call" | custom-call | tf_op jit(solution)/shard_map/combine/pallas_call | solution.py:515
  32.0 0.1 collective-permute-start.7
  32.0 1.6 %collective-permute-start.8 = (f32[2,2048]{1,0:T(2,128)S(1)}, f32[2,2048]{1,0:T(2,128)S(1)}, u32[]{:S(2)}, u32[]{:S(2)}) collective-permute-start(f32[2,2048]{1,0:T(2,128)S(1)} %get-tuple-element.31._after.s0), channel_id=1, source_target_pairs={{0,2},{1,3},{2,0},{3,1},{4,6},{5,7},{6,4},{7,5},{8,10},{9,11},{10,... | collective-permute-start | bytes 49160 | tf_op jit(solution)/shard_map/ppermute | solution.py:536
  33.6 0.3 collective-permute-start.9
  33.9 0.1 reshape_tile.3.gain_ref
  34.0 0.8 %own.1.own_ref = f32[64,32,128]{2,1,0:T(8,128)S(1)} custom-call(bf16[4096,256]{1,0:T(8,128)(2,1)S(1)} %get-tuple-element.30.f_ref, f32[2,2048]{1,0:T(2,128)S(1)} %get-tuple-element.31._after.s0), custom_call_target="tpu_custom_call" | custom-call | tf_op jit(solution)/shard_map/own/pallas_call | solution.py:527
  34.8 0.0 collective-permute-done.7.s1
  34.8 1.0 %collective-permute-done.8.s2 = f32[2,2048]{1,0:T(2,128)S(1)} collective-permute-done((f32[2,2048]{1,0:T(2,128)S(1)}, f32[2,2048]{1,0:T(2,128)S(1)}, u32[]{:S(2)}, u32[]{:S(2)}) %collective-permute-start.8) | collective-permute-done | bytes 16416 | tf_op jit(solution)/shard_map/ppermute | solution.py:536
  35.8 0.9 %collective-permute-done.9.s3 = f32[2,2048]{1,0:T(2,128)S(1)} collective-permute-done((f32[2,2048]{1,0:T(2,128)S(1)}, f32[2,2048]{1,0:T(2,128)S(1)}, u32[]{:S(2)}, u32[]{:S(2)}) %collective-permute-start.9) | collective-permute-done | bytes 16416 | tf_op jit(solution)/shard_map/ppermute | solution.py:536
  36.8 1.4 %norm.1 = (bf16[64,32,128]{2,1,0:T(8,128)(2,1)S(1)}, bf16[8,32,128]{2,1,0:T(8,128)(2,1)}) custom-call(f32[64,32,128]{2,1,0:T(8,128)S(1)} %get-tuple-element.29.conv_ref, f32[64,32,128]{2,1,0:T(8,128)S(1)} %own.1.own_ref, f32[1,128]{1,0:T(1,128)S(1)} %reshape_tile.3.gain_ref, bf16[32,256]{1,0:T(8,128)(2,1)S(1)} %copy-done, s32[1,8]{1,0:T(1,128)S(1)} %copy-done.3, ...), custom_call_target="tpu_custom_call" | custom-call | tf_op jit(solution)/shard_map/norm/pallas_call | solution.py:539
  38.2 4.2 %all-to-all-start = ((bf16[8,32,128]{2,1,0:T(8,128)(2,1)}), bf16[8,32,128]{2,1,0:T(8,128)(2,1)S(1)}, u32[]{:S(2)}, u32[]{:S(2)}) async-start(bf16[8,32,128]{2,1,0:T(8,128)(2,1)} %get-tuple-element.33), calls=%async_computation | async-start | bytes 131072 | tf_op jit(solution)/shard_map/all_to_all | solution.py:559
  42.4 1.3 %unpack.1 = bf16[64,64,64]{2,1,0:T(8,128)(2,1)} custom-call(bf16[64,32,128]{2,1,0:T(8,128)(2,1)S(1)} %get-tuple-element.32.whole_ref), custom_call_target="tpu_custom_call" | custom-call | tf_op jit(solution)/shard_map/unpack/pallas_call | solution.py:560
  43.7 5.6 %all-to-all-done.landed_ref = bf16[8,32,128]{2,1,0:T(8,128)(2,1)S(1)} async-done(((bf16[8,32,128]{2,1,0:T(8,128)(2,1)}), bf16[8,32,128]{2,1,0:T(8,128)(2,1)S(1)}, u32[]{:S(2)}, u32[]{:S(2)}) %all-to-all-start) | async-done | bytes 65568 | tf_op jit(solution)/shard_map/all_to_all | solution.py:559
  49.3 0.8 %place.1 = bf16[8,64,64]{2,1,0:T(8,128)(2,1)} custom-call(s32[1,8]{1,0:T(1,128)S(1)} %copy-done.2, bf16[8,32,128]{2,1,0:T(8,128)(2,1)S(1)} %all-to-all-done.landed_ref), custom_call_target="tpu_custom_call" | custom-call | tf_op jit(solution)/shard_map/place/pallas_call | solution.py:568
  (11 shorter events, 0.0 us)
Async XLA Ops:
  8.6 12.2 %collective-permute-start = (bf16[16,32,128]{2,1,0:T(8,128)(2,1)S(1)}, bf16[16,32,128]{2,1,0:T(8,128)(2,1)S(1)}, u32[]{:S(2)}, u32[]{:S(2)}) collective-permute-start(bf16[16,32,128]{2,1,0:T(8,128)(2,1)S(1)} %get-tuple-element.23), channel_id=1, source_target_pairs={{0,16},{16,0},{4,20},{20,4},{8,24},{24,8},{12,28},{28,12},{1,17},{... | collective-permute-start | bytes 393224 | tf_op jit(solution)/shard_map/ppermute | solution.py:477
  12.7 8.1 %collective-permute-start.1 = (bf16[16,32,128]{2,1,0:T(8,128)(2,1)S(1)}, bf16[16,32,128]{2,1,0:T(8,128)(2,1)S(1)}, u32[]{:S(2)}, u32[]{:S(2)}) collective-permute-start(bf16[16,32,128]{2,1,0:T(8,128)(2,1)S(1)} %get-tuple-element.24), channel_id=1, source_target_pairs={{0,8},{8,0},{4,12},{12,4},{16,24},{24,16},{20,28},{28,20},{1,9},{9... | collective-permute-start | bytes 393224 | tf_op jit(solution)/shard_map/ppermute | solution.py:477
  14.1 14.0 %collective-permute-start.2 = (bf16[16,32,128]{2,1,0:T(8,128)(2,1)S(1)}, bf16[16,32,128]{2,1,0:T(8,128)(2,1)S(1)}, u32[]{:S(2)}, u32[]{:S(2)}) collective-permute-start(bf16[16,32,128]{2,1,0:T(8,128)(2,1)S(1)} %get-tuple-element.25), channel_id=1, source_target_pairs={{0,4},{4,0},{8,12},{12,8},{16,20},{20,16},{24,28},{28,24},{1,5},{5... | collective-permute-start | bytes 393224 | tf_op jit(solution)/shard_map/ppermute | solution.py:477
  18.0 10.9 %collective-permute-start.3 = (bf16[16,32,128]{2,1,0:T(8,128)(2,1)S(1)}, bf16[16,32,128]{2,1,0:T(8,128)(2,1)S(1)}, u32[]{:S(2)}, u32[]{:S(2)}) collective-permute-start(bf16[16,32,128]{2,1,0:T(8,128)(2,1)S(1)} %get-tuple-element.22._after), channel_id=1, source_target_pairs={{4,16},{16,4},{0,8},{8,0},{12,20},{20,12},{24,28},{28,24},{5,17},{... | collective-permute-start | bytes 393224 | tf_op jit(solution)/shard_map/ppermute | solution.py:487
  19.2 9.8 %collective-permute-start.4 = (bf16[16,32,128]{2,1,0:T(8,128)(2,1)S(1)}, bf16[16,32,128]{2,1,0:T(8,128)(2,1)S(1)}, u32[]{:S(2)}, u32[]{:S(2)}) collective-permute-start(bf16[16,32,128]{2,1,0:T(8,128)(2,1)S(1)} %get-tuple-element.26), channel_id=1, source_target_pairs={{8,16},{16,8},{0,4},{4,0},{12,24},{24,12},{20,28},{28,20},{9,17},{... | collective-permute-start | bytes 393224 | tf_op jit(solution)/shard_map/ppermute | solution.py:487
  20.7 8.3 %collective-permute-start.5 = (bf16[16,32,128]{2,1,0:T(8,128)(2,1)S(1)}, bf16[16,32,128]{2,1,0:T(8,128)(2,1)S(1)}, u32[]{:S(2)}, u32[]{:S(2)}) collective-permute-start(bf16[16,32,128]{2,1,0:T(8,128)(2,1)S(1)} %get-tuple-element.27), channel_id=1, source_target_pairs={{0,12},{12,0},{4,8},{8,4},{16,28},{28,16},{20,24},{24,20},{1,13},{... | collective-permute-start | bytes 393224 | tf_op jit(solution)/shard_map/ppermute | solution.py:487
  20.8 7.3 %copy-start.1 = (s32[1,128]{1,0:T(1,128)S(1)}, s32[1,128]{1,0:T(1,128)}, u32[]{:S(2)}) copy-start(s32[1,128]{1,0:T(1,128)} %list_v.3) | copy-start | bytes 1540
  20.8 13.1 %copy-start.4 = (bf16[64]{0:T(256)(128)(2,1)S(1)}, bf16[64]{0:T(256)(128)(2,1)}, u32[]{:S(2)}) copy-start(bf16[64]{0:T(256)(128)(2,1)} %param.10) | copy-start | bytes 388
  20.8 15.9 %copy-start = (bf16[32,256]{1,0:T(8,128)(2,1)S(1)}, bf16[32,256]{1,0:T(8,128)(2,1)}, u32[]{:S(2)}) copy-start(bf16[32,256]{1,0:T(8,128)(2,1)} %constant.2.clone.pool_ref) | copy-start | bytes 49156
  20.8 15.9 %copy-start.3 = (s32[1,8]{1,0:T(1,128)S(1)}, s32[1,8]{1,0:T(1,128)}, u32[]{:S(2)}) copy-start(s32[1,8]{1,0:T(1,128)} %slot_v.1) | copy-start | bytes 100
  20.9 28.5 %copy-start.2 = (s32[1,8]{1,0:T(1,128)S(1)}, s32[1,8]{1,0:T(1,128)}, u32[]{:S(2)}) copy-start(s32[1,8]{1,0:T(1,128)} %place_ref.1) | copy-start | bytes 100
  20.9 10.0 %collective-permute-start.6 = (bf16[16,32,128]{2,1,0:T(8,128)(2,1)S(1)}, bf16[16,32,128]{2,1,0:T(8,128)(2,1)S(1)}, u32[]{:S(2)}, u32[]{:S(2)}) collective-permute-start(bf16[16,32,128]{2,1,0:T(8,128)(2,1)S(1)} %get-tuple-element.28), channel_id=1, source_target_pairs={{8,20},{20,8},{0,4},{4,0},{12,16},{16,12},{24,28},{28,24},{9,21},{... | collective-permute-start | bytes 393224 | tf_op jit(solution)/shard_map/ppermute | solution.py:487
  32.0 2.9 %collective-permute-start.7 = (f32[2,2048]{1,0:T(2,128)S(1)}, f32[2,2048]{1,0:T(2,128)S(1)}, u32[]{:S(2)}, u32[]{:S(2)}) collective-permute-start(f32[2,2048]{1,0:T(2,128)S(1)} %get-tuple-element.31._after.s0), channel_id=1, source_target_pairs={{0,1},{1,0},{2,3},{3,2},{4,5},{5,4},{6,7},{7,6},{8,9},{9,8},{10,11... | collective-permute-start | bytes 49160 | tf_op jit(solution)/shard_map/ppermute | solution.py:536
  32.0 3.8 %collective-permute-start.8 = (f32[2,2048]{1,0:T(2,128)S(1)}, f32[2,2048]{1,0:T(2,128)S(1)}, u32[]{:S(2)}, u32[]{:S(2)}) collective-permute-start(f32[2,2048]{1,0:T(2,128)S(1)} %get-tuple-element.31._after.s0), channel_id=1, source_target_pairs={{0,2},{1,3},{2,0},{3,1},{4,6},{5,7},{6,4},{7,5},{8,10},{9,11},{10,... | collective-permute-start | bytes 49160 | tf_op jit(solution)/shard_map/ppermute | solution.py:536
  33.6 3.2 %collective-permute-start.9 = (f32[2,2048]{1,0:T(2,128)S(1)}, f32[2,2048]{1,0:T(2,128)S(1)}, u32[]{:S(2)}, u32[]{:S(2)}) collective-permute-start(f32[2,2048]{1,0:T(2,128)S(1)} %get-tuple-element.31._after.s0), channel_id=1, source_target_pairs={{0,3},{1,2},{2,1},{3,0},{4,7},{5,6},{6,5},{7,4},{8,11},{9,10},{10,... | collective-permute-start | bytes 49160 | tf_op jit(solution)/shard_map/ppermute | solution.py:536
  38.2 11.1 %all-to-all-start = ((bf16[8,32,128]{2,1,0:T(8,128)(2,1)}), bf16[8,32,128]{2,1,0:T(8,128)(2,1)S(1)}, u32[]{:S(2)}, u32[]{:S(2)}) async-start(bf16[8,32,128]{2,1,0:T(8,128)(2,1)} %get-tuple-element.33), calls=%async_computation | async-start | bytes 131072 | tf_op jit(solution)/shard_map/all_to_all | solution.py:559
